TPU v7x, 256 devices: a whole 4x4x8 slice. The times are simulated.
256 devices in a mesh: ctx: 64 (over y_hi, z, x), tp: 4 (over y_lo, core).
Axes of the slice: x: 4, y: 4 (y_hi: 2, y_lo: 2; y = y_hi * 2 + y_lo), z: 8, core: 2. Of those that a mesh axis runs over, the one named last changes fastest.
Arguments:
- ids: int32 [32768], P('ctx'), may hold values from 0 to 511
- embed_table: bfloat16 [512, 4096], P(None, 'tp'), may hold values from -126 to 126
- norm_gain: float32 [4096], replicated, may hold values from 0.1 to 1.9
- in_weight: bfloat16 [3, 4096, 4096], P(None, 'ctx', 'tp'), may hold values from -0.09375 to 0.09375
- in_scale: float32 [3, 4096], P(None, 'tp'), may hold values from 0.1 to 1.9
- short_filter: float32 [3, 7, 4096], P(None, None, 'tp'), may hold values from -2.4 to 2.4
- long_filter: float32 [128, 256], P(None, 'tp'), may hold values from -0.9 to 0.9
- decay: float32 [256], P('tp'), may hold values from 0.003 to 0.1
Outputs:
- mixed: bfloat16 [32768, 4096], P('ctx', 'tp')
All inputs are finite; a program needn't handle non-finite values.
Results may differ from a plain program's by a relative error of at most 0.009.
Values may be sent and summed in bfloat16 or wider, within the bound.
No kernel may reach another device: no remote copies, remote signals or barrier semaphores. Data moves between devices by JAX's collectives and lax.ppermute only.
A program may use at most 128 MiB of HBM per device.

v0:
```python
import jax
import jax.numpy as jnp
from jax import lax
from jax.sharding import PartitionSpec as P

GROUP = 16
SHORT_TAPS = 7
LONG_TAPS = 128


def passed_along(value, axis, steps):
    count = lax.axis_size(axis)
    pairs = [(source, (source + steps) % count) for source in range(count)]
    return lax.ppermute(value, axis, pairs)


def toeplitz(long_filter, decay):
    steps = jnp.arange(LONG_TAPS, dtype=jnp.float32)
    taps = (long_filter * jnp.exp(-decay[None, :] * steps[:, None])).astype(jnp.bfloat16)
    offset = (
        jnp.arange(LONG_TAPS, dtype=jnp.int32)[:, None]
        - jnp.arange(LONG_TAPS, dtype=jnp.int32)[None, :]
    )
    lower = jnp.take(taps, jnp.clip(offset, 0, LONG_TAPS - 1), axis=0)
    upper = jnp.take(taps, jnp.clip(offset + LONG_TAPS, 0, LONG_TAPS - 1), axis=0)
    zero_tap = jnp.zeros((), jnp.bfloat16)
    toep_near = jnp.where((offset >= 0)[:, :, None], lower, zero_tap)
    toep_far = jnp.where((offset < 0)[:, :, None], upper, zero_tap)
    return (toep_near, toep_far)


def short_conv(extended, filt, out_len):
    margin = SHORT_TAPS - 1
    total = jnp.zeros((extended.shape[0], out_len, extended.shape[2]), jnp.float32)
    for k in range(SHORT_TAPS):
        window = extended[:, margin - k : margin - k + out_len, :].astype(jnp.float32)
        total = total + filt[:, k, None, :] * window
    return total


def per_device(ids, embed_table, norm_gain, in_weight, in_scale, short_filter, long_filter, decay):
    rows = ids.shape[0]
    vocab = embed_table.shape[0]
    width_local = embed_table.shape[1]
    onehot = (ids[:, None] == lax.iota(jnp.int32, vocab)[None, :]).astype(jnp.bfloat16)
    local = jnp.dot(onehot, embed_table, preferred_element_type=jnp.float32).astype(jnp.bfloat16)
    local_f = local.astype(jnp.float32)
    total = lax.psum(jnp.sum(local_f * local_f, axis=1), "tp")
    full_width = width_local * lax.axis_size("tp")
    gain = lax.dynamic_slice_in_dim(norm_gain, lax.axis_index("tp") * width_local, width_local, 0)
    scaled = local_f * lax.rsqrt(total[:, None] / full_width + 1e-06) * gain[None, :]
    features = lax.all_gather(scaled.astype(jnp.bfloat16), "tp", axis=1, tiled=True)

    def add_one(piece):
        return jnp.dot(features, piece, preferred_element_type=jnp.float32)

    def project_stream(weight):
        return add_one(lax.all_gather(weight, "ctx", axis=0, tiled=True))

    summed = jnp.stack([project_stream(in_weight[p]) for p in range(3)], axis=0)
    proj = (summed * in_scale[:, None, :]).astype(jnp.bfloat16)
    margin = SHORT_TAPS - 1
    before = passed_along(proj[:, rows - margin :, :], "ctx", 1)
    streams = short_conv(jnp.concatenate([before, proj], axis=1), short_filter, rows)
    gate = streams[0]
    inner = (streams[1] * streams[2]).astype(jnp.bfloat16)
    previous = passed_along(inner[rows - LONG_TAPS :], "ctx", 1)
    extended = jnp.concatenate([previous, inner], axis=0)
    groups_local = long_filter.shape[1]
    blocks = extended.reshape(rows // LONG_TAPS + 1, LONG_TAPS, groups_local, GROUP)
    toep_near, toep_far = toeplitz(long_filter, decay)
    conv = jnp.einsum("tsg,bsgc->btgc", toep_near, blocks[1:], preferred_element_type=jnp.float32)
    conv = conv + jnp.einsum(
        "tsg,bsgc->btgc", toep_far, blocks[:-1], preferred_element_type=jnp.float32
    )
    conv = conv.reshape(rows, width_local)
    return (gate * conv).astype(jnp.bfloat16)


def solution(mesh):
    placed = (
        P("ctx"),
        P(None, "tp"),
        P(),
        P(None, "ctx", "tp"),
        P(None, "tp"),
        P(None, None, "tp"),
        P(None, "tp"),
        P("tp"),
    )
    return jax.shard_map(
        per_device, mesh=mesh, in_specs=placed, out_specs=P("ctx", "tp"), check_vma=False
    )
```

profile of v0, /device:TPU:8, one launch (start us, length us, event | category | flops | bytes accessed | tf_op | source)
XLA Modules:
  0.0 709.9 jit_solution(41815037206658026)
XLA Ops:
  6.5 0.0 copy-start
  6.5 0.0 copy-start.5
  6.5 0.0 copy-start.7
  6.5 0.0 copy-start.9
  6.5 0.0 copy-start.6
  6.5 0.0 all-gather.8.cloned.1.call-start
  6.6 1.2 copy-done
  7.8 1.5 fusion.12
  9.3 5.7 psum.7
  15.0 0.7 dynamic_slice.3
  15.7 1.3 fusion.14
  17.0 0.0 all-gather.8.cloned.1.call-update
  17.0 0.0 all-gather.10.cloned.1.call-start
  17.1 0.0 copy-done.5
  17.1 0.8 fusion.56
  17.9 0.0 all-gather.10.cloned.1.call-update
  17.9 0.0 all-gather.12.cloned.1.call-start
  17.9 0.7 all-gather.12.cloned.1.call-update
  18.6 0.0 all-gather.14.cloned.1.call-start
  18.7 0.5 all-gather.14.cloned.1.call-update
  19.2 0.0 copy-done.7
  19.2 0.1 copy.16
  19.3 0.0 copy-done.9
  19.5 0.0 copy-done.6
  19.5 0.1 fusion.57
  19.6 48.7 %all-gather.8.cloned.1.call-done = bf16[512,4096]{1,0:T(8,128)(2,1)} async-done(((bf16[512,1024]{1,0:T(8,128)(2,1)}), bf16[512,4096]{1,0:T(8,128)(2,1)}) %all-gather.8.cloned.1.call-update) | async-done | bytes 4194320 | tf_op jit(solution)/shard_map/all_gather | solution.py:52
  68.4 152.4 %all-gather.10.cloned.1.call-done = bf16[1,4096,1024]{2,1,0:T(8,128)(2,1)} async-done(((bf16[1,64,1024]{2,1,0:T(8,128)(2,1)}), bf16[1,4096,1024]{2,1,0:T(8,128)(2,1)}) %all-gather.10.cloned.1.call-update) | async-done | bytes 8388624 | tf_op jit(solution)/shard_map/all_gather | solution.py:58
  220.8 8.1 %fusion.26 = f32[1,512,1024]{2,1,0:T(8,128)S(1)} fusion(bf16[512,4096]{1,0:T(8,128)(2,1)} %all-gather.8.cloned.1.call-done, bf16[1,4096,1024]{2,1,0:T(8,128)(2,1)} %all-gather.10.cloned.1.call-done), kind=kOutput, calls=%fused_computation.47 | convolution fusion | flops 4294967296 | bytes 14680064 | tf_op jit(solution)/shard_map/dot_general | solution.py:55
  228.9 139.4 %all-gather.12.cloned.1.call-done = bf16[1,4096,1024]{2,1,0:T(8,128)(2,1)} async-done(((bf16[1,64,1024]{2,1,0:T(8,128)(2,1)}), bf16[1,4096,1024]{2,1,0:T(8,128)(2,1)}) %all-gather.12.cloned.1.call-update) | async-done | bytes 8388624 | tf_op jit(solution)/shard_map/all_gather | solution.py:58
  368.3 10.5 %fusion.29 = f32[1,512,1024]{2,1,0:T(8,128)} fusion(bf16[512,4096]{1,0:T(8,128)(2,1)} %all-gather.8.cloned.1.call-done, bf16[1,4096,1024]{2,1,0:T(8,128)(2,1)} %all-gather.12.cloned.1.call-done), kind=kOutput, calls=%fused_computation.48 | convolution fusion | flops 4294967296 | bytes 14680064 | tf_op jit(solution)/shard_map/dot_general | solution.py:55
  378.7 0.0 copy-start.8
  378.7 136.9 %all-gather.14.cloned.1.call-done = bf16[1,4096,1024]{2,1,0:T(8,128)(2,1)} async-done(((bf16[1,64,1024]{2,1,0:T(8,128)(2,1)}), bf16[1,4096,1024]{2,1,0:T(8,128)(2,1)}) %all-gather.14.cloned.1.call-update) | async-done | bytes 8388624 | tf_op jit(solution)/shard_map/all_gather | solution.py:58
  515.6 8.3 %fusion.32 = f32[1,512,1024]{2,1,0:T(8,128)S(1)} fusion(bf16[512,4096]{1,0:T(8,128)(2,1)} %all-gather.8.cloned.1.call-done, bf16[1,4096,1024]{2,1,0:T(8,128)(2,1)} %all-gather.14.cloned.1.call-done), kind=kOutput, calls=%fused_computation.49 | convolution fusion | flops 4294967296 | bytes 14680064 | tf_op jit(solution)/shard_map/dot_general | solution.py:55
  523.9 0.0 copy-done.8
  523.9 0.0 copy-done.4
  523.9 0.9 fusion.6
  524.9 0.0 copy-start.3
  524.9 1.7 copy-done.3
  526.6 1.7 collective-permute-start
  528.3 57.8 %gather_fusion.1 = bf16[16384,64]{1,0:T(8,128)(2,1)} fusion(bf16[128,64]{1,0:T(8,128)(2,1)S(1)} %multiply_convert_fusion, s32[16384]{0:T(1024)S(1)} %bitcast_clamp_fusion), kind=kCustom, calls=%fused_computation.1.clone | custom fusion | bytes 4259840 | tf_op jit(solution)/shard_map/jit(_take)/gather | solution.py:25
  586.2 5.7 copy.20
  591.9 57.8 %gather_fusion = bf16[16384,64]{1,0:T(8,128)(2,1)} fusion(bf16[128,64]{1,0:T(8,128)(2,1)S(1)} %multiply_convert_fusion, s32[16384]{0:T(1024)S(1)} %bitcast_clamp_fusion.1), kind=kCustom, calls=%fused_computation.clone | custom fusion | bytes 4259840 | tf_op jit(solution)/shard_map/jit(_take)/gather | solution.py:24
  649.7 4.8 copy.17
  654.5 0.0 collective-permute-done
  654.5 13.6 %multiply_add_fusion = f32[3,512,1024]{2,1,0:T(8,128)S(1)} fusion(bf16[3,512,1024]{2,1,0:T(8,128)(2,1)} %copy-done.3, bf16[3,6,1024]{2,1,0:T(8,128)(2,1)S(1)} %collective-permute-done, f32[3,1024]{1,0:T(4,128)S(1)} %get-tuple-element.18, f32[3,1024]{1,0:T(4,128)S(1)} %get-tuple-element.19, f32[3,1024]{1,0:T(4,128)S(1)} %get-tuple-element.20, ...), kind=kLoop, calls=%fused_computation.15 | loop fusion | flops 59768832 | bytes 9560064 | tf_op jit(solution)/shard_map/add | solution.py:37
  668.1 0.0 copy-start.2
  668.1 2.6 copy-done.2
  670.8 0.3 fusion.15
  671.1 0.7 slice_bitcast_fusion.1
  671.8 1.3 copy.15
  673.1 1.5 collective-permute-start.1
  674.6 1.3 convert_element_type.62
  675.9 2.5 fusion.62
  678.5 6.9 collective-permute-done.1
  685.4 1.0 pad_maximum_fusion.1
  686.5 2.3 copy.19
  688.7 2.1 slice.97
  690.9 3.5 fusion.18
  694.3 1.6 add_bitcast_fusion
  695.9 1.0 copy.22
  696.9 1.6 copy.46
  698.5 2.0 copy.23
  700.5 2.9 fusion.17
  703.3 0.0 copy-done.1
  (14 shorter events, 0.3 us)
Async XLA Ops:
  6.5 1.2 copy-start
  6.5 10.5 %copy-start.5 = (bf16[3,64,1024]{2,1,0:T(8,128)(2,1)S(1)}, bf16[3,64,1024]{2,1,0:T(8,128)(2,1)}, u32[]{:S(2)}) copy-start(bf16[3,64,1024]{2,1,0:T(8,128)(2,1)} %param.13) | copy-start | bytes 1179652
  6.5 12.7 %copy-start.7 = (f32[128,64]{0,1:T(8,128)S(1)}, f32[128,64]{0,1:T(8,128)}, u32[]{:S(2)}) copy-start(f32[128,64]{0,1:T(8,128)} %param.16) | copy-start | bytes 98308
  6.5 12.8 %copy-start.9 = (f32[64]{0:T(128)S(1)}, f32[64]{0:T(128)}, u32[]{:S(2)}) copy-start(f32[64]{0:T(128)} %param.17) | copy-start | bytes 772
  6.5 12.9 %copy-start.6 = (f32[3,7,1024]{2,1,0:T(8,128)S(1)}, f32[3,7,1024]{2,1,0:T(8,128)}, u32[]{:S(2)}) copy-start(f32[3,7,1024]{2,1,0:T(8,128)} %param.15) | copy-start | bytes 258052
  6.5 61.8 %all-gather.8.cloned.1.call-start = ((), (), s32[]{:S(2)}) async-start(), calls=%async_computation | async-start | bytes 5242880 | tf_op jit(solution)/shard_map/all_gather | solution.py:52
  17.0 203.7 %all-gather.10.cloned.1.call-start = ((), (), s32[]{:S(2)}) async-start(), calls=%async_computation.1 | async-start | bytes 8519680 | tf_op jit(solution)/shard_map/all_gather | solution.py:58
  17.9 350.4 %all-gather.12.cloned.1.call-start = ((), (), s32[]{:S(2)}) async-start(), calls=%async_computation.2 | async-start | bytes 8519680 | tf_op jit(solution)/shard_map/all_gather | solution.py:58
  18.6 497.0 %all-gather.14.cloned.1.call-start = ((), (), s32[]{:S(2)}) async-start(), calls=%async_computation.3 | async-start | bytes 8519680 | tf_op jit(solution)/shard_map/all_gather | solution.py:58
  378.7 145.2 %copy-start.8 = (f32[3,1024]{1,0:T(4,128)S(1)}, f32[3,1024]{1,0:T(4,128)}, u32[]{:S(2)}) copy-start(f32[3,1024]{1,0:T(4,128)} %param.14) | copy-start | bytes 36868
  515.6 8.3 %copy-start.4 = (f32[1,512,1024]{2,1,0:T(8,128)S(1)}, f32[1,512,1024]{2,1,0:T(8,128)}, u32[]{:S(2)}) copy-start(f32[1,512,1024]{2,1,0:T(8,128)} %fusion.29) | copy-start | bytes 6291460
  524.9 1.7 copy-start.3
  526.6 128.0 %collective-permute-start = (bf16[3,6,1024]{2,1,0:T(8,128)(2,1)S(1)}, bf16[3,6,1024]{2,1,0:T(8,128)(2,1)S(1)}, u32[]{:S(2)}, u32[]{:S(2)}) collective-permute-start(bf16[3,6,1024]{2,1,0:T(8,128)(2,1)S(1)} %slice.102), channel_id=1, source_target_pairs={{0,4},{4,8},{8,12},{12,16},{16,20},{20,24},{24,28},{28,32},{32,36}... | collective-permute-start | bytes 110600 | tf_op jit(solution)/shard_map/ppermute | solution.py:14
  668.1 2.7 copy-start.2
  673.1 12.3 %collective-permute-start.1 = (bf16[128,1024]{1,0:T(8,128)(2,1)}, bf16[128,1024]{1,0:T(8,128)(2,1)S(1)}, u32[]{:S(2)}, u32[]{:S(2)}) collective-permute-start(bf16[128,1024]{1,0:T(8,128)(2,1)} %slice_bitcast_fusion.1), channel_id=1, source_target_pairs={{0,4},{4,8},{8,12},{12,16},{16,20},{20,24},{24,28},{28,32},{32,36}... | collective-permute-start | bytes 786440 | tf_op jit(solution)/shard_map/ppermute | solution.py:14
  698.5 4.9 copy-start.1
Sparse Core Ops, SparseCore 0:
  17.1 51.1 all-gather.7
  71.9 148.8 all-gather.9
  224.2 143.9 all-gather.11
  371.6 143.9 all-gather.13
where the time goes:
time: 710 us
  waiting for transfers between devices  486 us (68%)
  local copies, waits for them, and re-layouts  146 us (21%)
  matrix products  33.5 us (5%)
  other arithmetic  22.8 us (3%)
  between operations  13.4 us (2%)
    all_gather x3, waiting for transfers between devices, project_stream(): return add_one(lax.all_gather(weight, 'ctx', axis=0, tiled=True))  429 us
    gather x2, local copies, waits for them, and re-layouts, toeplitz(): jnp.take(taps, jnp.clip(offset + LONG_TAPS, 0, LONG_TAPS - 1), axis=0)  63.5 us
    gather x2, local copies, waits for them, and re-layouts, toeplitz(): lower = jnp.take(taps, jnp.clip(offset, 0, LONG_TAPS - 1), axis=0)  62.6 us
    all_gather x1, waiting for transfers between devices, per_device(): lax.all_gather(scaled.astype(jnp.bfloat16), 'tp', axis=1, tiled=True)  48.7 us
    dot_general x3, matrix products, add_one(): return jnp.dot(features, piece, preferred_element_type=jnp.float32)  26.9 us
  transfers between devices with their start and end apart: 6, of which 5 were waited for; matrix products, arithmetic and copies ran while one was open for 21% of the time, Pallas kernels for 0%

commit v1 on v0

v1 whole, which is shorter than its diff:
```python
import jax
import jax.numpy as jnp
import numpy as np
from jax import lax
from jax.experimental import pallas as pl
from jax.experimental.pallas import tpu as pltpu
from jax.sharding import Mesh, PartitionSpec as P

GROUP = 16
SHORT_TAPS = 7
LONG_TAPS = 128
LANES = 128
HALO = 144
STREAMS = 3
BF = jnp.bfloat16
F32 = jnp.float32


def shifted(value, axis, steps):
    count = lax.axis_size(axis)
    pairs = [(source, (source + steps) % count) for source in range(count)]
    return lax.ppermute(value, axis, pairs)


def partial_kernel(normed_ref, pieces_ref, out_ref, weight_ref):
    rows = weight_ref.shape[0] // pieces_ref.shape[0]
    for source in range(pieces_ref.shape[0]):
        for p in range(STREAMS):
            weight_ref[source * rows : (source + 1) * rows, p * LANES : (p + 1) * LANES] = (
                pieces_ref[source, p * rows : (p + 1) * rows, :]
            )
    out_ref[...] = jnp.dot(
        normed_ref[...], weight_ref[...], preferred_element_type=F32
    ).astype(BF)


def partial_table(normed, pieces, rows):
    vocab, depth = normed.shape
    return pl.pallas_call(
        partial_kernel,
        out_shape=jax.ShapeDtypeStruct((vocab, STREAMS * LANES), BF),
        in_specs=[pl.BlockSpec(memory_space=pltpu.VMEM)] * 2,
        out_specs=pl.BlockSpec(memory_space=pltpu.VMEM),
        scratch_shapes=[pltpu.VMEM((depth, STREAMS * LANES), BF)],
        cost_estimate=pl.CostEstimate(
            flops=2 * vocab * depth * STREAMS * LANES, bytes_accessed=1500000, transcendentals=0
        ),
        name="partial_table",
    )(normed, pieces)


def toeplitz_kernel(taps_ref, out_ref):
    for g in range(taps_ref.shape[0]):
        row = jnp.broadcast_to(taps_ref[g : g + 1, :], (LONG_TAPS, 2 * LONG_TAPS))
        out_ref[g * LONG_TAPS : (g + 1) * LONG_TAPS, :] = pltpu.roll(
            row, 0, 1, stride=1, stride_axis=0
        ).astype(BF)


def toeplitz(taps_row):
    groups = taps_row.shape[0]
    return pl.pallas_call(
        toeplitz_kernel,
        out_shape=jax.ShapeDtypeStruct((groups * LONG_TAPS, 2 * LONG_TAPS), BF),
        in_specs=[pl.BlockSpec(memory_space=pltpu.VMEM)],
        out_specs=pl.BlockSpec(memory_space=pltpu.VMEM),
        cost_estimate=pl.CostEstimate(flops=1000000, bytes_accessed=530000, transcendentals=0),
        name="toeplitz",
    )(taps_row)


def mix_kernel(tile_ref, ids_ref, *refs):
    tables = refs[:8]
    filt_ref, toep_ref, out_ref, table_ref, proj_ref, inner_ref = refs[8:]
    piece = tables[0].shape[0]
    vocab = table_ref.shape[0]
    extent = ids_ref.shape[1]
    tokens = out_ref.shape[1]

    @pl.when(pl.program_id(0) == 0)
    def _():
        for j in range(8):
            table_ref[j * piece : (j + 1) * piece, :] = tables[j][...]

    hot = ids_ref[0] == lax.broadcasted_iota(jnp.int32, (extent, vocab), 1)
    proj = jnp.dot(
        jnp.where(hot, 1.0, 0.0).astype(BF), table_ref[...], preferred_element_type=F32
    )
    for p in range(STREAMS):
        proj_ref[p] = proj[:, p * LANES : (p + 1) * LANES]

    def short(p, start):
        total = jnp.zeros((extent - start, LANES), F32)
        for k in range(SHORT_TAPS):
            total = total + filt_ref[p, k : k + 1, :] * proj_ref[p, start - k : extent - k, :]
        return total

    first = HALO - LONG_TAPS
    inner_ref[...] = (short(1, first) * short(2, first)).astype(BF)
    gate = short(0, HALO)
    lane_group = lax.broadcasted_iota(jnp.int32, (LONG_TAPS, LANES), 1) // GROUP
    for pair in range(tokens // (2 * LONG_TAPS)):
        base = pair * 2 * LONG_TAPS
        window = jnp.concatenate(
            [
                inner_ref[base : base + 2 * LONG_TAPS, :],
                inner_ref[base + LONG_TAPS : base + 3 * LONG_TAPS, :],
            ],
            axis=1,
        )
        full = jnp.dot(toep_ref[...], window, preferred_element_type=F32)
        for half in range(2):
            conv = full[:LONG_TAPS, half * LANES : (half + 1) * LANES]
            for g in range(1, LANES // GROUP):
                conv = jnp.where(
                    lane_group == g,
                    full[g * LONG_TAPS : (g + 1) * LONG_TAPS, half * LANES : (half + 1) * LANES],
                    conv,
                )
            at = base + half * LONG_TAPS
            out_ref[0, at : at + LONG_TAPS, :] = (gate[at : at + LONG_TAPS] * conv).astype(BF)


def mixed_blocks(tile, windows, tables, short_filter, toep):
    blocks, extent, _ = windows.shape
    tokens = extent - HALO
    vocab = 8 * tables[0].shape[0]
    whole = pl.BlockSpec(tables[0].shape, lambda i, t: (0, 0))
    return pl.pallas_call(
        mix_kernel,
        out_shape=jax.ShapeDtypeStruct((blocks, tokens, LANES), BF),
        grid_spec=pltpu.PrefetchScalarGridSpec(
            num_scalar_prefetch=1,
            grid=(blocks,),
            in_specs=[pl.BlockSpec((1, extent, 1), lambda i, t: (i, 0, 0))]
            + [whole] * 8
            + [
                pl.BlockSpec((STREAMS, SHORT_TAPS, LANES), lambda i, t: (0, 0, t[0])),
                pl.BlockSpec(toep.shape, lambda i, t: (0, 0)),
            ],
            out_specs=pl.BlockSpec((1, tokens, LANES), lambda i, t: (i, 0, 0)),
            scratch_shapes=[
                pltpu.VMEM((vocab, STREAMS * LANES), BF),
                pltpu.VMEM((STREAMS, extent, LANES), F32),
                pltpu.VMEM((tokens + LONG_TAPS, LANES), BF),
            ],
        ),
        cost_estimate=pl.CostEstimate(
            flops=5000000000, bytes_accessed=4000000, transcendentals=0
        ),
        name="mixed_blocks",
    )(tile, windows, *tables, short_filter, toep)


def per_device(ids, embed_table, norm_gain, in_weight, in_scale, short_filter, long_filter, decay):
    tokens = ids.shape[0]
    vocab, width_local = embed_table.shape
    rows = in_weight.shape[1]
    spread = ("yh", "x")
    tiles = width_local // LANES
    z = lax.axis_index("z")
    yl = lax.axis_index("yl")
    core = lax.axis_index("core")
    tile = lax.axis_index("yh") * 4 + lax.axis_index("x")
    z_count = lax.axis_size("z")

    chunk = 4 * rows
    own = lax.dynamic_slice_in_dim(embed_table, (z % 4) * chunk, chunk, 1)
    tp = ("z", "yl", "core")

    def spot(zi, yi, ci):
        return (zi * 2 + yi) * 2 + ci

    holders = [(zi, yi, zi // 4) for zi in range(z_count) for yi in range(2)]
    to_core = [(spot(a, b, c), spot(a, b, 1 - c)) for a, b, c in holders]
    to_chip = [(spot(a, b, c), spot(a, 1 - b, c)) for a, b, c in holders]
    to_both = [(spot(a, b, c), spot(a, 1 - b, 1 - c)) for a, b, c in holders]
    got_core = lax.ppermute(own, tp, to_core)
    got_chip = lax.ppermute(own, tp, to_chip)
    got_both = lax.ppermute(own, tp, to_both)
    local_f = embed_table.astype(F32)
    squares = jnp.sum(local_f * local_f, axis=1)
    others = [shifted(squares, ("yl", "core"), s) for s in (1, 2, 3)]

    by_tile = in_weight.reshape(STREAMS * rows, tiles, LANES).transpose(1, 0, 2)
    coded = jnp.concatenate([ids >> 4, ids & 15]).astype(BF).reshape(1, -1, LANES)
    load = jnp.concatenate(
        [by_tile, jnp.broadcast_to(coded, (tiles,) + coded.shape[1:])], axis=1
    )
    pieces = lax.all_to_all(load, spread, 0, 0, tiled=True)

    total = squares + others[0] + others[1] + others[2]
    mine = core == z // 4
    near = jnp.where(mine, own, got_core)
    far = jnp.where(mine, got_chip, got_both)
    low = jnp.where(yl == 0, near, far)
    high = jnp.where(yl == 0, far, near)
    features = jnp.concatenate([low, high], axis=1).astype(F32)
    full_width = norm_gain.shape[0]
    gain = jnp.concatenate(
        [
            lax.dynamic_slice_in_dim(norm_gain, z * chunk, chunk, 0),
            lax.dynamic_slice_in_dim(norm_gain, full_width // 2 + z * chunk, chunk, 0),
        ]
    )
    normed = (features * lax.rsqrt(total[:, None] / full_width + 1e-06) * gain[None, :]).astype(BF)

    partial = partial_table(normed, pieces, rows)
    swapped = lax.all_to_all(
        partial.reshape(z_count, vocab // z_count, STREAMS * LANES), "z", 0, 0, tiled=True
    )
    scale = lax.dynamic_slice_in_dim(in_scale, tile * LANES, LANES, 1).reshape(1, STREAMS * LANES)
    piece = (jnp.sum(swapped.astype(F32), axis=0) * scale).astype(BF)
    ups, downs = [piece], []
    for _ in range(4):
        ups.append(shifted(ups[-1], "z", 1))
    last = piece
    for _ in range(3):
        last = shifted(last, "z", -1)
        downs.append(last)
    tables = ups + downs[::-1]

    got = pieces[:, STREAMS * rows :, :].astype(jnp.int32).reshape(tiles, 2, tokens)
    block_ids = got[:, 0] * 16 + got[:, 1]
    tails = block_ids[:, tokens - HALO :]
    edges = jnp.stack([tails[3], tails[7]])
    before = shifted(edges, "z", 1)
    before = jnp.where(z == 0, before[::-1], before)
    lead = jnp.concatenate([before[:1], tails[0:3], before[1:], tails[4:7]], axis=0)
    windows = jnp.concatenate([lead, block_ids], axis=1)
    share = vocab // z_count
    windows = ((z - windows // share) % z_count) * share + windows % share

    groups = LANES // GROUP
    steps = jnp.arange(LONG_TAPS, dtype=F32)
    filt = lax.dynamic_slice_in_dim(long_filter, tile * groups, groups, 1)
    rate = lax.dynamic_slice_in_dim(decay, tile * groups, groups, 0)
    taps = (filt * jnp.exp(-rate[None, :] * steps[:, None])).astype(BF).astype(F32)
    taps_row = jnp.pad(taps[::-1].T, ((0, 0), (1, LONG_TAPS - 1)))

    blocks = mixed_blocks(
        tile.reshape(1).astype(jnp.int32), windows[:, :, None], tables, short_filter,
        toeplitz(taps_row),
    )
    result = lax.all_to_all(blocks, spread, 0, 0, tiled=True)
    return result.transpose(1, 0, 2).reshape(tokens, width_local)


def solution(mesh):
    fine = Mesh(mesh.devices.reshape(2, 8, 4, 2, 2), ("yh", "z", "x", "yl", "core"))
    ctx = ("yh", "z", "x")
    tp = ("yl", "core")
    placed = (
        P(ctx),
        P(None, tp),
        P(),
        P(None, ctx, tp),
        P(None, tp),
        P(None, None, tp),
        P(None, tp),
        P(tp),
    )
    return jax.shard_map(
        per_device, mesh=fine, in_specs=placed, out_specs=P(ctx, tp), check_vma=False
    )
```

time: 710 us -> 110 us (0.15)
  waiting for transfers between devices: 486 us -> 20.3 us
  local copies, waits for them, and re-layouts: 146 us -> 9.39 us
  matrix products: 33.5 us -> 0 us
  starting transfers between devices: 3.36 us -> 31.9 us
  Pallas kernels: 0 us -> 15.9 us
  blocking collectives: 5.73 us -> 19.9 us
  between operations: 13.4 us -> 0.28 us
  other arithmetic: 22.8 us -> 11 us
    all_gather x4 -> x0, waiting for transfers between devices: 477 us -> none  [the longest x3 429 us: project_stream(): return add_one(lax.all_gather(weight, 'ctx', axis=0, tiled=True))]
    gather x4 -> x0, local copies, waits for them, and re-layouts: 126 us -> none  [the longest x2 63.5 us: toeplitz(): jnp.take(taps, jnp.clip(offset + LONG_TAPS, 0, LONG_TAPS - 1), axis=0)]
    dot_general x6 -> x0, matrix products: 33.5 us -> none  [the longest x3 26.9 us: add_one(): return jnp.dot(features, piece, preferred_element_type=jnp.float32)]
    all_to_all x0 -> x1, blocking collectives: none -> 19.9 us  [per_device(): result = lax.all_to_all(blocks, spread, 0, 0, tiled=True)]
    ppermute x2 -> x14, starting transfers between devices: 3.2 us -> 20.1 us  [the longest x11 14.6 us: shifted(): return lax.ppermute(value, axis, pairs)]
    pallas_call x0 -> x3, Pallas kernels: none -> 15.9 us  [the longest x1 11.9 us: mixed_blocks(): pl.pallas_call(mix_kernel, out_shape=jax.ShapeDtypeStruct((blocks, tokens...]
    all_to_all x0 -> x2, starting transfers between devices: none -> 11.8 us  [the longest x1 6.62 us: per_device(): lax.all_to_all(partial.reshape(z_count, vocab // z_count, STREAMS * LANES...]
    add x1 -> x2, other arithmetic: 13.6 us -> 4.76 us  [the longest x1 4.74 us: per_device(): windows = (z - windows // share) % z_count * share + windows % share]
  transfers between devices with their start and end apart: 6 -> 16, of which waited for: 5 -> 7; matrix products, arithmetic and copies ran while one was open for 21% -> 14% of each run, Pallas kernels for 0% -> 2%
where the time goes in v1:
time: 110 us; the launch traced here: 109 us
  starting transfers between devices  31.9 us (29%)
  waiting for transfers between devices  20.3 us (18%)
  blocking collectives  19.9 us (18%)
  Pallas kernels  15.9 us (14%)
  other arithmetic  11 us (10%)
  local copies, waits for them, and re-layouts  9.39 us (9%)
    all_to_all x1, blocking collectives, per_device(): result = lax.all_to_all(blocks, spread, 0, 0, tiled=True)  19.9 us
    ppermute x11, starting transfers between devices, shifted(): return lax.ppermute(value, axis, pairs)  14.6 us
    ppermute x11, waiting for transfers between devices, shifted(): return lax.ppermute(value, axis, pairs)  13.3 us
    pallas_call x1, Pallas kernels, mixed_blocks(): pl.pallas_call(mix_kernel, out_shape=jax.ShapeDtypeStruct((blocks, tokens...  11.9 us
    all_to_all x1, starting transfers between devices, per_device(): lax.all_to_all(partial.reshape(z_count, vocab // z_count, STREAMS * LANES...  6.62 us
    all_to_all x1, starting transfers between devices, per_device(): pieces = lax.all_to_all(load, spread, 0, 0, tiled=True)  5.21 us
    all_to_all x1, waiting for transfers between devices, per_device(): lax.all_to_all(partial.reshape(z_count, vocab // z_count, STREAMS * LANES...  5.03 us
    add x1, other arithmetic, per_device(): windows = (z - windows // share) % z_count * share + windows % share  4.74 us
  transfers between devices with their start and end apart: 16, of which 7 were waited for; matrix products, arithmetic and copies ran while one was open for 14% of the time, Pallas kernels for 2%

profile of v1, /device:TPU:8, one launch (start us, length us, event | category | flops | bytes accessed | tf_op | source)
XLA Modules:
  0.0 108.7 jit_solution(10284723902632836456)
XLA Ops:
  0.0 0.0 copy-start
  0.0 1.5 %multiply_reduce_fusion = f32[512]{0:T(512)S(1)} fusion(bf16[512,1024]{1,0:T(8,128)(2,1)} %param.9), kind=kLoop, calls=%fused_computation.14 | loop fusion | flops 1572352 | bytes 1050624 | tf_op jit(solution)/shard_map/reduce_sum | solution.py:182
  1.5 0.1 collective-permute-start.6
  1.6 2.3 %collective-permute-start.5 = (f32[512]{0:T(512)S(1)}, f32[512]{0:T(512)S(1)}, u32[]{:S(2)}, u32[]{:S(2)}) collective-permute-start(f32[512]{0:T(512)S(1)} %multiply_reduce_fusion), channel_id=1, source_target_pairs={{0,2},{1,3},{2,0},{3,1},{4,6},{5,7},{6,4},{7,5},{8,10},{9,11},{10,... | collective-permute-start | bytes 6152 | tf_op jit(solution)/shard_map/ppermute | solution.py:22
  3.9 0.1 collective-permute-start.4
  4.0 1.0 constant_dynamic-slice_fusion
  5.0 2.2 %collective-permute-start.2 = (bf16[512,256]{1,0:T(8,128)(2,1)S(1)}, bf16[512,256]{1,0:T(8,128)(2,1)S(1)}, u32[]{:S(2)}, u32[]{:S(2)}) collective-permute-start(bf16[512,256]{1,0:T(8,128)(2,1)S(1)} %constant_dynamic-slice_fusion), channel_id=1, source_target_pairs={{0,2},{2,0},{16,18},{18,16},{32,34},{34,32},{48,50},{50,48},{65,67... | collective-permute-start | bytes 786440 | tf_op jit(solution)/shard_map/ppermute | solution.py:179
  7.2 2.0 %collective-permute-start.3 = (bf16[512,256]{1,0:T(8,128)(2,1)S(1)}, bf16[512,256]{1,0:T(8,128)(2,1)S(1)}, u32[]{:S(2)}, u32[]{:S(2)}) collective-permute-start(bf16[512,256]{1,0:T(8,128)(2,1)S(1)} %constant_dynamic-slice_fusion), channel_id=1, source_target_pairs={{0,3},{2,1},{16,19},{18,17},{32,35},{34,33},{48,51},{50,49},{65,66... | collective-permute-start | bytes 786440 | tf_op jit(solution)/shard_map/ppermute | solution.py:180
  9.2 0.7 fusion.6
  9.9 1.1 copy.46
  11.0 0.1 copy.50
  11.1 0.8 pad_maximum_fusion
  11.8 5.2 %all-to-all-start = ((bf16[8,200,128]{2,1,0:T(8,128)(2,1)}), bf16[8,200,128]{2,1,0:T(8,128)(2,1)S(1)}, u32[]{:S(2)}, u32[]{:S(2)}) async-start(bf16[8,200,128]{2,1,0:T(8,128)(2,1)} %pad_maximum_fusion), calls=%async_computation | async-start | bytes 819200 | tf_op jit(solution)/shard_map/all_to_all | solution.py:190
  17.1 0.1 dynamic-slice_negate_fusion
  17.1 0.8 fusion.5
  17.9 0.8 fusion.8
  18.7 0.0 collective-permute-done.6
  18.7 1.3 %collective-permute-start.1 = (bf16[512,256]{1,0:T(8,128)(2,1)S(1)}, bf16[512,256]{1,0:T(8,128)(2,1)S(1)}, u32[]{:S(2)}, u32[]{:S(2)}) collective-permute-start(bf16[512,256]{1,0:T(8,128)(2,1)S(1)} %constant_dynamic-slice_fusion), channel_id=1, source_target_pairs={{0,1},{2,3},{16,17},{18,19},{32,33},{34,35},{48,49},{50,51},{65,64... | collective-permute-start | bytes 786440 | tf_op jit(solution)/shard_map/ppermute | solution.py:178
  20.1 0.1 rev.7
  20.1 0.7 pad.4.taps_ref
  20.8 1.7 %toeplitz.1.refs_9_ = bf16[1024,256]{1,0:T(8,128)(2,1)} custom-call(f32[8,256]{1,0:T(8,128)} %pad.4.taps_ref), custom_call_target="tpu_custom_call" | custom-call | flops 1000000 | bytes 530000 | tf_op jit(solution)/shard_map/toeplitz/pallas_call | solution.py:62
  22.5 0.0 collective-permute-done.5
  22.5 0.0 collective-permute-done.4
  22.5 0.0 collective-permute-done.2
  22.5 0.0 collective-permute-done.3
  22.5 0.0 collective-permute-done.1
  22.5 1.1 %broadcast_select_fusion.3 = (bf16[512,256]{1,0:T(8,128)(2,1)S(1)}, bf16[512,256]{1,0:T(8,128)(2,1)S(1)}) fusion(pred[]{:T(512)S(6)} %eq.16, bf16[512,256]{1,0:T(8,128)(2,1)S(1)} %collective-permute-done.1, pred[]{:T(512)S(6)} %eq.17, bf16[512,256]{1,0:T(8,128)(2,1)S(1)} %collective-permute-done.2, bf16[512,256]{1,0:T(8,128)(2,1)S(1)} %collective-permute-done.3, ...), kind=kLoop, calls=%fused_computation.22 | loop fusion | flops 524288 | bytes 1572870 | tf_op jit(solution)/shard_map/jit(_where)/select_n | solution.py:196
  23.7 1.0 multiply_convert_fusion.normed_ref
  24.6 2.0 %all-to-all-done.pieces_ref = bf16[8,200,128]{2,1,0:T(8,128)(2,1)S(1)} async-done(((bf16[8,200,128]{2,1,0:T(8,128)(2,1)}), bf16[8,200,128]{2,1,0:T(8,128)(2,1)S(1)}, u32[]{:S(2)}, u32[]{:S(2)}) %all-to-all-start) | async-done | bytes 409632 | tf_op jit(solution)/shard_map/all_to_all | solution.py:190
  26.7 0.1 fusion.10
  26.8 0.6 copy-done.1
  27.4 2.4 %partial_table.1 = bf16[512,384]{1,0:T(8,128)(2,1)} custom-call(bf16[512,512]{1,0:T(8,128)(2,1)} %multiply_convert_fusion.normed_ref, bf16[8,200,128]{2,1,0:T(8,128)(2,1)} %copy-done.1), custom_call_target="tpu_custom_call" | custom-call | flops 201326592 | bytes 1500000 | tf_op jit(solution)/shard_map/partial_table/pallas_call | solution.py:39
  29.8 6.6 %all-to-all-start.1 = ((bf16[8,64,384]{2,1,0:T(8,128)(2,1)}), bf16[8,64,384]{2,1,0:T(8,128)(2,1)S(1)}, u32[]{:S(2)}, u32[]{:S(2)}) async-start(bf16[8,64,384]{2,1,0:T(8,128)(2,1)} %bitcast.28), calls=%async_computation.1 | async-start | bytes 786432 | tf_op jit(solution)/shard_map/all_to_all | solution.py:209
  36.4 2.1 %collective-permute-start = (s32[2,144]{1,0:T(2,128)S(1)}, s32[2,144]{1,0:T(2,128)S(1)}, u32[]{:S(2)}, u32[]{:S(2)}) collective-permute-start(s32[2,144]{1,0:T(2,128)S(1)} %pad_add_fusion.1), channel_id=1, source_target_pairs={{0,16},{16,32},{32,48},{48,64},{64,80},{80,96},{96,112},{112,0},{1... | collective-permute-start | bytes 3464 | tf_op jit(solution)/shard_map/ppermute | solution.py:22
  38.5 0.1 fusion.9
  38.6 8.8 %collective-permute-done = s32[2,144]{1,0:T(2,128)S(1)} collective-permute-done((s32[2,144]{1,0:T(2,128)S(1)}, s32[2,144]{1,0:T(2,128)S(1)}, u32[]{:S(2)}, u32[]{:S(2)}) %collective-permute-start) | collective-permute-done | bytes 1184 | tf_op jit(solution)/shard_map/ppermute | solution.py:22
  47.4 5.0 %all-to-all-done.1 = bf16[8,64,384]{2,1,0:T(8,128)(2,1)S(1)} async-done(((bf16[8,64,384]{2,1,0:T(8,128)(2,1)}), bf16[8,64,384]{2,1,0:T(8,128)(2,1)S(1)}, u32[]{:S(2)}, u32[]{:S(2)}) %all-to-all-start.1) | async-done | bytes 393248 | tf_op jit(solution)/shard_map/all_to_all | solution.py:209
  52.5 0.1 convert_reduce_fusion
  52.5 0.0 copy-start.2
  52.6 0.4 collective-permute-start.7
  53.0 3.0 %collective-permute-start.11 = (bf16[64,384]{1,0:T(8,128)(2,1)S(1)}, bf16[64,384]{1,0:T(8,128)(2,1)S(1)}, u32[]{:S(2)}, u32[]{:S(2)}) collective-permute-start(bf16[64,384]{1,0:T(8,128)(2,1)S(1)} %multiply_convert_fusion.1.refs_0_), channel_id=1, source_target_pairs={{0,112},{16,0},{32,16},{48,32},{64,48},{80,64},{96,80},{112,96},{1... | collective-permute-start | bytes 147464 | tf_op jit(solution)/shard_map/ppermute | solution.py:22
  56.0 2.0 %collective-permute-done.7.refs_1_ = bf16[64,384]{1,0:T(8,128)(2,1)S(1)} collective-permute-done((bf16[64,384]{1,0:T(8,128)(2,1)S(1)}, bf16[64,384]{1,0:T(8,128)(2,1)S(1)}, u32[]{:S(2)}, u32[]{:S(2)}) %collective-permute-start.7) | collective-permute-done | bytes 49184 | tf_op jit(solution)/shard_map/ppermute | solution.py:22
  57.9 0.0 collective-permute-start.8
  57.9 0.1 pad_add_fusion
  58.0 0.0 collective-permute-done.11.refs_7_
  58.0 3.3 %collective-permute-start.12 = (bf16[64,384]{1,0:T(8,128)(2,1)S(1)}, bf16[64,384]{1,0:T(8,128)(2,1)}, u32[]{:S(2)}, u32[]{:S(2)}) collective-permute-start(bf16[64,384]{1,0:T(8,128)(2,1)S(1)} %collective-permute-done.11.refs_7_), channel_id=1, source_target_pairs={{0,112},{16,0},{32,16},{48,32},{64,48},{80,64},{96,80},{112,96},{1... | collective-permute-start | bytes 147464 | tf_op jit(solution)/shard_map/ppermute | solution.py:22
  61.3 2.0 %collective-permute-done.8.refs_2_ = bf16[64,384]{1,0:T(8,128)(2,1)} collective-permute-done((bf16[64,384]{1,0:T(8,128)(2,1)S(1)}, bf16[64,384]{1,0:T(8,128)(2,1)}, u32[]{:S(2)}, u32[]{:S(2)}) %collective-permute-start.8) | collective-permute-done | bytes 49184 | tf_op jit(solution)/shard_map/ppermute | solution.py:22
  63.3 0.0 collective-permute-start.9
  63.3 0.1 broadcast_compare_fusion
  63.4 1.1 copy.27
  64.5 0.8 copy.22
  65.3 0.0 collective-permute-done.12.refs_6_
  65.3 3.3 %collective-permute-start.13 = (bf16[64,384]{1,0:T(8,128)(2,1)}, bf16[64,384]{1,0:T(8,128)(2,1)S(1)}, u32[]{:S(2)}, u32[]{:S(2)}) collective-permute-start(bf16[64,384]{1,0:T(8,128)(2,1)} %collective-permute-done.12.refs_6_), channel_id=1, source_target_pairs={{0,112},{16,0},{32,16},{48,32},{64,48},{80,64},{96,80},{112,96},{1... | collective-permute-start | bytes 147464 | tf_op jit(solution)/shard_map/ppermute | solution.py:22
  68.6 0.3 collective-permute-done.9.refs_3_
  69.0 0.0 collective-permute-start.10
  69.0 4.7 %fusion.3.ids_ref = s32[8,656,1]{2,1,0:T(8,128)} fusion(pred[8,656,1]{2,1,0:T(8,128)(4,1)S(1)} %copy.27, s32[8,656,1]{2,1,0:T(8,128)S(1)} %copy.22, s32[]{:T(128)S(6)} %axis_index.59), kind=kLoop, calls=%fused_computation.11 | loop fusion | flops 167936 | bytes 47236 | tf_op jit(solution)/shard_map/add | solution.py:232
  73.7 0.0 collective-permute-done.13.refs_5_
  73.7 0.6 copy-done.5
  74.3 0.1 collective-permute-done.10.refs_4_
  74.5 0.6 copy-done.6
  75.1 11.9 %mixed_blocks.1 = bf16[8,512,128]{2,1,0:T(8,128)(2,1)} custom-call(s32[1]{0:T(128)} %bitcast.tile_ref, s32[8,656,1]{2,1,0:T(8,128)} %fusion.3.ids_ref, bf16[64,384]{1,0:T(8,128)(2,1)} %copy-done.2, bf16[64,384]{1,0:T(8,128)(2,1)} %copy-done.3, bf16[64,384]{1,0:T(8,128)(2,1)} %collective-permute-done.8.refs_2_, ...), custom_call_target="tpu_custom_call" | custom-call | flops 5000000000 | bytes 4000000 | tf_op jit(solution)/shard_map/mixed_blocks/pallas_call | solution.py:129
  87.0 19.9 %all_to_all.15 = bf16[8,512,128]{2,1,0:T(8,128)(2,1)S(1)} all-to-all(bf16[8,512,128]{2,1,0:T(8,128)(2,1)} %mixed_blocks.1), channel_id=1, replica_groups=mesh['yh'=2,'z'=8,'x'=4,'yl'=2,'core'=2] {'yh','x'}, dimensions={0} | all-to-all | bytes 2097152 | tf_op jit(solution)/shard_map/all_to_all | solution.py:245
  106.8 0.5 copy.29
  107.3 1.3 %copy.30 = bf16[512,1024]{1,0:T(8,128)(2,1)} copy(bf16[512,1024]{0,1:T(8,128)(2,1)S(1)} %bitcast.25) | data formatting | bytes 2097152 | tf_op jit(solution)/shard_map/reshape | solution.py:246
  (26 shorter events, 0.2 us)
Async XLA Ops:
  0.0 20.0 %copy-start = (f32[3,1024]{1,0:T(4,128)S(1)}, f32[3,1024]{1,0:T(4,128)}, u32[]{:S(2)}) copy-start(f32[3,1024]{1,0:T(4,128)} %param.12) | copy-start | bytes 36868
  0.0 17.1 %copy-start.7 = (f32[64]{0:T(128)S(1)}, f32[64]{0:T(128)}, u32[]{:S(2)}) copy-start(f32[64]{0:T(128)} %param.15) | copy-start | bytes 772
  1.5 17.2 %collective-permute-start.6 = (f32[512]{0:T(512)S(1)}, f32[512]{0:T(512)S(1)}, u32[]{:S(2)}, u32[]{:S(2)}) collective-permute-start(f32[512]{0:T(512)S(1)} %multiply_reduce_fusion), channel_id=1, source_target_pairs={{0,3},{1,0},{2,1},{3,2},{4,7},{5,4},{6,5},{7,6},{8,11},{9,8},{10,9... | collective-permute-start | bytes 6152 | tf_op jit(solution)/shard_map/ppermute | solution.py:22
  1.6 20.9 %collective-permute-start.5 = (f32[512]{0:T(512)S(1)}, f32[512]{0:T(512)S(1)}, u32[]{:S(2)}, u32[]{:S(2)}) collective-permute-start(f32[512]{0:T(512)S(1)} %multiply_reduce_fusion), channel_id=1, source_target_pairs={{0,2},{1,3},{2,0},{3,1},{4,6},{5,7},{6,4},{7,5},{8,10},{9,11},{10,... | collective-permute-start | bytes 6152 | tf_op jit(solution)/shard_map/ppermute | solution.py:22
  3.9 18.6 %collective-permute-start.4 = (f32[512]{0:T(512)S(1)}, f32[512]{0:T(512)S(1)}, u32[]{:S(2)}, u32[]{:S(2)}) collective-permute-start(f32[512]{0:T(512)S(1)} %multiply_reduce_fusion), channel_id=1, source_target_pairs={{0,1},{1,2},{2,3},{3,0},{4,5},{5,6},{6,7},{7,4},{8,9},{9,10},{10,1... | collective-permute-start | bytes 6152 | tf_op jit(solution)/shard_map/ppermute | solution.py:22
  5.0 17.5 %collective-permute-start.2 = (bf16[512,256]{1,0:T(8,128)(2,1)S(1)}, bf16[512,256]{1,0:T(8,128)(2,1)S(1)}, u32[]{:S(2)}, u32[]{:S(2)}) collective-permute-start(bf16[512,256]{1,0:T(8,128)(2,1)S(1)} %constant_dynamic-slice_fusion), channel_id=1, source_target_pairs={{0,2},{2,0},{16,18},{18,16},{32,34},{34,32},{48,50},{50,48},{65,67... | collective-permute-start | bytes 786440 | tf_op jit(solution)/shard_map/ppermute | solution.py:179
  7.2 15.3 %collective-permute-start.3 = (bf16[512,256]{1,0:T(8,128)(2,1)S(1)}, bf16[512,256]{1,0:T(8,128)(2,1)S(1)}, u32[]{:S(2)}, u32[]{:S(2)}) collective-permute-start(bf16[512,256]{1,0:T(8,128)(2,1)S(1)} %constant_dynamic-slice_fusion), channel_id=1, source_target_pairs={{0,3},{2,1},{16,19},{18,17},{32,35},{34,33},{48,51},{50,49},{65,66... | collective-permute-start | bytes 786440 | tf_op jit(solution)/shard_map/ppermute | solution.py:180
  11.8 14.8 %all-to-all-start = ((bf16[8,200,128]{2,1,0:T(8,128)(2,1)}), bf16[8,200,128]{2,1,0:T(8,128)(2,1)S(1)}, u32[]{:S(2)}, u32[]{:S(2)}) async-start(bf16[8,200,128]{2,1,0:T(8,128)(2,1)} %pad_maximum_fusion), calls=%async_computation | async-start | bytes 819200 | tf_op jit(solution)/shard_map/all_to_all | solution.py:190
  18.7 3.8 %collective-permute-start.1 = (bf16[512,256]{1,0:T(8,128)(2,1)S(1)}, bf16[512,256]{1,0:T(8,128)(2,1)S(1)}, u32[]{:S(2)}, u32[]{:S(2)}) collective-permute-start(bf16[512,256]{1,0:T(8,128)(2,1)S(1)} %constant_dynamic-slice_fusion), channel_id=1, source_target_pairs={{0,1},{2,3},{16,17},{18,19},{32,33},{34,35},{48,49},{50,51},{65,64... | collective-permute-start | bytes 786440 | tf_op jit(solution)/shard_map/ppermute | solution.py:178
  26.6 0.8 copy-start.1
  29.8 22.7 %all-to-all-start.1 = ((bf16[8,64,384]{2,1,0:T(8,128)(2,1)}), bf16[8,64,384]{2,1,0:T(8,128)(2,1)S(1)}, u32[]{:S(2)}, u32[]{:S(2)}) async-start(bf16[8,64,384]{2,1,0:T(8,128)(2,1)} %bitcast.28), calls=%async_computation.1 | async-start | bytes 786432 | tf_op jit(solution)/shard_map/all_to_all | solution.py:209
  36.4 11.0 %collective-permute-start = (s32[2,144]{1,0:T(2,128)S(1)}, s32[2,144]{1,0:T(2,128)S(1)}, u32[]{:S(2)}, u32[]{:S(2)}) collective-permute-start(s32[2,144]{1,0:T(2,128)S(1)} %pad_add_fusion.1), channel_id=1, source_target_pairs={{0,16},{16,32},{32,48},{48,64},{64,80},{80,96},{96,112},{112,0},{1... | collective-permute-start | bytes 3464 | tf_op jit(solution)/shard_map/ppermute | solution.py:22
  52.5 21.2 %copy-start.2 = (bf16[64,384]{1,0:T(8,128)(2,1)}, bf16[64,384]{1,0:T(8,128)(2,1)S(1)}, u32[]{:S(2)}) copy-start(bf16[64,384]{1,0:T(8,128)(2,1)S(1)} %multiply_convert_fusion.1.refs_0_) | copy-start | bytes 147460
  52.6 5.4 %collective-permute-start.7 = (bf16[64,384]{1,0:T(8,128)(2,1)S(1)}, bf16[64,384]{1,0:T(8,128)(2,1)S(1)}, u32[]{:S(2)}, u32[]{:S(2)}) collective-permute-start(bf16[64,384]{1,0:T(8,128)(2,1)S(1)} %multiply_convert_fusion.1.refs_0_), channel_id=1, source_target_pairs={{0,16},{16,32},{32,48},{48,64},{64,80},{80,96},{96,112},{112,0},{1... | collective-permute-start | bytes 147464 | tf_op jit(solution)/shard_map/ppermute | solution.py:22
  53.0 5.0 %collective-permute-start.11 = (bf16[64,384]{1,0:T(8,128)(2,1)S(1)}, bf16[64,384]{1,0:T(8,128)(2,1)S(1)}, u32[]{:S(2)}, u32[]{:S(2)}) collective-permute-start(bf16[64,384]{1,0:T(8,128)(2,1)S(1)} %multiply_convert_fusion.1.refs_0_), channel_id=1, source_target_pairs={{0,112},{16,0},{32,16},{48,32},{64,48},{80,64},{96,80},{112,96},{1... | collective-permute-start | bytes 147464 | tf_op jit(solution)/shard_map/ppermute | solution.py:22
  57.9 15.8 %copy-start.3 = (bf16[64,384]{1,0:T(8,128)(2,1)}, bf16[64,384]{1,0:T(8,128)(2,1)S(1)}, u32[]{:S(2)}) copy-start(bf16[64,384]{1,0:T(8,128)(2,1)S(1)} %collective-permute-done.7.refs_1_) | copy-start | bytes 147460
  57.9 5.4 %collective-permute-start.8 = (bf16[64,384]{1,0:T(8,128)(2,1)S(1)}, bf16[64,384]{1,0:T(8,128)(2,1)}, u32[]{:S(2)}, u32[]{:S(2)}) collective-permute-start(bf16[64,384]{1,0:T(8,128)(2,1)S(1)} %collective-permute-done.7.refs_1_), channel_id=1, source_target_pairs={{0,16},{16,32},{32,48},{48,64},{64,80},{80,96},{96,112},{112,0},{1... | collective-permute-start | bytes 147464 | tf_op jit(solution)/shard_map/ppermute | solution.py:22
  58.0 15.7 %copy-start.4 = (bf16[64,384]{1,0:T(8,128)(2,1)}, bf16[64,384]{1,0:T(8,128)(2,1)S(1)}, u32[]{:S(2)}) copy-start(bf16[64,384]{1,0:T(8,128)(2,1)S(1)} %collective-permute-done.11.refs_7_) | copy-start | bytes 147460
  58.0 7.3 %collective-permute-start.12 = (bf16[64,384]{1,0:T(8,128)(2,1)S(1)}, bf16[64,384]{1,0:T(8,128)(2,1)}, u32[]{:S(2)}, u32[]{:S(2)}) collective-permute-start(bf16[64,384]{1,0:T(8,128)(2,1)S(1)} %collective-permute-done.11.refs_7_), channel_id=1, source_target_pairs={{0,112},{16,0},{32,16},{48,32},{64,48},{80,64},{96,80},{112,96},{1... | collective-permute-start | bytes 147464 | tf_op jit(solution)/shard_map/ppermute | solution.py:22
  63.3 5.6 %collective-permute-start.9 = (bf16[64,384]{1,0:T(8,128)(2,1)}, bf16[64,384]{1,0:T(8,128)(2,1)}, u32[]{:S(2)}, u32[]{:S(2)}) collective-permute-start(bf16[64,384]{1,0:T(8,128)(2,1)} %collective-permute-done.8.refs_2_), channel_id=1, source_target_pairs={{0,16},{16,32},{32,48},{48,64},{64,80},{80,96},{96,112},{112,0},{1... | collective-permute-start | bytes 147464 | tf_op jit(solution)/shard_map/ppermute | solution.py:22
  65.3 8.4 %collective-permute-start.13 = (bf16[64,384]{1,0:T(8,128)(2,1)}, bf16[64,384]{1,0:T(8,128)(2,1)S(1)}, u32[]{:S(2)}, u32[]{:S(2)}) collective-permute-start(bf16[64,384]{1,0:T(8,128)(2,1)} %collective-permute-done.12.refs_6_), channel_id=1, source_target_pairs={{0,112},{16,0},{32,16},{48,32},{64,48},{80,64},{96,80},{112,96},{1... | collective-permute-start | bytes 147464 | tf_op jit(solution)/shard_map/ppermute | solution.py:22
  69.0 5.5 %collective-permute-start.10 = (bf16[64,384]{1,0:T(8,128)(2,1)}, bf16[64,384]{1,0:T(8,128)(2,1)S(1)}, u32[]{:S(2)}, u32[]{:S(2)}) collective-permute-start(bf16[64,384]{1,0:T(8,128)(2,1)} %collective-permute-done.9.refs_3_), channel_id=1, source_target_pairs={{0,16},{16,32},{32,48},{48,64},{64,80},{80,96},{96,112},{112,0},{1... | collective-permute-start | bytes 147464 | tf_op jit(solution)/shard_map/ppermute | solution.py:22
  73.7 0.6 copy-start.5
  74.5 0.6 copy-start.6

commit v2 on v0

v2 whole, which is shorter than its diff:
```python
import jax
import jax.numpy as jnp
import numpy as np
from jax import lax
from jax.experimental import pallas as pl
from jax.experimental.pallas import tpu as pltpu
from jax.sharding import Mesh, PartitionSpec as P

GROUP = 16
SHORT_TAPS = 7
LONG_TAPS = 128
LANES = 128
HALO = 144
TAIL = 256
STREAMS = 3
BF = jnp.bfloat16
F32 = jnp.float32


def shifted(value, axis, steps):
    count = lax.axis_size(axis)
    pairs = [(source, (source + steps) % count) for source in range(count)]
    return lax.ppermute(value, axis, pairs)


def payload_kernel(weight_ref, ids_ref, tail_ref, out_ref):
    rows = weight_ref.shape[1]
    values = jnp.concatenate(
        [tail_ref[...], ids_ref[...], jnp.zeros((2, LANES), jnp.int32)], axis=0
    )
    coded = jnp.concatenate([values >> 4, values & 15], axis=0).astype(F32).astype(BF)
    for tile in range(out_ref.shape[0]):
        for p in range(STREAMS):
            out_ref[tile, p * rows : (p + 1) * rows, :] = weight_ref[
                p, :, tile * LANES : (tile + 1) * LANES
            ]
        out_ref[tile, STREAMS * rows :, :] = coded


def in_vmem(count):
    return [pl.BlockSpec(memory_space=pltpu.VMEM)] * count


def cost(flops, moved):
    return pl.CostEstimate(flops=flops, bytes_accessed=moved, transcendentals=0)


def payload(in_weight, ids_rows, tail_rows):
    streams, rows, width = in_weight.shape
    return pl.pallas_call(
        payload_kernel,
        out_shape=jax.ShapeDtypeStruct((width // LANES, streams * rows + 16, LANES), BF),
        in_specs=in_vmem(3),
        out_specs=pl.BlockSpec(memory_space=pltpu.VMEM),
        cost_estimate=cost(0, 800000),
        name="payload",
    )(in_weight, ids_rows, tail_rows)


def partial_kernel(flag_ref, own_ref, core_ref, chip_ref, both_ref, pieces_ref, out_ref):
    rows = (pieces_ref.shape[1] - 16) // STREAMS
    half = own_ref.shape[1]
    weight = jnp.concatenate(
        [
            pieces_ref[:, p * rows : (p + 1) * rows, :].reshape(2 * half, LANES)
            for p in range(STREAMS)
        ],
        axis=1,
    )
    mine = flag_ref[0] == 1
    swap = flag_ref[1] == 1
    near = jnp.where(mine, own_ref[...], core_ref[...])
    far = jnp.where(mine, chip_ref[...], both_ref[...])
    features = jnp.concatenate(
        [jnp.where(swap, far, near), jnp.where(swap, near, far)], axis=1
    )
    out_ref[...] = jnp.dot(features, weight, preferred_element_type=F32).astype(BF)


def partial_table(flags, own, got_core, got_chip, got_both, pieces):
    vocab, half = own.shape
    return pl.pallas_call(
        partial_kernel,
        out_shape=jax.ShapeDtypeStruct((vocab, STREAMS * LANES), BF),
        in_specs=[pl.BlockSpec(memory_space=pltpu.SMEM)] + in_vmem(5),
        out_specs=pl.BlockSpec(memory_space=pltpu.VMEM),
        cost_estimate=cost(4 * vocab * half * STREAMS * LANES, 2000000),
        name="partial_table",
    )(flags, own, got_core, got_chip, got_both, pieces)


def toeplitz_kernel(taps_ref, out_ref):
    for g in range(taps_ref.shape[0]):
        row = jnp.broadcast_to(taps_ref[g : g + 1, :], (LONG_TAPS, 2 * LONG_TAPS))
        out_ref[g * LONG_TAPS : (g + 1) * LONG_TAPS, :] = pltpu.roll(
            row, 0, 1, stride=1, stride_axis=0
        ).astype(BF)


def toeplitz(taps_row):
    groups = taps_row.shape[0]
    return pl.pallas_call(
        toeplitz_kernel,
        out_shape=jax.ShapeDtypeStruct((groups * LONG_TAPS, 2 * LONG_TAPS), BF),
        in_specs=in_vmem(1),
        out_specs=pl.BlockSpec(memory_space=pltpu.VMEM),
        cost_estimate=cost(2000000, 1060000),
        name="toeplitz",
    )(taps_row)


def table_kernel(*refs):
    pieces, out_ref = refs[:-1], refs[-1]
    share = pieces[0].shape[0] // 2
    width = pieces[0].shape[1]
    for j, piece in enumerate(pieces):
        for half in range(2):
            out_ref[j * share : (j + 1) * share, half * width : (half + 1) * width] = piece[
                half * share : (half + 1) * share, :
            ]


def joined_table(pieces):
    rows, width = pieces[0].shape
    return pl.pallas_call(
        table_kernel,
        out_shape=jax.ShapeDtypeStruct((len(pieces) * rows // 2, 2 * width), BF),
        in_specs=in_vmem(len(pieces)),
        out_specs=pl.BlockSpec(memory_space=pltpu.VMEM),
        cost_estimate=cost(0, 1600000),
        name="joined_table",
    )(*pieces)


def mix_kernel(spot_ref, ids_ref, table_ref, filt_ref, toep_ref, out_ref, proj_ref, inner_ref):
    block, z, z_count = spot_ref[0], spot_ref[1], spot_ref[2]
    vocab = table_ref.shape[0]
    share = vocab // 8
    tokens = out_ref.shape[0]
    extent = tokens + HALO
    coded = ids_ref[block].astype(F32)
    known = (coded[:8] * 16.0 + coded[8:]).astype(jnp.int32)
    turned = ((z - known // share + z_count) % z_count) * share + known % share
    column = jnp.transpose(turned.astype(F32))
    parts = [column[LANES - (HALO - LANES) :, 0:1]]
    for j in range(1, tokens // LANES + 2):
        parts.append(column[:, j : j + 1])
    wanted = jnp.concatenate(parts, axis=0).astype(jnp.int32)
    hot = wanted == lax.broadcasted_iota(jnp.int32, (extent, vocab), 1)
    proj = jnp.dot(
        jnp.where(hot, 1.0, 0.0).astype(BF), table_ref[...], preferred_element_type=F32
    )
    for part in range(2 * STREAMS):
        proj_ref[part] = proj[:, part * LANES : (part + 1) * LANES]

    first = HALO - LONG_TAPS
    lane_group = lax.broadcasted_iota(jnp.int32, (LONG_TAPS, LANES), 1) // GROUP
    groups = LANES // GROUP
    for half in range(2):

        def short(p, start):
            total = jnp.zeros((extent - start, LANES), F32)
            for k in range(SHORT_TAPS):
                tap = filt_ref[half, p * SHORT_TAPS + k : p * SHORT_TAPS + k + 1, :]
                total = total + tap * proj_ref[half * STREAMS + p, start - k : extent - k, :]
            return total

        inner_ref[half] = (short(1, first) * short(2, first)).astype(BF)
        gate = short(0, HALO)
        for pair in range(tokens // (2 * LONG_TAPS)):
            base = pair * 2 * LONG_TAPS
            window = jnp.concatenate(
                [
                    inner_ref[half, base : base + 2 * LONG_TAPS, :],
                    inner_ref[half, base + LONG_TAPS : base + 3 * LONG_TAPS, :],
                ],
                axis=1,
            )
            full = jnp.dot(
                toep_ref[half * groups * LONG_TAPS : (half + 1) * groups * LONG_TAPS, :],
                window,
                preferred_element_type=F32,
            )
            for side in range(2):
                lanes = slice(side * LANES, (side + 1) * LANES)
                conv = full[:LONG_TAPS, lanes]
                for g in range(1, groups):
                    conv = jnp.where(
                        lane_group == g, full[g * LONG_TAPS : (g + 1) * LONG_TAPS, lanes], conv
                    )
                at = base + side * LONG_TAPS
                out_ref[at : at + LONG_TAPS, half * LANES : (half + 1) * LANES] = (
                    gate[at : at + LONG_TAPS] * conv
                ).astype(BF)


def mixed_block(spot, coded, table, filt, toep, tokens):
    return pl.pallas_call(
        mix_kernel,
        out_shape=jax.ShapeDtypeStruct((tokens, 2 * LANES), BF),
        in_specs=[pl.BlockSpec(memory_space=pltpu.SMEM)] + in_vmem(4),
        out_specs=pl.BlockSpec(memory_space=pltpu.VMEM),
        scratch_shapes=[
            pltpu.VMEM((2 * STREAMS, tokens + HALO, LANES), F32),
            pltpu.VMEM((2, tokens + LONG_TAPS, LANES), BF),
        ],
        cost_estimate=cost(1500000000, 3000000),
        name="mixed_block",
    )(spot, coded, table, filt, toep)


def place_kernel(x_ref, *refs):
    sources, out_ref = refs[:-1], refs[-1]
    half = out_ref.shape[1] // 2
    for step, source in enumerate(sources):
        at = ((x_ref[0] + 4 - step) % 4) * LANES
        for side in range(2):
            out_ref[:, pl.ds(pl.multiple_of(side * half + at, LANES), LANES)] = source[
                :, side * LANES : (side + 1) * LANES
            ]


def placed_columns(x, sources):
    tokens, width = sources[0].shape
    return pl.pallas_call(
        place_kernel,
        out_shape=jax.ShapeDtypeStruct((tokens, width * len(sources)), BF),
        in_specs=[pl.BlockSpec(memory_space=pltpu.SMEM)] + in_vmem(len(sources)),
        out_specs=pl.BlockSpec(memory_space=pltpu.VMEM),
        cost_estimate=cost(0, 2000000),
        name="placed_columns",
    )(x, *sources)


def per_device(ids, embed_table, norm_gain, in_weight, in_scale, short_filter, long_filter, decay):
    tokens = ids.shape[0]
    vocab, width_local = embed_table.shape
    rows = in_weight.shape[1]
    yh = lax.axis_index("yh")
    z = lax.axis_index("z")
    x = lax.axis_index("x")
    yl = lax.axis_index("yl")
    core = lax.axis_index("core")
    x_count = lax.axis_size("x")
    z_count = lax.axis_size("z")
    tile = yh * x_count + x
    full_width = norm_gain.shape[0]

    ids_rows = ids.reshape(-1, LANES)
    tail_rows = shifted(ids_rows[(tokens - TAIL) // LANES :], ("yh", "z", "x"), 1)
    load = payload(in_weight, ids_rows, tail_rows)
    pieces = lax.all_to_all(load, ("yh", "x"), 0, 0, tiled=True)

    chunk = x_count * rows
    gain = lax.dynamic_slice_in_dim(norm_gain, yl * (full_width // 2) + z * chunk, chunk, 0)
    own = lax.dynamic_slice_in_dim(embed_table, (z % 4) * chunk, chunk, 1)
    own = (own.astype(F32) * gain[None, :]).astype(BF)
    tp = ("z", "yl", "core")

    def spot(zi, yi, ci):
        return (zi * 2 + yi) * 2 + ci

    holders = [(zi, yi, zi // 4) for zi in range(z_count) for yi in range(2)]
    got_core = lax.ppermute(own, tp, [(spot(a, b, c), spot(a, b, 1 - c)) for a, b, c in holders])
    got_chip = lax.ppermute(own, tp, [(spot(a, b, c), spot(a, 1 - b, c)) for a, b, c in holders])
    got_both = lax.ppermute(
        own, tp, [(spot(a, b, c), spot(a, 1 - b, 1 - c)) for a, b, c in holders]
    )
    local_f = embed_table.astype(F32)
    squares = jnp.sum(local_f * local_f, axis=1)
    others = [shifted(squares, ("yl", "core"), s) for s in (1, 2, 3)]
    total = squares + others[0] + others[1] + others[2]

    flags = jnp.stack([core == z // 4, yl == 1]).astype(jnp.int32)
    partial = partial_table(flags, own, got_core, got_chip, got_both, pieces)
    share = vocab // z_count
    swapped = lax.all_to_all(
        partial.reshape(z_count, share, STREAMS * LANES), "z", 0, 0, tiled=True
    )
    scale = lax.dynamic_slice_in_dim(in_scale, tile * LANES, LANES, 1).reshape(1, STREAMS * LANES)
    norm = lax.rsqrt(lax.dynamic_slice_in_dim(total, z * share, share, 0) / full_width + 1e-06)
    piece = (jnp.sum(swapped.astype(F32), axis=0) * norm[:, None] * scale).astype(BF)
    other = shifted(piece, "yh", 1)
    both = jnp.concatenate(
        [jnp.where(yh == 0, piece, other), jnp.where(yh == 0, other, piece)], axis=0
    )
    ups, downs, last = [both], [], both
    for step in range(4):
        ups.append(shifted(ups[-1], "z", 1))
        if step < 3:
            last = shifted(last, "z", -1)
            downs.append(last)
    table = joined_table(ups + downs[::-1])

    groups = LANES // GROUP
    steps = jnp.arange(LONG_TAPS, dtype=F32)
    filt = long_filter.reshape(LONG_TAPS, 2, x_count, groups)
    filt = lax.dynamic_index_in_dim(filt, x, 2, keepdims=False).reshape(LONG_TAPS, 2 * groups)
    rate = lax.dynamic_index_in_dim(decay.reshape(2, x_count, groups), x, 1, keepdims=False)
    taps = (filt * jnp.exp(-rate.reshape(1, -1) * steps[:, None])).astype(BF).astype(F32)
    toep = toeplitz(jnp.pad(taps[::-1].T, ((0, 0), (1, LONG_TAPS - 1))))
    near_filter = short_filter.reshape(STREAMS * SHORT_TAPS, 2, x_count, LANES)
    near_filter = lax.dynamic_index_in_dim(near_filter, x, 2, keepdims=False).transpose(1, 0, 2)

    coded = pieces[:, STREAMS * rows :, :]
    sources = {}
    for step in (2, 1, 3, 0):
        where = jnp.stack([yh * x_count + (x + step) % x_count, z, jnp.int32(z_count)])
        block = mixed_block(where.astype(jnp.int32), coded, table, near_filter, toep, tokens)
        if step:
            table, block = lax.optimization_barrier((table, block))
            sources[step] = shifted(block, "x", step)
        else:
            sources[0] = block
    return placed_columns(
        x.reshape(1).astype(jnp.int32), [sources[step] for step in range(x_count)]
    )


def solution(mesh):
    fine = Mesh(mesh.devices.reshape(2, 8, 4, 2, 2), ("yh", "z", "x", "yl", "core"))
    ctx = ("yh", "z", "x")
    tp = ("yl", "core")
    placed = (
        P(ctx),
        P(None, tp),
        P(),
        P(None, ctx, tp),
        P(None, tp),
        P(None, None, tp),
        P(None, tp),
        P(tp),
    )
    return jax.shard_map(
        per_device, mesh=fine, in_specs=placed, out_specs=P(ctx, tp), check_vma=False
    )
```

time: 710 us -> 118 us (0.17)
  waiting for transfers between devices: 486 us -> 41.8 us
  local copies, waits for them, and re-layouts: 146 us -> 8.12 us
  matrix products: 33.5 us -> 0 us
  Pallas kernels: 0 us -> 29.5 us
  starting transfers between devices: 3.36 us -> 32.6 us
  other arithmetic: 22.8 us -> 3.97 us
  between operations: 13.4 us -> 0.26 us
    all_gather x4 -> x0, waiting for transfers between devices: 477 us -> none  [the longest x3 429 us: project_stream(): return add_one(lax.all_gather(weight, 'ctx', axis=0, tiled=True))]
    gather x4 -> x0, local copies, waits for them, and re-layouts: 126 us -> none  [the longest x2 63.5 us: toeplitz(): jnp.take(taps, jnp.clip(offset + LONG_TAPS, 0, LONG_TAPS - 1), axis=0)]
    dot_general x6 -> x0, matrix products: 33.5 us -> none  [the longest x3 26.9 us: add_one(): return jnp.dot(features, piece, preferred_element_type=jnp.float32)]
    pallas_call x0 -> x9, Pallas kernels: none -> 29.5 us  [the longest x4 18.4 us: mixed_block(): pl.pallas_call(mix_kernel, out_shape=jax.ShapeDtypeStruct((tokens, 2 * LA...]
    ppermute x2 -> x18, waiting for transfers between devices: 6.95 us -> 31.7 us  [the longest x15 25.6 us: shifted(): return lax.ppermute(value, axis, pairs)]
    ppermute x2 -> x18, starting transfers between devices: 3.2 us -> 25.6 us  [the longest x15 19.8 us: shifted(): return lax.ppermute(value, axis, pairs)]
    add x1, other arithmetic: 13.6 us -> 0.01 us  [per_device(): total = squares + others[0] + others[1] + others[2]]
    all_to_all x0 -> x2, waiting for transfers between devices: none -> 10 us  [the longest x1 10 us: per_device(): lax.all_to_all(partial.reshape(z_count, share, STREAMS * LANES), 'z', 0,...]
  transfers between devices with their start and end apart: 6 -> 20, of which waited for: 5 -> 13; matrix products, arithmetic and copies ran while one was open for 21% -> 6% of each run, Pallas kernels for 0% -> 6%
where the time goes in v2:
time: 118 us; the launch traced here: 116 us
  waiting for transfers between devices  41.8 us (35%)
  starting transfers between devices  32.6 us (28%)
  Pallas kernels  29.5 us (25%)
  local copies, waits for them, and re-layouts  8.12 us (7%)
  other arithmetic  3.97 us (3%)
    ppermute x15, waiting for transfers between devices, shifted(): return lax.ppermute(value, axis, pairs)  25.6 us
    ppermute x15, starting transfers between devices, shifted(): return lax.ppermute(value, axis, pairs)  19.8 us
    pallas_call x4, Pallas kernels, mixed_block(): pl.pallas_call(mix_kernel, out_shape=jax.ShapeDtypeStruct((tokens, 2 * LA...  18.4 us
    all_to_all x1, waiting for transfers between devices, per_device(): lax.all_to_all(partial.reshape(z_count, share, STREAMS * LANES), 'z', 0,...  10 us
    ppermute x1, waiting for transfers between devices, per_device(): lax.ppermute(own, tp, [(spot(a, b, c), spot(a, 1 - b, c)) for a, b, c in...  4.24 us
    unnamed x47, local copies, waits for them, and re-layouts  4.24 us
    all_to_all x1, starting transfers between devices, per_device(): pieces = lax.all_to_all(load, ('yh', 'x'), 0, 0, tiled=True)  3.46 us
    all_to_all x1, starting transfers between devices, per_device(): lax.all_to_all(partial.reshape(z_count, share, STREAMS * LANES), 'z', 0,...  3.45 us
  transfers between devices with their start and end apart: 20, of which 13 were waited for; matrix products, arithmetic and copies ran while one was open for 6% of the time, Pallas kernels for 6%

profile of v2, /device:TPU:8, one launch (start us, length us, event | category | flops | bytes accessed | tf_op | source)
XLA Modules:
  0.0 116.1 jit_solution(6412512206805792466)
XLA Ops:
  0.0 0.8 slice_bitcast_fusion
  0.8 1.5 %collective-permute-start = (s32[2,128]{1,0:T(2,128)S(1)}, s32[2,128]{1,0:T(2,128)S(1)}, u32[]{:S(2)}, u32[]{:S(2)}) collective-permute-start(s32[2,128]{1,0:T(2,128)S(1)} %slice_bitcast_fusion), channel_id=1, source_target_pairs={{0,4},{4,8},{8,12},{12,16},{16,20},{20,24},{24,28},{28,32},{32,36}... | collective-permute-start | bytes 3080 | tf_op jit(solution)/shard_map/ppermute | solution.py:23
  2.3 0.8 dynamic_slice.25
  3.0 9.1 %collective-permute-done.tail_ref = s32[2,128]{1,0:T(2,128)S(1)} collective-permute-done((s32[2,128]{1,0:T(2,128)S(1)}, s32[2,128]{1,0:T(2,128)S(1)}, u32[]{:S(2)}, u32[]{:S(2)}) %collective-permute-start) | collective-permute-done | bytes 1056 | tf_op jit(solution)/shard_map/ppermute | solution.py:23
  12.1 0.6 copy-done.19
  12.7 1.8 %payload.1 = bf16[8,208,128]{2,1,0:T(8,128)(2,1)} custom-call(bf16[3,64,1024]{2,1,0:T(8,128)(2,1)} %weight_ref.1, s32[4,128]{1,0:T(4,128)} %bitcast.35, s32[2,128]{1,0:T(2,128)} %copy-done.19), custom_call_target="tpu_custom_call" | custom-call | bytes 800000 | tf_op jit(solution)/shard_map/payload/pallas_call | solution.py:50
  14.5 3.5 %all-to-all-start = ((bf16[8,208,128]{2,1,0:T(8,128)(2,1)}), bf16[8,208,128]{2,1,0:T(8,128)(2,1)S(1)}, u32[]{:S(2)}, u32[]{:S(2)}) async-start(bf16[8,208,128]{2,1,0:T(8,128)(2,1)} %payload.1), calls=%async_computation | async-start | bytes 851968 | tf_op jit(solution)/shard_map/all_to_all | solution.py:252
  18.0 0.1 multiply_convert_fusion.own_ref
  18.1 1.8 %collective-permute-start.3 = (bf16[512,256]{1,0:T(8,128)(2,1)S(1)}, bf16[512,256]{1,0:T(8,128)(2,1)S(1)}, u32[]{:S(2)}, u32[]{:S(2)}) collective-permute-start(bf16[512,256]{1,0:T(8,128)(2,1)S(1)} %multiply_convert_fusion.own_ref), channel_id=1, source_target_pairs={{0,3},{2,1},{16,19},{18,17},{32,35},{34,33},{48,51},{50,49},{65,66... | collective-permute-start | bytes 786440 | tf_op jit(solution)/shard_map/ppermute | solution.py:266
  20.0 2.7 %collective-permute-start.2 = (bf16[512,256]{1,0:T(8,128)(2,1)S(1)}, bf16[512,256]{1,0:T(8,128)(2,1)S(1)}, u32[]{:S(2)}, u32[]{:S(2)}) collective-permute-start(bf16[512,256]{1,0:T(8,128)(2,1)S(1)} %multiply_convert_fusion.own_ref), channel_id=1, source_target_pairs={{0,2},{2,0},{16,18},{18,16},{32,34},{34,32},{48,50},{50,48},{65,67... | collective-permute-start | bytes 786440 | tf_op jit(solution)/shard_map/ppermute | solution.py:265
  22.7 1.3 %collective-permute-start.1 = (bf16[512,256]{1,0:T(8,128)(2,1)S(1)}, bf16[512,256]{1,0:T(8,128)(2,1)S(1)}, u32[]{:S(2)}, u32[]{:S(2)}) collective-permute-start(bf16[512,256]{1,0:T(8,128)(2,1)S(1)} %multiply_convert_fusion.own_ref), channel_id=1, source_target_pairs={{0,1},{2,3},{16,17},{18,19},{32,33},{34,35},{48,49},{50,51},{65,64... | collective-permute-start | bytes 786440 | tf_op jit(solution)/shard_map/ppermute | solution.py:264
  24.0 0.6 add_convert_fusion.flag_ref
  24.6 1.9 %collective-permute-done.3.both_ref = bf16[512,256]{1,0:T(8,128)(2,1)S(1)} collective-permute-done((bf16[512,256]{1,0:T(8,128)(2,1)S(1)}, bf16[512,256]{1,0:T(8,128)(2,1)S(1)}, u32[]{:S(2)}, u32[]{:S(2)}) %collective-permute-start.3) | collective-permute-done | bytes 262176 | tf_op jit(solution)/shard_map/ppermute | solution.py:266
  26.5 4.2 %collective-permute-done.2.chip_ref = bf16[512,256]{1,0:T(8,128)(2,1)S(1)} collective-permute-done((bf16[512,256]{1,0:T(8,128)(2,1)S(1)}, bf16[512,256]{1,0:T(8,128)(2,1)S(1)}, u32[]{:S(2)}, u32[]{:S(2)}) %collective-permute-start.2) | collective-permute-done | bytes 262176 | tf_op jit(solution)/shard_map/ppermute | solution.py:265
  30.8 0.7 copy-done.9
  31.4 0.1 copy-done.10
  31.6 0.8 copy-done.1
  32.3 2.5 %partial_table.1 = bf16[512,384]{1,0:T(8,128)(2,1)} custom-call(s32[2]{0:T(128)} %add_convert_fusion.flag_ref, bf16[512,256]{1,0:T(8,128)(2,1)} %copy-done.3, bf16[512,256]{1,0:T(8,128)(2,1)} %copy-done.10, bf16[512,256]{1,0:T(8,128)(2,1)} %copy-done.9, bf16[512,256]{1,0:T(8,128)(2,1)} %copy-done.8, bf16[8,208,128]{2,1,0:T(8,128)(2,1)} %copy-done.1), custom_call_target="tpu_custom_call" | custom-call | flops 201326592 | bytes 2000000 | tf_op jit(solution)/shard_map/partial_table/pallas_call | solution.py:82
  34.9 3.5 %all-to-all-start.1 = ((bf16[8,64,384]{2,1,0:T(8,128)(2,1)}), bf16[8,64,384]{2,1,0:T(8,128)(2,1)S(1)}, u32[]{:S(2)}, u32[]{:S(2)}) async-start(bf16[8,64,384]{2,1,0:T(8,128)(2,1)} %bitcast.29), calls=%async_computation.1 | async-start | bytes 786432 | tf_op jit(solution)/shard_map/all_to_all | solution.py:277
  38.3 0.3 multiply_reduce_fusion
  38.6 0.7 collective-permute-start.6
  39.4 1.3 %collective-permute-start.5 = (f32[512]{0:T(512)S(1)}, f32[512]{0:T(512)S(1)}, u32[]{:S(2)}, u32[]{:S(2)}) collective-permute-start(f32[512]{0:T(512)S(1)} %multiply_reduce_fusion), channel_id=1, source_target_pairs={{0,2},{1,3},{2,0},{3,1},{4,6},{5,7},{6,4},{7,5},{8,10},{9,11},{10,... | collective-permute-start | bytes 6152 | tf_op jit(solution)/shard_map/ppermute | solution.py:23
  40.7 2.3 %collective-permute-done.5 = f32[512]{0:T(512)S(1)} collective-permute-done((f32[512]{0:T(512)S(1)}, f32[512]{0:T(512)S(1)}, u32[]{:S(2)}, u32[]{:S(2)}) %collective-permute-start.5) | collective-permute-done | bytes 2080 | tf_op jit(solution)/shard_map/ppermute | solution.py:23
  42.9 0.7 collective-permute-done.4
  43.6 0.1 add_rsqrt_fusion
  43.7 10.0 %all-to-all-done.1 = bf16[8,64,384]{2,1,0:T(8,128)(2,1)S(1)} async-done(((bf16[8,64,384]{2,1,0:T(8,128)(2,1)}), bf16[8,64,384]{2,1,0:T(8,128)(2,1)S(1)}, u32[]{:S(2)}, u32[]{:S(2)}) %all-to-all-start.1) | async-done | bytes 393248 | tf_op jit(solution)/shard_map/all_to_all | solution.py:277
  53.7 0.1 convert_reduce_fusion
  53.8 0.1 multiply_convert_fusion.1
  53.9 2.5 %collective-permute-start.7 = (bf16[64,384]{1,0:T(8,128)(2,1)S(1)}, bf16[64,384]{1,0:T(8,128)(2,1)S(1)}, u32[]{:S(2)}, u32[]{:S(2)}) collective-permute-start(bf16[64,384]{1,0:T(8,128)(2,1)S(1)} %multiply_convert_fusion.1), channel_id=1, source_target_pairs={{0,128},{128,0},{1,129},{129,1},{2,130},{130,2},{3,131},{131,3},{4... | collective-permute-start | bytes 147464 | tf_op jit(solution)/shard_map/ppermute | solution.py:23
  56.4 0.1 reshape.51
  56.5 0.1 neg.12
  56.6 3.0 %collective-permute-done.7 = bf16[64,384]{1,0:T(8,128)(2,1)S(1)} collective-permute-done((bf16[64,384]{1,0:T(8,128)(2,1)S(1)}, bf16[64,384]{1,0:T(8,128)(2,1)S(1)}, u32[]{:S(2)}, u32[]{:S(2)}) %collective-permute-start.7) | collective-permute-done | bytes 49184 | tf_op jit(solution)/shard_map/ppermute | solution.py:23
  59.6 0.1 broadcast_select_fusion.1
  59.7 0.6 collective-permute-start.8
  60.3 0.8 fusion.1
  61.1 0.1 rev.3
  61.2 2.7 %collective-permute-start.12 = (bf16[128,384]{1,0:T(8,128)(2,1)S(1)}, bf16[128,384]{1,0:T(8,128)(2,1)S(1)}, u32[]{:S(2)}, u32[]{:S(2)}) collective-permute-start(bf16[128,384]{1,0:T(8,128)(2,1)S(1)} %pad_maximum_fusion.refs_0_), channel_id=1, source_target_pairs={{0,112},{16,0},{32,16},{48,32},{64,48},{80,64},{96,80},{112,96},{1... | collective-permute-start | bytes 294920 | tf_op jit(solution)/shard_map/ppermute | solution.py:23
  64.0 1.6 %collective-permute-done.8.refs_1_ = bf16[128,384]{1,0:T(8,128)(2,1)S(1)} collective-permute-done((bf16[128,384]{1,0:T(8,128)(2,1)S(1)}, bf16[128,384]{1,0:T(8,128)(2,1)S(1)}, u32[]{:S(2)}, u32[]{:S(2)}) %collective-permute-start.8) | collective-permute-done | bytes 98336 | tf_op jit(solution)/shard_map/ppermute | solution.py:23
  65.6 0.6 copy.14
  66.2 0.7 pad.4.taps_ref
  66.9 2.0 %toeplitz.1.toep_ref = bf16[2048,256]{1,0:T(8,128)(2,1)} custom-call(f32[16,256]{1,0:T(8,128)} %pad.4.taps_ref), custom_call_target="tpu_custom_call" | custom-call | flops 2000000 | bytes 1060000 | tf_op jit(solution)/shard_map/toeplitz/pallas_call | solution.py:102
  68.9 3.2 %collective-permute-start.13 = (bf16[128,384]{1,0:T(8,128)(2,1)S(1)}, bf16[128,384]{1,0:T(8,128)(2,1)S(1)}, u32[]{:S(2)}, u32[]{:S(2)}) collective-permute-start(bf16[128,384]{1,0:T(8,128)(2,1)S(1)} %collective-permute-done.12.refs_7_), channel_id=1, source_target_pairs={{0,112},{16,0},{32,16},{48,32},{64,48},{80,64},{96,80},{112,96},{1... | collective-permute-start | bytes 294920 | tf_op jit(solution)/shard_map/ppermute | solution.py:23
  72.2 0.6 pad_add_fusion
  72.8 1.6 %collective-permute-done.13.refs_6_ = bf16[128,384]{1,0:T(8,128)(2,1)S(1)} collective-permute-done((bf16[128,384]{1,0:T(8,128)(2,1)S(1)}, bf16[128,384]{1,0:T(8,128)(2,1)S(1)}, u32[]{:S(2)}, u32[]{:S(2)}) %collective-permute-start.13) | collective-permute-done | bytes 98336 | tf_op jit(solution)/shard_map/ppermute | solution.py:23
  74.4 3.6 %collective-permute-start.14 = (bf16[128,384]{1,0:T(8,128)(2,1)S(1)}, bf16[128,384]{1,0:T(8,128)(2,1)S(1)}, u32[]{:S(2)}, u32[]{:S(2)}) collective-permute-start(bf16[128,384]{1,0:T(8,128)(2,1)S(1)} %collective-permute-done.13.refs_6_), channel_id=1, source_target_pairs={{0,112},{16,0},{32,16},{48,32},{64,48},{80,64},{96,80},{112,96},{1... | collective-permute-start | bytes 294920 | tf_op jit(solution)/shard_map/ppermute | solution.py:23
  78.0 0.2 collective-permute-done.10.refs_3_
  78.2 0.6 pad_add_fusion.2.spot_ref
  78.8 1.4 %slice.20.ids_ref = bf16[8,16,128]{2,1,0:T(8,128)(2,1)} slice(bf16[8,208,128]{2,1,0:T(8,128)(2,1)} %copy-done.1), slice={[0:8], [192:208], [0:128]} | slice | bytes 65536 | tf_op jit(solution)/shard_map/slice | solution.py:305
  80.1 0.1 collective-permute-done.14.refs_5_
  80.2 3.8 %collective-permute-done.11.refs_4_ = bf16[128,384]{1,0:T(8,128)(2,1)S(1)} collective-permute-done((bf16[128,384]{1,0:T(8,128)(2,1)S(1)}, bf16[128,384]{1,0:T(8,128)(2,1)S(1)}, u32[]{:S(2)}, u32[]{:S(2)}) %collective-permute-start.11) | collective-permute-done | bytes 98336 | tf_op jit(solution)/shard_map/ppermute | solution.py:23
  84.0 0.6 copy-done.17
  84.7 2.2 %joined_table.1.table_ref = bf16[512,768]{1,0:T(8,128)(2,1)} custom-call(bf16[128,384]{1,0:T(8,128)(2,1)} %copy-done.4, bf16[128,384]{1,0:T(8,128)(2,1)} %copy-done.11, bf16[128,384]{1,0:T(8,128)(2,1)} %copy-done.13, bf16[128,384]{1,0:T(8,128)(2,1)} %copy-done.15, bf16[128,384]{1,0:T(8,128)(2,1)} %copy-done.17, bf16[128,384]{1,0:T(8,128)(2,1)} %copy-done.16, ...), custom_call_target="tpu_custom_call" | custom-call | bytes 1600000 | tf_op jit(solution)/shard_map/joined_table/pallas_call | solution.py:125
  86.8 4.6 %mixed_block.4 = bf16[512,256]{1,0:T(8,128)(2,1)} custom-call(s32[3]{0:T(128)} %pad_add_fusion.2.spot_ref, bf16[8,16,128]{2,1,0:T(8,128)(2,1)} %slice.20.ids_ref, bf16[512,768]{1,0:T(8,128)(2,1)} %joined_table.1.table_ref, f32[2,21,128]{2,1,0:T(8,128)} %bitcast.31, bf16[2048,256]{1,0:T(8,128)(2,1)} %toeplitz.1.toep_ref), custom_call_target="tpu_custom_call" | custom-call | flops 1500000000 | bytes 3000000 | tf_op jit(solution)/shard_map/mixed_block/pallas_call | solution.py:198
  91.4 4.6 %mixed_block.5 = bf16[512,256]{1,0:T(8,128)(2,1)} custom-call(s32[3]{0:T(128)} %get-tuple-element.20.spot_ref, bf16[8,16,128]{2,1,0:T(8,128)(2,1)} %slice.20.ids_ref, bf16[512,768]{1,0:T(8,128)(2,1)} %joined_table.1.table_ref, f32[2,21,128]{2,1,0:T(8,128)} %bitcast.32, bf16[2048,256]{1,0:T(8,128)(2,1)} %toeplitz.1.toep_ref), custom_call_target="tpu_custom_call" | custom-call | flops 1500000000 | bytes 3000000 | tf_op jit(solution)/shard_map/mixed_block/pallas_call | solution.py:198
  96.0 4.7 %mixed_block.6 = bf16[512,256]{1,0:T(8,128)(2,1)} custom-call(s32[3]{0:T(128)} %get-tuple-element.19.spot_ref, bf16[8,16,128]{2,1,0:T(8,128)(2,1)} %slice.20.ids_ref, bf16[512,768]{1,0:T(8,128)(2,1)} %joined_table.1.table_ref, f32[2,21,128]{2,1,0:T(8,128)} %bitcast.33, bf16[2048,256]{1,0:T(8,128)(2,1)} %toeplitz.1.toep_ref), custom_call_target="tpu_custom_call" | custom-call | flops 1500000000 | bytes 3000000 | tf_op jit(solution)/shard_map/mixed_block/pallas_call | solution.py:198
  100.7 1.8 %collective-permute-start.17 = (bf16[512,256]{1,0:T(8,128)(2,1)}, bf16[512,256]{1,0:T(8,128)(2,1)S(1)}, u32[]{:S(2)}, u32[]{:S(2)}) collective-permute-start(bf16[512,256]{1,0:T(8,128)(2,1)} %mixed_block.6), channel_id=1, source_target_pairs={{0,12},{4,0},{8,4},{12,8},{1,13},{5,1},{9,5},{13,9},{2,14},{6,2},{... | collective-permute-start | bytes 786440 | tf_op jit(solution)/shard_map/ppermute | solution.py:23
  102.5 0.2 collective-permute-start.15
  102.7 1.5 %collective-permute-start.16 = (bf16[512,256]{1,0:T(8,128)(2,1)S(1)}, bf16[512,256]{1,0:T(8,128)(2,1)S(1)}, u32[]{:S(2)}, u32[]{:S(2)}) collective-permute-start(bf16[512,256]{1,0:T(8,128)(2,1)S(1)} %copy-done.21), channel_id=1, source_target_pairs={{0,8},{4,12},{8,0},{12,4},{1,9},{5,13},{9,1},{13,5},{2,10},{6,14},... | collective-permute-start | bytes 786440 | tf_op jit(solution)/shard_map/ppermute | solution.py:23
  104.2 0.7 pad_add_fusion.3.spot_ref
  104.9 4.6 %mixed_block.7.refs_0_ = bf16[512,256]{1,0:T(8,128)(2,1)} custom-call(s32[3]{0:T(128)} %pad_add_fusion.3.spot_ref, bf16[8,16,128]{2,1,0:T(8,128)(2,1)} %slice.20.ids_ref, bf16[512,768]{1,0:T(8,128)(2,1)} %joined_table.1.table_ref, f32[2,21,128]{2,1,0:T(8,128)} %bitcast.34, bf16[2048,256]{1,0:T(8,128)(2,1)} %toeplitz.1.toep_ref), custom_call_target="tpu_custom_call" | custom-call | flops 1500000000 | bytes 3000000 | tf_op jit(solution)/shard_map/mixed_block/pallas_call | solution.py:198
  109.5 3.4 %collective-permute-done.15.refs_1_ = bf16[512,256]{1,0:T(8,128)(2,1)S(1)} collective-permute-done((bf16[512,256]{1,0:T(8,128)(2,1)S(1)}, bf16[512,256]{1,0:T(8,128)(2,1)S(1)}, u32[]{:S(2)}, u32[]{:S(2)}) %collective-permute-start.15) | collective-permute-done | bytes 262176 | tf_op jit(solution)/shard_map/ppermute | solution.py:23
  112.9 0.7 copy-done.6
  113.6 0.1 copy-done.7
  113.7 2.5 %placed_columns.1 = bf16[512,1024]{1,0:T(8,128)(2,1)} custom-call(s32[1]{0:T(128)} %bitcast.x_ref, bf16[512,256]{1,0:T(8,128)(2,1)} %mixed_block.7.refs_0_, bf16[512,256]{1,0:T(8,128)(2,1)} %copy-done.6, bf16[512,256]{1,0:T(8,128)(2,1)} %copy-done.7, bf16[512,256]{1,0:T(8,128)(2,1)} %copy-done.5), custom_call_target="tpu_custom_call" | custom-call | bytes 2000000 | tf_op jit(solution)/shard_map/placed_columns/pallas_call | solution.py:225
  (56 shorter events, 0.3 us)
Async XLA Ops:
  0.0 40.6 %copy-start = (f32[3,1024]{1,0:T(4,128)S(1)}, f32[3,1024]{1,0:T(4,128)}, u32[]{:S(2)}) copy-start(f32[3,1024]{1,0:T(4,128)} %param.12) | copy-start | bytes 36868
  0.0 18.0 %copy-start.2 = (bf16[512,1024]{1,0:T(8,128)(2,1)S(1)}, bf16[512,1024]{1,0:T(8,128)(2,1)}, u32[]{:S(2)}) copy-start(bf16[512,1024]{1,0:T(8,128)(2,1)} %param.9) | copy-start | bytes 3145732
  0.8 11.3 %collective-permute-start = (s32[2,128]{1,0:T(2,128)S(1)}, s32[2,128]{1,0:T(2,128)S(1)}, u32[]{:S(2)}, u32[]{:S(2)}) collective-permute-start(s32[2,128]{1,0:T(2,128)S(1)} %slice_bitcast_fusion), channel_id=1, source_target_pairs={{0,4},{4,8},{8,12},{12,16},{16,20},{20,24},{24,28},{28,32},{32,36}... | collective-permute-start | bytes 3080 | tf_op jit(solution)/shard_map/ppermute | solution.py:23
  12.1 0.6 copy-start.19
  14.5 16.2 %all-to-all-start = ((bf16[8,208,128]{2,1,0:T(8,128)(2,1)}), bf16[8,208,128]{2,1,0:T(8,128)(2,1)S(1)}, u32[]{:S(2)}, u32[]{:S(2)}) async-start(bf16[8,208,128]{2,1,0:T(8,128)(2,1)} %payload.1), calls=%async_computation | async-start | bytes 851968 | tf_op jit(solution)/shard_map/all_to_all | solution.py:252
  18.1 12.7 %copy-start.3 = (bf16[512,256]{1,0:T(8,128)(2,1)}, bf16[512,256]{1,0:T(8,128)(2,1)S(1)}, u32[]{:S(2)}) copy-start(bf16[512,256]{1,0:T(8,128)(2,1)S(1)} %multiply_convert_fusion.own_ref) | copy-start | bytes 786436
  18.1 8.4 %collective-permute-start.3 = (bf16[512,256]{1,0:T(8,128)(2,1)S(1)}, bf16[512,256]{1,0:T(8,128)(2,1)S(1)}, u32[]{:S(2)}, u32[]{:S(2)}) collective-permute-start(bf16[512,256]{1,0:T(8,128)(2,1)S(1)} %multiply_convert_fusion.own_ref), channel_id=1, source_target_pairs={{0,3},{2,1},{16,19},{18,17},{32,35},{34,33},{48,51},{50,49},{65,66... | collective-permute-start | bytes 786440 | tf_op jit(solution)/shard_map/ppermute | solution.py:266
  20.0 10.8 %collective-permute-start.2 = (bf16[512,256]{1,0:T(8,128)(2,1)S(1)}, bf16[512,256]{1,0:T(8,128)(2,1)S(1)}, u32[]{:S(2)}, u32[]{:S(2)}) collective-permute-start(bf16[512,256]{1,0:T(8,128)(2,1)S(1)} %multiply_convert_fusion.own_ref), channel_id=1, source_target_pairs={{0,2},{2,0},{16,18},{18,16},{32,34},{34,32},{48,50},{50,48},{65,67... | collective-permute-start | bytes 786440 | tf_op jit(solution)/shard_map/ppermute | solution.py:265
  22.7 8.1 %collective-permute-start.1 = (bf16[512,256]{1,0:T(8,128)(2,1)S(1)}, bf16[512,256]{1,0:T(8,128)(2,1)S(1)}, u32[]{:S(2)}, u32[]{:S(2)}) collective-permute-start(bf16[512,256]{1,0:T(8,128)(2,1)S(1)} %multiply_convert_fusion.own_ref), channel_id=1, source_target_pairs={{0,1},{2,3},{16,17},{18,19},{32,33},{34,35},{48,49},{50,51},{65,64... | collective-permute-start | bytes 786440 | tf_op jit(solution)/shard_map/ppermute | solution.py:264
  26.5 4.3 %copy-start.8 = (bf16[512,256]{1,0:T(8,128)(2,1)}, bf16[512,256]{1,0:T(8,128)(2,1)S(1)}, u32[]{:S(2)}) copy-start(bf16[512,256]{1,0:T(8,128)(2,1)S(1)} %collective-permute-done.3.both_ref) | copy-start | bytes 786436
  30.7 0.7 copy-start.9
  30.7 0.8 copy-start.10
  31.6 0.8 copy-start.1
  34.9 18.9 %all-to-all-start.1 = ((bf16[8,64,384]{2,1,0:T(8,128)(2,1)}), bf16[8,64,384]{2,1,0:T(8,128)(2,1)S(1)}, u32[]{:S(2)}, u32[]{:S(2)}) async-start(bf16[8,64,384]{2,1,0:T(8,128)(2,1)} %bitcast.29), calls=%async_computation.1 | async-start | bytes 786432 | tf_op jit(solution)/shard_map/all_to_all | solution.py:277
  38.3 18.1 %copy-start.20 = (f32[64]{0:T(128)S(1)}, f32[64]{0:T(128)}, u32[]{:S(2)}) copy-start(f32[64]{0:T(128)} %param.15) | copy-start | bytes 772
  38.3 22.8 %copy-start.18 = (f32[3,7,1024]{2,1,0:T(8,128)S(1)}, f32[3,7,1024]{2,1,0:T(8,128)}, u32[]{:S(2)}) copy-start(f32[3,7,1024]{2,1,0:T(8,128)} %param.13) | copy-start | bytes 258052
  38.6 2.0 %collective-permute-start.6 = (f32[512]{0:T(512)S(1)}, f32[512]{0:T(512)S(1)}, u32[]{:S(2)}, u32[]{:S(2)}) collective-permute-start(f32[512]{0:T(512)S(1)} %multiply_reduce_fusion), channel_id=1, source_target_pairs={{0,3},{1,0},{2,1},{3,2},{4,7},{5,4},{6,5},{7,6},{8,11},{9,8},{10,9... | collective-permute-start | bytes 6152 | tf_op jit(solution)/shard_map/ppermute | solution.py:23
  39.4 3.6 %collective-permute-start.5 = (f32[512]{0:T(512)S(1)}, f32[512]{0:T(512)S(1)}, u32[]{:S(2)}, u32[]{:S(2)}) collective-permute-start(f32[512]{0:T(512)S(1)} %multiply_reduce_fusion), channel_id=1, source_target_pairs={{0,2},{1,3},{2,0},{3,1},{4,6},{5,7},{6,4},{7,5},{8,10},{9,11},{10,... | collective-permute-start | bytes 6152 | tf_op jit(solution)/shard_map/ppermute | solution.py:23
  40.6 3.0 %collective-permute-start.4 = (f32[512]{0:T(512)S(1)}, f32[512]{0:T(512)S(1)}, u32[]{:S(2)}, u32[]{:S(2)}) collective-permute-start(f32[512]{0:T(512)S(1)} %multiply_reduce_fusion), channel_id=1, source_target_pairs={{0,1},{1,2},{2,3},{3,0},{4,5},{5,6},{6,7},{7,4},{8,9},{9,10},{10,1... | collective-permute-start | bytes 6152 | tf_op jit(solution)/shard_map/ppermute | solution.py:23
  53.9 5.7 %collective-permute-start.7 = (bf16[64,384]{1,0:T(8,128)(2,1)S(1)}, bf16[64,384]{1,0:T(8,128)(2,1)S(1)}, u32[]{:S(2)}, u32[]{:S(2)}) collective-permute-start(bf16[64,384]{1,0:T(8,128)(2,1)S(1)} %multiply_convert_fusion.1), channel_id=1, source_target_pairs={{0,128},{128,0},{1,129},{129,1},{2,130},{130,2},{3,131},{131,3},{4... | collective-permute-start | bytes 147464 | tf_op jit(solution)/shard_map/ppermute | solution.py:23
  59.7 24.3 %copy-start.4 = (bf16[128,384]{1,0:T(8,128)(2,1)}, bf16[128,384]{1,0:T(8,128)(2,1)S(1)}, u32[]{:S(2)}) copy-start(bf16[128,384]{1,0:T(8,128)(2,1)S(1)} %pad_maximum_fusion.refs_0_) | copy-start | bytes 294916
  59.7 5.9 %collective-permute-start.8 = (bf16[128,384]{1,0:T(8,128)(2,1)S(1)}, bf16[128,384]{1,0:T(8,128)(2,1)S(1)}, u32[]{:S(2)}, u32[]{:S(2)}) collective-permute-start(bf16[128,384]{1,0:T(8,128)(2,1)S(1)} %pad_maximum_fusion.refs_0_), channel_id=1, source_target_pairs={{0,16},{16,32},{32,48},{48,64},{64,80},{80,96},{96,112},{112,0},{1... | collective-permute-start | bytes 294920 | tf_op jit(solution)/shard_map/ppermute | solution.py:23
  61.2 7.7 %collective-permute-start.12 = (bf16[128,384]{1,0:T(8,128)(2,1)S(1)}, bf16[128,384]{1,0:T(8,128)(2,1)S(1)}, u32[]{:S(2)}, u32[]{:S(2)}) collective-permute-start(bf16[128,384]{1,0:T(8,128)(2,1)S(1)} %pad_maximum_fusion.refs_0_), channel_id=1, source_target_pairs={{0,112},{16,0},{32,16},{48,32},{64,48},{80,64},{96,80},{112,96},{1... | collective-permute-start | bytes 294920 | tf_op jit(solution)/shard_map/ppermute | solution.py:23
  65.6 18.4 %copy-start.11 = (bf16[128,384]{1,0:T(8,128)(2,1)}, bf16[128,384]{1,0:T(8,128)(2,1)S(1)}, u32[]{:S(2)}) copy-start(bf16[128,384]{1,0:T(8,128)(2,1)S(1)} %collective-permute-done.8.refs_1_) | copy-start | bytes 294916
  65.6 6.6 %collective-permute-start.9 = (bf16[128,384]{1,0:T(8,128)(2,1)S(1)}, bf16[128,384]{1,0:T(8,128)(2,1)S(1)}, u32[]{:S(2)}, u32[]{:S(2)}) collective-permute-start(bf16[128,384]{1,0:T(8,128)(2,1)S(1)} %collective-permute-done.8.refs_1_), channel_id=1, source_target_pairs={{0,16},{16,32},{32,48},{48,64},{64,80},{80,96},{96,112},{112,0},{1... | collective-permute-start | bytes 294920 | tf_op jit(solution)/shard_map/ppermute | solution.py:23
  68.9 15.1 %copy-start.12 = (bf16[128,384]{1,0:T(8,128)(2,1)}, bf16[128,384]{1,0:T(8,128)(2,1)S(1)}, u32[]{:S(2)}) copy-start(bf16[128,384]{1,0:T(8,128)(2,1)S(1)} %collective-permute-done.12.refs_7_) | copy-start | bytes 294916
  68.9 5.4 %collective-permute-start.13 = (bf16[128,384]{1,0:T(8,128)(2,1)S(1)}, bf16[128,384]{1,0:T(8,128)(2,1)S(1)}, u32[]{:S(2)}, u32[]{:S(2)}) collective-permute-start(bf16[128,384]{1,0:T(8,128)(2,1)S(1)} %collective-permute-done.12.refs_7_), channel_id=1, source_target_pairs={{0,112},{16,0},{32,16},{48,32},{64,48},{80,64},{96,80},{112,96},{1... | collective-permute-start | bytes 294920 | tf_op jit(solution)/shard_map/ppermute | solution.py:23
  72.2 11.8 %copy-start.13 = (bf16[128,384]{1,0:T(8,128)(2,1)}, bf16[128,384]{1,0:T(8,128)(2,1)S(1)}, u32[]{:S(2)}) copy-start(bf16[128,384]{1,0:T(8,128)(2,1)S(1)} %collective-permute-done.9.refs_2_) | copy-start | bytes 294916
  72.2 6.0 %collective-permute-start.10 = (bf16[128,384]{1,0:T(8,128)(2,1)S(1)}, bf16[128,384]{1,0:T(8,128)(2,1)S(1)}, u32[]{:S(2)}, u32[]{:S(2)}) collective-permute-start(bf16[128,384]{1,0:T(8,128)(2,1)S(1)} %collective-permute-done.9.refs_2_), channel_id=1, source_target_pairs={{0,16},{16,32},{32,48},{48,64},{64,80},{80,96},{96,112},{112,0},{1... | collective-permute-start | bytes 294920 | tf_op jit(solution)/shard_map/ppermute | solution.py:23
  74.4 9.6 %copy-start.14 = (bf16[128,384]{1,0:T(8,128)(2,1)}, bf16[128,384]{1,0:T(8,128)(2,1)S(1)}, u32[]{:S(2)}) copy-start(bf16[128,384]{1,0:T(8,128)(2,1)S(1)} %collective-permute-done.13.refs_6_) | copy-start | bytes 294916
  74.4 5.8 %collective-permute-start.14 = (bf16[128,384]{1,0:T(8,128)(2,1)S(1)}, bf16[128,384]{1,0:T(8,128)(2,1)S(1)}, u32[]{:S(2)}, u32[]{:S(2)}) collective-permute-start(bf16[128,384]{1,0:T(8,128)(2,1)S(1)} %collective-permute-done.13.refs_6_), channel_id=1, source_target_pairs={{0,112},{16,0},{32,16},{48,32},{64,48},{80,64},{96,80},{112,96},{1... | collective-permute-start | bytes 294920 | tf_op jit(solution)/shard_map/ppermute | solution.py:23
  78.2 5.9 %copy-start.15 = (bf16[128,384]{1,0:T(8,128)(2,1)}, bf16[128,384]{1,0:T(8,128)(2,1)S(1)}, u32[]{:S(2)}) copy-start(bf16[128,384]{1,0:T(8,128)(2,1)S(1)} %collective-permute-done.10.refs_3_) | copy-start | bytes 294916
  78.2 5.8 %collective-permute-start.11 = (bf16[128,384]{1,0:T(8,128)(2,1)S(1)}, bf16[128,384]{1,0:T(8,128)(2,1)S(1)}, u32[]{:S(2)}, u32[]{:S(2)}) collective-permute-start(bf16[128,384]{1,0:T(8,128)(2,1)S(1)} %collective-permute-done.10.refs_3_), channel_id=1, source_target_pairs={{0,16},{16,32},{32,48},{48,64},{64,80},{80,96},{96,112},{112,0},{1... | collective-permute-start | bytes 294920 | tf_op jit(solution)/shard_map/ppermute | solution.py:23
  80.2 3.8 %copy-start.16 = (bf16[128,384]{1,0:T(8,128)(2,1)}, bf16[128,384]{1,0:T(8,128)(2,1)S(1)}, u32[]{:S(2)}) copy-start(bf16[128,384]{1,0:T(8,128)(2,1)S(1)} %collective-permute-done.14.refs_5_) | copy-start | bytes 294916
  84.0 0.6 copy-start.17
  96.0 6.5 %copy-start.22 = (bf16[512,256]{1,0:T(8,128)(2,1)S(1)}, bf16[512,256]{1,0:T(8,128)(2,1)}, u32[]{:S(2)}) copy-start(bf16[512,256]{1,0:T(8,128)(2,1)} %mixed_block.5) | copy-start | bytes 786436
  96.0 6.7 %copy-start.21 = (bf16[512,256]{1,0:T(8,128)(2,1)S(1)}, bf16[512,256]{1,0:T(8,128)(2,1)}, u32[]{:S(2)}) copy-start(bf16[512,256]{1,0:T(8,128)(2,1)} %mixed_block.4) | copy-start | bytes 786436
  100.7 8.8 %collective-permute-start.17 = (bf16[512,256]{1,0:T(8,128)(2,1)}, bf16[512,256]{1,0:T(8,128)(2,1)S(1)}, u32[]{:S(2)}, u32[]{:S(2)}) collective-permute-start(bf16[512,256]{1,0:T(8,128)(2,1)} %mixed_block.6), channel_id=1, source_target_pairs={{0,12},{4,0},{8,4},{12,8},{1,13},{5,1},{9,5},{13,9},{2,14},{6,2},{... | collective-permute-start | bytes 786440 | tf_op jit(solution)/shard_map/ppermute | solution.py:23
  102.5 10.4 %collective-permute-start.15 = (bf16[512,256]{1,0:T(8,128)(2,1)S(1)}, bf16[512,256]{1,0:T(8,128)(2,1)S(1)}, u32[]{:S(2)}, u32[]{:S(2)}) collective-permute-start(bf16[512,256]{1,0:T(8,128)(2,1)S(1)} %copy-done.22), channel_id=1, source_target_pairs={{0,4},{4,8},{8,12},{12,0},{1,5},{5,9},{9,13},{13,1},{2,6},{6,10},{... | collective-permute-start | bytes 786440 | tf_op jit(solution)/shard_map/ppermute | solution.py:23
  102.7 10.2 %collective-permute-start.16 = (bf16[512,256]{1,0:T(8,128)(2,1)S(1)}, bf16[512,256]{1,0:T(8,128)(2,1)S(1)}, u32[]{:S(2)}, u32[]{:S(2)}) collective-permute-start(bf16[512,256]{1,0:T(8,128)(2,1)S(1)} %copy-done.21), channel_id=1, source_target_pairs={{0,8},{4,12},{8,0},{12,4},{1,9},{5,13},{9,1},{13,5},{2,10},{6,14},... | collective-permute-start | bytes 786440 | tf_op jit(solution)/shard_map/ppermute | solution.py:23
  109.5 3.4 %copy-start.5 = (bf16[512,256]{1,0:T(8,128)(2,1)}, bf16[512,256]{1,0:T(8,128)(2,1)S(1)}, u32[]{:S(2)}) copy-start(bf16[512,256]{1,0:T(8,128)(2,1)S(1)} %collective-permute-done.17.refs_3_) | copy-start | bytes 786436
  112.9 0.7 copy-start.6
  112.9 0.8 copy-start.7

commit v3 on v2

v3 whole, which is shorter than its diff:
```python
import jax
import jax.numpy as jnp
import numpy as np
from jax import lax
from jax.experimental import pallas as pl
from jax.experimental.pallas import tpu as pltpu
from jax.sharding import Mesh, PartitionSpec as P

GROUP = 16
SHORT_TAPS = 7
LONG_TAPS = 128
LANES = 128
HALO = 144
STREAMS = 3
BF = jnp.bfloat16
F32 = jnp.float32


def shifted(value, axis, steps):
    count = lax.axis_size(axis)
    pairs = [(source, (source + steps) % count) for source in range(count)]
    return lax.ppermute(value, axis, pairs)


def payload_kernel(weight_ref, ids_ref, out_ref):
    rows = weight_ref.shape[1]
    values = ids_ref[...]
    coded = jnp.concatenate(
        [values >> 4, values & 15, jnp.zeros((8, LANES), jnp.int32)], axis=0
    ).astype(F32).astype(BF)
    for tile in range(out_ref.shape[0]):
        for p in range(STREAMS):
            out_ref[tile, p * rows : (p + 1) * rows, :] = weight_ref[
                p, :, tile * LANES : (tile + 1) * LANES
            ]
        out_ref[tile, STREAMS * rows :, :] = coded


def in_vmem(count):
    return [pl.BlockSpec(memory_space=pltpu.VMEM)] * count


def cost(flops, moved):
    return pl.CostEstimate(flops=flops, bytes_accessed=moved, transcendentals=0)


def payload(in_weight, ids_rows):
    streams, rows, width = in_weight.shape
    return pl.pallas_call(
        payload_kernel,
        out_shape=jax.ShapeDtypeStruct((width // LANES, streams * rows + 16, LANES), BF),
        in_specs=in_vmem(2),
        out_specs=pl.BlockSpec(memory_space=pltpu.VMEM),
        cost_estimate=cost(0, 800000),
        name="payload",
    )(in_weight, ids_rows)


def partial_kernel(flag_ref, own_ref, core_ref, chip_ref, both_ref, pieces_ref, out_ref):
    rows = (pieces_ref.shape[1] - 16) // STREAMS
    half = own_ref.shape[1]
    weight = jnp.concatenate(
        [
            pieces_ref[:, p * rows : (p + 1) * rows, :].reshape(2 * half, LANES)
            for p in range(STREAMS)
        ],
        axis=1,
    )
    mine = flag_ref[0] == 1
    swap = flag_ref[1] == 1
    near = jnp.where(mine, own_ref[...], core_ref[...])
    far = jnp.where(mine, chip_ref[...], both_ref[...])
    features = jnp.concatenate(
        [jnp.where(swap, far, near), jnp.where(swap, near, far)], axis=1
    )
    out_ref[...] = jnp.dot(features, weight, preferred_element_type=F32).astype(BF)


def partial_table(flags, own, got_core, got_chip, got_both, pieces):
    vocab, half = own.shape
    return pl.pallas_call(
        partial_kernel,
        out_shape=jax.ShapeDtypeStruct((vocab, STREAMS * LANES), BF),
        in_specs=[pl.BlockSpec(memory_space=pltpu.SMEM)] + in_vmem(5),
        out_specs=pl.BlockSpec(memory_space=pltpu.VMEM),
        cost_estimate=cost(4 * vocab * half * STREAMS * LANES, 2000000),
        name="partial_table",
    )(flags, own, got_core, got_chip, got_both, pieces)


def toeplitz_kernel(taps_ref, out_ref):
    for g in range(taps_ref.shape[0]):
        row = jnp.broadcast_to(taps_ref[g : g + 1, :], (LONG_TAPS, 2 * LONG_TAPS))
        out_ref[g * LONG_TAPS : (g + 1) * LONG_TAPS, :] = pltpu.roll(
            row, 0, 1, stride=1, stride_axis=0
        ).astype(BF)


def toeplitz(taps_row):
    groups = taps_row.shape[0]
    return pl.pallas_call(
        toeplitz_kernel,
        out_shape=jax.ShapeDtypeStruct((groups * LONG_TAPS, 2 * LONG_TAPS), BF),
        in_specs=in_vmem(1),
        out_specs=pl.BlockSpec(memory_space=pltpu.VMEM),
        cost_estimate=cost(2000000, 1060000),
        name="toeplitz",
    )(taps_row)


def column_of(coded, z, share, count):
    rows = coded.shape[0] // 2
    known = (coded[:rows] * 16.0 + coded[rows:]).astype(jnp.int32)
    bits = share.bit_length() - 1
    turned = (((z - (known >> bits)) & (count - 1)) << bits) + (known & (share - 1))
    padded = jnp.concatenate([turned.astype(F32), jnp.zeros((8 - rows, LANES), F32)], axis=0)
    return jnp.transpose(padded).astype(jnp.int32)


def one_hot(column, vocab):
    hit = column == lax.broadcasted_iota(jnp.int32, (column.shape[0], vocab), 1)
    return jnp.where(hit, 1.0, 0.0).astype(BF)


def mix_kernel(spot_ref, ids_ref, *refs):
    tables = refs[:8]
    filt_ref, toep_ref, out_ref, table_ref, proj_ref, lead_ref, inner_ref, gate_ref = refs[8:]
    z = spot_ref[0]
    step = pl.program_id(0)
    share, width = tables[0].shape
    vocab = table_ref.shape[0]
    tokens = out_ref.shape[1]
    groups = LANES // GROUP
    margin = proj_ref.shape[1] - tokens
    lead = lead_ref.shape[1]
    chunk = 64

    @pl.when(step == 0)
    def _():
        for j in range(8):
            table_ref[j * share : (j + 1) * share, :] = tables[j][:share, :]

    def short(source, p, start, count):
        total = None
        for k in range(SHORT_TAPS):
            tap = filt_ref[p, k : k + 1, :]
            term = tap * source[p, start - k : start - k + count, :]
            total = term if total is None else total + term
        return total

    @pl.when(step % 4 == 0)
    def _():
        segment = step // 4
        segment = jnp.where(z == 0, 1 - segment, segment)
        coded = tables[1][share:, :LANES].astype(F32)
        coded = jnp.where(segment == 0, coded[:4], coded[4:8])
        column = column_of(coded, z, share, 8)
        column = jnp.concatenate([column[2 * LANES - lead :, 0:1], column[:, 1:2]], axis=0)
        proj = jnp.dot(one_hot(column, vocab), table_ref[...], preferred_element_type=F32)
        for p in range(STREAMS):
            lead_ref[p] = proj[:, p * LANES : (p + 1) * LANES]
            proj_ref[p, :margin, :] = lead_ref[p, lead - margin :, :]
        for at in range(0, LONG_TAPS, chunk):
            left = short(lead_ref, 1, lead - LONG_TAPS + at, chunk)
            right = short(lead_ref, 2, lead - LONG_TAPS + at, chunk)
            inner_ref[at : at + chunk, :] = (left * right).astype(BF)

    @pl.when(step % 4 != 0)
    def _():
        for p in range(STREAMS):
            proj_ref[p, :margin, :] = proj_ref[p, tokens:, :]
        inner_ref[:LONG_TAPS, :] = inner_ref[tokens:, :]

    coded = ids_ref[0].astype(F32)
    column = column_of(coded[: 2 * tokens // LANES], z, share, 8)
    column = jnp.concatenate([column[:, j : j + 1] for j in range(tokens // LANES)], axis=0)
    proj = jnp.dot(one_hot(column, vocab), table_ref[...], preferred_element_type=F32)
    for p in range(STREAMS):
        proj_ref[p, margin:, :] = proj[:, p * LANES : (p + 1) * LANES]
    for at in range(0, tokens, chunk):
        left = short(proj_ref, 1, margin + at, chunk)
        right = short(proj_ref, 2, margin + at, chunk)
        inner_ref[LONG_TAPS + at : LONG_TAPS + at + chunk, :] = (left * right).astype(BF)
        gate_ref[at : at + chunk, :] = short(proj_ref, 0, margin + at, chunk)

    lane_group = lax.broadcasted_iota(jnp.int32, (LONG_TAPS, LANES), 1) // GROUP
    for base in range(0, tokens, 2 * LONG_TAPS):
        window = jnp.concatenate(
            [
                inner_ref[base : base + 2 * LONG_TAPS, :],
                inner_ref[base + LONG_TAPS : base + 3 * LONG_TAPS, :],
            ],
            axis=1,
        )
        full = jnp.dot(toep_ref[...], window, preferred_element_type=F32)
        for side in range(2):
            lanes = slice(side * LANES, (side + 1) * LANES)
            conv = full[:LONG_TAPS, lanes]
            for g in range(1, groups):
                conv = jnp.where(
                    lane_group == g, full[g * LONG_TAPS : (g + 1) * LONG_TAPS, lanes], conv
                )
            at = base + side * LONG_TAPS
            out_ref[0, at : at + LONG_TAPS, :] = (gate_ref[at : at + LONG_TAPS, :] * conv).astype(
                BF
            )


def mixed_blocks(spot, pieces, tables, filt, toep, tokens):
    blocks, held, _ = pieces.shape
    share, width = tables[0].shape

    def whole(value):
        return pl.BlockSpec(value.shape, lambda i: (0,) * value.ndim)

    return pl.pallas_call(
        mix_kernel,
        out_shape=jax.ShapeDtypeStruct((blocks, tokens, LANES), BF),
        grid=(blocks,),
        in_specs=[
            pl.BlockSpec(memory_space=pltpu.SMEM),
            pl.BlockSpec((1, 16, LANES), lambda i: (i, held // 16 - 1, 0)),
        ]
        + [whole(table) for table in tables]
        + [whole(filt), whole(toep)],
        out_specs=pl.BlockSpec((1, tokens, LANES), lambda i: (i, 0, 0)),
        scratch_shapes=[
            pltpu.VMEM((8 * share, width), BF),
            pltpu.VMEM((STREAMS, tokens + 8, LANES), F32),
            pltpu.VMEM((STREAMS, HALO, LANES), F32),
            pltpu.VMEM((tokens + LONG_TAPS, LANES), BF),
            pltpu.VMEM((tokens, LANES), F32),
        ],
        cost_estimate=cost(5000000000, 4000000),
        name="mixed_blocks",
    )(spot, pieces, *tables, filt, toep)


def per_device(ids, embed_table, norm_gain, in_weight, in_scale, short_filter, long_filter, decay):
    tokens = ids.shape[0]
    vocab, width_local = embed_table.shape
    rows = in_weight.shape[1]
    yh = lax.axis_index("yh")
    z = lax.axis_index("z")
    x = lax.axis_index("x")
    yl = lax.axis_index("yl")
    core = lax.axis_index("core")
    x_count = lax.axis_size("x")
    z_count = lax.axis_size("z")
    tile = yh * x_count + x
    full_width = norm_gain.shape[0]

    load = payload(in_weight, ids.reshape(-1, LANES))
    pieces = lax.all_to_all(load, ("yh", "x"), 0, 0, tiled=True)

    chunk = x_count * rows
    gain = lax.dynamic_slice_in_dim(norm_gain, yl * (full_width // 2) + z * chunk, chunk, 0)
    own = lax.dynamic_slice_in_dim(embed_table, (z % 4) * chunk, chunk, 1)
    own = (own.astype(F32) * gain[None, :]).astype(BF)
    around = ("yh", "z", "yl", "core")

    def spot(y, zi, ci):
        return ((y // 2 % 2 * z_count + zi) * 2 + y % 2) * 2 + ci

    holders = [(y, zi, zi // 4) for y in range(4) for zi in range(z_count)]
    got_core = lax.ppermute(
        own, around, [(spot(a, b, c), spot(a, b, 1 - c)) for a, b, c in holders]
    )
    got_chip = lax.ppermute(
        own, around, [(spot(a, b, c), spot((a + 1) % 4, b, c)) for a, b, c in holders]
    )
    got_both = lax.ppermute(
        own, around, [(spot(a, b, c), spot((a + 3) % 4, b, 1 - c)) for a, b, c in holders]
    )
    local_f = embed_table.astype(F32)
    squares = jnp.sum(local_f * local_f, axis=1)
    others = [shifted(squares, ("yl", "core"), s) for s in (1, 2, 3)]
    total = squares + others[0] + others[1] + others[2]

    flags = jnp.stack([core == z // 4, yl == 1]).astype(jnp.int32)
    partial = partial_table(flags, own, got_core, got_chip, got_both, pieces)
    share = vocab // z_count
    swapped = lax.all_to_all(
        partial.reshape(z_count, share, STREAMS * LANES), "z", 0, 0, tiled=True
    )
    scale = lax.dynamic_slice_in_dim(in_scale, tile * LANES, LANES, 1).reshape(1, STREAMS * LANES)
    norm = lax.rsqrt(lax.dynamic_slice_in_dim(total, z * share, share, 0) / full_width + 1e-06)
    piece = (jnp.sum(swapped.astype(F32), axis=0) * norm[:, None] * scale).astype(BF)
    coded = pieces[x_count - 1 :: x_count, STREAMS * rows :, :].reshape(2, 2, 8, LANES)[:, 0]
    edges = jnp.concatenate([coded[:, 2:4], coded[:, 6:8]], axis=1).reshape(8, LANES)
    edges = jnp.pad(edges, ((0, 8), (0, (STREAMS - 1) * LANES)))
    ups = [piece, shifted(jnp.concatenate([piece, edges], axis=0), "z", 1)]
    downs, last = [], piece
    for _ in range(3):
        ups.append(shifted(ups[-1][:share], "z", 1))
        last = shifted(last, "z", -1)
        downs.append(last)
    tables = ups + downs[::-1]

    groups = LANES // GROUP
    steps = jnp.arange(LONG_TAPS, dtype=F32)
    filt = lax.dynamic_slice_in_dim(long_filter, tile * groups, groups, 1)
    rate = lax.dynamic_slice_in_dim(decay, tile * groups, groups, 0)
    taps = (filt * jnp.exp(-rate[None, :] * steps[:, None])).astype(BF).astype(F32)
    toep = toeplitz(jnp.pad(taps[::-1].T, ((0, 0), (1, LONG_TAPS - 1))))
    near_filter = lax.dynamic_slice_in_dim(short_filter, tile * LANES, LANES, 2)

    blocks = mixed_blocks(
        z.reshape(1).astype(jnp.int32), pieces, tables, near_filter, toep, tokens
    )
    result = lax.all_to_all(blocks, ("yh", "x"), 0, 0, tiled=True)
    return result.transpose(1, 0, 2).reshape(tokens, width_local)


def solution(mesh):
    fine = Mesh(mesh.devices.reshape(2, 8, 4, 2, 2), ("yh", "z", "x", "yl", "core"))
    ctx = ("yh", "z", "x")
    tp = ("yl", "core")
    placed = (
        P(ctx),
        P(None, tp),
        P(),
        P(None, ctx, tp),
        P(None, tp),
        P(None, None, tp),
        P(None, tp),
        P(tp),
    )
    return jax.shard_map(
        per_device, mesh=fine, in_specs=placed, out_specs=P(ctx, tp), check_vma=False
    )
```

time: 118 us -> 109 us (0.924); the launches traced: 116 us -> 109 us
  blocking collectives: 0 us -> 16.6 us
  waiting for transfers between devices: 41.8 us -> 29.1 us
  Pallas kernels: 29.5 us -> 19.3 us
  local copies, waits for them, and re-layouts: 8.12 us -> 6.7 us
    ppermute x15 -> x10, waiting for transfers between devices: 25.6 us -> 7.61 us  [shifted(): return lax.ppermute(value, axis, pairs)]
    all_to_all x0 -> x1, blocking collectives: none -> 16.6 us  [per_device(): result = lax.all_to_all(blocks, ('yh', 'x'), 0, 0, tiled=True)]
    pallas_call x6 -> x1, Pallas kernels: 23.1 us -> 13.3 us  [mixed_blocks(): pl.pallas_call(mix_kernel, out_shape=jax.ShapeDtypeStruct((blocks, tokens...]
    ppermute x15 -> x10, starting transfers between devices: 19.8 us -> 12.4 us  [shifted(): return lax.ppermute(value, axis, pairs)]
    all_to_all x1, waiting for transfers between devices: 0.01 us -> 5.89 us  [per_device(): pieces = lax.all_to_all(load, ('yh', 'x'), 0, 0, tiled=True)]
    ppermute x3, waiting for transfers between devices: 6.11 us -> 0.99 us  [the longest x1 0.99 us: per_device(): lax.ppermute(own, around, [(spot(a, b, c), spot(a, b, 1 - c)) for a, b, c...]
    all_to_all x1, waiting for transfers between devices: 10 us -> 14.6 us  [per_device(): lax.all_to_all(partial.reshape(z_count, share, STREAMS * LANES), 'z', 0,...]
    all_to_all x1, starting transfers between devices: 3.46 us -> 7.07 us  [per_device(): pieces = lax.all_to_all(load, ('yh', 'x'), 0, 0, tiled=True)]
  transfers between devices with their start and end apart: 20 -> 15, of which waited for: 13 -> 7; matrix products, arithmetic and copies ran while one was open for 6% -> 6% of each run, Pallas kernels for 6% -> 3%
where the time goes in v3:
time: 109 us
  starting transfers between devices  32.3 us (30%)
  waiting for transfers between devices  29.1 us (27%)
  Pallas kernels  19.3 us (18%)
  blocking collectives  16.6 us (15%)
  local copies, waits for them, and re-layouts  6.7 us (6%)
  other arithmetic  4.29 us (4%)
    all_to_all x1, blocking collectives, per_device(): result = lax.all_to_all(blocks, ('yh', 'x'), 0, 0, tiled=True)  16.6 us
    all_to_all x1, waiting for transfers between devices, per_device(): lax.all_to_all(partial.reshape(z_count, share, STREAMS * LANES), 'z', 0,...  14.6 us
    pallas_call x1, Pallas kernels, mixed_blocks(): pl.pallas_call(mix_kernel, out_shape=jax.ShapeDtypeStruct((blocks, tokens...  13.3 us
    ppermute x10, starting transfers between devices, shifted(): return lax.ppermute(value, axis, pairs)  12.4 us
    ppermute x10, waiting for transfers between devices, shifted(): return lax.ppermute(value, axis, pairs)  7.61 us
    all_to_all x1, starting transfers between devices, per_device(): pieces = lax.all_to_all(load, ('yh', 'x'), 0, 0, tiled=True)  7.07 us
    all_to_all x1, starting transfers between devices, per_device(): lax.all_to_all(partial.reshape(z_count, share, STREAMS * LANES), 'z', 0,...  6.03 us
    all_to_all x1, waiting for transfers between devices, per_device(): pieces = lax.all_to_all(load, ('yh', 'x'), 0, 0, tiled=True)  5.89 us
  transfers between devices with their start and end apart: 15, of which 7 were waited for; matrix products, arithmetic and copies ran while one was open for 6% of the time, Pallas kernels for 3%

profile of v3, /device:TPU:8, one launch (start us, length us, event | category | flops | bytes accessed | tf_op | source)
XLA Modules:
  0.0 108.6 jit_solution(13111120837954626252)
XLA Ops:
  0.0 0.0 copy-start
  0.0 1.5 %multiply_reduce_fusion = f32[512]{0:T(512)S(1)} fusion(bf16[512,1024]{1,0:T(8,128)(2,1)} %param.9), kind=kLoop, calls=%fused_computation | loop fusion | flops 1572352 | bytes 1050624 | tf_op jit(solution)/shard_map/reduce_sum | solution.py:276
  1.5 0.1 collective-permute-start.5
  1.6 2.3 %collective-permute-start.4 = (f32[512]{0:T(512)S(1)}, f32[512]{0:T(512)S(1)}, u32[]{:S(2)}, u32[]{:S(2)}) collective-permute-start(f32[512]{0:T(512)S(1)} %multiply_reduce_fusion), channel_id=1, source_target_pairs={{0,2},{1,3},{2,0},{3,1},{4,6},{5,7},{6,4},{7,5},{8,10},{9,11},{10,... | collective-permute-start | bytes 6152 | tf_op jit(solution)/shard_map/ppermute | solution.py:22
  3.9 0.1 collective-permute-start.3
  4.0 0.8 dynamic_slice.22
  4.8 1.0 multiply_convert_fusion.own_ref
  5.8 0.0 copy-start.2
  5.8 3.5 %collective-permute-start.2 = (bf16[512,256]{1,0:T(8,128)(2,1)S(1)}, bf16[512,256]{1,0:T(8,128)(2,1)S(1)}, u32[]{:S(2)}, u32[]{:S(2)}) collective-permute-start(bf16[512,256]{1,0:T(8,128)(2,1)S(1)} %multiply_convert_fusion.own_ref), channel_id=1, source_target_pairs={{0,131},{16,147},{32,163},{48,179},{65,194},{81,210},{97,226},{113... | collective-permute-start | bytes 786440 | tf_op jit(solution)/shard_map/ppermute | solution.py:272
  9.3 2.0 %collective-permute-start.1 = (bf16[512,256]{1,0:T(8,128)(2,1)S(1)}, bf16[512,256]{1,0:T(8,128)(2,1)S(1)}, u32[]{:S(2)}, u32[]{:S(2)}) collective-permute-start(bf16[512,256]{1,0:T(8,128)(2,1)S(1)} %multiply_convert_fusion.own_ref), channel_id=1, source_target_pairs={{0,2},{16,18},{32,34},{48,50},{65,67},{81,83},{97,99},{113,115},{2... | collective-permute-start | bytes 786440 | tf_op jit(solution)/shard_map/ppermute | solution.py:269
  11.4 1.8 %payload.1 = bf16[8,208,128]{2,1,0:T(8,128)(2,1)} custom-call(bf16[3,64,1024]{2,1,0:T(8,128)(2,1)} %weight_ref.1, s32[4,128]{1,0:T(4,128)} %bitcast.22), custom_call_target="tpu_custom_call" | custom-call | bytes 800000 | tf_op jit(solution)/shard_map/payload/pallas_call | solution.py:49
  13.2 7.1 %all-to-all-start = ((bf16[8,208,128]{2,1,0:T(8,128)(2,1)}), bf16[8,208,128]{2,1,0:T(8,128)(2,1)S(1)}, u32[]{:S(2)}, u32[]{:S(2)}) async-start(bf16[8,208,128]{2,1,0:T(8,128)(2,1)} %payload.1), calls=%async_computation | async-start | bytes 851968 | tf_op jit(solution)/shard_map/all_to_all | solution.py:254
  20.3 0.7 dynamic-slice_bitcast_fusion
  20.9 0.7 add_convert_fusion.flag_ref
  21.6 0.0 collective-permute-done.5
  21.6 1.3 %collective-permute-start = (bf16[512,256]{1,0:T(8,128)(2,1)S(1)}, bf16[512,256]{1,0:T(8,128)(2,1)S(1)}, u32[]{:S(2)}, u32[]{:S(2)}) collective-permute-start(bf16[512,256]{1,0:T(8,128)(2,1)S(1)} %multiply_convert_fusion.own_ref), channel_id=1, source_target_pairs={{0,1},{16,17},{32,33},{48,49},{65,64},{81,80},{97,96},{113,112},{2... | collective-permute-start | bytes 786440 | tf_op jit(solution)/shard_map/ppermute | solution.py:266
  22.9 0.0 collective-permute-done.4
  22.9 0.0 collective-permute-done.3
  22.9 0.1 add_rsqrt_fusion
  23.0 0.0 collective-permute-done.2.both_ref
  23.0 0.0 collective-permute-done.1.chip_ref
  23.0 0.0 copy-start.4
  23.0 1.0 collective-permute-done.core_ref
  24.0 5.9 %all-to-all-done.pieces_ref.ids_ref = bf16[8,208,128]{2,1,0:T(8,128)(2,1)S(1)} async-done(((bf16[8,208,128]{2,1,0:T(8,128)(2,1)}), bf16[8,208,128]{2,1,0:T(8,128)(2,1)S(1)}, u32[]{:S(2)}, u32[]{:S(2)}) %all-to-all-start) | async-done | bytes 426016 | tf_op jit(solution)/shard_map/all_to_all | solution.py:254
  29.9 0.0 copy-done.2
  29.9 0.0 copy-done.3
  30.0 0.7 copy-done.1
  30.7 2.5 %partial_table.1 = bf16[512,384]{1,0:T(8,128)(2,1)} custom-call(s32[2]{0:T(128)} %add_convert_fusion.flag_ref, bf16[512,256]{1,0:T(8,128)(2,1)} %copy-done.2, bf16[512,256]{1,0:T(8,128)(2,1)} %copy-done.5, bf16[512,256]{1,0:T(8,128)(2,1)} %copy-done.4, bf16[512,256]{1,0:T(8,128)(2,1)} %copy-done.3, bf16[8,208,128]{2,1,0:T(8,128)(2,1)} %copy-done.1), custom_call_target="tpu_custom_call" | custom-call | flops 201326592 | bytes 2000000 | tf_op jit(solution)/shard_map/partial_table/pallas_call | solution.py:81
  33.2 6.0 %all-to-all-start.1 = ((bf16[8,64,384]{2,1,0:T(8,128)(2,1)}), bf16[8,64,384]{2,1,0:T(8,128)(2,1)S(1)}, u32[]{:S(2)}, u32[]{:S(2)}) async-start(bf16[8,64,384]{2,1,0:T(8,128)(2,1)} %bitcast.19), calls=%async_computation.1 | async-start | bytes 786432 | tf_op jit(solution)/shard_map/all_to_all | solution.py:283
  39.3 0.7 slice_bitcast_fusion
  40.0 14.6 %all-to-all-done.1 = bf16[8,64,384]{2,1,0:T(8,128)(2,1)S(1)} async-done(((bf16[8,64,384]{2,1,0:T(8,128)(2,1)}), bf16[8,64,384]{2,1,0:T(8,128)(2,1)S(1)}, u32[]{:S(2)}, u32[]{:S(2)}) %all-to-all-start.1) | async-done | bytes 393248 | tf_op jit(solution)/shard_map/all_to_all | solution.py:283
  54.6 0.1 convert_reduce_fusion
  54.7 0.1 multiply_convert_fusion.1.refs_0_
  54.8 0.6 collective-permute-start.6
  55.4 2.7 %collective-permute-start.10 = (bf16[64,384]{1,0:T(8,128)(2,1)S(1)}, bf16[64,384]{1,0:T(8,128)(2,1)S(1)}, u32[]{:S(2)}, u32[]{:S(2)}) collective-permute-start(bf16[64,384]{1,0:T(8,128)(2,1)S(1)} %multiply_convert_fusion.1.refs_0_), channel_id=1, source_target_pairs={{0,112},{16,0},{32,16},{48,32},{64,48},{80,64},{96,80},{112,96},{1... | collective-permute-start | bytes 147464 | tf_op jit(solution)/shard_map/ppermute | solution.py:22
  58.1 2.2 %collective-permute-done.6.refs_1_ = bf16[80,384]{1,0:T(8,128)(2,1)S(1)} collective-permute-done((bf16[80,384]{1,0:T(8,128)(2,1)S(1)}, bf16[80,384]{1,0:T(8,128)(2,1)S(1)}, u32[]{:S(2)}, u32[]{:S(2)}) %collective-permute-start.6) | collective-permute-done | bytes 61472 | tf_op jit(solution)/shard_map/ppermute | solution.py:22
  60.3 0.1 collective-permute-start.7
  60.4 0.0 copy-done.14
  60.4 0.1 dynamic-slice_negate_fusion
  60.5 0.0 collective-permute-done.10.refs_7_
  60.5 3.2 %collective-permute-start.11 = (bf16[64,384]{1,0:T(8,128)(2,1)S(1)}, bf16[64,384]{1,0:T(8,128)(2,1)S(1)}, u32[]{:S(2)}, u32[]{:S(2)}) collective-permute-start(bf16[64,384]{1,0:T(8,128)(2,1)S(1)} %collective-permute-done.10.refs_7_), channel_id=1, source_target_pairs={{0,112},{16,0},{32,16},{48,32},{64,48},{80,64},{96,80},{112,96},{1... | collective-permute-start | bytes 147464 | tf_op jit(solution)/shard_map/ppermute | solution.py:22
  63.7 2.0 %collective-permute-done.7.refs_2_ = bf16[64,384]{1,0:T(8,128)(2,1)S(1)} collective-permute-done((bf16[64,384]{1,0:T(8,128)(2,1)S(1)}, bf16[64,384]{1,0:T(8,128)(2,1)S(1)}, u32[]{:S(2)}, u32[]{:S(2)}) %collective-permute-start.7) | collective-permute-done | bytes 49184 | tf_op jit(solution)/shard_map/ppermute | solution.py:22
  65.7 0.0 collective-permute-start.8
  65.7 0.8 fusion.2
  66.5 0.0 collective-permute-done.11.refs_6_
  66.5 3.3 %collective-permute-start.12 = (bf16[64,384]{1,0:T(8,128)(2,1)S(1)}, bf16[64,384]{1,0:T(8,128)(2,1)S(1)}, u32[]{:S(2)}, u32[]{:S(2)}) collective-permute-start(bf16[64,384]{1,0:T(8,128)(2,1)S(1)} %collective-permute-done.11.refs_6_), channel_id=1, source_target_pairs={{0,112},{16,0},{32,16},{48,32},{64,48},{80,64},{96,80},{112,96},{1... | collective-permute-start | bytes 147464 | tf_op jit(solution)/shard_map/ppermute | solution.py:22
  69.8 1.2 %collective-permute-done.8.refs_3_ = bf16[64,384]{1,0:T(8,128)(2,1)S(1)} collective-permute-done((bf16[64,384]{1,0:T(8,128)(2,1)S(1)}, bf16[64,384]{1,0:T(8,128)(2,1)S(1)}, u32[]{:S(2)}, u32[]{:S(2)}) %collective-permute-start.8) | collective-permute-done | bytes 49184 | tf_op jit(solution)/shard_map/ppermute | solution.py:22
  71.0 0.0 collective-permute-start.9
  71.0 0.6 constant_dynamic-slice_fusion.refs_8_
  71.6 0.1 rev.3
  71.7 0.7 pad.9.taps_ref
  72.4 1.7 %toeplitz.1.refs_9_ = bf16[1024,256]{1,0:T(8,128)(2,1)} custom-call(f32[8,256]{1,0:T(8,128)} %pad.9.taps_ref), custom_call_target="tpu_custom_call" | custom-call | flops 2000000 | bytes 1060000 | tf_op jit(solution)/shard_map/toeplitz/pallas_call | solution.py:101
  74.1 0.0 collective-permute-done.12.refs_5_
  74.1 2.2 %collective-permute-done.9.refs_4_ = bf16[64,384]{1,0:T(8,128)(2,1)S(1)} collective-permute-done((bf16[64,384]{1,0:T(8,128)(2,1)S(1)}, bf16[64,384]{1,0:T(8,128)(2,1)S(1)}, u32[]{:S(2)}, u32[]{:S(2)}) %collective-permute-start.9) | collective-permute-done | bytes 49184 | tf_op jit(solution)/shard_map/ppermute | solution.py:22
  76.3 0.0 copy-done.7
  76.3 0.0 copy-done.9
  76.3 0.0 copy-done.10
  76.3 0.0 copy-done.11
  76.3 0.0 copy-done.12
  76.3 0.6 copy-done.13
  76.9 13.3 %mixed_blocks.1 = bf16[8,512,128]{2,1,0:T(8,128)(2,1)} custom-call(s32[1]{0:T(128)} %bitcast.spot_ref, bf16[8,208,128]{2,1,0:T(8,128)(2,1)} %copy-done.1, bf16[64,384]{1,0:T(8,128)(2,1)} %copy-done.6, bf16[80,384]{1,0:T(8,128)(2,1)} %copy-done.7, bf16[64,384]{1,0:T(8,128)(2,1)} %copy-done.9, bf16[64,384]{1,0:T(8,128)(2,1)} %copy-done.11, ...), custom_call_target="tpu_custom_call" | custom-call | flops 5000000000 | bytes 4000000 | tf_op jit(solution)/shard_map/mixed_blocks/pallas_call | solution.py:216
  90.2 16.6 %all_to_all.15 = bf16[8,512,128]{2,1,0:T(8,128)(2,1)S(1)} all-to-all(bf16[8,512,128]{2,1,0:T(8,128)(2,1)} %mixed_blocks.1), channel_id=1, replica_groups=mesh['yh'=2,'z'=8,'x'=4,'yl'=2,'core'=2] {'yh','x'}, dimensions={0} | all-to-all | bytes 2097152 | tf_op jit(solution)/shard_map/all_to_all | solution.py:311
  106.7 0.5 copy.11
  107.3 1.3 %copy.12 = bf16[512,1024]{1,0:T(8,128)(2,1)} copy(bf16[512,1024]{0,1:T(8,128)(2,1)S(1)} %bitcast.18) | data formatting | bytes 2097152 | tf_op jit(solution)/shard_map/reshape | solution.py:312
  (23 shorter events, 0.1 us)
Async XLA Ops:
  0.0 71.0 %copy-start = (f32[3,7,1024]{2,1,0:T(8,128)S(1)}, f32[3,7,1024]{2,1,0:T(8,128)}, u32[]{:S(2)}) copy-start(f32[3,7,1024]{2,1,0:T(8,128)} %param.13) | copy-start | bytes 258052
  1.5 20.1 %collective-permute-start.5 = (f32[512]{0:T(512)S(1)}, f32[512]{0:T(512)S(1)}, u32[]{:S(2)}, u32[]{:S(2)}) collective-permute-start(f32[512]{0:T(512)S(1)} %multiply_reduce_fusion), channel_id=1, source_target_pairs={{0,3},{1,0},{2,1},{3,2},{4,7},{5,4},{6,5},{7,6},{8,11},{9,8},{10,9... | collective-permute-start | bytes 6152 | tf_op jit(solution)/shard_map/ppermute | solution.py:22
  1.6 21.3 %collective-permute-start.4 = (f32[512]{0:T(512)S(1)}, f32[512]{0:T(512)S(1)}, u32[]{:S(2)}, u32[]{:S(2)}) collective-permute-start(f32[512]{0:T(512)S(1)} %multiply_reduce_fusion), channel_id=1, source_target_pairs={{0,2},{1,3},{2,0},{3,1},{4,6},{5,7},{6,4},{7,5},{8,10},{9,11},{10,... | collective-permute-start | bytes 6152 | tf_op jit(solution)/shard_map/ppermute | solution.py:22
  3.9 19.0 %collective-permute-start.3 = (f32[512]{0:T(512)S(1)}, f32[512]{0:T(512)S(1)}, u32[]{:S(2)}, u32[]{:S(2)}) collective-permute-start(f32[512]{0:T(512)S(1)} %multiply_reduce_fusion), channel_id=1, source_target_pairs={{0,1},{1,2},{2,3},{3,0},{4,5},{5,6},{6,7},{7,4},{8,9},{9,10},{10,1... | collective-permute-start | bytes 6152 | tf_op jit(solution)/shard_map/ppermute | solution.py:22
  5.8 24.1 %copy-start.2 = (bf16[512,256]{1,0:T(8,128)(2,1)}, bf16[512,256]{1,0:T(8,128)(2,1)S(1)}, u32[]{:S(2)}) copy-start(bf16[512,256]{1,0:T(8,128)(2,1)S(1)} %multiply_convert_fusion.own_ref) | copy-start | bytes 786436
  5.8 17.2 %collective-permute-start.2 = (bf16[512,256]{1,0:T(8,128)(2,1)S(1)}, bf16[512,256]{1,0:T(8,128)(2,1)S(1)}, u32[]{:S(2)}, u32[]{:S(2)}) collective-permute-start(bf16[512,256]{1,0:T(8,128)(2,1)S(1)} %multiply_convert_fusion.own_ref), channel_id=1, source_target_pairs={{0,131},{16,147},{32,163},{48,179},{65,194},{81,210},{97,226},{113... | collective-permute-start | bytes 786440 | tf_op jit(solution)/shard_map/ppermute | solution.py:272
  9.3 13.7 %collective-permute-start.1 = (bf16[512,256]{1,0:T(8,128)(2,1)S(1)}, bf16[512,256]{1,0:T(8,128)(2,1)S(1)}, u32[]{:S(2)}, u32[]{:S(2)}) collective-permute-start(bf16[512,256]{1,0:T(8,128)(2,1)S(1)} %multiply_convert_fusion.own_ref), channel_id=1, source_target_pairs={{0,2},{16,18},{32,34},{48,50},{65,67},{81,83},{97,99},{113,115},{2... | collective-permute-start | bytes 786440 | tf_op jit(solution)/shard_map/ppermute | solution.py:269
  13.2 16.7 %all-to-all-start = ((bf16[8,208,128]{2,1,0:T(8,128)(2,1)}), bf16[8,208,128]{2,1,0:T(8,128)(2,1)S(1)}, u32[]{:S(2)}, u32[]{:S(2)}) async-start(bf16[8,208,128]{2,1,0:T(8,128)(2,1)} %payload.1), calls=%async_computation | async-start | bytes 851968 | tf_op jit(solution)/shard_map/all_to_all | solution.py:254
  21.6 2.4 %collective-permute-start = (bf16[512,256]{1,0:T(8,128)(2,1)S(1)}, bf16[512,256]{1,0:T(8,128)(2,1)S(1)}, u32[]{:S(2)}, u32[]{:S(2)}) collective-permute-start(bf16[512,256]{1,0:T(8,128)(2,1)S(1)} %multiply_convert_fusion.own_ref), channel_id=1, source_target_pairs={{0,1},{16,17},{32,33},{48,49},{65,64},{81,80},{97,96},{113,112},{2... | collective-permute-start | bytes 786440 | tf_op jit(solution)/shard_map/ppermute | solution.py:266
  23.0 6.9 %copy-start.3 = (bf16[512,256]{1,0:T(8,128)(2,1)}, bf16[512,256]{1,0:T(8,128)(2,1)S(1)}, u32[]{:S(2)}) copy-start(bf16[512,256]{1,0:T(8,128)(2,1)S(1)} %collective-permute-done.2.both_ref) | copy-start | bytes 786436
  23.0 6.9 %copy-start.4 = (bf16[512,256]{1,0:T(8,128)(2,1)}, bf16[512,256]{1,0:T(8,128)(2,1)S(1)}, u32[]{:S(2)}) copy-start(bf16[512,256]{1,0:T(8,128)(2,1)S(1)} %collective-permute-done.1.chip_ref) | copy-start | bytes 786436
  24.0 5.9 %copy-start.5 = (bf16[512,256]{1,0:T(8,128)(2,1)}, bf16[512,256]{1,0:T(8,128)(2,1)S(1)}, u32[]{:S(2)}) copy-start(bf16[512,256]{1,0:T(8,128)(2,1)S(1)} %collective-permute-done.core_ref) | copy-start | bytes 786436
  29.9 0.8 copy-start.1
  33.2 27.2 %copy-start.14 = (f32[64]{0:T(128)S(1)}, f32[64]{0:T(128)}, u32[]{:S(2)}) copy-start(f32[64]{0:T(128)} %param.15) | copy-start | bytes 772
  33.2 21.4 %all-to-all-start.1 = ((bf16[8,64,384]{2,1,0:T(8,128)(2,1)}), bf16[8,64,384]{2,1,0:T(8,128)(2,1)S(1)}, u32[]{:S(2)}, u32[]{:S(2)}) async-start(bf16[8,64,384]{2,1,0:T(8,128)(2,1)} %bitcast.19), calls=%async_computation.1 | async-start | bytes 786432 | tf_op jit(solution)/shard_map/all_to_all | solution.py:283
  54.8 21.5 %copy-start.6 = (bf16[64,384]{1,0:T(8,128)(2,1)}, bf16[64,384]{1,0:T(8,128)(2,1)S(1)}, u32[]{:S(2)}) copy-start(bf16[64,384]{1,0:T(8,128)(2,1)S(1)} %multiply_convert_fusion.1.refs_0_) | copy-start | bytes 147460
  54.8 5.5 %collective-permute-start.6 = (bf16[80,384]{1,0:T(8,128)(2,1)S(1)}, bf16[80,384]{1,0:T(8,128)(2,1)S(1)}, u32[]{:S(2)}, u32[]{:S(2)}) collective-permute-start(bf16[80,384]{1,0:T(8,128)(2,1)S(1)} %fusion.1), channel_id=1, source_target_pairs={{0,16},{16,32},{32,48},{48,64},{64,80},{80,96},{96,112},{112,0},{1... | collective-permute-start | bytes 184328 | tf_op jit(solution)/shard_map/ppermute | solution.py:22
  55.4 5.1 %collective-permute-start.10 = (bf16[64,384]{1,0:T(8,128)(2,1)S(1)}, bf16[64,384]{1,0:T(8,128)(2,1)S(1)}, u32[]{:S(2)}, u32[]{:S(2)}) collective-permute-start(bf16[64,384]{1,0:T(8,128)(2,1)S(1)} %multiply_convert_fusion.1.refs_0_), channel_id=1, source_target_pairs={{0,112},{16,0},{32,16},{48,32},{64,48},{80,64},{96,80},{112,96},{1... | collective-permute-start | bytes 147464 | tf_op jit(solution)/shard_map/ppermute | solution.py:22
  60.3 16.0 %copy-start.7 = (bf16[80,384]{1,0:T(8,128)(2,1)}, bf16[80,384]{1,0:T(8,128)(2,1)S(1)}, u32[]{:S(2)}) copy-start(bf16[80,384]{1,0:T(8,128)(2,1)S(1)} %collective-permute-done.6.refs_1_) | copy-start | bytes 184324
  60.3 5.4 %collective-permute-start.7 = (bf16[64,384]{1,0:T(8,128)(2,1)S(1)}, bf16[64,384]{1,0:T(8,128)(2,1)S(1)}, u32[]{:S(2)}, u32[]{:S(2)}) collective-permute-start(bf16[64,384]{1,0:T(8,128)(2,1)S(1)} %slice.23), channel_id=1, source_target_pairs={{0,16},{16,32},{32,48},{48,64},{64,80},{80,96},{96,112},{112,0},{1... | collective-permute-start | bytes 147464 | tf_op jit(solution)/shard_map/ppermute | solution.py:22
  60.5 15.8 %copy-start.8 = (bf16[64,384]{1,0:T(8,128)(2,1)}, bf16[64,384]{1,0:T(8,128)(2,1)S(1)}, u32[]{:S(2)}) copy-start(bf16[64,384]{1,0:T(8,128)(2,1)S(1)} %collective-permute-done.10.refs_7_) | copy-start | bytes 147460
  60.5 6.0 %collective-permute-start.11 = (bf16[64,384]{1,0:T(8,128)(2,1)S(1)}, bf16[64,384]{1,0:T(8,128)(2,1)S(1)}, u32[]{:S(2)}, u32[]{:S(2)}) collective-permute-start(bf16[64,384]{1,0:T(8,128)(2,1)S(1)} %collective-permute-done.10.refs_7_), channel_id=1, source_target_pairs={{0,112},{16,0},{32,16},{48,32},{64,48},{80,64},{96,80},{112,96},{1... | collective-permute-start | bytes 147464 | tf_op jit(solution)/shard_map/ppermute | solution.py:22
  65.7 10.6 %copy-start.9 = (bf16[64,384]{1,0:T(8,128)(2,1)}, bf16[64,384]{1,0:T(8,128)(2,1)S(1)}, u32[]{:S(2)}) copy-start(bf16[64,384]{1,0:T(8,128)(2,1)S(1)} %collective-permute-done.7.refs_2_) | copy-start | bytes 147460
  65.7 5.3 %collective-permute-start.8 = (bf16[64,384]{1,0:T(8,128)(2,1)S(1)}, bf16[64,384]{1,0:T(8,128)(2,1)S(1)}, u32[]{:S(2)}, u32[]{:S(2)}) collective-permute-start(bf16[64,384]{1,0:T(8,128)(2,1)S(1)} %collective-permute-done.7.refs_2_), channel_id=1, source_target_pairs={{0,16},{16,32},{32,48},{48,64},{64,80},{80,96},{96,112},{112,0},{1... | collective-permute-start | bytes 147464 | tf_op jit(solution)/shard_map/ppermute | solution.py:22
  66.5 9.8 %copy-start.10 = (bf16[64,384]{1,0:T(8,128)(2,1)}, bf16[64,384]{1,0:T(8,128)(2,1)S(1)}, u32[]{:S(2)}) copy-start(bf16[64,384]{1,0:T(8,128)(2,1)S(1)} %collective-permute-done.11.refs_6_) | copy-start | bytes 147460
  66.5 7.6 %collective-permute-start.12 = (bf16[64,384]{1,0:T(8,128)(2,1)S(1)}, bf16[64,384]{1,0:T(8,128)(2,1)S(1)}, u32[]{:S(2)}, u32[]{:S(2)}) collective-permute-start(bf16[64,384]{1,0:T(8,128)(2,1)S(1)} %collective-permute-done.11.refs_6_), channel_id=1, source_target_pairs={{0,112},{16,0},{32,16},{48,32},{64,48},{80,64},{96,80},{112,96},{1... | collective-permute-start | bytes 147464 | tf_op jit(solution)/shard_map/ppermute | solution.py:22
  71.0 5.3 %copy-start.11 = (bf16[64,384]{1,0:T(8,128)(2,1)}, bf16[64,384]{1,0:T(8,128)(2,1)S(1)}, u32[]{:S(2)}) copy-start(bf16[64,384]{1,0:T(8,128)(2,1)S(1)} %collective-permute-done.8.refs_3_) | copy-start | bytes 147460
  71.0 5.3 %collective-permute-start.9 = (bf16[64,384]{1,0:T(8,128)(2,1)S(1)}, bf16[64,384]{1,0:T(8,128)(2,1)S(1)}, u32[]{:S(2)}, u32[]{:S(2)}) collective-permute-start(bf16[64,384]{1,0:T(8,128)(2,1)S(1)} %collective-permute-done.8.refs_3_), channel_id=1, source_target_pairs={{0,16},{16,32},{32,48},{48,64},{64,80},{80,96},{96,112},{112,0},{1... | collective-permute-start | bytes 147464 | tf_op jit(solution)/shard_map/ppermute | solution.py:22
  74.1 2.3 %copy-start.12 = (bf16[64,384]{1,0:T(8,128)(2,1)}, bf16[64,384]{1,0:T(8,128)(2,1)S(1)}, u32[]{:S(2)}) copy-start(bf16[64,384]{1,0:T(8,128)(2,1)S(1)} %collective-permute-done.12.refs_5_) | copy-start | bytes 147460
  76.3 0.6 copy-start.13

commit v4 on v3

--- a/solution.py
+++ b/solution.py
@@ -91,16 +91,15 @@
 def toeplitz_kernel(taps_ref, out_ref):
     for g in range(taps_ref.shape[0]):
         row = jnp.broadcast_to(taps_ref[g : g + 1, :], (LONG_TAPS, 2 * LONG_TAPS))
-        out_ref[g * LONG_TAPS : (g + 1) * LONG_TAPS, :] = pltpu.roll(
-            row, 0, 1, stride=1, stride_axis=0
-        ).astype(BF)
+        block = pltpu.roll(row, 0, 1, stride=1, stride_axis=0)
+        out_ref[g] = jnp.transpose(block).astype(BF)
 
 
 def toeplitz(taps_row):
     groups = taps_row.shape[0]
     return pl.pallas_call(
         toeplitz_kernel,
-        out_shape=jax.ShapeDtypeStruct((groups * LONG_TAPS, 2 * LONG_TAPS), BF),
+        out_shape=jax.ShapeDtypeStruct((groups, 2 * LONG_TAPS, LONG_TAPS), BF),
         in_specs=in_vmem(1),
         out_specs=pl.BlockSpec(memory_space=pltpu.VMEM),
         cost_estimate=cost(2000000, 1060000),
@@ -122,23 +121,66 @@
     return jnp.where(hit, 1.0, 0.0).astype(BF)
 
 
-def mix_kernel(spot_ref, ids_ref, *refs):
+def hot_kernel(spot_ref, ids_ref, edge_ref, out_ref, lead_ref):
+    z = spot_ref[0]
+    share = edge_ref.shape[0] - 16
+    vocab = out_ref.shape[2]
+    tokens = out_ref.shape[1]
+    lead = lead_ref.shape[0] // 2
+
+    @pl.when(pl.program_id(0) == 0)
+    def _():
+        coded = edge_ref[share:, :LANES].astype(F32)
+        first, second = coded[:4], coded[4:8]
+        wrapped = z == 0
+        for segment, rows in enumerate(
+            (jnp.where(wrapped, second, first), jnp.where(wrapped, first, second))
+        ):
+            column = column_of(rows, z, share, 8)
+            column = jnp.concatenate([column[2 * LANES - lead :, 0:1], column[:, 1:2]], axis=0)
+            lead_ref[segment * lead : (segment + 1) * lead, :] = one_hot(column, vocab)
+
+    coded = ids_ref[0].astype(F32)
+    column = column_of(coded[: 2 * tokens // LANES], z, share, 8)
+    for j in range(tokens // LANES):
+        out_ref[0, j * LANES : (j + 1) * LANES, :] = one_hot(column[:, j : j + 1], vocab)
+
+
+def hot_rows(spot, pieces, edge_piece, tokens, vocab):
+    blocks, held, _ = pieces.shape
+    return pl.pallas_call(
+        hot_kernel,
+        out_shape=(
+            jax.ShapeDtypeStruct((blocks, tokens, vocab), BF),
+            jax.ShapeDtypeStruct((2 * HALO, vocab), BF),
+        ),
+        grid=(blocks,),
+        in_specs=[
+            pl.BlockSpec(memory_space=pltpu.SMEM),
+            pl.BlockSpec((1, 16, LANES), lambda i: (i, held // 16 - 1, 0)),
+            pl.BlockSpec(edge_piece.shape, lambda i: (0, 0)),
+        ],
+        out_specs=(
+            pl.BlockSpec((1, tokens, vocab), lambda i: (i, 0, 0)),
+            pl.BlockSpec((2 * HALO, vocab), lambda i: (0, 0)),
+        ),
+        cost_estimate=cost(5000000, 4500000),
+        name="hot_rows",
+    )(spot, pieces, edge_piece)
+
+
+def mix_kernel(hot_ref, lead_hot_ref, *refs):
     tables = refs[:8]
-    filt_ref, toep_ref, out_ref, table_ref, proj_ref, lead_ref, inner_ref, gate_ref = refs[8:]
-    z = spot_ref[0]
+    filt_ref, toep_ref, out_ref = refs[8:11]
+    table_ref, lead_ref, head_ref, edge_ref = refs[11:15]
+    next_ref, proj_ref, fresh_ref, inner_ref, fresh_gate_ref, gate_ref, conv_ref = refs[15:]
     step = pl.program_id(0)
     share, width = tables[0].shape
-    vocab = table_ref.shape[0]
     tokens = out_ref.shape[1]
     groups = LANES // GROUP
     margin = proj_ref.shape[1] - tokens
-    lead = lead_ref.shape[1]
+    lead = lead_hot_ref.shape[0] // 2
     chunk = 64
-
-    @pl.when(step == 0)
-    def _():
-        for j in range(8):
-            table_ref[j * share : (j + 1) * share, :] = tables[j][:share, :]
 
     def short(source, p, start, count):
         total = None
@@ -148,66 +190,80 @@
             total = term if total is None else total + term
         return total
 
-    @pl.when(step % 4 == 0)
+    @pl.when(step == 0)
     def _():
-        segment = step // 4
-        segment = jnp.where(z == 0, 1 - segment, segment)
-        coded = tables[1][share:, :LANES].astype(F32)
-        coded = jnp.where(segment == 0, coded[:4], coded[4:8])
-        column = column_of(coded, z, share, 8)
-        column = jnp.concatenate([column[2 * LANES - lead :, 0:1], column[:, 1:2]], axis=0)
-        proj = jnp.dot(one_hot(column, vocab), table_ref[...], preferred_element_type=F32)
+        for j in range(8):
+            table_ref[j * share : (j + 1) * share, :] = tables[j][:share, :]
+        proj = jnp.dot(lead_hot_ref[...], table_ref[...], preferred_element_type=F32)
         for p in range(STREAMS):
             lead_ref[p] = proj[:, p * LANES : (p + 1) * LANES]
-            proj_ref[p, :margin, :] = lead_ref[p, lead - margin :, :]
-        for at in range(0, LONG_TAPS, chunk):
-            left = short(lead_ref, 1, lead - LONG_TAPS + at, chunk)
-            right = short(lead_ref, 2, lead - LONG_TAPS + at, chunk)
-            inner_ref[at : at + chunk, :] = (left * right).astype(BF)
-
-    @pl.when(step % 4 != 0)
-    def _():
+        for segment in range(2):
+            for p in range(STREAMS):
+                head_ref[segment, p] = lead_ref[
+                    p, (segment + 1) * lead - margin : (segment + 1) * lead, :
+                ]
+            for at in range(0, LONG_TAPS, chunk):
+                start = (segment + 1) * lead - LONG_TAPS + at
+                fresh_ref[at : at + chunk, :] = short(lead_ref, 1, start, chunk) * short(
+                    lead_ref, 2, start, chunk
+                )
+            edge_ref[segment] = jnp.transpose(fresh_ref[:LONG_TAPS, :]).astype(BF)
+
+    count = tokens // LONG_TAPS
+
+    def select(begin, end):
+        proj = jnp.dot(hot_ref[0, begin:end, :], table_ref[...], preferred_element_type=F32)
         for p in range(STREAMS):
-            proj_ref[p, :margin, :] = proj_ref[p, tokens:, :]
-        inner_ref[:LONG_TAPS, :] = inner_ref[tokens:, :]
-
-    coded = ids_ref[0].astype(F32)
-    column = column_of(coded[: 2 * tokens // LANES], z, share, 8)
-    column = jnp.concatenate([column[:, j : j + 1] for j in range(tokens // LANES)], axis=0)
-    proj = jnp.dot(one_hot(column, vocab), table_ref[...], preferred_element_type=F32)
-    for p in range(STREAMS):
-        proj_ref[p, margin:, :] = proj[:, p * LANES : (p + 1) * LANES]
-    for at in range(0, tokens, chunk):
+            next_ref[p, begin:end, :] = proj[:, p * LANES : (p + 1) * LANES]
+
+    def filtered(at):
         left = short(proj_ref, 1, margin + at, chunk)
         right = short(proj_ref, 2, margin + at, chunk)
-        inner_ref[LONG_TAPS + at : LONG_TAPS + at + chunk, :] = (left * right).astype(BF)
-        gate_ref[at : at + chunk, :] = short(proj_ref, 0, margin + at, chunk)
-
-    lane_group = lax.broadcasted_iota(jnp.int32, (LONG_TAPS, LANES), 1) // GROUP
-    for base in range(0, tokens, 2 * LONG_TAPS):
-        window = jnp.concatenate(
-            [
-                inner_ref[base : base + 2 * LONG_TAPS, :],
-                inner_ref[base + LONG_TAPS : base + 3 * LONG_TAPS, :],
-            ],
-            axis=1,
+        fresh_ref[at : at + chunk, :] = left * right
+        fresh_gate_ref[at : at + chunk, :] = short(proj_ref, 0, margin + at, chunk)
+
+    def convolved(g):
+        rows = slice(g * GROUP, (g + 1) * GROUP)
+        windows = jnp.concatenate(
+            [inner_ref[rows, j * LONG_TAPS : (j + 2) * LONG_TAPS] for j in range(count)], axis=0
         )
-        full = jnp.dot(toep_ref[...], window, preferred_element_type=F32)
-        for side in range(2):
-            lanes = slice(side * LANES, (side + 1) * LANES)
-            conv = full[:LONG_TAPS, lanes]
-            for g in range(1, groups):
-                conv = jnp.where(
-                    lane_group == g, full[g * LONG_TAPS : (g + 1) * LONG_TAPS, lanes], conv
-                )
-            at = base + side * LONG_TAPS
-            out_ref[0, at : at + LONG_TAPS, :] = (gate_ref[at : at + LONG_TAPS, :] * conv).astype(
-                BF
+        full = jnp.dot(windows, toep_ref[g], preferred_element_type=F32)
+        for j in range(count):
+            conv_ref[j, rows, :] = full[j * GROUP : (j + 1) * GROUP]
+
+    select(0, tokens)
+    for g in range(groups):
+        convolved(g)
+        filtered(g * chunk)
+
+    @pl.when(step >= 0)
+    def _():
+        for j in range(count):
+            at = j * LONG_TAPS
+            conv = jnp.transpose(conv_ref[j])
+            out_ref[0, at : at + LONG_TAPS, :] = (gate_ref[at : at + LONG_TAPS, :] * conv).astype(BF)
+
+        starts = step % 4 == 0
+        segment = jnp.minimum(step // 4, 1)
+        for p in range(STREAMS):
+            proj_ref[p, :margin, :] = jnp.where(
+                starts, head_ref[segment, p], proj_ref[p, tokens:, :]
             )
-
-
-def mixed_blocks(spot, pieces, tables, filt, toep, tokens):
-    blocks, held, _ = pieces.shape
+            proj_ref[p, margin:, :] = next_ref[p]
+        starts = (step + 3) % 4 == 0
+        segment = jnp.minimum((step + 3) // 4 - 1, 1)
+        segment = jnp.maximum(segment, 0)
+        inner_ref[:, :LONG_TAPS] = jnp.where(starts, edge_ref[segment], inner_ref[:, tokens:])
+        for j in range(count):
+            at = j * LONG_TAPS
+            inner_ref[:, LONG_TAPS + at : 2 * LONG_TAPS + at] = jnp.transpose(
+                fresh_ref[at : at + LONG_TAPS, :]
+            ).astype(BF)
+        gate_ref[...] = fresh_gate_ref[...]
+
+
+def mixed_blocks(hot, lead_hot, tables, filt, toep):
+    blocks, tokens, vocab = hot.shape
     share, width = tables[0].shape
 
     def whole(value):
@@ -216,24 +272,30 @@
     return pl.pallas_call(
         mix_kernel,
         out_shape=jax.ShapeDtypeStruct((blocks, tokens, LANES), BF),
-        grid=(blocks,),
+        grid=(blocks + 2,),
         in_specs=[
-            pl.BlockSpec(memory_space=pltpu.SMEM),
-            pl.BlockSpec((1, 16, LANES), lambda i: (i, held // 16 - 1, 0)),
+            pl.BlockSpec((1, tokens, vocab), lambda i: (jnp.minimum(i, blocks - 1), 0, 0)),
+            whole(lead_hot),
         ]
         + [whole(table) for table in tables]
         + [whole(filt), whole(toep)],
-        out_specs=pl.BlockSpec((1, tokens, LANES), lambda i: (i, 0, 0)),
+        out_specs=pl.BlockSpec((1, tokens, LANES), lambda i: (jnp.maximum(i - 2, 0), 0, 0)),
         scratch_shapes=[
             pltpu.VMEM((8 * share, width), BF),
+            pltpu.VMEM((STREAMS, 2 * HALO, LANES), F32),
+            pltpu.VMEM((2, STREAMS, 8, LANES), F32),
+            pltpu.VMEM((2, LONG_TAPS, LANES), BF),
+            pltpu.VMEM((STREAMS, tokens, LANES), F32),
             pltpu.VMEM((STREAMS, tokens + 8, LANES), F32),
-            pltpu.VMEM((STREAMS, HALO, LANES), F32),
-            pltpu.VMEM((tokens + LONG_TAPS, LANES), BF),
             pltpu.VMEM((tokens, LANES), F32),
+            pltpu.VMEM((LANES, tokens + LONG_TAPS), BF),
+            pltpu.VMEM((tokens, LANES), F32),
+            pltpu.VMEM((tokens, LANES), F32),
+            pltpu.VMEM((tokens // LONG_TAPS, LANES, LONG_TAPS), F32),
         ],
-        cost_estimate=cost(5000000000, 4000000),
+        cost_estimate=cost(5000000000, 6000000),
         name="mixed_blocks",
-    )(spot, pieces, *tables, filt, toep)
+    )(hot, lead_hot, *tables, filt, toep)
 
 
 def per_device(ids, embed_table, norm_gain, in_weight, in_scale, short_filter, long_filter, decay):
@@ -251,11 +313,22 @@
     full_width = norm_gain.shape[0]
 
     load = payload(in_weight, ids.reshape(-1, LANES))
+    load, own_table = lax.optimization_barrier((load, embed_table))
     pieces = lax.all_to_all(load, ("yh", "x"), 0, 0, tiled=True)
+
+    groups = LANES // GROUP
+    steps = jnp.arange(LONG_TAPS, dtype=F32)
+    filt = lax.dynamic_slice_in_dim(long_filter, tile * groups, groups, 1)
+    rate = lax.dynamic_slice_in_dim(decay, tile * groups, groups, 0)
+    filt, rate, load = lax.optimization_barrier((filt, rate, load))
+    taps = (filt * jnp.exp(-rate[None, :] * steps[:, None])).astype(BF).astype(F32)
+    toep = toeplitz(jnp.pad(taps[::-1].T, ((0, 0), (1, LONG_TAPS - 1))))
+    near_filter = lax.dynamic_slice_in_dim(short_filter, tile * LANES, LANES, 2)
+    scale = lax.dynamic_slice_in_dim(in_scale, tile * LANES, LANES, 1).reshape(1, STREAMS * LANES)
 
     chunk = x_count * rows
     gain = lax.dynamic_slice_in_dim(norm_gain, yl * (full_width // 2) + z * chunk, chunk, 0)
-    own = lax.dynamic_slice_in_dim(embed_table, (z % 4) * chunk, chunk, 1)
+    own = lax.dynamic_slice_in_dim(own_table, (z % 4) * chunk, chunk, 1)
     own = (own.astype(F32) * gain[None, :]).astype(BF)
     around = ("yh", "z", "yl", "core")
 
@@ -272,18 +345,21 @@
     got_both = lax.ppermute(
         own, around, [(spot(a, b, c), spot((a + 3) % 4, b, 1 - c)) for a, b, c in holders]
     )
-    local_f = embed_table.astype(F32)
+    flags = jnp.stack([core == z // 4, yl == 1]).astype(jnp.int32)
+    pieces, toep, near_filter, scale = lax.optimization_barrier(
+        (pieces, toep, near_filter, scale)
+    )
+    partial = partial_table(flags, own, got_core, got_chip, got_both, pieces)
+    partial, own_table = lax.optimization_barrier((partial, own_table))
+    share = vocab // z_count
+    swapped = lax.all_to_all(
+        partial.reshape(z_count, share, STREAMS * LANES), "z", 0, 0, tiled=True
+    )
+    local_f = own_table.astype(F32)
     squares = jnp.sum(local_f * local_f, axis=1)
     others = [shifted(squares, ("yl", "core"), s) for s in (1, 2, 3)]
     total = squares + others[0] + others[1] + others[2]
 
-    flags = jnp.stack([core == z // 4, yl == 1]).astype(jnp.int32)
-    partial = partial_table(flags, own, got_core, got_chip, got_both, pieces)
-    share = vocab // z_count
-    swapped = lax.all_to_all(
-        partial.reshape(z_count, share, STREAMS * LANES), "z", 0, 0, tiled=True
-    )
-    scale = lax.dynamic_slice_in_dim(in_scale, tile * LANES, LANES, 1).reshape(1, STREAMS * LANES)
     norm = lax.rsqrt(lax.dynamic_slice_in_dim(total, z * share, share, 0) / full_width + 1e-06)
     piece = (jnp.sum(swapped.astype(F32), axis=0) * norm[:, None] * scale).astype(BF)
     coded = pieces[x_count - 1 :: x_count, STREAMS * rows :, :].reshape(2, 2, 8, LANES)[:, 0]
@@ -297,17 +373,8 @@
         downs.append(last)
     tables = ups + downs[::-1]
 
-    groups = LANES // GROUP
-    steps = jnp.arange(LONG_TAPS, dtype=F32)
-    filt = lax.dynamic_slice_in_dim(long_filter, tile * groups, groups, 1)
-    rate = lax.dynamic_slice_in_dim(decay, tile * groups, groups, 0)
-    taps = (filt * jnp.exp(-rate[None, :] * steps[:, None])).astype(BF).astype(F32)
-    toep = toeplitz(jnp.pad(taps[::-1].T, ((0, 0), (1, LONG_TAPS - 1))))
-    near_filter = lax.dynamic_slice_in_dim(short_filter, tile * LANES, LANES, 2)
-
-    blocks = mixed_blocks(
-        z.reshape(1).astype(jnp.int32), pieces, tables, near_filter, toep, tokens
-    )
+    hot, lead_hot = hot_rows(z.reshape(1).astype(jnp.int32), pieces, tables[1], tokens, vocab)
+    blocks = mixed_blocks(hot, lead_hot, tables, near_filter, toep)
     result = lax.all_to_all(blocks, ("yh", "x"), 0, 0, tiled=True)
     return result.transpose(1, 0, 2).reshape(tokens, width_local)
 

time: 109 us -> 112 us (1.028)
  Pallas kernels: 19.3 us -> 24.4 us
  waiting for transfers between devices: 29.1 us -> 25.6 us
  other arithmetic: 4.29 us -> 2.22 us
    pallas_call x1 -> x2, Pallas kernels: 1.71 us -> 8.01 us  [the longest x1 6.13 us: hot_rows(): pl.pallas_call(hot_kernel, out_shape=(jax.ShapeDtypeStruct((blocks, token...]
    all_to_all x1, starting transfers between devices: 6.03 us -> 8.55 us  [per_device(): lax.all_to_all(partial.reshape(z_count, share, STREAMS * LANES), 'z', 0,...]
    ppermute x1, starting transfers between devices: 3.52 us -> 1.31 us  [per_device(): lax.ppermute(own, around, [(spot(a, b, c), spot((a + 3) % 4, b, 1 - c)) f...]
    ppermute x10, starting transfers between devices: 12.4 us -> 10.4 us  [shifted(): return lax.ppermute(value, axis, pairs)]
    ppermute x1, starting transfers between devices: 2 us -> 3.99 us  [per_device(): lax.ppermute(own, around, [(spot(a, b, c), spot((a + 1) % 4, b, c)) for a...]
    all_to_all x1, waiting for transfers between devices: 5.89 us -> 4.31 us  [per_device(): pieces = lax.all_to_all(load, ('yh', 'x'), 0, 0, tiled=True)]
    unnamed x30 -> x34, local copies, waits for them, and re-layouts: 1.35 us -> 2.87 us
    ppermute x10, waiting for transfers between devices: 7.61 us -> 6.33 us  [shifted(): return lax.ppermute(value, axis, pairs)]
  transfers between devices with their start and end apart: 15 -> 15, of which waited for: 7 -> 5; matrix products, arithmetic and copies ran while one was open for 6% -> 3% of each run, Pallas kernels for 3% -> 7%
where the time goes in v4:
time: 112 us; the launch traced here: 111 us
  starting transfers between devices  32.8 us (29%)
  waiting for transfers between devices  25.6 us (23%)
  Pallas kernels  24.4 us (22%)
  blocking collectives  17.7 us (16%)
  local copies, waits for them, and re-layouts  7.68 us (7%)
  other arithmetic  2.22 us (2%)
    all_to_all x1, blocking collectives, per_device(): result = lax.all_to_all(blocks, ('yh', 'x'), 0, 0, tiled=True)  17.7 us
    all_to_all x1, waiting for transfers between devices, per_device(): lax.all_to_all(partial.reshape(z_count, share, STREAMS * LANES), 'z', 0,...  14.9 us
    pallas_call x1, Pallas kernels, mixed_blocks(): pl.pallas_call(mix_kernel, out_shape=jax.ShapeDtypeStruct((blocks, tokens...  12 us
    ppermute x10, starting transfers between devices, shifted(): return lax.ppermute(value, axis, pairs)  10.4 us
    all_to_all x1, starting transfers between devices, per_device(): lax.all_to_all(partial.reshape(z_count, share, STREAMS * LANES), 'z', 0,...  8.55 us
    all_to_all x1, starting transfers between devices, per_device(): pieces = lax.all_to_all(load, ('yh', 'x'), 0, 0, tiled=True)  7.25 us
    ppermute x10, waiting for transfers between devices, shifted(): return lax.ppermute(value, axis, pairs)  6.33 us
    pallas_call x1, Pallas kernels, hot_rows(): pl.pallas_call(hot_kernel, out_shape=(jax.ShapeDtypeStruct((blocks, token...  6.13 us
  transfers between devices with their start and end apart: 15, of which 5 were waited for; matrix products, arithmetic and copies ran while one was open for 3% of the time, Pallas kernels for 7%

profile of v4, /device:TPU:8, one launch (start us, length us, event | category | flops | bytes accessed | tf_op | source)
XLA Modules:
  0.0 110.7 jit_solution(11417265605860735229)
XLA Ops:
  0.0 0.0 copy-start
  0.0 1.9 %payload.1 = bf16[8,208,128]{2,1,0:T(8,128)(2,1)} custom-call(bf16[3,64,1024]{2,1,0:T(8,128)(2,1)} %weight_ref.1, s32[4,128]{1,0:T(4,128)} %bitcast.27), custom_call_target="tpu_custom_call" | custom-call | bytes 800000 | tf_op jit(solution)/shard_map/payload/pallas_call | solution.py:49
  1.9 0.8 dynamic_slice.26
  2.7 1.0 multiply_convert_fusion.own_ref
  3.7 0.0 copy-start.3
  3.7 1.3 %collective-permute-start.2 = (bf16[512,256]{1,0:T(8,128)(2,1)S(1)}, bf16[512,256]{1,0:T(8,128)(2,1)S(1)}, u32[]{:S(2)}, u32[]{:S(2)}) collective-permute-start(bf16[512,256]{1,0:T(8,128)(2,1)S(1)} %multiply_convert_fusion.own_ref), channel_id=1, source_target_pairs={{0,131},{16,147},{32,163},{48,179},{65,194},{81,210},{97,226},{113... | collective-permute-start | bytes 786440 | tf_op jit(solution)/shard_map/ppermute | solution.py:345
  5.0 4.0 %collective-permute-start.1 = (bf16[512,256]{1,0:T(8,128)(2,1)S(1)}, bf16[512,256]{1,0:T(8,128)(2,1)S(1)}, u32[]{:S(2)}, u32[]{:S(2)}) collective-permute-start(bf16[512,256]{1,0:T(8,128)(2,1)S(1)} %multiply_convert_fusion.own_ref), channel_id=1, source_target_pairs={{0,2},{16,18},{32,34},{48,50},{65,67},{81,83},{97,99},{113,115},{2... | collective-permute-start | bytes 786440 | tf_op jit(solution)/shard_map/ppermute | solution.py:342
  9.0 1.3 %collective-permute-start = (bf16[512,256]{1,0:T(8,128)(2,1)S(1)}, bf16[512,256]{1,0:T(8,128)(2,1)S(1)}, u32[]{:S(2)}, u32[]{:S(2)}) collective-permute-start(bf16[512,256]{1,0:T(8,128)(2,1)S(1)} %multiply_convert_fusion.own_ref), channel_id=1, source_target_pairs={{0,1},{16,17},{32,33},{48,49},{65,64},{81,80},{97,96},{113,112},{2... | collective-permute-start | bytes 786440 | tf_op jit(solution)/shard_map/ppermute | solution.py:339
  10.3 7.3 %all-to-all-start = ((bf16[8,208,128]{2,1,0:T(8,128)(2,1)}), bf16[8,208,128]{2,1,0:T(8,128)(2,1)S(1)}, u32[]{:S(2)}, u32[]{:S(2)}) async-start(bf16[8,208,128]{2,1,0:T(8,128)(2,1)} %payload.1), calls=%async_computation | async-start | bytes 851968 | tf_op jit(solution)/shard_map/all_to_all | solution.py:317
  17.6 0.7 constant_dynamic-slice_fusion.1
  18.3 0.0 copy-done
  18.3 0.6 constant_dynamic-slice_fusion.refs_8_
  18.9 0.7 dynamic-slice_bitcast_fusion
  19.6 0.0 copy-done.15
  19.6 0.1 dynamic_slice.22
  19.7 0.1 fusion.2
  19.7 0.6 add_convert_fusion.flag_ref
  20.3 0.1 rev.3
  20.4 0.7 pad.8.taps_ref
  21.1 1.9 %toeplitz.1.refs_9_ = bf16[8,256,128]{2,1,0:T(8,128)(2,1)} custom-call(f32[8,256]{1,0:T(8,128)} %pad.8.taps_ref), custom_call_target="tpu_custom_call" | custom-call | flops 2000000 | bytes 1060000 | tf_op jit(solution)/shard_map/toeplitz/pallas_call | solution.py:100
  23.0 4.3 %all-to-all-done.pieces_ref.ids_ref = bf16[8,208,128]{2,1,0:T(8,128)(2,1)S(1)} async-done(((bf16[8,208,128]{2,1,0:T(8,128)(2,1)}), bf16[8,208,128]{2,1,0:T(8,128)(2,1)S(1)}, u32[]{:S(2)}, u32[]{:S(2)}) %all-to-all-start) | async-done | bytes 426016 | tf_op jit(solution)/shard_map/all_to_all | solution.py:317
  27.3 0.0 collective-permute-done.2.both_ref
  27.3 0.0 copy-start.4
  27.3 0.0 collective-permute-done.1.chip_ref
  27.3 0.0 collective-permute-done.core_ref
  27.3 0.7 copy-done.1
  28.0 0.1 copy-done.4
  28.1 0.1 copy-done.5
  28.2 0.7 copy-done.6
  28.9 2.5 %partial_table.1 = bf16[512,384]{1,0:T(8,128)(2,1)} custom-call(s32[2]{0:T(128)} %add_convert_fusion.flag_ref, bf16[512,256]{1,0:T(8,128)(2,1)} %copy-done.3, bf16[512,256]{1,0:T(8,128)(2,1)} %copy-done.6, bf16[512,256]{1,0:T(8,128)(2,1)} %copy-done.5, bf16[512,256]{1,0:T(8,128)(2,1)} %copy-done.4, bf16[8,208,128]{2,1,0:T(8,128)(2,1)} %copy-done.1), custom_call_target="tpu_custom_call" | custom-call | flops 201326592 | bytes 2000000 | tf_op jit(solution)/shard_map/partial_table/pallas_call | solution.py:81
  31.4 0.3 multiply_reduce_fusion
  31.7 0.1 collective-permute-start.5
  31.8 0.2 collective-permute-start.4
  32.0 0.3 collective-permute-start.3
  32.3 8.6 %all-to-all-start.1 = ((bf16[8,64,384]{2,1,0:T(8,128)(2,1)}), bf16[8,64,384]{2,1,0:T(8,128)(2,1)S(1)}, u32[]{:S(2)}, u32[]{:S(2)}) async-start(bf16[8,64,384]{2,1,0:T(8,128)(2,1)} %bitcast.23), calls=%async_computation.1 | async-start | bytes 786432 | tf_op jit(solution)/shard_map/all_to_all | solution.py:355
  40.9 0.0 collective-permute-done.5
  40.9 0.0 collective-permute-done.4
  40.9 0.0 collective-permute-done.3
  41.0 0.1 add_rsqrt_fusion
  41.0 14.9 %all-to-all-done.1 = bf16[8,64,384]{2,1,0:T(8,128)(2,1)S(1)} async-done(((bf16[8,64,384]{2,1,0:T(8,128)(2,1)}), bf16[8,64,384]{2,1,0:T(8,128)(2,1)S(1)}, u32[]{:S(2)}, u32[]{:S(2)}) %all-to-all-start.1) | async-done | bytes 393248 | tf_op jit(solution)/shard_map/all_to_all | solution.py:355
  56.0 0.1 convert_reduce_fusion
  56.0 0.1 multiply_convert_fusion.1.refs_0_
  56.1 0.6 collective-permute-start.6
  56.8 2.7 %collective-permute-start.10 = (bf16[64,384]{1,0:T(8,128)(2,1)S(1)}, bf16[64,384]{1,0:T(8,128)(2,1)S(1)}, u32[]{:S(2)}, u32[]{:S(2)}) collective-permute-start(bf16[64,384]{1,0:T(8,128)(2,1)S(1)} %multiply_convert_fusion.1.refs_0_), channel_id=1, source_target_pairs={{0,112},{16,0},{32,16},{48,32},{64,48},{80,64},{96,80},{112,96},{1... | collective-permute-start | bytes 147464 | tf_op jit(solution)/shard_map/ppermute | solution.py:22
  59.5 2.2 %collective-permute-done.6.edge_ref.refs_1_ = bf16[80,384]{1,0:T(8,128)(2,1)S(1)} collective-permute-done((bf16[80,384]{1,0:T(8,128)(2,1)S(1)}, bf16[80,384]{1,0:T(8,128)(2,1)S(1)}, u32[]{:S(2)}, u32[]{:S(2)}) %collective-permute-start.6) | collective-permute-done | bytes 61472 | tf_op jit(solution)/shard_map/ppermute | solution.py:22
  61.7 0.1 collective-permute-start.7
  61.8 0.0 collective-permute-done.10.refs_7_
  61.8 3.2 %collective-permute-start.11 = (bf16[64,384]{1,0:T(8,128)(2,1)S(1)}, bf16[64,384]{1,0:T(8,128)(2,1)S(1)}, u32[]{:S(2)}, u32[]{:S(2)}) collective-permute-start(bf16[64,384]{1,0:T(8,128)(2,1)S(1)} %collective-permute-done.10.refs_7_), channel_id=1, source_target_pairs={{0,112},{16,0},{32,16},{48,32},{64,48},{80,64},{96,80},{112,96},{1... | collective-permute-start | bytes 147464 | tf_op jit(solution)/shard_map/ppermute | solution.py:22
  65.0 2.1 %collective-permute-done.7.refs_2_ = bf16[64,384]{1,0:T(8,128)(2,1)S(1)} collective-permute-done((bf16[64,384]{1,0:T(8,128)(2,1)S(1)}, bf16[64,384]{1,0:T(8,128)(2,1)S(1)}, u32[]{:S(2)}, u32[]{:S(2)}) %collective-permute-start.7) | collective-permute-done | bytes 49184 | tf_op jit(solution)/shard_map/ppermute | solution.py:22
  67.0 0.0 collective-permute-start.8
  67.0 0.0 collective-permute-done.11.refs_6_
  67.1 0.0 copy-start.11
  67.1 3.2 %collective-permute-start.12 = (bf16[64,384]{1,0:T(8,128)(2,1)S(1)}, bf16[64,384]{1,0:T(8,128)(2,1)S(1)}, u32[]{:S(2)}, u32[]{:S(2)}) collective-permute-start(bf16[64,384]{1,0:T(8,128)(2,1)S(1)} %collective-permute-done.11.refs_6_), channel_id=1, source_target_pairs={{0,112},{16,0},{32,16},{48,32},{64,48},{80,64},{96,80},{112,96},{1... | collective-permute-start | bytes 147464 | tf_op jit(solution)/shard_map/ppermute | solution.py:22
  70.3 2.1 %collective-permute-done.8.refs_3_ = bf16[64,384]{1,0:T(8,128)(2,1)S(1)} collective-permute-done((bf16[64,384]{1,0:T(8,128)(2,1)S(1)}, bf16[64,384]{1,0:T(8,128)(2,1)S(1)}, u32[]{:S(2)}, u32[]{:S(2)}) %collective-permute-start.8) | collective-permute-done | bytes 49184 | tf_op jit(solution)/shard_map/ppermute | solution.py:22
  72.3 0.0 collective-permute-start.9
  72.4 6.1 %hot_rows.1 = (bf16[8,512,512]{2,1,0:T(8,128)(2,1)}, bf16[288,512]{1,0:T(8,128)(2,1)}) custom-call(s32[1]{0:T(128)} %bitcast.spot_ref, bf16[8,208,128]{2,1,0:T(8,128)(2,1)} %copy-done.1, bf16[80,384]{1,0:T(8,128)(2,1)} %copy-done.7), custom_call_target="tpu_custom_call" | custom-call | flops 5000000 | bytes 4500000 | tf_op jit(solution)/shard_map/hot_rows/pallas_call | solution.py:151
  78.5 0.0 collective-permute-done.12.refs_5_
  78.5 0.0 collective-permute-done.9.refs_4_
  78.6 0.6 copy-done.13
  79.1 0.0 copy-done.14
  79.1 12.0 %mixed_blocks.1 = bf16[8,512,128]{2,1,0:T(8,128)(2,1)} custom-call(bf16[8,512,512]{2,1,0:T(8,128)(2,1)} %get-tuple-element.25.hot_ref, bf16[288,512]{1,0:T(8,128)(2,1)} %get-tuple-element.26.lead_hot_ref, bf16[64,384]{1,0:T(8,128)(2,1)} %copy-done.8, bf16[80,384]{1,0:T(8,128)(2,1)} %copy-done.7, bf16[64,384]{1,0:T(8,128)(2,1)} %copy-done.10, ...), custom_call_target="tpu_custom_call" | custom-call | flops 5000000000 | bytes 6000000 | tf_op jit(solution)/shard_map/mixed_blocks/pallas_call | solution.py:272
  91.1 17.7 %all_to_all.15 = bf16[8,512,128]{2,1,0:T(8,128)(2,1)S(1)} all-to-all(bf16[8,512,128]{2,1,0:T(8,128)(2,1)} %mixed_blocks.1), channel_id=1, replica_groups=mesh['yh'=2,'z'=8,'x'=4,'yl'=2,'core'=2] {'yh','x'}, dimensions={0} | all-to-all | bytes 2097152 | tf_op jit(solution)/shard_map/all_to_all | solution.py:378
  108.8 0.5 copy.11
  109.4 1.3 %copy.12 = bf16[512,1024]{1,0:T(8,128)(2,1)} copy(bf16[512,1024]{0,1:T(8,128)(2,1)S(1)} %bitcast.22) | data formatting | bytes 2097152 | tf_op jit(solution)/shard_map/reshape | solution.py:379
  (30 shorter events, 0.1 us)
Async XLA Ops:
  0.0 18.3 %copy-start = (f32[3,7,1024]{2,1,0:T(8,128)S(1)}, f32[3,7,1024]{2,1,0:T(8,128)}, u32[]{:S(2)}) copy-start(f32[3,7,1024]{2,1,0:T(8,128)} %param.13) | copy-start | bytes 258052
  0.0 19.6 %copy-start.15 = (f32[64]{0:T(128)S(1)}, f32[64]{0:T(128)}, u32[]{:S(2)}) copy-start(f32[64]{0:T(128)} %param.15) | copy-start | bytes 772
  1.9 29.6 %copy-start.2 = (bf16[512,1024]{1,0:T(8,128)(2,1)S(1)}, bf16[512,1024]{1,0:T(8,128)(2,1)}, u32[]{:S(2)}) copy-start(bf16[512,1024]{1,0:T(8,128)(2,1)} %param.9) | copy-start | bytes 3145732
  3.7 23.6 %copy-start.3 = (bf16[512,256]{1,0:T(8,128)(2,1)}, bf16[512,256]{1,0:T(8,128)(2,1)S(1)}, u32[]{:S(2)}) copy-start(bf16[512,256]{1,0:T(8,128)(2,1)S(1)} %multiply_convert_fusion.own_ref) | copy-start | bytes 786436
  3.7 23.6 %collective-permute-start.2 = (bf16[512,256]{1,0:T(8,128)(2,1)S(1)}, bf16[512,256]{1,0:T(8,128)(2,1)S(1)}, u32[]{:S(2)}, u32[]{:S(2)}) collective-permute-start(bf16[512,256]{1,0:T(8,128)(2,1)S(1)} %multiply_convert_fusion.own_ref), channel_id=1, source_target_pairs={{0,131},{16,147},{32,163},{48,179},{65,194},{81,210},{97,226},{113... | collective-permute-start | bytes 786440 | tf_op jit(solution)/shard_map/ppermute | solution.py:345
  5.0 22.3 %collective-permute-start.1 = (bf16[512,256]{1,0:T(8,128)(2,1)S(1)}, bf16[512,256]{1,0:T(8,128)(2,1)S(1)}, u32[]{:S(2)}, u32[]{:S(2)}) collective-permute-start(bf16[512,256]{1,0:T(8,128)(2,1)S(1)} %multiply_convert_fusion.own_ref), channel_id=1, source_target_pairs={{0,2},{16,18},{32,34},{48,50},{65,67},{81,83},{97,99},{113,115},{2... | collective-permute-start | bytes 786440 | tf_op jit(solution)/shard_map/ppermute | solution.py:342
  9.0 18.3 %collective-permute-start = (bf16[512,256]{1,0:T(8,128)(2,1)S(1)}, bf16[512,256]{1,0:T(8,128)(2,1)S(1)}, u32[]{:S(2)}, u32[]{:S(2)}) collective-permute-start(bf16[512,256]{1,0:T(8,128)(2,1)S(1)} %multiply_convert_fusion.own_ref), channel_id=1, source_target_pairs={{0,1},{16,17},{32,33},{48,49},{65,64},{81,80},{97,96},{113,112},{2... | collective-permute-start | bytes 786440 | tf_op jit(solution)/shard_map/ppermute | solution.py:339
  10.3 16.9 %all-to-all-start = ((bf16[8,208,128]{2,1,0:T(8,128)(2,1)}), bf16[8,208,128]{2,1,0:T(8,128)(2,1)S(1)}, u32[]{:S(2)}, u32[]{:S(2)}) async-start(bf16[8,208,128]{2,1,0:T(8,128)(2,1)} %payload.1), calls=%async_computation | async-start | bytes 851968 | tf_op jit(solution)/shard_map/all_to_all | solution.py:317
  27.3 0.8 copy-start.1
  27.3 0.8 copy-start.4
  27.3 0.9 copy-start.5
  28.2 0.7 copy-start.6
  31.7 9.2 %collective-permute-start.5 = (f32[512]{0:T(512)S(1)}, f32[512]{0:T(512)S(1)}, u32[]{:S(2)}, u32[]{:S(2)}) collective-permute-start(f32[512]{0:T(512)S(1)} %multiply_reduce_fusion), channel_id=1, source_target_pairs={{0,3},{1,0},{2,1},{3,2},{4,7},{5,4},{6,5},{7,6},{8,11},{9,8},{10,9... | collective-permute-start | bytes 6152 | tf_op jit(solution)/shard_map/ppermute | solution.py:22
  31.8 9.1 %collective-permute-start.4 = (f32[512]{0:T(512)S(1)}, f32[512]{0:T(512)S(1)}, u32[]{:S(2)}, u32[]{:S(2)}) collective-permute-start(f32[512]{0:T(512)S(1)} %multiply_reduce_fusion), channel_id=1, source_target_pairs={{0,2},{1,3},{2,0},{3,1},{4,6},{5,7},{6,4},{7,5},{8,10},{9,11},{10,... | collective-permute-start | bytes 6152 | tf_op jit(solution)/shard_map/ppermute | solution.py:22
  32.0 8.9 %collective-permute-start.3 = (f32[512]{0:T(512)S(1)}, f32[512]{0:T(512)S(1)}, u32[]{:S(2)}, u32[]{:S(2)}) collective-permute-start(f32[512]{0:T(512)S(1)} %multiply_reduce_fusion), channel_id=1, source_target_pairs={{0,1},{1,2},{2,3},{3,0},{4,5},{5,6},{6,7},{7,4},{8,9},{9,10},{10,1... | collective-permute-start | bytes 6152 | tf_op jit(solution)/shard_map/ppermute | solution.py:22
  32.3 23.7 %all-to-all-start.1 = ((bf16[8,64,384]{2,1,0:T(8,128)(2,1)}), bf16[8,64,384]{2,1,0:T(8,128)(2,1)S(1)}, u32[]{:S(2)}, u32[]{:S(2)}) async-start(bf16[8,64,384]{2,1,0:T(8,128)(2,1)} %bitcast.23), calls=%async_computation.1 | async-start | bytes 786432 | tf_op jit(solution)/shard_map/all_to_all | solution.py:355
  56.1 22.4 %copy-start.8 = (bf16[64,384]{1,0:T(8,128)(2,1)}, bf16[64,384]{1,0:T(8,128)(2,1)S(1)}, u32[]{:S(2)}) copy-start(bf16[64,384]{1,0:T(8,128)(2,1)S(1)} %multiply_convert_fusion.1.refs_0_) | copy-start | bytes 147460
  56.1 5.5 %collective-permute-start.6 = (bf16[80,384]{1,0:T(8,128)(2,1)S(1)}, bf16[80,384]{1,0:T(8,128)(2,1)S(1)}, u32[]{:S(2)}, u32[]{:S(2)}) collective-permute-start(bf16[80,384]{1,0:T(8,128)(2,1)S(1)} %fusion.1), channel_id=1, source_target_pairs={{0,16},{16,32},{32,48},{48,64},{64,80},{80,96},{96,112},{112,0},{1... | collective-permute-start | bytes 184328 | tf_op jit(solution)/shard_map/ppermute | solution.py:22
  56.8 5.0 %collective-permute-start.10 = (bf16[64,384]{1,0:T(8,128)(2,1)S(1)}, bf16[64,384]{1,0:T(8,128)(2,1)S(1)}, u32[]{:S(2)}, u32[]{:S(2)}) collective-permute-start(bf16[64,384]{1,0:T(8,128)(2,1)S(1)} %multiply_convert_fusion.1.refs_0_), channel_id=1, source_target_pairs={{0,112},{16,0},{32,16},{48,32},{64,48},{80,64},{96,80},{112,96},{1... | collective-permute-start | bytes 147464 | tf_op jit(solution)/shard_map/ppermute | solution.py:22
  61.7 10.7 %copy-start.7 = (bf16[80,384]{1,0:T(8,128)(2,1)}, bf16[80,384]{1,0:T(8,128)(2,1)S(1)}, u32[]{:S(2)}) copy-start(bf16[80,384]{1,0:T(8,128)(2,1)S(1)} %collective-permute-done.6.edge_ref.refs_1_) | copy-start | bytes 184324
  61.7 5.4 %collective-permute-start.7 = (bf16[64,384]{1,0:T(8,128)(2,1)S(1)}, bf16[64,384]{1,0:T(8,128)(2,1)S(1)}, u32[]{:S(2)}, u32[]{:S(2)}) collective-permute-start(bf16[64,384]{1,0:T(8,128)(2,1)S(1)} %slice.23), channel_id=1, source_target_pairs={{0,16},{16,32},{32,48},{48,64},{64,80},{80,96},{96,112},{112,0},{1... | collective-permute-start | bytes 147464 | tf_op jit(solution)/shard_map/ppermute | solution.py:22
  61.8 16.8 %copy-start.9 = (bf16[64,384]{1,0:T(8,128)(2,1)}, bf16[64,384]{1,0:T(8,128)(2,1)S(1)}, u32[]{:S(2)}) copy-start(bf16[64,384]{1,0:T(8,128)(2,1)S(1)} %collective-permute-done.10.refs_7_) | copy-start | bytes 147460
  61.8 5.3 %collective-permute-start.11 = (bf16[64,384]{1,0:T(8,128)(2,1)S(1)}, bf16[64,384]{1,0:T(8,128)(2,1)S(1)}, u32[]{:S(2)}, u32[]{:S(2)}) collective-permute-start(bf16[64,384]{1,0:T(8,128)(2,1)S(1)} %collective-permute-done.10.refs_7_), channel_id=1, source_target_pairs={{0,112},{16,0},{32,16},{48,32},{64,48},{80,64},{96,80},{112,96},{1... | collective-permute-start | bytes 147464 | tf_op jit(solution)/shard_map/ppermute | solution.py:22
  67.0 11.5 %copy-start.10 = (bf16[64,384]{1,0:T(8,128)(2,1)}, bf16[64,384]{1,0:T(8,128)(2,1)S(1)}, u32[]{:S(2)}) copy-start(bf16[64,384]{1,0:T(8,128)(2,1)S(1)} %collective-permute-done.7.refs_2_) | copy-start | bytes 147460
  67.0 5.3 %collective-permute-start.8 = (bf16[64,384]{1,0:T(8,128)(2,1)S(1)}, bf16[64,384]{1,0:T(8,128)(2,1)S(1)}, u32[]{:S(2)}, u32[]{:S(2)}) collective-permute-start(bf16[64,384]{1,0:T(8,128)(2,1)S(1)} %collective-permute-done.7.refs_2_), channel_id=1, source_target_pairs={{0,16},{16,32},{32,48},{48,64},{64,80},{80,96},{96,112},{112,0},{1... | collective-permute-start | bytes 147464 | tf_op jit(solution)/shard_map/ppermute | solution.py:22
  67.1 11.5 %copy-start.11 = (bf16[64,384]{1,0:T(8,128)(2,1)}, bf16[64,384]{1,0:T(8,128)(2,1)S(1)}, u32[]{:S(2)}) copy-start(bf16[64,384]{1,0:T(8,128)(2,1)S(1)} %collective-permute-done.11.refs_6_) | copy-start | bytes 147460
  67.1 11.4 %collective-permute-start.12 = (bf16[64,384]{1,0:T(8,128)(2,1)S(1)}, bf16[64,384]{1,0:T(8,128)(2,1)S(1)}, u32[]{:S(2)}, u32[]{:S(2)}) collective-permute-start(bf16[64,384]{1,0:T(8,128)(2,1)S(1)} %collective-permute-done.11.refs_6_), channel_id=1, source_target_pairs={{0,112},{16,0},{32,16},{48,32},{64,48},{80,64},{96,80},{112,96},{1... | collective-permute-start | bytes 147464 | tf_op jit(solution)/shard_map/ppermute | solution.py:22
  72.3 6.2 %copy-start.12 = (bf16[64,384]{1,0:T(8,128)(2,1)}, bf16[64,384]{1,0:T(8,128)(2,1)S(1)}, u32[]{:S(2)}) copy-start(bf16[64,384]{1,0:T(8,128)(2,1)S(1)} %collective-permute-done.8.refs_3_) | copy-start | bytes 147460
  72.3 6.1 %collective-permute-start.9 = (bf16[64,384]{1,0:T(8,128)(2,1)S(1)}, bf16[64,384]{1,0:T(8,128)(2,1)S(1)}, u32[]{:S(2)}, u32[]{:S(2)}) collective-permute-start(bf16[64,384]{1,0:T(8,128)(2,1)S(1)} %collective-permute-done.8.refs_3_), channel_id=1, source_target_pairs={{0,16},{16,32},{32,48},{48,64},{64,80},{80,96},{96,112},{112,0},{1... | collective-permute-start | bytes 147464 | tf_op jit(solution)/shard_map/ppermute | solution.py:22
  78.5 0.6 copy-start.13
  78.5 0.6 copy-start.14

commit v5 on v4

v5 whole, which is shorter than its diff:
```python
import jax
import jax.numpy as jnp
import numpy as np
from jax import lax
from jax.experimental import pallas as pl
from jax.experimental.pallas import tpu as pltpu
from jax.sharding import Mesh, PartitionSpec as P

GROUP = 16
SHORT_TAPS = 7
LONG_TAPS = 128
LANES = 128
HALO = 144
STREAMS = 3
BF = jnp.bfloat16
F32 = jnp.float32


def shifted(value, axis, steps):
    count = lax.axis_size(axis)
    pairs = [(source, (source + steps) % count) for source in range(count)]
    return lax.ppermute(value, axis, pairs)


def payload_kernel(weight_ref, ids_ref, out_ref):
    streams, rows, width = weight_ref.shape
    tiles = width // LANES
    columns = out_ref.shape[0] // tiles
    values = ids_ref[...]
    coded = jnp.where(values < 256, values, 255 - values).astype(F32)
    coded = jnp.concatenate([coded, jnp.zeros_like(coded)], axis=0)
    for tile in range(tiles):
        lanes = slice(tile * LANES, (tile + 1) * LANES)
        pair = jnp.concatenate([weight_ref[0, :, lanes], weight_ref[1, :, lanes]], axis=0)
        third = weight_ref[2, :, lanes].astype(F32)
        third = jnp.concatenate([third, pltpu.roll(third, LANES - 8, 1)], axis=0)
        pair = jnp.transpose(pair.astype(F32))
        third = jnp.transpose(third)
        for part in range(columns):
            to = (tile // 4 * columns + part) * 4 + tile % 4
            at = part * GROUP
            out_ref[to, :GROUP, :] = pair[at : at + GROUP].astype(BF)
            out_ref[to, GROUP:, :] = jnp.concatenate([third[at : at + 8], coded], axis=0).astype(
                BF
            )


def in_vmem(count):
    return [pl.BlockSpec(memory_space=pltpu.VMEM)] * count


def cost(flops, moved):
    return pl.CostEstimate(flops=flops, bytes_accessed=moved, transcendentals=0)


def payload(in_weight, ids_rows, parts):
    return pl.pallas_call(
        payload_kernel,
        out_shape=jax.ShapeDtypeStruct((parts, 2 * GROUP, LANES), BF),
        in_specs=in_vmem(2),
        out_specs=pl.BlockSpec(memory_space=pltpu.VMEM),
        cost_estimate=cost(0, 900000),
        name="payload",
    )(in_weight, ids_rows)


def norm_kernel(spot_ref, own_ref, core_ref, up_ref, down_ref, far_up_ref, far_down_ref, *refs):
    gain_ref, out_ref = refs
    vocab, width = own_ref.shape
    quarter = [spot_ref[j] for j in range(4)]
    chunk = 32

    def some(read, at):
        parts = [value.astype(F32) for value in read]
        squares = sum(jnp.sum(part * part, axis=1, keepdims=True) for part in parts)
        factor = lax.rsqrt(squares / (4 * width) + 1e-06)
        for j, part in enumerate(parts):
            gain = gain_ref[:, pl.ds(pl.multiple_of(quarter[j] * width, LANES), width)]
            out_ref[quarter[j], pl.ds(at, chunk), :] = (part * factor * gain).astype(BF)

    def step(i, _):
        near = pl.ds(pl.multiple_of(i * chunk, chunk), chunk)
        at = pl.multiple_of(vocab // 2 + i * chunk, chunk)
        far = pl.ds(at, chunk)
        some([own_ref[near, :], core_ref[near, :], up_ref[near, :], far_up_ref[near, :]], near.start)
        some([own_ref[far, :], core_ref[far, :], down_ref[near, :], far_down_ref[near, :]], at)
        return 0

    lax.fori_loop(0, vocab // 2 // chunk, step, 0)


def normed_rows(spot, own, got_core, got_up, got_down, far_up, far_down, gain):
    vocab, width = own.shape
    return pl.pallas_call(
        norm_kernel,
        out_shape=jax.ShapeDtypeStruct((4, vocab, width), BF),
        in_specs=[pl.BlockSpec(memory_space=pltpu.SMEM)] + in_vmem(7),
        out_specs=pl.BlockSpec(memory_space=pltpu.VMEM),
        cost_estimate=cost(20 * vocab * width, 8 * 2 * vocab * width),
        name="normed_rows",
    )(spot, own, got_core, got_up, got_down, far_up, far_down, gain)


def table_kernel(normed_ref, pieces_ref, scale_ref, out_ref, weight_ref):
    quarters, _, width = normed_ref.shape
    low = lax.broadcasted_iota(jnp.int32, (GROUP, LANES), 1) < LANES // 2
    for m in range(pieces_ref.shape[0] // 2):
        lanes = slice(m * LANES, (m + 1) * LANES)
        first = pieces_ref[2 * m, :GROUP, :].astype(F32)
        second = pieces_ref[2 * m + 1, :GROUP, :].astype(F32)
        weight_ref[:GROUP, lanes] = jnp.where(low, first, pltpu.roll(second, 64, 1)).astype(BF)
        weight_ref[GROUP : 2 * GROUP, lanes] = jnp.where(
            low, pltpu.roll(first, 64, 1), second
        ).astype(BF)
        first = pieces_ref[2 * m, GROUP:, :].astype(F32)[:8]
        second = pieces_ref[2 * m + 1, GROUP:, :].astype(F32)[:8]
        third = jnp.concatenate(
            [
                jnp.where(low[:8], first, pltpu.roll(second, 64, 1)),
                jnp.where(low[:8], pltpu.roll(first, 64, 1), second),
            ],
            axis=0,
        )
        weight_ref[2 * GROUP :, lanes] = third.astype(BF)
    total = None
    for q in range(quarters):
        term = lax.dot_general(
            weight_ref[:, q * width : (q + 1) * width],
            normed_ref[q],
            (((1,), (1,)), ((), ())),
            preferred_element_type=F32,
        )
        total = term if total is None else total + term
    out_ref[...] = (total * scale_ref[...]).astype(BF)


def table_piece(normed, pieces, scale):
    quarters, vocab, width = normed.shape
    rows = STREAMS * GROUP
    return pl.pallas_call(
        table_kernel,
        out_shape=jax.ShapeDtypeStruct((rows, vocab), BF),
        in_specs=in_vmem(3),
        out_specs=pl.BlockSpec(memory_space=pltpu.VMEM),
        scratch_shapes=[pltpu.VMEM((rows, quarters * width), BF)],
        cost_estimate=cost(2 * rows * vocab * quarters * width, 5000000),
        name="table_piece",
    )(normed, pieces, scale)


def toeplitz_kernel(taps_ref, out_ref):
    for g in range(taps_ref.shape[0]):
        row = jnp.broadcast_to(taps_ref[g : g + 1, :], (LONG_TAPS, 2 * LONG_TAPS))
        block = pltpu.roll(row, 0, 1, stride=1, stride_axis=0)
        out_ref[g] = jnp.transpose(block).astype(BF)


def toeplitz(taps_row):
    groups = taps_row.shape[0]
    return pl.pallas_call(
        toeplitz_kernel,
        out_shape=jax.ShapeDtypeStruct((groups, 2 * LONG_TAPS, LONG_TAPS), BF),
        in_specs=in_vmem(1),
        out_specs=pl.BlockSpec(memory_space=pltpu.VMEM),
        cost_estimate=cost(2000000, 1060000),
        name="toeplitz",
    )(taps_row)


def column_of(coded):
    known = jnp.where(coded < 0.0, 255.0 - coded, coded)
    rows = known.shape[0]
    padded = jnp.concatenate([known, jnp.zeros((8 - rows, LANES), F32)], axis=0)
    return jnp.transpose(padded).astype(jnp.int32)


def one_hot(column, vocab):
    hit = column == lax.broadcasted_iota(jnp.int32, (column.shape[0], vocab), 1)
    return jnp.where(hit, 1.0, 0.0).astype(BF)


def ids_of(pieces_ref, index):
    return pieces_ref[index, GROUP:, :].astype(F32)[8:12]


def hot_kernel(spot_ref, pieces_ref, out_ref, lead_ref):
    z = spot_ref[0]
    step = pl.program_id(0)
    devices = pieces_ref.shape[0]
    half, tokens, vocab = out_ref.shape
    lead = lead_ref.shape[0] // 2

    @pl.when(step == 0)
    def _():
        for segment in range(2):
            start = segment * (devices // 2) + z * 4
            rows = ids_of(pieces_ref, (start + devices - 1) % devices)
            column = column_of(rows[2:])
            column = jnp.concatenate([column[2 * LANES - lead :, 0:1], column[:, 1:2]], axis=0)
            lead_ref[segment * lead : (segment + 1) * lead, :] = one_hot(column, vocab)

    for block in range(half):
        index = step * half + block
        source = index // 4 * (devices // 2) + z * 4 + index % 4
        column = column_of(ids_of(pieces_ref, source))
        for j in range(tokens // LANES):
            out_ref[block, j * LANES : (j + 1) * LANES, :] = one_hot(column[:, j : j + 1], vocab)


def hot_rows(spot, pieces, blocks, tokens, vocab):
    half = 2
    return pl.pallas_call(
        hot_kernel,
        out_shape=(
            jax.ShapeDtypeStruct((blocks, tokens, vocab), BF),
            jax.ShapeDtypeStruct((2 * HALO, vocab), BF),
        ),
        grid=(blocks // half,),
        in_specs=[
            pl.BlockSpec(memory_space=pltpu.SMEM),
            pl.BlockSpec(pieces.shape, lambda i: (0, 0, 0)),
        ],
        out_specs=(
            pl.BlockSpec((half, tokens, vocab), lambda i: (i, 0, 0)),
            pl.BlockSpec((2 * HALO, vocab), lambda i: (0, 0)),
        ),
        cost_estimate=cost(5000000, 4500000),
        name="hot_rows",
    )(spot, pieces)


def mix_kernel(spot_ref, hot_ref, lead_hot_ref, *refs):
    tables = refs[:8]
    filt_ref, toep_ref, out_ref = refs[8:11]
    table_ref, lead_ref, head_ref, edge_ref = refs[11:15]
    next_ref, proj_ref, fresh_ref, inner_ref, fresh_gate_ref, gate_ref, conv_ref, flat_ref = refs[15:]
    step = pl.program_id(0)
    tokens = out_ref.shape[1]
    groups = LANES // GROUP
    margin = proj_ref.shape[1] - tokens
    lead = lead_hot_ref.shape[0] // 2
    chunk = 64

    def short(source, p, start, count):
        total = None
        for k in range(SHORT_TAPS):
            tap = filt_ref[p, k : k + 1, :]
            term = tap * source[p, start - k : start - k + count, :]
            total = term if total is None else total + term
        return total

    @pl.when(step == 0)
    def _():
        for j, piece in enumerate(tables):
            at = (spot_ref[0] + len(tables) - j) % len(tables) * GROUP
            for p in range(STREAMS):
                flat_ref[p, pl.ds(pl.multiple_of(at, GROUP), GROUP), :] = piece[
                    p * GROUP : (p + 1) * GROUP, :
                ]
        for p in range(STREAMS):
            table_ref[:, p * LANES : (p + 1) * LANES] = jnp.transpose(
                flat_ref[p].astype(F32)
            ).astype(BF)
        proj = jnp.dot(lead_hot_ref[...], table_ref[...], preferred_element_type=F32)
        for p in range(STREAMS):
            lead_ref[p] = proj[:, p * LANES : (p + 1) * LANES]
        for segment in range(2):
            for p in range(STREAMS):
                head_ref[segment, p] = lead_ref[
                    p, (segment + 1) * lead - margin : (segment + 1) * lead, :
                ]
            for at in range(0, LONG_TAPS, chunk):
                start = (segment + 1) * lead - LONG_TAPS + at
                fresh_ref[at : at + chunk, :] = short(lead_ref, 1, start, chunk) * short(
                    lead_ref, 2, start, chunk
                )
            edge_ref[segment] = jnp.transpose(fresh_ref[:LONG_TAPS, :]).astype(BF)

    count = tokens // LONG_TAPS

    def select(begin, end):
        proj = jnp.dot(hot_ref[0, begin:end, :], table_ref[...], preferred_element_type=F32)
        for p in range(STREAMS):
            next_ref[p, begin:end, :] = proj[:, p * LANES : (p + 1) * LANES]

    def filtered(at):
        left = short(proj_ref, 1, margin + at, chunk)
        right = short(proj_ref, 2, margin + at, chunk)
        fresh_ref[at : at + chunk, :] = left * right
        fresh_gate_ref[at : at + chunk, :] = short(proj_ref, 0, margin + at, chunk)

    def convolved(g):
        rows = slice(g * GROUP, (g + 1) * GROUP)
        windows = jnp.concatenate(
            [inner_ref[rows, j * LONG_TAPS : (j + 2) * LONG_TAPS] for j in range(count)], axis=0
        )
        full = jnp.dot(windows, toep_ref[g], preferred_element_type=F32)
        for j in range(count):
            conv_ref[j, rows, :] = full[j * GROUP : (j + 1) * GROUP]

    select(0, tokens)
    for g in range(groups):
        convolved(g)
        filtered(g * chunk)

    @pl.when(step >= 0)
    def _():
        for j in range(count):
            at = j * LONG_TAPS
            conv = jnp.transpose(conv_ref[j])
            out_ref[0, at : at + LONG_TAPS, :] = (gate_ref[at : at + LONG_TAPS, :] * conv).astype(BF)

        starts = step % 4 == 0
        segment = jnp.minimum(step // 4, 1)
        for p in range(STREAMS):
            proj_ref[p, :margin, :] = jnp.where(
                starts, head_ref[segment, p], proj_ref[p, tokens:, :]
            )
            proj_ref[p, margin:, :] = next_ref[p]
        starts = (step + 3) % 4 == 0
        segment = jnp.minimum((step + 3) // 4 - 1, 1)
        segment = jnp.maximum(segment, 0)
        inner_ref[:, :LONG_TAPS] = jnp.where(starts, edge_ref[segment], inner_ref[:, tokens:])
        for j in range(count):
            at = j * LONG_TAPS
            inner_ref[:, LONG_TAPS + at : 2 * LONG_TAPS + at] = jnp.transpose(
                fresh_ref[at : at + LONG_TAPS, :]
            ).astype(BF)
        gate_ref[...] = fresh_gate_ref[...]


def mixed_blocks(spot, hot, lead_hot, tables, filt, toep):
    blocks, tokens, vocab = hot.shape
    width = STREAMS * LANES

    def whole(value):
        return pl.BlockSpec(value.shape, lambda i: (0,) * value.ndim)

    return pl.pallas_call(
        mix_kernel,
        out_shape=jax.ShapeDtypeStruct((blocks, tokens, LANES), BF),
        grid=(blocks + 2,),
        in_specs=[
            pl.BlockSpec(memory_space=pltpu.SMEM),
            pl.BlockSpec((1, tokens, vocab), lambda i: (jnp.minimum(i, blocks - 1), 0, 0)),
            whole(lead_hot),
        ]
        + [whole(table) for table in tables]
        + [whole(filt), whole(toep)],
        out_specs=pl.BlockSpec((1, tokens, LANES), lambda i: (jnp.maximum(i - 2, 0), 0, 0)),
        scratch_shapes=[
            pltpu.VMEM((vocab, width), BF),
            pltpu.VMEM((STREAMS, 2 * HALO, LANES), F32),
            pltpu.VMEM((2, STREAMS, 8, LANES), F32),
            pltpu.VMEM((2, LONG_TAPS, LANES), BF),
            pltpu.VMEM((STREAMS, tokens, LANES), F32),
            pltpu.VMEM((STREAMS, tokens + 8, LANES), F32),
            pltpu.VMEM((tokens, LANES), F32),
            pltpu.VMEM((LANES, tokens + LONG_TAPS), BF),
            pltpu.VMEM((tokens, LANES), F32),
            pltpu.VMEM((tokens, LANES), F32),
            pltpu.VMEM((tokens // LONG_TAPS, LANES, LONG_TAPS), F32),
            pltpu.VMEM((STREAMS, LANES, vocab), BF),
        ],
        cost_estimate=cost(5000000000, 6000000),
        name="mixed_blocks",
    )(spot, hot, lead_hot, *tables, filt, toep)


def per_device(ids, embed_table, norm_gain, in_weight, in_scale, short_filter, long_filter, decay):
    tokens = ids.shape[0]
    vocab, width_local = embed_table.shape
    yh = lax.axis_index("yh")
    z = lax.axis_index("z")
    x = lax.axis_index("x")
    yl = lax.axis_index("yl")
    core = lax.axis_index("core")
    x_count = lax.axis_size("x")
    z_count = lax.axis_size("z")
    ctx = ("yh", "z", "x")
    tile = yh * x_count + x
    tiles = width_local // LANES

    y = ("yh", "yl")
    got_up = shifted(embed_table[: vocab // 2], y, -1)
    got_down = shifted(embed_table[vocab // 2 :], y, 1)
    got_core = shifted(embed_table, "core", 1)

    load = payload(in_weight, ids.reshape(-1, LANES), tiles * z_count)
    pieces = lax.all_to_all(load, ctx, 0, 0, tiled=True)

    groups = LANES // GROUP
    steps = jnp.arange(LONG_TAPS, dtype=F32)
    filt = lax.dynamic_slice_in_dim(long_filter, tile * groups, groups, 1)
    rate = lax.dynamic_slice_in_dim(decay, tile * groups, groups, 0)
    filt, rate, load = lax.optimization_barrier((filt, rate, load))
    taps = (filt * jnp.exp(-rate[None, :] * steps[:, None])).astype(BF).astype(F32)
    toep = toeplitz(jnp.pad(taps[::-1].T, ((0, 0), (1, LONG_TAPS - 1))))
    near_filter = lax.dynamic_slice_in_dim(short_filter, tile * LANES, LANES, 2)
    scale = lax.dynamic_slice_in_dim(in_scale, tile * LANES + z * GROUP, GROUP, 1)
    scale = scale.reshape(STREAMS * GROUP, 1)

    far_up = shifted(got_up, "core", 1)
    far_down = shifted(got_down, "core", 1)
    mine = yl * 2 + core
    order = jnp.stack([mine, mine ^ 1, mine ^ 2, mine ^ 3]).astype(jnp.int32)
    normed = normed_rows(
        order, embed_table, got_core, got_up, got_down, far_up, far_down, norm_gain.reshape(1, -1)
    )
    pieces, toep, near_filter, normed = lax.optimization_barrier(
        (pieces, toep, near_filter, normed)
    )
    piece = table_piece(normed, pieces, scale)
    ups, downs, last = [piece], [], piece
    for step in range(4):
        ups.append(shifted(ups[-1], "z", 1))
        if step < 3:
            last = shifted(last, "z", -1)
            downs.append(last)

    spot = z.reshape(1).astype(jnp.int32)
    hot, lead_hot = hot_rows(spot, pieces, tiles, tokens, vocab)
    blocks = mixed_blocks(spot, hot, lead_hot, ups + downs[::-1], near_filter, toep)
    result = lax.all_to_all(blocks, ("yh", "x"), 0, 0, tiled=True)
    return result.transpose(1, 0, 2).reshape(tokens, width_local)


def solution(mesh):
    fine = Mesh(mesh.devices.reshape(2, 8, 4, 2, 2), ("yh", "z", "x", "yl", "core"))
    ctx = ("yh", "z", "x")
    tp = ("yl", "core")
    placed = (
        P(ctx),
        P(None, tp),
        P(),
        P(None, ctx, tp),
        P(None, tp),
        P(None, None, tp),
        P(None, tp),
        P(tp),
    )
    return jax.shard_map(
        per_device, mesh=fine, in_specs=placed, out_specs=P(ctx, tp), check_vma=False
    )
```

time: 112 us -> 100 us (0.89); the launches traced: 111 us -> 99.8 us
  waiting for transfers between devices: 25.6 us -> 12.2 us
  Pallas kernels: 24.4 us -> 31.1 us
  starting transfers between devices: 32.8 us -> 27.5 us
  local copies, waits for them, and re-layouts: 7.68 us -> 10.7 us
  other arithmetic: 2.22 us -> 0.69 us
    all_to_all x2 -> x1, waiting for transfers between devices: 19.2 us -> 5.13 us  [per_device(): pieces = lax.all_to_all(load, ctx, 0, 0, tiled=True)]
    pallas_call x2 -> x3, Pallas kernels: 4.38 us -> 12.7 us  [the longest x1 6.08 us: normed_rows(): pl.pallas_call(norm_kernel, out_shape=jax.ShapeDtypeStruct((4, vocab, wid...]
    ppermute x3 -> x0, starting transfers between devices: 6.6 us -> none  [the longest x1 3.99 us: per_device(): lax.ppermute(own, around, [(spot(a, b, c), spot((a + 1) % 4, b, c)) for a...]
    ppermute x10 -> x12, starting transfers between devices: 10.4 us -> 12.8 us  [shifted(): return lax.ppermute(value, axis, pairs)]
    slice x2 -> x1, local copies, waits for them, and re-layouts: 0.01 us -> 2.09 us  [per_device(): got_down = shifted(embed_table[vocab // 2:], y, 1)]
    pallas_call x1, Pallas kernels: 6.13 us -> 4.36 us  [hot_rows(): pl.pallas_call(hot_kernel, out_shape=(jax.ShapeDtypeStruct((blocks, token...]
    convert_element_type x3 -> x0, other arithmetic: 1.67 us -> none  [the longest x1 1 us: per_device(): own = (own.astype(F32) * gain[None, :]).astype(BF)]
    all_to_all x2 -> x1, starting transfers between devices: 15.8 us -> 14.7 us  [per_device(): pieces = lax.all_to_all(load, ctx, 0, 0, tiled=True)]
  transfers between devices with their start and end apart: 15 -> 13, of which waited for: 5 -> 5; matrix products, arithmetic and copies ran while one was open for 3% -> 5% of each run, Pallas kernels for 7% -> 15%
where the time goes in v5:
time: 100 us; the launch traced here: 99.8 us
  Pallas kernels  31.1 us (31%)
  starting transfers between devices  27.5 us (28%)
  blocking collectives  17.5 us (18%)
  waiting for transfers between devices  12.2 us (12%)
  local copies, waits for them, and re-layouts  10.7 us (11%)
    all_to_all x1, blocking collectives, per_device(): result = lax.all_to_all(blocks, ('yh', 'x'), 0, 0, tiled=True)  17.5 us
    all_to_all x1, starting transfers between devices, per_device(): pieces = lax.all_to_all(load, ctx, 0, 0, tiled=True)  14.7 us
    ppermute x12, starting transfers between devices, shifted(): return lax.ppermute(value, axis, pairs)  12.8 us
    pallas_call x1, Pallas kernels, mixed_blocks(): pl.pallas_call(mix_kernel, out_shape=jax.ShapeDtypeStruct((blocks, tokens...  12.2 us
    ppermute x12, waiting for transfers between devices, shifted(): return lax.ppermute(value, axis, pairs)  7.11 us
    pallas_call x1, Pallas kernels, normed_rows(): pl.pallas_call(norm_kernel, out_shape=jax.ShapeDtypeStruct((4, vocab, wid...  6.08 us
    all_to_all x1, waiting for transfers between devices, per_device(): pieces = lax.all_to_all(load, ctx, 0, 0, tiled=True)  5.13 us
    pallas_call x1, Pallas kernels, table_piece(): pl.pallas_call(table_kernel, out_shape=jax.ShapeDtypeStruct((rows, vocab)...  4.39 us
  transfers between devices with their start and end apart: 13, of which 5 were waited for; matrix products, arithmetic and copies ran while one was open for 5% of the time, Pallas kernels for 15%

profile of v5, /device:TPU:8, one launch (start us, length us, event | category | flops | bytes accessed | tf_op | source)
XLA Modules:
  0.0 99.8 jit_solution(13470125993553110449)
XLA Ops:
  0.0 0.0 copy-start
  0.0 2.1 %fusion.1 = (bf16[256,1024]{1,0:T(8,128)(2,1)}, bf16[256,1024]{1,0:T(8,128)(2,1)S(1)}) fusion(bf16[512,1024]{1,0:T(8,128)(2,1)} %own_ref.1), kind=kLoop, calls=%fused_computation.6 | loop fusion | bytes 2097152 | tf_op jit(solution)/shard_map/slice | solution.py:386
  2.1 2.2 %collective-permute-start.1 = (bf16[256,1024]{1,0:T(8,128)(2,1)S(1)}, bf16[256,1024]{1,0:T(8,128)(2,1)S(1)}, u32[]{:S(2)}, u32[]{:S(2)}) collective-permute-start(bf16[256,1024]{1,0:T(8,128)(2,1)S(1)} %get-tuple-element.22), channel_id=1, source_target_pairs={{0,130},{2,0},{128,2},{130,128},{1,131},{3,1},{129,3},{131,129},{4... | collective-permute-start | bytes 1572872 | tf_op jit(solution)/shard_map/ppermute | solution.py:22
  4.3 0.0 collective-permute-start.2
  4.3 0.0 collective-permute-start
  4.3 2.2 %payload.1 = bf16[64,32,128]{2,1,0:T(8,128)(2,1)} custom-call(bf16[3,64,1024]{2,1,0:T(8,128)(2,1)} %weight_ref.1, s32[4,128]{1,0:T(4,128)} %bitcast.14), custom_call_target="tpu_custom_call" | custom-call | bytes 900000 | tf_op jit(solution)/shard_map/payload/pallas_call | solution.py:57
  6.5 14.7 %all-to-all-start = ((bf16[64,32,128]{2,1,0:T(8,128)(2,1)}), bf16[64,32,128]{2,1,0:T(8,128)(2,1)S(1)}, u32[]{:S(2)}, u32[]{:S(2)}) async-start(bf16[64,32,128]{2,1,0:T(8,128)(2,1)} %payload.1), calls=%async_computation | async-start | bytes 1048576 | tf_op jit(solution)/shard_map/all_to_all | solution.py:390
  21.2 0.7 dynamic_slice.13
  22.0 0.7 constant_dynamic-slice_fusion.2
  22.7 0.0 collective-permute-done.1.up_ref
  22.7 0.0 copy-start.3
  22.7 0.3 collective-permute-start.3
  23.0 0.0 collective-permute-done.2.down_ref
  23.0 0.0 copy-start.4
  23.0 0.3 collective-permute-start.4
  23.3 0.1 fusion
  23.4 0.1 rev.3
  23.4 0.8 constant_dynamic-slice_fusion
  24.2 0.7 reshape.22.scale_ref
  24.9 0.7 pad.4.taps_ref
  25.6 1.9 %toeplitz.1.refs_9_ = bf16[8,256,128]{2,1,0:T(8,128)(2,1)} custom-call(f32[8,256]{1,0:T(8,128)} %pad.4.taps_ref), custom_call_target="tpu_custom_call" | custom-call | flops 2000000 | bytes 1060000 | tf_op jit(solution)/shard_map/toeplitz/pallas_call | solution.py:160
  27.5 0.6 pad_add_fusion.spot_ref
  28.1 0.0 copy-done
  28.1 0.6 constant_dynamic-slice_fusion.1.refs_8_
  28.7 0.0 collective-permute-done.3.far_up_ref
  28.7 0.0 copy-start.5
  28.7 0.0 collective-permute-done.4.far_down_ref
  28.7 0.0 collective-permute-done.core_ref
  28.7 0.0 copy-start.2
  28.7 0.0 copy-done.3
  28.7 0.0 copy-done.4
  28.7 0.8 copy-done.5
  29.5 0.3 copy-done.2
  29.8 6.1 %normed_rows.1.normed_ref = bf16[4,512,1024]{2,1,0:T(8,128)(2,1)} custom-call(s32[4]{0:T(128)} %pad_add_fusion.spot_ref, bf16[512,1024]{1,0:T(8,128)(2,1)} %own_ref.1, bf16[512,1024]{1,0:T(8,128)(2,1)} %copy-done.2, bf16[256,1024]{1,0:T(8,128)(2,1)} %copy-done.3, bf16[256,1024]{1,0:T(8,128)(2,1)} %copy-done.4, bf16[256,1024]{1,0:T(8,128)(2,1)} %copy-done.5, ...), custom_call_target="tpu_custom_call" | custom-call | flops 10485760 | bytes 8388608 | tf_op jit(solution)/shard_map/normed_rows/pallas_call | solution.py:94
  35.9 5.1 %all-to-all-done.pieces_ref = bf16[64,32,128]{2,1,0:T(8,128)(2,1)S(1)} async-done(((bf16[64,32,128]{2,1,0:T(8,128)(2,1)}), bf16[64,32,128]{2,1,0:T(8,128)(2,1)S(1)}, u32[]{:S(2)}, u32[]{:S(2)}) %all-to-all-start) | async-done | bytes 524320 | tf_op jit(solution)/shard_map/all_to_all | solution.py:390
  41.0 0.0 copy-start.1
  41.0 0.8 copy-done.1
  41.8 4.4 %table_piece.1.refs_0_ = bf16[48,512]{1,0:T(8,128)(2,1)} custom-call(bf16[4,512,1024]{2,1,0:T(8,128)(2,1)} %normed_rows.1.normed_ref, bf16[64,32,128]{2,1,0:T(8,128)(2,1)} %copy-done.1, f32[48,1]{1,0:T(8,128)} %reshape.22.scale_ref), custom_call_target="tpu_custom_call" | custom-call | flops 201326592 | bytes 5000000 | tf_op jit(solution)/shard_map/table_piece/pallas_call | solution.py:140
  46.2 2.2 %collective-permute-start.5 = (bf16[48,512]{1,0:T(8,128)(2,1)}, bf16[48,512]{1,0:T(8,128)(2,1)S(1)}, u32[]{:S(2)}, u32[]{:S(2)}) collective-permute-start(bf16[48,512]{1,0:T(8,128)(2,1)} %table_piece.1.refs_0_), channel_id=1, source_target_pairs={{0,16},{16,32},{32,48},{48,64},{64,80},{80,96},{96,112},{112,0},{1... | collective-permute-start | bytes 147464 | tf_op jit(solution)/shard_map/ppermute | solution.py:22
  48.4 1.1 %collective-permute-start.9 = (bf16[48,512]{1,0:T(8,128)(2,1)}, bf16[48,512]{1,0:T(8,128)(2,1)S(1)}, u32[]{:S(2)}, u32[]{:S(2)}) collective-permute-start(bf16[48,512]{1,0:T(8,128)(2,1)} %table_piece.1.refs_0_), channel_id=1, source_target_pairs={{0,112},{16,0},{32,16},{48,32},{64,48},{80,64},{96,80},{112,96},{1... | collective-permute-start | bytes 147464 | tf_op jit(solution)/shard_map/ppermute | solution.py:22
  49.5 2.3 %collective-permute-done.5.refs_1_ = bf16[48,512]{1,0:T(8,128)(2,1)S(1)} collective-permute-done((bf16[48,512]{1,0:T(8,128)(2,1)}, bf16[48,512]{1,0:T(8,128)(2,1)S(1)}, u32[]{:S(2)}, u32[]{:S(2)}) %collective-permute-start.5) | collective-permute-done | bytes 49184 | tf_op jit(solution)/shard_map/ppermute | solution.py:22
  51.7 1.0 collective-permute-start.6
  52.7 0.0 collective-permute-done.9.refs_7_
  52.7 2.3 %collective-permute-start.10 = (bf16[48,512]{1,0:T(8,128)(2,1)S(1)}, bf16[48,512]{1,0:T(8,128)(2,1)S(1)}, u32[]{:S(2)}, u32[]{:S(2)}) collective-permute-start(bf16[48,512]{1,0:T(8,128)(2,1)S(1)} %collective-permute-done.9.refs_7_), channel_id=1, source_target_pairs={{0,112},{16,0},{32,16},{48,32},{64,48},{80,64},{96,80},{112,96},{1... | collective-permute-start | bytes 147464 | tf_op jit(solution)/shard_map/ppermute | solution.py:22
  55.0 2.1 %collective-permute-done.6.refs_2_ = bf16[48,512]{1,0:T(8,128)(2,1)S(1)} collective-permute-done((bf16[48,512]{1,0:T(8,128)(2,1)S(1)}, bf16[48,512]{1,0:T(8,128)(2,1)S(1)}, u32[]{:S(2)}, u32[]{:S(2)}) %collective-permute-start.6) | collective-permute-done | bytes 49184 | tf_op jit(solution)/shard_map/ppermute | solution.py:22
  57.0 0.3 collective-permute-start.7
  57.3 0.0 collective-permute-done.10.refs_6_
  57.3 3.2 %collective-permute-start.11 = (bf16[48,512]{1,0:T(8,128)(2,1)S(1)}, bf16[48,512]{1,0:T(8,128)(2,1)S(1)}, u32[]{:S(2)}, u32[]{:S(2)}) collective-permute-start(bf16[48,512]{1,0:T(8,128)(2,1)S(1)} %collective-permute-done.10.refs_6_), channel_id=1, source_target_pairs={{0,112},{16,0},{32,16},{48,32},{64,48},{80,64},{96,80},{112,96},{1... | collective-permute-start | bytes 147464 | tf_op jit(solution)/shard_map/ppermute | solution.py:22
  60.5 1.8 %collective-permute-done.7.refs_3_ = bf16[48,512]{1,0:T(8,128)(2,1)S(1)} collective-permute-done((bf16[48,512]{1,0:T(8,128)(2,1)S(1)}, bf16[48,512]{1,0:T(8,128)(2,1)S(1)}, u32[]{:S(2)}, u32[]{:S(2)}) %collective-permute-start.7) | collective-permute-done | bytes 49184 | tf_op jit(solution)/shard_map/ppermute | solution.py:22
  62.4 0.0 collective-permute-start.8
  62.4 4.4 %hot_rows.1 = (bf16[8,512,512]{2,1,0:T(8,128)(2,1)}, bf16[288,512]{1,0:T(8,128)(2,1)}) custom-call(s32[1]{0:T(128)} %bitcast.spot_ref, bf16[64,32,128]{2,1,0:T(8,128)(2,1)} %copy-done.1), custom_call_target="tpu_custom_call" | custom-call | flops 5000000 | bytes 4500000 | tf_op jit(solution)/shard_map/hot_rows/pallas_call | solution.py:212
  66.7 0.0 collective-permute-done.11.refs_5_
  66.7 0.9 collective-permute-done.8.refs_4_
  67.7 0.0 copy-done.6
  67.7 0.0 copy-done.7
  67.7 0.0 copy-done.8
  67.7 0.0 copy-done.9
  67.7 0.0 copy-done.10
  67.7 0.0 copy-done.11
  67.7 0.6 copy-done.12
  68.3 12.2 %mixed_blocks.1 = bf16[8,512,128]{2,1,0:T(8,128)(2,1)} custom-call(s32[1]{0:T(128)} %bitcast.spot_ref, bf16[8,512,512]{2,1,0:T(8,128)(2,1)} %get-tuple-element.16.hot_ref, bf16[288,512]{1,0:T(8,128)(2,1)} %get-tuple-element.17.lead_hot_ref, bf16[48,512]{1,0:T(8,128)(2,1)} %table_piece.1.refs_0_, bf16[48,512]{1,0:T(8,128)(2,1)} %copy-done.6, ...), custom_call_target="tpu_custom_call" | custom-call | flops 5000000000 | bytes 6000000 | tf_op jit(solution)/shard_map/mixed_blocks/pallas_call | solution.py:339
  80.4 17.5 %all_to_all.10 = bf16[8,512,128]{2,1,0:T(8,128)(2,1)S(1)} all-to-all(bf16[8,512,128]{2,1,0:T(8,128)(2,1)} %mixed_blocks.1), channel_id=1, replica_groups=mesh['yh'=2,'z'=8,'x'=4,'yl'=2,'core'=2] {'yh','x'}, dimensions={0} | all-to-all | bytes 2097152 | tf_op jit(solution)/shard_map/all_to_all | solution.py:424
  98.0 0.5 copy.11
  98.5 1.3 %copy.12 = bf16[512,1024]{1,0:T(8,128)(2,1)} copy(bf16[512,1024]{0,1:T(8,128)(2,1)S(1)} %bitcast.11) | data formatting | bytes 2097152 | tf_op jit(solution)/shard_map/reshape | solution.py:425
  (8 shorter events, 0.0 us)
Async XLA Ops:
  0.0 28.1 %copy-start = (f32[3,7,1024]{2,1,0:T(8,128)S(1)}, f32[3,7,1024]{2,1,0:T(8,128)}, u32[]{:S(2)}) copy-start(f32[3,7,1024]{2,1,0:T(8,128)} %param.13) | copy-start | bytes 258052
  2.1 20.6 %collective-permute-start.1 = (bf16[256,1024]{1,0:T(8,128)(2,1)S(1)}, bf16[256,1024]{1,0:T(8,128)(2,1)S(1)}, u32[]{:S(2)}, u32[]{:S(2)}) collective-permute-start(bf16[256,1024]{1,0:T(8,128)(2,1)S(1)} %get-tuple-element.22), channel_id=1, source_target_pairs={{0,130},{2,0},{128,2},{130,128},{1,131},{3,1},{129,3},{131,129},{4... | collective-permute-start | bytes 1572872 | tf_op jit(solution)/shard_map/ppermute | solution.py:22
  4.3 18.7 %collective-permute-start.2 = (bf16[256,1024]{1,0:T(8,128)(2,1)}, bf16[256,1024]{1,0:T(8,128)(2,1)S(1)}, u32[]{:S(2)}, u32[]{:S(2)}) collective-permute-start(bf16[256,1024]{1,0:T(8,128)(2,1)} %get-tuple-element.21), channel_id=1, source_target_pairs={{0,2},{2,128},{128,130},{130,0},{1,3},{3,129},{129,131},{131,1},{4... | collective-permute-start | bytes 1572872 | tf_op jit(solution)/shard_map/ppermute | solution.py:22
  4.3 24.4 %collective-permute-start = (bf16[512,1024]{1,0:T(8,128)(2,1)}, bf16[512,1024]{1,0:T(8,128)(2,1)S(1)}, u32[]{:S(2)}, u32[]{:S(2)}) collective-permute-start(bf16[512,1024]{1,0:T(8,128)(2,1)} %own_ref.1), channel_id=1, source_target_pairs={{0,1},{1,0},{2,3},{3,2},{4,5},{5,4},{6,7},{7,6},{8,9},{9,8},{10,11... | collective-permute-start | bytes 3145736 | tf_op jit(solution)/shard_map/ppermute | solution.py:22
  6.5 34.5 %all-to-all-start = ((bf16[64,32,128]{2,1,0:T(8,128)(2,1)}), bf16[64,32,128]{2,1,0:T(8,128)(2,1)S(1)}, u32[]{:S(2)}, u32[]{:S(2)}) async-start(bf16[64,32,128]{2,1,0:T(8,128)(2,1)} %payload.1), calls=%async_computation | async-start | bytes 1048576 | tf_op jit(solution)/shard_map/all_to_all | solution.py:390
  22.7 6.0 %copy-start.3 = (bf16[256,1024]{1,0:T(8,128)(2,1)}, bf16[256,1024]{1,0:T(8,128)(2,1)S(1)}, u32[]{:S(2)}) copy-start(bf16[256,1024]{1,0:T(8,128)(2,1)S(1)} %collective-permute-done.1.up_ref) | copy-start | bytes 1572868
  22.7 6.0 %collective-permute-start.3 = (bf16[256,1024]{1,0:T(8,128)(2,1)S(1)}, bf16[256,1024]{1,0:T(8,128)(2,1)S(1)}, u32[]{:S(2)}, u32[]{:S(2)}) collective-permute-start(bf16[256,1024]{1,0:T(8,128)(2,1)S(1)} %collective-permute-done.1.up_ref), channel_id=1, source_target_pairs={{0,1},{1,0},{2,3},{3,2},{4,5},{5,4},{6,7},{7,6},{8,9},{9,8},{10,11... | collective-permute-start | bytes 1572872 | tf_op jit(solution)/shard_map/ppermute | solution.py:22
  23.0 5.7 %copy-start.4 = (bf16[256,1024]{1,0:T(8,128)(2,1)}, bf16[256,1024]{1,0:T(8,128)(2,1)S(1)}, u32[]{:S(2)}) copy-start(bf16[256,1024]{1,0:T(8,128)(2,1)S(1)} %collective-permute-done.2.down_ref) | copy-start | bytes 1572868
  23.0 5.7 %collective-permute-start.4 = (bf16[256,1024]{1,0:T(8,128)(2,1)S(1)}, bf16[256,1024]{1,0:T(8,128)(2,1)}, u32[]{:S(2)}, u32[]{:S(2)}) collective-permute-start(bf16[256,1024]{1,0:T(8,128)(2,1)S(1)} %collective-permute-done.2.down_ref), channel_id=1, source_target_pairs={{0,1},{1,0},{2,3},{3,2},{4,5},{5,4},{6,7},{7,6},{8,9},{9,8},{10,11... | collective-permute-start | bytes 1572872 | tf_op jit(solution)/shard_map/ppermute | solution.py:22
  28.7 0.8 copy-start.5
  28.7 1.1 %copy-start.2 = (bf16[512,1024]{1,0:T(8,128)(2,1)}, bf16[512,1024]{1,0:T(8,128)(2,1)S(1)}, u32[]{:S(2)}) copy-start(bf16[512,1024]{1,0:T(8,128)(2,1)S(1)} %collective-permute-done.core_ref) | copy-start | bytes 3145732
  41.0 0.8 copy-start.1
  46.2 5.5 %collective-permute-start.5 = (bf16[48,512]{1,0:T(8,128)(2,1)}, bf16[48,512]{1,0:T(8,128)(2,1)S(1)}, u32[]{:S(2)}, u32[]{:S(2)}) collective-permute-start(bf16[48,512]{1,0:T(8,128)(2,1)} %table_piece.1.refs_0_), channel_id=1, source_target_pairs={{0,16},{16,32},{32,48},{48,64},{64,80},{80,96},{96,112},{112,0},{1... | collective-permute-start | bytes 147464 | tf_op jit(solution)/shard_map/ppermute | solution.py:22
  48.4 4.3 %collective-permute-start.9 = (bf16[48,512]{1,0:T(8,128)(2,1)}, bf16[48,512]{1,0:T(8,128)(2,1)S(1)}, u32[]{:S(2)}, u32[]{:S(2)}) collective-permute-start(bf16[48,512]{1,0:T(8,128)(2,1)} %table_piece.1.refs_0_), channel_id=1, source_target_pairs={{0,112},{16,0},{32,16},{48,32},{64,48},{80,64},{96,80},{112,96},{1... | collective-permute-start | bytes 147464 | tf_op jit(solution)/shard_map/ppermute | solution.py:22
  51.7 15.9 %copy-start.6 = (bf16[48,512]{1,0:T(8,128)(2,1)}, bf16[48,512]{1,0:T(8,128)(2,1)S(1)}, u32[]{:S(2)}) copy-start(bf16[48,512]{1,0:T(8,128)(2,1)S(1)} %collective-permute-done.5.refs_1_) | copy-start | bytes 147460
  51.7 5.3 %collective-permute-start.6 = (bf16[48,512]{1,0:T(8,128)(2,1)S(1)}, bf16[48,512]{1,0:T(8,128)(2,1)S(1)}, u32[]{:S(2)}, u32[]{:S(2)}) collective-permute-start(bf16[48,512]{1,0:T(8,128)(2,1)S(1)} %collective-permute-done.5.refs_1_), channel_id=1, source_target_pairs={{0,16},{16,32},{32,48},{48,64},{64,80},{80,96},{96,112},{112,0},{1... | collective-permute-start | bytes 147464 | tf_op jit(solution)/shard_map/ppermute | solution.py:22
  52.7 15.0 %copy-start.7 = (bf16[48,512]{1,0:T(8,128)(2,1)}, bf16[48,512]{1,0:T(8,128)(2,1)S(1)}, u32[]{:S(2)}) copy-start(bf16[48,512]{1,0:T(8,128)(2,1)S(1)} %collective-permute-done.9.refs_7_) | copy-start | bytes 147460
  52.7 4.6 %collective-permute-start.10 = (bf16[48,512]{1,0:T(8,128)(2,1)S(1)}, bf16[48,512]{1,0:T(8,128)(2,1)S(1)}, u32[]{:S(2)}, u32[]{:S(2)}) collective-permute-start(bf16[48,512]{1,0:T(8,128)(2,1)S(1)} %collective-permute-done.9.refs_7_), channel_id=1, source_target_pairs={{0,112},{16,0},{32,16},{48,32},{64,48},{80,64},{96,80},{112,96},{1... | collective-permute-start | bytes 147464 | tf_op jit(solution)/shard_map/ppermute | solution.py:22
  57.0 10.6 %copy-start.8 = (bf16[48,512]{1,0:T(8,128)(2,1)}, bf16[48,512]{1,0:T(8,128)(2,1)S(1)}, u32[]{:S(2)}) copy-start(bf16[48,512]{1,0:T(8,128)(2,1)S(1)} %collective-permute-done.6.refs_2_) | copy-start | bytes 147460
  57.0 5.3 %collective-permute-start.7 = (bf16[48,512]{1,0:T(8,128)(2,1)S(1)}, bf16[48,512]{1,0:T(8,128)(2,1)S(1)}, u32[]{:S(2)}, u32[]{:S(2)}) collective-permute-start(bf16[48,512]{1,0:T(8,128)(2,1)S(1)} %collective-permute-done.6.refs_2_), channel_id=1, source_target_pairs={{0,16},{16,32},{32,48},{48,64},{64,80},{80,96},{96,112},{112,0},{1... | collective-permute-start | bytes 147464 | tf_op jit(solution)/shard_map/ppermute | solution.py:22
  57.3 10.4 %copy-start.9 = (bf16[48,512]{1,0:T(8,128)(2,1)}, bf16[48,512]{1,0:T(8,128)(2,1)S(1)}, u32[]{:S(2)}) copy-start(bf16[48,512]{1,0:T(8,128)(2,1)S(1)} %collective-permute-done.10.refs_6_) | copy-start | bytes 147460
  57.3 9.4 %collective-permute-start.11 = (bf16[48,512]{1,0:T(8,128)(2,1)S(1)}, bf16[48,512]{1,0:T(8,128)(2,1)S(1)}, u32[]{:S(2)}, u32[]{:S(2)}) collective-permute-start(bf16[48,512]{1,0:T(8,128)(2,1)S(1)} %collective-permute-done.10.refs_6_), channel_id=1, source_target_pairs={{0,112},{16,0},{32,16},{48,32},{64,48},{80,64},{96,80},{112,96},{1... | collective-permute-start | bytes 147464 | tf_op jit(solution)/shard_map/ppermute | solution.py:22
  62.4 5.3 %copy-start.10 = (bf16[48,512]{1,0:T(8,128)(2,1)}, bf16[48,512]{1,0:T(8,128)(2,1)S(1)}, u32[]{:S(2)}) copy-start(bf16[48,512]{1,0:T(8,128)(2,1)S(1)} %collective-permute-done.7.refs_3_) | copy-start | bytes 147460
  62.4 5.3 %collective-permute-start.8 = (bf16[48,512]{1,0:T(8,128)(2,1)S(1)}, bf16[48,512]{1,0:T(8,128)(2,1)S(1)}, u32[]{:S(2)}, u32[]{:S(2)}) collective-permute-start(bf16[48,512]{1,0:T(8,128)(2,1)S(1)} %collective-permute-done.7.refs_3_), channel_id=1, source_target_pairs={{0,16},{16,32},{32,48},{48,64},{64,80},{80,96},{96,112},{112,0},{1... | collective-permute-start | bytes 147464 | tf_op jit(solution)/shard_map/ppermute | solution.py:22
  66.7 1.0 copy-start.11
  67.7 0.6 copy-start.12

commit v6 on v5

--- a/solution.py
+++ b/solution.py
@@ -11,6 +11,7 @@
 LONG_TAPS = 128
 LANES = 128
 HALO = 144
+GRANT = 24 * 1024 * 1024
 STREAMS = 3
 BF = jnp.bfloat16
 F32 = jnp.float32
@@ -22,7 +23,14 @@
     return lax.ppermute(value, axis, pairs)
 
 
-def payload_kernel(weight_ref, ids_ref, out_ref):
+def payload_kernel(weight_ref, ids_ref, table_ref, out_ref, upper_ref, lower_ref, sems):
+    half = upper_ref.shape[0]
+    copies = [
+        pltpu.make_async_copy(table_ref.at[pl.ds(0, half), :], upper_ref, sems.at[0]),
+        pltpu.make_async_copy(table_ref.at[pl.ds(half, half), :], lower_ref, sems.at[1]),
+    ]
+    for copy in copies:
+        copy.start()
     streams, rows, width = weight_ref.shape
     tiles = width // LANES
     columns = out_ref.shape[0] // tiles
@@ -43,6 +51,8 @@
             out_ref[to, GROUP:, :] = jnp.concatenate([third[at : at + 8], coded], axis=0).astype(
                 BF
             )
+    for copy in copies:
+        copy.wait()
 
 
 def in_vmem(count):
@@ -53,56 +63,72 @@
     return pl.CostEstimate(flops=flops, bytes_accessed=moved, transcendentals=0)
 
 
-def payload(in_weight, ids_rows, parts):
+def payload(in_weight, ids_rows, embed_table, parts):
+    vocab, width = embed_table.shape
+    half = jax.ShapeDtypeStruct((vocab // 2, width), BF)
     return pl.pallas_call(
         payload_kernel,
-        out_shape=jax.ShapeDtypeStruct((parts, 2 * GROUP, LANES), BF),
-        in_specs=in_vmem(2),
-        out_specs=pl.BlockSpec(memory_space=pltpu.VMEM),
-        cost_estimate=cost(0, 900000),
+        out_shape=(jax.ShapeDtypeStruct((parts, 2 * GROUP, LANES), BF), half, half),
+        in_specs=in_vmem(3),
+        out_specs=(pl.BlockSpec(memory_space=pltpu.VMEM),)
+        + (pl.BlockSpec(memory_space=pl.ANY),) * 2,
+        scratch_shapes=[pltpu.SemaphoreType.DMA((2,))],
+        compiler_params=pltpu.CompilerParams(vmem_limit_bytes=GRANT),
+        cost_estimate=cost(0, 2900000),
         name="payload",
-    )(in_weight, ids_rows)
-
-
-def norm_kernel(spot_ref, own_ref, core_ref, up_ref, down_ref, far_up_ref, far_down_ref, *refs):
-    gain_ref, out_ref = refs
-    vocab, width = own_ref.shape
+    )(in_weight, ids_rows, embed_table)
+
+
+def norm_kernel(spot_ref, *refs):
+    shards, gain_ref, out_ref, token_ref = refs[:6], refs[6], refs[7], refs[8]
+    token_ref[...] = jnp.zeros_like(token_ref)
+    vocab, width = shards[0].shape
     quarter = [spot_ref[j] for j in range(4)]
-    chunk = 32
-
-    def some(read, at):
-        parts = [value.astype(F32) for value in read]
-        squares = sum(jnp.sum(part * part, axis=1, keepdims=True) for part in parts)
-        factor = lax.rsqrt(squares / (4 * width) + 1e-06)
-        for j, part in enumerate(parts):
-            gain = gain_ref[:, pl.ds(pl.multiple_of(quarter[j] * width, LANES), width)]
-            out_ref[quarter[j], pl.ds(at, chunk), :] = (part * factor * gain).astype(BF)
-
-    def step(i, _):
-        near = pl.ds(pl.multiple_of(i * chunk, chunk), chunk)
-        at = pl.multiple_of(vocab // 2 + i * chunk, chunk)
-        far = pl.ds(at, chunk)
-        some([own_ref[near, :], core_ref[near, :], up_ref[near, :], far_up_ref[near, :]], near.start)
-        some([own_ref[far, :], core_ref[far, :], down_ref[near, :], far_down_ref[near, :]], at)
-        return 0
-
-    lax.fori_loop(0, vocab // 2 // chunk, step, 0)
-
-
-def normed_rows(spot, own, got_core, got_up, got_down, far_up, far_down, gain):
-    vocab, width = own.shape
+    chunk = 16
+
+    for half in range(2):
+        read = (shards[0], shards[1], shards[2 + half], shards[4 + half])
+
+        def step(i, _, half=half, read=read):
+            near = pl.ds(pl.multiple_of(i * chunk, chunk), chunk)
+            at = pl.ds(pl.multiple_of(half * (vocab // 2) + i * chunk, chunk), chunk)
+            rows = (at, at, near, near)
+            squares = 0.0
+            for shard, row in zip(read, rows):
+                part = shard[row, :].astype(F32)
+                squares = squares + jnp.sum(part * part, axis=1, keepdims=True)
+            factor = lax.rsqrt(squares / (4 * width) + 1e-06)
+            for j, (shard, row) in enumerate(zip(read, rows)):
+                gain = gain_ref[:, pl.ds(pl.multiple_of(quarter[j] * width, LANES), width)]
+                out_ref[quarter[j], at, :] = (shard[row, :].astype(F32) * factor * gain).astype(BF)
+            return 0
+
+        lax.fori_loop(0, vocab // 2 // chunk, step, 0, unroll=2)
+
+
+def normed_rows(spot, shards, gain):
+    vocab, width = shards[0].shape
     return pl.pallas_call(
         norm_kernel,
-        out_shape=jax.ShapeDtypeStruct((4, vocab, width), BF),
+        out_shape=(
+            jax.ShapeDtypeStruct((4, vocab, width), BF),
+            jax.ShapeDtypeStruct((8, LANES), F32),
+        ),
         in_specs=[pl.BlockSpec(memory_space=pltpu.SMEM)] + in_vmem(7),
-        out_specs=pl.BlockSpec(memory_space=pltpu.VMEM),
+        out_specs=tuple(in_vmem(2)),
+        compiler_params=pltpu.CompilerParams(vmem_limit_bytes=GRANT),
         cost_estimate=cost(20 * vocab * width, 8 * 2 * vocab * width),
         name="normed_rows",
-    )(spot, own, got_core, got_up, got_down, far_up, far_down, gain)
-
-
-def table_kernel(normed_ref, pieces_ref, scale_ref, out_ref, weight_ref):
+    )(spot, *shards, gain)
+
+
+def table_kernel(far_ref, pieces_ref, scale_ref, _, out_ref, weight_ref, normed_ref, sems):
     quarters, _, width = normed_ref.shape
+    copies = [
+        pltpu.make_async_copy(far_ref.at[q], normed_ref.at[q], sems.at[q]) for q in range(quarters)
+    ]
+    for copy in copies:
+        copy.start()
     low = lax.broadcasted_iota(jnp.int32, (GROUP, LANES), 1) < LANES // 2
     for m in range(pieces_ref.shape[0] // 2):
         lanes = slice(m * LANES, (m + 1) * LANES)
@@ -124,6 +150,7 @@
         weight_ref[2 * GROUP :, lanes] = third.astype(BF)
     total = None
     for q in range(quarters):
+        copies[q].wait()
         term = lax.dot_general(
             weight_ref[:, q * width : (q + 1) * width],
             normed_ref[q],
@@ -134,18 +161,23 @@
     out_ref[...] = (total * scale_ref[...]).astype(BF)
 
 
-def table_piece(normed, pieces, scale):
+def table_piece(normed, pieces, scale, token):
     quarters, vocab, width = normed.shape
     rows = STREAMS * GROUP
     return pl.pallas_call(
         table_kernel,
         out_shape=jax.ShapeDtypeStruct((rows, vocab), BF),
-        in_specs=in_vmem(3),
+        in_specs=[pl.BlockSpec(memory_space=pltpu.HBM)] + in_vmem(3),
         out_specs=pl.BlockSpec(memory_space=pltpu.VMEM),
-        scratch_shapes=[pltpu.VMEM((rows, quarters * width), BF)],
+        scratch_shapes=[
+            pltpu.VMEM((rows, quarters * width), BF),
+            pltpu.VMEM(normed.shape, BF),
+            pltpu.SemaphoreType.DMA((quarters,)),
+        ],
+        compiler_params=pltpu.CompilerParams(vmem_limit_bytes=GRANT),
         cost_estimate=cost(2 * rows * vocab * quarters * width, 5000000),
         name="table_piece",
-    )(normed, pieces, scale)
+    )(normed, pieces, scale, token)
 
 
 def toeplitz_kernel(taps_ref, out_ref):
@@ -162,6 +194,7 @@
         out_shape=jax.ShapeDtypeStruct((groups, 2 * LONG_TAPS, LONG_TAPS), BF),
         in_specs=in_vmem(1),
         out_specs=pl.BlockSpec(memory_space=pltpu.VMEM),
+        compiler_params=pltpu.CompilerParams(vmem_limit_bytes=GRANT),
         cost_estimate=cost(2000000, 1060000),
         name="toeplitz",
     )(taps_row)
@@ -224,6 +257,7 @@
             pl.BlockSpec((half, tokens, vocab), lambda i: (i, 0, 0)),
             pl.BlockSpec((2 * HALO, vocab), lambda i: (0, 0)),
         ),
+        compiler_params=pltpu.CompilerParams(vmem_limit_bytes=GRANT),
         cost_estimate=cost(5000000, 4500000),
         name="hot_rows",
     )(spot, pieces)
@@ -362,9 +396,37 @@
             pltpu.VMEM((tokens // LONG_TAPS, LANES, LONG_TAPS), F32),
             pltpu.VMEM((STREAMS, LANES, vocab), BF),
         ],
+        compiler_params=pltpu.CompilerParams(vmem_limit_bytes=GRANT),
         cost_estimate=cost(5000000000, 6000000),
         name="mixed_blocks",
     )(spot, hot, lead_hot, *tables, filt, toep)
+
+
+def place_kernel(blocks_ref, out_ref, sems):
+    copies = [
+        pltpu.make_async_copy(
+            blocks_ref.at[j], out_ref.at[:, pl.ds(j * LANES, LANES)], sems.at[j]
+        )
+        for j in range(blocks_ref.shape[0])
+    ]
+    for copy in copies:
+        copy.start()
+    for copy in copies:
+        copy.wait()
+
+
+def placed_columns(blocks):
+    count, tokens, lanes = blocks.shape
+    return pl.pallas_call(
+        place_kernel,
+        out_shape=jax.ShapeDtypeStruct((tokens, count * lanes), BF),
+        in_specs=in_vmem(1),
+        out_specs=pl.BlockSpec(memory_space=pl.ANY),
+        scratch_shapes=[pltpu.SemaphoreType.DMA((count,))],
+        compiler_params=pltpu.CompilerParams(vmem_limit_bytes=GRANT),
+        cost_estimate=cost(0, 2000000),
+        name="placed_columns",
+    )(blocks)
 
 
 def per_device(ids, embed_table, norm_gain, in_weight, in_scale, short_filter, long_filter, decay):
@@ -381,12 +443,10 @@
     tile = yh * x_count + x
     tiles = width_local // LANES
 
-    y = ("yh", "yl")
-    got_up = shifted(embed_table[: vocab // 2], y, -1)
-    got_down = shifted(embed_table[vocab // 2 :], y, 1)
+    load, upper, lower = payload(in_weight, ids.reshape(-1, LANES), embed_table, tiles * z_count)
+    got_up = shifted(upper, ("yh", "yl"), -1)
+    got_down = shifted(lower, ("yh", "yl"), 1)
     got_core = shifted(embed_table, "core", 1)
-
-    load = payload(in_weight, ids.reshape(-1, LANES), tiles * z_count)
     pieces = lax.all_to_all(load, ctx, 0, 0, tiled=True)
 
     groups = LANES // GROUP
@@ -404,13 +464,13 @@
     far_down = shifted(got_down, "core", 1)
     mine = yl * 2 + core
     order = jnp.stack([mine, mine ^ 1, mine ^ 2, mine ^ 3]).astype(jnp.int32)
-    normed = normed_rows(
-        order, embed_table, got_core, got_up, got_down, far_up, far_down, norm_gain.reshape(1, -1)
+    normed, token = normed_rows(
+        order, [embed_table, got_core, got_up, got_down, far_up, far_down], norm_gain.reshape(1, -1)
     )
-    pieces, toep, near_filter, normed = lax.optimization_barrier(
-        (pieces, toep, near_filter, normed)
+    pieces, toep, near_filter, token = lax.optimization_barrier(
+        (pieces, toep, near_filter, token)
     )
-    piece = table_piece(normed, pieces, scale)
+    piece = table_piece(normed, pieces, scale, token)
     ups, downs, last = [piece], [], piece
     for step in range(4):
         ups.append(shifted(ups[-1], "z", 1))
@@ -422,7 +482,7 @@
     hot, lead_hot = hot_rows(spot, pieces, tiles, tokens, vocab)
     blocks = mixed_blocks(spot, hot, lead_hot, ups + downs[::-1], near_filter, toep)
     result = lax.all_to_all(blocks, ("yh", "x"), 0, 0, tiled=True)
-    return result.transpose(1, 0, 2).reshape(tokens, width_local)
+    return placed_columns(result)
 
 
 def solution(mesh):

time: 100 us -> 96.9 us (0.969)
  Pallas kernels: 31.1 us -> 22.2 us
  waiting for transfers between devices: 12.2 us -> 18.2 us
    unnamed x26 -> x16, local copies, waits for them, and re-layouts: 2.5 us -> 8.39 us
    all_to_all x1, waiting for transfers between devices: 5.13 us -> 8.7 us  [per_device(): pieces = lax.all_to_all(load, ctx, 0, 0, tiled=True)]
    pallas_call x1, Pallas kernels: 4.36 us -> 1.76 us  [hot_rows(): pl.pallas_call(hot_kernel, out_shape=(jax.ShapeDtypeStruct((blocks, token...]
    pallas_call x1, Pallas kernels: 4.39 us -> 1.97 us  [table_piece(): pl.pallas_call(table_kernel, out_shape=jax.ShapeDtypeStruct((rows, vocab)...]
    ppermute x12, waiting for transfers between devices: 7.11 us -> 9.49 us  [shifted(): return lax.ppermute(value, axis, pairs)]
    pallas_call x1, Pallas kernels: 12.2 us -> 9.88 us  [mixed_blocks(): pl.pallas_call(mix_kernel, out_shape=jax.ShapeDtypeStruct((blocks, tokens...]
    slice x1 -> x0, local copies, waits for them, and re-layouts: 2.09 us -> none  [per_device(): got_down = shifted(embed_table[vocab // 2:], y, 1)]
    pallas_call x1, Pallas kernels: 1.89 us -> 0.39 us  [toeplitz(): pl.pallas_call(toeplitz_kernel, out_shape=jax.ShapeDtypeStruct((groups, 2...]
  transfers between devices with their start and end apart: 13 -> 13, of which waited for: 5 -> 5; matrix products, arithmetic and copies ran while one was open for 5% -> 3% of each run, Pallas kernels for 15% -> 6%
where the time goes in v6:
time: 96.9 us; the launch traced here: 96.4 us
  starting transfers between devices  27.5 us (28%)
  Pallas kernels  22.2 us (23%)
  waiting for transfers between devices  18.2 us (19%)
  blocking collectives  17.3 us (18%)
  local copies, waits for them, and re-layouts  10.8 us (11%)
    all_to_all x1, blocking collectives, per_device(): result = lax.all_to_all(blocks, ('yh', 'x'), 0, 0, tiled=True)  17.3 us
    all_to_all x1, starting transfers between devices, per_device(): pieces = lax.all_to_all(load, ctx, 0, 0, tiled=True)  14.7 us
    ppermute x12, starting transfers between devices, shifted(): return lax.ppermute(value, axis, pairs)  12.8 us
    pallas_call x1, Pallas kernels, mixed_blocks(): pl.pallas_call(mix_kernel, out_shape=jax.ShapeDtypeStruct((blocks, tokens...  9.88 us
    ppermute x12, waiting for transfers between devices, shifted(): return lax.ppermute(value, axis, pairs)  9.49 us
    all_to_all x1, waiting for transfers between devices, per_device(): pieces = lax.all_to_all(load, ctx, 0, 0, tiled=True)  8.7 us
    unnamed x16, local copies, waits for them, and re-layouts  8.39 us
    pallas_call x1, Pallas kernels, normed_rows(): pl.pallas_call(norm_kernel, out_shape=(jax.ShapeDtypeStruct((4, vocab, wi...  4.09 us
  transfers between devices with their start and end apart: 13, of which 5 were waited for; matrix products, arithmetic and copies ran while one was open for 3% of the time, Pallas kernels for 6%

profile of v6, /device:TPU:8, one launch (start us, length us, event | category | flops | bytes accessed | tf_op | source)
XLA Modules:
  0.0 96.4 jit_solution(15092033710214555854)
XLA Ops:
  0.0 0.0 copy-start
  0.0 0.0 copy-start.5
  0.0 1.0 %copy-done.5 = bf16[3,64,1024]{2,1,0:T(8,128)(2,1)S(1)} copy-done((bf16[3,64,1024]{2,1,0:T(8,128)(2,1)S(1)}, bf16[3,64,1024]{2,1,0:T(8,128)(2,1)}, u32[]{:S(2)}) %copy-start.5) | copy-done | bytes 393240
  1.0 0.0 copy-start.7
  1.0 0.7 copy-done.7
  1.7 3.1 %payload.1 = (bf16[64,32,128]{2,1,0:T(8,128)(2,1)}, bf16[256,1024]{1,0:T(8,128)(2,1)S(1)}, bf16[256,1024]{1,0:T(8,128)(2,1)}) custom-call(bf16[3,64,1024]{2,1,0:T(8,128)(2,1)S(1)} %copy-done.5, s32[4,128]{1,0:T(4,128)S(1)} %bitcast.9, bf16[512,1024]{1,0:T(8,128)(2,1)} %refs_0_.1), custom_call_target="tpu_custom_call" | custom-call | bytes 2900000 | tf_op jit(solution)/shard_map/payload/pallas_call | solution.py:69
  4.8 2.3 %collective-permute-start.1 = (bf16[256,1024]{1,0:T(8,128)(2,1)S(1)}, bf16[256,1024]{1,0:T(8,128)(2,1)S(1)}, u32[]{:S(2)}, u32[]{:S(2)}) collective-permute-start(bf16[256,1024]{1,0:T(8,128)(2,1)S(1)} %get-tuple-element.21), channel_id=1, source_target_pairs={{0,130},{2,0},{128,2},{130,128},{1,131},{3,1},{129,3},{131,129},{4... | collective-permute-start | bytes 1572872 | tf_op jit(solution)/shard_map/ppermute | solution.py:23
  7.1 0.0 collective-permute-start.2
  7.1 0.0 collective-permute-start
  7.1 14.7 %all-to-all-start = ((bf16[64,32,128]{2,1,0:T(8,128)(2,1)}), bf16[64,32,128]{2,1,0:T(8,128)(2,1)S(1)}, u32[]{:S(2)}, u32[]{:S(2)}) async-start(bf16[64,32,128]{2,1,0:T(8,128)(2,1)} %get-tuple-element.18), calls=%async_computation | async-start | bytes 1048576 | tf_op jit(solution)/shard_map/all_to_all | solution.py:450
  21.9 0.7 dynamic_slice.13
  22.6 0.7 constant_dynamic-slice_fusion.2
  23.3 0.0 collective-permute-done.1.refs_2_
  23.3 0.2 collective-permute-start.3
  23.5 0.0 collective-permute-done.2.refs_3_
  23.5 0.3 collective-permute-start.4
  23.8 0.1 fusion
  23.9 0.1 rev.3
  23.9 0.8 constant_dynamic-slice_fusion
  24.7 0.1 reshape.18.scale_ref
  24.8 0.1 pad.4.taps_ref
  24.9 0.4 toeplitz.1.refs_9_
  25.3 0.0 copy-start.3
  25.3 0.8 copy-done.3
  26.1 0.1 pad_add_fusion.spot_ref
  26.1 0.0 copy-done
  26.1 0.0 collective-permute-done.3.refs_4_
  26.2 0.0 collective-permute-done.4.refs_5_
  26.2 0.0 collective-permute-done.refs_1_
  26.2 0.0 copy-start.6
  26.2 0.7 copy-done.6
  26.9 4.1 %normed_rows.1 = (bf16[4,512,1024]{2,1,0:T(8,128)(2,1)S(1)}, f32[8,128]{1,0:T(8,128)S(1)}) custom-call(s32[4]{0:T(128)S(1)} %pad_add_fusion.spot_ref, bf16[512,1024]{1,0:T(8,128)(2,1)} %refs_0_.1, bf16[512,1024]{1,0:T(8,128)(2,1)S(1)} %collective-permute-done.refs_1_, bf16[256,1024]{1,0:T(8,128)(2,1)S(1)} %collective-permute-done.1.refs_2_, ...), custom_call_target="tpu_custom_call" | custom-call | flops 10485760 | bytes 8388608 | tf_op jit(solution)/shard_map/normed_rows/pallas_call | solution.py:111
  31.0 0.0 copy-start.1
  31.0 1.9 %copy-done.1 = bf16[4,512,1024]{2,1,0:T(8,128)(2,1)} copy-done((bf16[4,512,1024]{2,1,0:T(8,128)(2,1)}, bf16[4,512,1024]{2,1,0:T(8,128)(2,1)S(1)}, u32[]{:S(2)}) %copy-start.1) | copy-done | bytes 4194328
  32.9 8.7 %all-to-all-done.pieces_ref = bf16[64,32,128]{2,1,0:T(8,128)(2,1)S(1)} async-done(((bf16[64,32,128]{2,1,0:T(8,128)(2,1)}), bf16[64,32,128]{2,1,0:T(8,128)(2,1)S(1)}, u32[]{:S(2)}, u32[]{:S(2)}) %all-to-all-start) | async-done | bytes 524320 | tf_op jit(solution)/shard_map/all_to_all | solution.py:450
  41.6 0.0 copy-start.2
  41.6 2.2 %copy-done.2 = bf16[4,512,1024]{2,1,0:T(8,128)(2,1)S(1)} copy-done((bf16[4,512,1024]{2,1,0:T(8,128)(2,1)S(1)}, bf16[4,512,1024]{2,1,0:T(8,128)(2,1)}, u32[]{:S(2)}) %copy-start.2) | copy-done | bytes 4194328
  43.8 2.0 %table_piece.1.refs_0_ = bf16[48,512]{1,0:T(8,128)(2,1)S(1)} custom-call(bf16[4,512,1024]{2,1,0:T(8,128)(2,1)S(1)} %copy-done.2, bf16[64,32,128]{2,1,0:T(8,128)(2,1)S(1)} %all-to-all-done.pieces_ref, f32[48,1]{1,0:T(8,128)S(1)} %reshape.18.scale_ref, f32[8,128]{1,0:T(8,128)S(1)} %get-tuple-element.28._), custom_call_target="tpu_custom_call" | custom-call | flops 201326592 | bytes 5000000 | tf_op jit(solution)/shard_map/table_piece/pallas_call | solution.py:167
  45.8 2.3 %collective-permute-start.5 = (bf16[48,512]{1,0:T(8,128)(2,1)S(1)}, bf16[48,512]{1,0:T(8,128)(2,1)S(1)}, u32[]{:S(2)}, u32[]{:S(2)}) collective-permute-start(bf16[48,512]{1,0:T(8,128)(2,1)S(1)} %table_piece.1.refs_0_), channel_id=1, source_target_pairs={{0,16},{16,32},{32,48},{48,64},{64,80},{80,96},{96,112},{112,0},{1... | collective-permute-start | bytes 147464 | tf_op jit(solution)/shard_map/ppermute | solution.py:23
  48.1 1.1 %collective-permute-start.9 = (bf16[48,512]{1,0:T(8,128)(2,1)S(1)}, bf16[48,512]{1,0:T(8,128)(2,1)S(1)}, u32[]{:S(2)}, u32[]{:S(2)}) collective-permute-start(bf16[48,512]{1,0:T(8,128)(2,1)S(1)} %table_piece.1.refs_0_), channel_id=1, source_target_pairs={{0,112},{16,0},{32,16},{48,32},{64,48},{80,64},{96,80},{112,96},{1... | collective-permute-start | bytes 147464 | tf_op jit(solution)/shard_map/ppermute | solution.py:23
  49.1 2.1 %collective-permute-done.5.refs_1_ = bf16[48,512]{1,0:T(8,128)(2,1)S(1)} collective-permute-done((bf16[48,512]{1,0:T(8,128)(2,1)S(1)}, bf16[48,512]{1,0:T(8,128)(2,1)S(1)}, u32[]{:S(2)}, u32[]{:S(2)}) %collective-permute-start.5) | collective-permute-done | bytes 49184 | tf_op jit(solution)/shard_map/ppermute | solution.py:23
  51.2 1.0 %collective-permute-start.6 = (bf16[48,512]{1,0:T(8,128)(2,1)S(1)}, bf16[48,512]{1,0:T(8,128)(2,1)S(1)}, u32[]{:S(2)}, u32[]{:S(2)}) collective-permute-start(bf16[48,512]{1,0:T(8,128)(2,1)S(1)} %collective-permute-done.5.refs_1_), channel_id=1, source_target_pairs={{0,16},{16,32},{32,48},{48,64},{64,80},{80,96},{96,112},{112,0},{1... | collective-permute-start | bytes 147464 | tf_op jit(solution)/shard_map/ppermute | solution.py:23
  52.2 0.0 collective-permute-done.9.refs_7_
  52.2 2.3 %collective-permute-start.10 = (bf16[48,512]{1,0:T(8,128)(2,1)S(1)}, bf16[48,512]{1,0:T(8,128)(2,1)S(1)}, u32[]{:S(2)}, u32[]{:S(2)}) collective-permute-start(bf16[48,512]{1,0:T(8,128)(2,1)S(1)} %collective-permute-done.9.refs_7_), channel_id=1, source_target_pairs={{0,112},{16,0},{32,16},{48,32},{64,48},{80,64},{96,80},{112,96},{1... | collective-permute-start | bytes 147464 | tf_op jit(solution)/shard_map/ppermute | solution.py:23
  54.4 2.1 %collective-permute-done.6.refs_2_ = bf16[48,512]{1,0:T(8,128)(2,1)S(1)} collective-permute-done((bf16[48,512]{1,0:T(8,128)(2,1)S(1)}, bf16[48,512]{1,0:T(8,128)(2,1)S(1)}, u32[]{:S(2)}, u32[]{:S(2)}) %collective-permute-start.6) | collective-permute-done | bytes 49184 | tf_op jit(solution)/shard_map/ppermute | solution.py:23
  56.5 0.3 collective-permute-start.7
  56.8 0.0 collective-permute-done.10.refs_6_
  56.8 3.2 %collective-permute-start.11 = (bf16[48,512]{1,0:T(8,128)(2,1)S(1)}, bf16[48,512]{1,0:T(8,128)(2,1)S(1)}, u32[]{:S(2)}, u32[]{:S(2)}) collective-permute-start(bf16[48,512]{1,0:T(8,128)(2,1)S(1)} %collective-permute-done.10.refs_6_), channel_id=1, source_target_pairs={{0,112},{16,0},{32,16},{48,32},{64,48},{80,64},{96,80},{112,96},{1... | collective-permute-start | bytes 147464 | tf_op jit(solution)/shard_map/ppermute | solution.py:23
  60.0 1.8 %collective-permute-done.7.refs_3_ = bf16[48,512]{1,0:T(8,128)(2,1)S(1)} collective-permute-done((bf16[48,512]{1,0:T(8,128)(2,1)S(1)}, bf16[48,512]{1,0:T(8,128)(2,1)S(1)}, u32[]{:S(2)}, u32[]{:S(2)}) %collective-permute-start.7) | collective-permute-done | bytes 49184 | tf_op jit(solution)/shard_map/ppermute | solution.py:23
  61.8 0.0 collective-permute-start.8
  61.8 1.8 %hot_rows.1 = (bf16[8,512,512]{2,1,0:T(8,128)(2,1)S(1)}, bf16[288,512]{1,0:T(8,128)(2,1)S(1)}) custom-call(s32[1]{0:T(128)} %bitcast.spot_ref, bf16[64,32,128]{2,1,0:T(8,128)(2,1)S(1)} %all-to-all-done.pieces_ref), custom_call_target="tpu_custom_call" | custom-call | flops 5000000 | bytes 4500000 | tf_op jit(solution)/shard_map/hot_rows/pallas_call | solution.py:245
  63.6 0.0 collective-permute-done.11.refs_5_
  63.6 3.5 %collective-permute-done.8.refs_4_ = bf16[48,512]{1,0:T(8,128)(2,1)S(1)} collective-permute-done((bf16[48,512]{1,0:T(8,128)(2,1)S(1)}, bf16[48,512]{1,0:T(8,128)(2,1)S(1)}, u32[]{:S(2)}, u32[]{:S(2)}) %collective-permute-start.8) | collective-permute-done | bytes 49184 | tf_op jit(solution)/shard_map/ppermute | solution.py:23
  67.1 0.0 copy-start.4
  67.1 1.0 %copy-done.4 = bf16[8,256,128]{2,1,0:T(8,128)(2,1)S(1)} copy-done((bf16[8,256,128]{2,1,0:T(8,128)(2,1)S(1)}, bf16[8,256,128]{2,1,0:T(8,128)(2,1)}, u32[]{:S(2)}) %copy-start.4) | copy-done | bytes 524312
  68.2 9.9 %mixed_blocks.1 = bf16[8,512,128]{2,1,0:T(8,128)(2,1)S(1)} custom-call(s32[1]{0:T(128)} %bitcast.spot_ref, bf16[8,512,512]{2,1,0:T(8,128)(2,1)S(1)} %get-tuple-element.25.hot_ref, bf16[288,512]{1,0:T(8,128)(2,1)S(1)} %get-tuple-element.26.lead_hot_ref, bf16[48,512]{1,0:T(8,128)(2,1)S(1)} %table_piece.1.refs_0_, ...), custom_call_target="tpu_custom_call" | custom-call | flops 5000000000 | bytes 6000000 | tf_op jit(solution)/shard_map/mixed_blocks/pallas_call | solution.py:373
  78.0 17.3 %all_to_all.10.blocks_ref = bf16[8,512,128]{2,1,0:T(8,128)(2,1)S(1)} all-to-all(bf16[8,512,128]{2,1,0:T(8,128)(2,1)S(1)} %mixed_blocks.1), channel_id=1, replica_groups=mesh['yh'=2,'z'=8,'x'=4,'yl'=2,'core'=2] {'yh','x'}, dimensions={0} | all-to-all | bytes 2097152 | tf_op jit(solution)/shard_map/all_to_all | solution.py:484
  95.4 1.0 %placed_columns.1 = bf16[512,1024]{1,0:T(8,128)(2,1)} custom-call(bf16[8,512,128]{2,1,0:T(8,128)(2,1)S(1)} %all_to_all.10.blocks_ref), custom_call_target="tpu_custom_call" | custom-call | bytes 2000000 | tf_op jit(solution)/shard_map/placed_columns/pallas_call | solution.py:420
  (2 shorter events, 0.0 us)
Async XLA Ops:
  0.0 26.1 %copy-start = (f32[3,7,1024]{2,1,0:T(8,128)S(1)}, f32[3,7,1024]{2,1,0:T(8,128)}, u32[]{:S(2)}) copy-start(f32[3,7,1024]{2,1,0:T(8,128)} %param.13) | copy-start | bytes 258052
  0.0 1.0 %copy-start.5 = (bf16[3,64,1024]{2,1,0:T(8,128)(2,1)S(1)}, bf16[3,64,1024]{2,1,0:T(8,128)(2,1)}, u32[]{:S(2)}) copy-start(bf16[3,64,1024]{2,1,0:T(8,128)(2,1)} %weight_ref.1) | copy-start | bytes 1179652
  1.0 0.7 copy-start.7
  4.8 18.4 %collective-permute-start.1 = (bf16[256,1024]{1,0:T(8,128)(2,1)S(1)}, bf16[256,1024]{1,0:T(8,128)(2,1)S(1)}, u32[]{:S(2)}, u32[]{:S(2)}) collective-permute-start(bf16[256,1024]{1,0:T(8,128)(2,1)S(1)} %get-tuple-element.21), channel_id=1, source_target_pairs={{0,130},{2,0},{128,2},{130,128},{1,131},{3,1},{129,3},{131,129},{4... | collective-permute-start | bytes 1572872 | tf_op jit(solution)/shard_map/ppermute | solution.py:23
  7.1 16.4 %collective-permute-start.2 = (bf16[256,1024]{1,0:T(8,128)(2,1)}, bf16[256,1024]{1,0:T(8,128)(2,1)S(1)}, u32[]{:S(2)}, u32[]{:S(2)}) collective-permute-start(bf16[256,1024]{1,0:T(8,128)(2,1)} %get-tuple-element.22), channel_id=1, source_target_pairs={{0,2},{2,128},{128,130},{130,0},{1,3},{3,129},{129,131},{131,1},{4... | collective-permute-start | bytes 1572872 | tf_op jit(solution)/shard_map/ppermute | solution.py:23
  7.1 19.1 %collective-permute-start = (bf16[512,1024]{1,0:T(8,128)(2,1)}, bf16[512,1024]{1,0:T(8,128)(2,1)S(1)}, u32[]{:S(2)}, u32[]{:S(2)}) collective-permute-start(bf16[512,1024]{1,0:T(8,128)(2,1)} %refs_0_.1), channel_id=1, source_target_pairs={{0,1},{1,0},{2,3},{3,2},{4,5},{5,4},{6,7},{7,6},{8,9},{9,8},{10,11... | collective-permute-start | bytes 3145736 | tf_op jit(solution)/shard_map/ppermute | solution.py:23
  7.1 34.5 %all-to-all-start = ((bf16[64,32,128]{2,1,0:T(8,128)(2,1)}), bf16[64,32,128]{2,1,0:T(8,128)(2,1)S(1)}, u32[]{:S(2)}, u32[]{:S(2)}) async-start(bf16[64,32,128]{2,1,0:T(8,128)(2,1)} %get-tuple-element.18), calls=%async_computation | async-start | bytes 1048576 | tf_op jit(solution)/shard_map/all_to_all | solution.py:450
  23.3 2.9 %collective-permute-start.3 = (bf16[256,1024]{1,0:T(8,128)(2,1)S(1)}, bf16[256,1024]{1,0:T(8,128)(2,1)S(1)}, u32[]{:S(2)}, u32[]{:S(2)}) collective-permute-start(bf16[256,1024]{1,0:T(8,128)(2,1)S(1)} %collective-permute-done.1.refs_2_), channel_id=1, source_target_pairs={{0,1},{1,0},{2,3},{3,2},{4,5},{5,4},{6,7},{7,6},{8,9},{9,8},{10,11... | collective-permute-start | bytes 1572872 | tf_op jit(solution)/shard_map/ppermute | solution.py:23
  23.5 2.6 %collective-permute-start.4 = (bf16[256,1024]{1,0:T(8,128)(2,1)S(1)}, bf16[256,1024]{1,0:T(8,128)(2,1)}, u32[]{:S(2)}, u32[]{:S(2)}) collective-permute-start(bf16[256,1024]{1,0:T(8,128)(2,1)S(1)} %collective-permute-done.2.refs_3_), channel_id=1, source_target_pairs={{0,1},{1,0},{2,3},{3,2},{4,5},{5,4},{6,7},{7,6},{8,9},{9,8},{10,11... | collective-permute-start | bytes 1572872 | tf_op jit(solution)/shard_map/ppermute | solution.py:23
  25.3 0.8 copy-start.3
  26.2 0.7 copy-start.6
  31.0 1.9 %copy-start.1 = (bf16[4,512,1024]{2,1,0:T(8,128)(2,1)}, bf16[4,512,1024]{2,1,0:T(8,128)(2,1)S(1)}, u32[]{:S(2)}) copy-start(bf16[4,512,1024]{2,1,0:T(8,128)(2,1)S(1)} %get-tuple-element.27.far_ref) | copy-start | bytes 12582916
  41.6 2.2 %copy-start.2 = (bf16[4,512,1024]{2,1,0:T(8,128)(2,1)S(1)}, bf16[4,512,1024]{2,1,0:T(8,128)(2,1)}, u32[]{:S(2)}) copy-start(bf16[4,512,1024]{2,1,0:T(8,128)(2,1)} %copy-done.1) | copy-start | bytes 12582916
  45.8 5.4 %collective-permute-start.5 = (bf16[48,512]{1,0:T(8,128)(2,1)S(1)}, bf16[48,512]{1,0:T(8,128)(2,1)S(1)}, u32[]{:S(2)}, u32[]{:S(2)}) collective-permute-start(bf16[48,512]{1,0:T(8,128)(2,1)S(1)} %table_piece.1.refs_0_), channel_id=1, source_target_pairs={{0,16},{16,32},{32,48},{48,64},{64,80},{80,96},{96,112},{112,0},{1... | collective-permute-start | bytes 147464 | tf_op jit(solution)/shard_map/ppermute | solution.py:23
  48.1 4.1 %collective-permute-start.9 = (bf16[48,512]{1,0:T(8,128)(2,1)S(1)}, bf16[48,512]{1,0:T(8,128)(2,1)S(1)}, u32[]{:S(2)}, u32[]{:S(2)}) collective-permute-start(bf16[48,512]{1,0:T(8,128)(2,1)S(1)} %table_piece.1.refs_0_), channel_id=1, source_target_pairs={{0,112},{16,0},{32,16},{48,32},{64,48},{80,64},{96,80},{112,96},{1... | collective-permute-start | bytes 147464 | tf_op jit(solution)/shard_map/ppermute | solution.py:23
  51.2 5.3 %collective-permute-start.6 = (bf16[48,512]{1,0:T(8,128)(2,1)S(1)}, bf16[48,512]{1,0:T(8,128)(2,1)S(1)}, u32[]{:S(2)}, u32[]{:S(2)}) collective-permute-start(bf16[48,512]{1,0:T(8,128)(2,1)S(1)} %collective-permute-done.5.refs_1_), channel_id=1, source_target_pairs={{0,16},{16,32},{32,48},{48,64},{64,80},{80,96},{96,112},{112,0},{1... | collective-permute-start | bytes 147464 | tf_op jit(solution)/shard_map/ppermute | solution.py:23
  52.2 4.6 %collective-permute-start.10 = (bf16[48,512]{1,0:T(8,128)(2,1)S(1)}, bf16[48,512]{1,0:T(8,128)(2,1)S(1)}, u32[]{:S(2)}, u32[]{:S(2)}) collective-permute-start(bf16[48,512]{1,0:T(8,128)(2,1)S(1)} %collective-permute-done.9.refs_7_), channel_id=1, source_target_pairs={{0,112},{16,0},{32,16},{48,32},{64,48},{80,64},{96,80},{112,96},{1... | collective-permute-start | bytes 147464 | tf_op jit(solution)/shard_map/ppermute | solution.py:23
  56.5 5.3 %collective-permute-start.7 = (bf16[48,512]{1,0:T(8,128)(2,1)S(1)}, bf16[48,512]{1,0:T(8,128)(2,1)S(1)}, u32[]{:S(2)}, u32[]{:S(2)}) collective-permute-start(bf16[48,512]{1,0:T(8,128)(2,1)S(1)} %collective-permute-done.6.refs_2_), channel_id=1, source_target_pairs={{0,16},{16,32},{32,48},{48,64},{64,80},{80,96},{96,112},{112,0},{1... | collective-permute-start | bytes 147464 | tf_op jit(solution)/shard_map/ppermute | solution.py:23
  56.8 6.8 %collective-permute-start.11 = (bf16[48,512]{1,0:T(8,128)(2,1)S(1)}, bf16[48,512]{1,0:T(8,128)(2,1)S(1)}, u32[]{:S(2)}, u32[]{:S(2)}) collective-permute-start(bf16[48,512]{1,0:T(8,128)(2,1)S(1)} %collective-permute-done.10.refs_6_), channel_id=1, source_target_pairs={{0,112},{16,0},{32,16},{48,32},{64,48},{80,64},{96,80},{112,96},{1... | collective-permute-start | bytes 147464 | tf_op jit(solution)/shard_map/ppermute | solution.py:23
  61.8 5.3 %collective-permute-start.8 = (bf16[48,512]{1,0:T(8,128)(2,1)S(1)}, bf16[48,512]{1,0:T(8,128)(2,1)S(1)}, u32[]{:S(2)}, u32[]{:S(2)}) collective-permute-start(bf16[48,512]{1,0:T(8,128)(2,1)S(1)} %collective-permute-done.7.refs_3_), channel_id=1, source_target_pairs={{0,16},{16,32},{32,48},{48,64},{64,80},{80,96},{96,112},{112,0},{1... | collective-permute-start | bytes 147464 | tf_op jit(solution)/shard_map/ppermute | solution.py:23
  67.1 1.0 %copy-start.4 = (bf16[8,256,128]{2,1,0:T(8,128)(2,1)S(1)}, bf16[8,256,128]{2,1,0:T(8,128)(2,1)}, u32[]{:S(2)}) copy-start(bf16[8,256,128]{2,1,0:T(8,128)(2,1)} %copy-done.3) | copy-start | bytes 1572868

commit v7 on v6

--- a/solution.py
+++ b/solution.py
@@ -23,14 +23,26 @@
     return lax.ppermute(value, axis, pairs)
 
 
-def payload_kernel(weight_ref, ids_ref, table_ref, out_ref, upper_ref, lower_ref, sems):
+def payload_kernel(
+    far_weight_ref, far_ids_ref, table_ref, out_ref, upper_ref, lower_ref, weight_ref, ids_ref, sems
+):
     half = upper_ref.shape[0]
+    moves = [
+        (far_weight_ref.at[0], weight_ref.at[0]),
+        (far_weight_ref.at[1], weight_ref.at[1]),
+        (far_weight_ref.at[2], weight_ref.at[2]),
+        (far_ids_ref, ids_ref),
+        (table_ref.at[pl.ds(0, half), :], upper_ref),
+        (table_ref.at[pl.ds(half, half), :], lower_ref),
+    ]
     copies = [
-        pltpu.make_async_copy(table_ref.at[pl.ds(0, half), :], upper_ref, sems.at[0]),
-        pltpu.make_async_copy(table_ref.at[pl.ds(half, half), :], lower_ref, sems.at[1]),
+        pltpu.make_async_copy(source, target, sems.at[j])
+        for j, (source, target) in enumerate(moves)
     ]
     for copy in copies:
         copy.start()
+    for copy in copies[:4]:
+        copy.wait()
     streams, rows, width = weight_ref.shape
     tiles = width // LANES
     columns = out_ref.shape[0] // tiles
@@ -51,7 +63,7 @@
             out_ref[to, GROUP:, :] = jnp.concatenate([third[at : at + 8], coded], axis=0).astype(
                 BF
             )
-    for copy in copies:
+    for copy in copies[4:]:
         copy.wait()
 
 
@@ -69,11 +81,14 @@
     return pl.pallas_call(
         payload_kernel,
         out_shape=(jax.ShapeDtypeStruct((parts, 2 * GROUP, LANES), BF), half, half),
-        in_specs=in_vmem(3),
-        out_specs=(pl.BlockSpec(memory_space=pltpu.VMEM),)
-        + (pl.BlockSpec(memory_space=pl.ANY),) * 2,
-        scratch_shapes=[pltpu.SemaphoreType.DMA((2,))],
-        compiler_params=pltpu.CompilerParams(vmem_limit_bytes=GRANT),
+        in_specs=[pl.BlockSpec(memory_space=pl.ANY)] * 3,
+        out_specs=tuple(in_vmem(3)),
+        scratch_shapes=[
+            pltpu.VMEM(in_weight.shape, BF),
+            pltpu.VMEM(ids_rows.shape, jnp.int32),
+            pltpu.SemaphoreType.DMA((6,)),
+        ],
+        compiler_params=pltpu.CompilerParams(vmem_limit_bytes=66800000),
         cost_estimate=cost(0, 2900000),
         name="payload",
     )(in_weight, ids_rows, embed_table)
@@ -167,7 +182,7 @@
     return pl.pallas_call(
         table_kernel,
         out_shape=jax.ShapeDtypeStruct((rows, vocab), BF),
-        in_specs=[pl.BlockSpec(memory_space=pltpu.HBM)] + in_vmem(3),
+        in_specs=[pl.BlockSpec(memory_space=pl.ANY)] + in_vmem(3),
         out_specs=pl.BlockSpec(memory_space=pltpu.VMEM),
         scratch_shapes=[
             pltpu.VMEM((rows, quarters * width), BF),
@@ -446,7 +461,6 @@
     load, upper, lower = payload(in_weight, ids.reshape(-1, LANES), embed_table, tiles * z_count)
     got_up = shifted(upper, ("yh", "yl"), -1)
     got_down = shifted(lower, ("yh", "yl"), 1)
-    got_core = shifted(embed_table, "core", 1)
     pieces = lax.all_to_all(load, ctx, 0, 0, tiled=True)
 
     groups = LANES // GROUP
@@ -460,6 +474,8 @@
     scale = lax.dynamic_slice_in_dim(in_scale, tile * LANES + z * GROUP, GROUP, 1)
     scale = scale.reshape(STREAMS * GROUP, 1)
 
+    swapped, near_filter = lax.optimization_barrier((embed_table, near_filter))
+    got_core = shifted(swapped, "core", 1)
     far_up = shifted(got_up, "core", 1)
     far_down = shifted(got_down, "core", 1)
     mine = yl * 2 + core
@@ -470,6 +486,7 @@
     pieces, toep, near_filter, token = lax.optimization_barrier(
         (pieces, toep, near_filter, token)
     )
+    normed = pltpu.with_memory_space_constraint(normed, pltpu.HBM)
     piece = table_piece(normed, pieces, scale, token)
     ups, downs, last = [piece], [], piece
     for step in range(4):

time: 96.9 us -> 92.4 us (0.954)
  local copies, waits for them, and re-layouts: 10.8 us -> 7.09 us
    unnamed x16 -> x12, local copies, waits for them, and re-layouts: 8.39 us -> 4.68 us
    pallas_call x1, Pallas kernels: 1.97 us -> 3.07 us  [table_piece(): pl.pallas_call(table_kernel, out_shape=jax.ShapeDtypeStruct((rows, vocab)...]
  transfers between devices with their start and end apart: 13 -> 13, of which waited for: 5 -> 6; matrix products, arithmetic and copies ran while one was open for 3% -> 3% of each run, Pallas kernels for 6% -> 6%
where the time goes in v7:
time: 92.4 us; the launch traced here: 92 us
  starting transfers between devices  27.4 us (30%)
  Pallas kernels  22.5 us (24%)
  waiting for transfers between devices  17.5 us (19%)
  blocking collectives  17.3 us (19%)
  local copies, waits for them, and re-layouts  7.09 us (8%)
    all_to_all x1, blocking collectives, per_device(): result = lax.all_to_all(blocks, ('yh', 'x'), 0, 0, tiled=True)  17.3 us
    all_to_all x1, starting transfers between devices, per_device(): pieces = lax.all_to_all(load, ctx, 0, 0, tiled=True)  14.6 us
    ppermute x12, starting transfers between devices, shifted(): return lax.ppermute(value, axis, pairs)  12.7 us
    pallas_call x1, Pallas kernels, mixed_blocks(): pl.pallas_call(mix_kernel, out_shape=jax.ShapeDtypeStruct((blocks, tokens...  9.79 us
    ppermute x12, waiting for transfers between devices, shifted(): return lax.ppermute(value, axis, pairs)  9.67 us
    all_to_all x1, waiting for transfers between devices, per_device(): pieces = lax.all_to_all(load, ctx, 0, 0, tiled=True)  7.78 us
    unnamed x12, local copies, waits for them, and re-layouts  4.68 us
    pallas_call x1, Pallas kernels, normed_rows(): pl.pallas_call(norm_kernel, out_shape=(jax.ShapeDtypeStruct((4, vocab, wi...  3.78 us
  transfers between devices with their start and end apart: 13, of which 6 were waited for; matrix products, arithmetic and copies ran while one was open for 3% of the time, Pallas kernels for 6%

profile of v7, /device:TPU:8, one launch (start us, length us, event | category | flops | bytes accessed | tf_op | source)
XLA Modules:
  0.0 92.0 jit_solution(1149187906219659399)
XLA Ops:
  0.0 0.0 copy-start
  0.0 2.7 %payload.1 = (bf16[64,32,128]{2,1,0:T(8,128)(2,1)}, bf16[256,1024]{1,0:T(8,128)(2,1)}, bf16[256,1024]{1,0:T(8,128)(2,1)}) custom-call(bf16[3,64,1024]{2,1,0:T(8,128)(2,1)} %far_weight_ref.1, s32[4,128]{1,0:T(4,128)} %bitcast.10, bf16[512,1024]{1,0:T(8,128)(2,1)} %refs_0_.1), custom_call_target="tpu_custom_call" | custom-call | bytes 2900000 | tf_op jit(solution)/shard_map/payload/pallas_call | solution.py:81
  2.7 2.3 %collective-permute-start.1 = (bf16[256,1024]{1,0:T(8,128)(2,1)}, bf16[256,1024]{1,0:T(8,128)(2,1)S(1)}, u32[]{:S(2)}, u32[]{:S(2)}) collective-permute-start(bf16[256,1024]{1,0:T(8,128)(2,1)} %get-tuple-element.25), channel_id=1, source_target_pairs={{0,130},{2,0},{128,2},{130,128},{1,131},{3,1},{129,3},{131,129},{4... | collective-permute-start | bytes 1572872 | tf_op jit(solution)/shard_map/ppermute | solution.py:23
  5.0 0.0 collective-permute-start.2
  5.0 0.0 copy-done
  5.0 0.1 collective-permute-start
  5.1 14.6 %all-to-all-start = ((bf16[64,32,128]{2,1,0:T(8,128)(2,1)}), bf16[64,32,128]{2,1,0:T(8,128)(2,1)S(1)}, u32[]{:S(2)}, u32[]{:S(2)}) async-start(bf16[64,32,128]{2,1,0:T(8,128)(2,1)} %get-tuple-element.20), calls=%async_computation | async-start | bytes 1048576 | tf_op jit(solution)/shard_map/all_to_all | solution.py:464
  19.7 0.7 dynamic_slice.13
  20.4 0.0 collective-permute-done.1.refs_2_
  20.4 0.2 collective-permute-start.3
  20.7 0.0 collective-permute-done.2.refs_3_
  20.7 0.3 collective-permute-start.4
  21.0 0.7 constant_dynamic-slice_fusion.2
  21.7 0.1 fusion
  21.7 0.1 rev.3
  21.8 0.8 constant_dynamic-slice_fusion
  22.6 0.1 reshape.18.scale_ref
  22.7 0.1 pad.4.taps_ref
  22.7 0.4 toeplitz.1.refs_9_
  23.1 0.0 copy-start.3
  23.1 0.8 copy-done.3
  23.9 0.1 pad_add_fusion.spot_ref
  24.0 0.0 collective-permute-done.refs_1_
  24.0 0.0 collective-permute-done.3.refs_4_
  24.0 0.0 collective-permute-done.4.refs_5_
  24.0 0.0 copy-start.1
  24.0 1.2 %copy-done.1 = bf16[512,1024]{1,0:T(8,128)(2,1)S(1)} copy-done((bf16[512,1024]{1,0:T(8,128)(2,1)S(1)}, bf16[512,1024]{1,0:T(8,128)(2,1)}, u32[]{:S(2)}) %copy-start.1) | copy-done | bytes 1048600
  25.3 0.0 copy-start.5
  25.3 0.7 copy-done.5
  26.0 3.8 %normed_rows.1 = (bf16[4,512,1024]{2,1,0:T(8,128)(2,1)S(1)}, f32[8,128]{1,0:T(8,128)S(1)}) custom-call(s32[4]{0:T(128)S(1)} %pad_add_fusion.spot_ref, bf16[512,1024]{1,0:T(8,128)(2,1)S(1)} %copy-done.1, bf16[512,1024]{1,0:T(8,128)(2,1)S(1)} %collective-permute-done.refs_1_, bf16[256,1024]{1,0:T(8,128)(2,1)S(1)} %collective-permute-done.1.refs_2_, ...), custom_call_target="tpu_custom_call" | custom-call | flops 10485760 | bytes 8388608 | tf_op jit(solution)/shard_map/normed_rows/pallas_call | solution.py:126
  29.8 0.0 copy-start.2
  29.8 1.9 %copy-done.2 = bf16[4,512,1024]{2,1,0:T(8,128)(2,1)} copy-done((bf16[4,512,1024]{2,1,0:T(8,128)(2,1)}, bf16[4,512,1024]{2,1,0:T(8,128)(2,1)S(1)}, u32[]{:S(2)}) %copy-start.2) | copy-done | bytes 4194328
  31.7 0.0 copy-start.4
  31.7 7.8 %all-to-all-done.pieces_ref = bf16[64,32,128]{2,1,0:T(8,128)(2,1)S(1)} async-done(((bf16[64,32,128]{2,1,0:T(8,128)(2,1)}), bf16[64,32,128]{2,1,0:T(8,128)(2,1)S(1)}, u32[]{:S(2)}, u32[]{:S(2)}) %all-to-all-start) | async-done | bytes 524320 | tf_op jit(solution)/shard_map/all_to_all | solution.py:464
  39.5 3.1 %table_piece.1.refs_0_ = bf16[48,512]{1,0:T(8,128)(2,1)S(1)} custom-call(bf16[4,512,1024]{2,1,0:T(8,128)(2,1)} %copy-done.2, bf16[64,32,128]{2,1,0:T(8,128)(2,1)S(1)} %all-to-all-done.pieces_ref, f32[48,1]{1,0:T(8,128)S(1)} %reshape.18.scale_ref, f32[8,128]{1,0:T(8,128)S(1)} %get-tuple-element.32._), custom_call_target="tpu_custom_call" | custom-call | flops 201326592 | bytes 5000000 | tf_op jit(solution)/shard_map/table_piece/pallas_call | solution.py:182
  42.6 2.3 %collective-permute-start.5 = (bf16[48,512]{1,0:T(8,128)(2,1)S(1)}, bf16[48,512]{1,0:T(8,128)(2,1)S(1)}, u32[]{:S(2)}, u32[]{:S(2)}) collective-permute-start(bf16[48,512]{1,0:T(8,128)(2,1)S(1)} %table_piece.1.refs_0_), channel_id=1, source_target_pairs={{0,16},{16,32},{32,48},{48,64},{64,80},{80,96},{96,112},{112,0},{1... | collective-permute-start | bytes 147464 | tf_op jit(solution)/shard_map/ppermute | solution.py:23
  44.9 1.0 %collective-permute-start.9 = (bf16[48,512]{1,0:T(8,128)(2,1)S(1)}, bf16[48,512]{1,0:T(8,128)(2,1)S(1)}, u32[]{:S(2)}, u32[]{:S(2)}) collective-permute-start(bf16[48,512]{1,0:T(8,128)(2,1)S(1)} %table_piece.1.refs_0_), channel_id=1, source_target_pairs={{0,112},{16,0},{32,16},{48,32},{64,48},{80,64},{96,80},{112,96},{1... | collective-permute-start | bytes 147464 | tf_op jit(solution)/shard_map/ppermute | solution.py:23
  45.9 2.1 %collective-permute-done.5.refs_1_ = bf16[48,512]{1,0:T(8,128)(2,1)S(1)} collective-permute-done((bf16[48,512]{1,0:T(8,128)(2,1)S(1)}, bf16[48,512]{1,0:T(8,128)(2,1)S(1)}, u32[]{:S(2)}, u32[]{:S(2)}) %collective-permute-start.5) | collective-permute-done | bytes 49184 | tf_op jit(solution)/shard_map/ppermute | solution.py:23
  48.0 1.2 %collective-permute-start.6 = (bf16[48,512]{1,0:T(8,128)(2,1)S(1)}, bf16[48,512]{1,0:T(8,128)(2,1)S(1)}, u32[]{:S(2)}, u32[]{:S(2)}) collective-permute-start(bf16[48,512]{1,0:T(8,128)(2,1)S(1)} %collective-permute-done.5.refs_1_), channel_id=1, source_target_pairs={{0,16},{16,32},{32,48},{48,64},{64,80},{80,96},{96,112},{112,0},{1... | collective-permute-start | bytes 147464 | tf_op jit(solution)/shard_map/ppermute | solution.py:23
  49.1 0.2 collective-permute-done.9.refs_7_
  49.3 1.9 %collective-permute-start.10 = (bf16[48,512]{1,0:T(8,128)(2,1)S(1)}, bf16[48,512]{1,0:T(8,128)(2,1)S(1)}, u32[]{:S(2)}, u32[]{:S(2)}) collective-permute-start(bf16[48,512]{1,0:T(8,128)(2,1)S(1)} %collective-permute-done.9.refs_7_), channel_id=1, source_target_pairs={{0,112},{16,0},{32,16},{48,32},{64,48},{80,64},{96,80},{112,96},{1... | collective-permute-start | bytes 147464 | tf_op jit(solution)/shard_map/ppermute | solution.py:23
  51.2 2.1 %collective-permute-done.6.refs_2_ = bf16[48,512]{1,0:T(8,128)(2,1)S(1)} collective-permute-done((bf16[48,512]{1,0:T(8,128)(2,1)S(1)}, bf16[48,512]{1,0:T(8,128)(2,1)S(1)}, u32[]{:S(2)}, u32[]{:S(2)}) %collective-permute-start.6) | collective-permute-done | bytes 49184 | tf_op jit(solution)/shard_map/ppermute | solution.py:23
  53.3 0.2 collective-permute-start.7
  53.5 0.0 collective-permute-done.10.refs_6_
  53.5 3.3 %collective-permute-start.11 = (bf16[48,512]{1,0:T(8,128)(2,1)S(1)}, bf16[48,512]{1,0:T(8,128)(2,1)S(1)}, u32[]{:S(2)}, u32[]{:S(2)}) collective-permute-start(bf16[48,512]{1,0:T(8,128)(2,1)S(1)} %collective-permute-done.10.refs_6_), channel_id=1, source_target_pairs={{0,112},{16,0},{32,16},{48,32},{64,48},{80,64},{96,80},{112,96},{1... | collective-permute-start | bytes 147464 | tf_op jit(solution)/shard_map/ppermute | solution.py:23
  56.8 1.8 %collective-permute-done.7.refs_3_ = bf16[48,512]{1,0:T(8,128)(2,1)S(1)} collective-permute-done((bf16[48,512]{1,0:T(8,128)(2,1)S(1)}, bf16[48,512]{1,0:T(8,128)(2,1)S(1)}, u32[]{:S(2)}, u32[]{:S(2)}) %collective-permute-start.7) | collective-permute-done | bytes 49184 | tf_op jit(solution)/shard_map/ppermute | solution.py:23
  58.6 0.0 collective-permute-start.8
  58.6 1.8 %hot_rows.1 = (bf16[8,512,512]{2,1,0:T(8,128)(2,1)S(1)}, bf16[288,512]{1,0:T(8,128)(2,1)S(1)}) custom-call(s32[1]{0:T(128)} %bitcast.spot_ref, bf16[64,32,128]{2,1,0:T(8,128)(2,1)S(1)} %all-to-all-done.pieces_ref), custom_call_target="tpu_custom_call" | custom-call | flops 5000000 | bytes 4500000 | tf_op jit(solution)/shard_map/hot_rows/pallas_call | solution.py:260
  60.3 0.0 collective-permute-done.11.refs_5_
  60.4 3.5 %collective-permute-done.8.refs_4_ = bf16[48,512]{1,0:T(8,128)(2,1)S(1)} collective-permute-done((bf16[48,512]{1,0:T(8,128)(2,1)S(1)}, bf16[48,512]{1,0:T(8,128)(2,1)S(1)}, u32[]{:S(2)}, u32[]{:S(2)}) %collective-permute-start.8) | collective-permute-done | bytes 49184 | tf_op jit(solution)/shard_map/ppermute | solution.py:23
  63.9 0.0 copy-done.4
  63.9 9.8 %mixed_blocks.1 = bf16[8,512,128]{2,1,0:T(8,128)(2,1)S(1)} custom-call(s32[1]{0:T(128)} %bitcast.spot_ref, bf16[8,512,512]{2,1,0:T(8,128)(2,1)S(1)} %get-tuple-element.29.hot_ref, bf16[288,512]{1,0:T(8,128)(2,1)S(1)} %get-tuple-element.30.lead_hot_ref, bf16[48,512]{1,0:T(8,128)(2,1)S(1)} %table_piece.1.refs_0_, ...), custom_call_target="tpu_custom_call" | custom-call | flops 5000000000 | bytes 6000000 | tf_op jit(solution)/shard_map/mixed_blocks/pallas_call | solution.py:388
  73.7 17.3 %all_to_all.10.blocks_ref = bf16[8,512,128]{2,1,0:T(8,128)(2,1)S(1)} all-to-all(bf16[8,512,128]{2,1,0:T(8,128)(2,1)S(1)} %mixed_blocks.1), channel_id=1, replica_groups=mesh['yh'=2,'z'=8,'x'=4,'yl'=2,'core'=2] {'yh','x'}, dimensions={0} | all-to-all | bytes 2097152 | tf_op jit(solution)/shard_map/all_to_all | solution.py:501
  91.0 1.0 %placed_columns.1 = bf16[512,1024]{1,0:T(8,128)(2,1)} custom-call(bf16[8,512,128]{2,1,0:T(8,128)(2,1)S(1)} %all_to_all.10.blocks_ref), custom_call_target="tpu_custom_call" | custom-call | bytes 2000000 | tf_op jit(solution)/shard_map/placed_columns/pallas_call | solution.py:435
  (2 shorter events, 0.0 us)
Async XLA Ops:
  0.0 5.0 %copy-start = (f32[3,7,1024]{2,1,0:T(8,128)S(1)}, f32[3,7,1024]{2,1,0:T(8,128)}, u32[]{:S(2)}) copy-start(f32[3,7,1024]{2,1,0:T(8,128)} %param.13) | copy-start | bytes 258052
  2.7 17.8 %collective-permute-start.1 = (bf16[256,1024]{1,0:T(8,128)(2,1)}, bf16[256,1024]{1,0:T(8,128)(2,1)S(1)}, u32[]{:S(2)}, u32[]{:S(2)}) collective-permute-start(bf16[256,1024]{1,0:T(8,128)(2,1)} %get-tuple-element.25), channel_id=1, source_target_pairs={{0,130},{2,0},{128,2},{130,128},{1,131},{3,1},{129,3},{131,129},{4... | collective-permute-start | bytes 1572872 | tf_op jit(solution)/shard_map/ppermute | solution.py:23
  5.0 15.7 %collective-permute-start.2 = (bf16[256,1024]{1,0:T(8,128)(2,1)}, bf16[256,1024]{1,0:T(8,128)(2,1)S(1)}, u32[]{:S(2)}, u32[]{:S(2)}) collective-permute-start(bf16[256,1024]{1,0:T(8,128)(2,1)} %get-tuple-element.26), channel_id=1, source_target_pairs={{0,2},{2,128},{128,130},{130,0},{1,3},{3,129},{129,131},{131,1},{4... | collective-permute-start | bytes 1572872 | tf_op jit(solution)/shard_map/ppermute | solution.py:23
  5.0 19.1 %collective-permute-start = (bf16[512,1024]{1,0:T(8,128)(2,1)}, bf16[512,1024]{1,0:T(8,128)(2,1)S(1)}, u32[]{:S(2)}, u32[]{:S(2)}) collective-permute-start(bf16[512,1024]{1,0:T(8,128)(2,1)} %refs_0_.1), channel_id=1, source_target_pairs={{0,1},{1,0},{2,3},{3,2},{4,5},{5,4},{6,7},{7,6},{8,9},{9,8},{10,11... | collective-permute-start | bytes 3145736 | tf_op jit(solution)/shard_map/ppermute | solution.py:23
  5.1 34.4 %all-to-all-start = ((bf16[64,32,128]{2,1,0:T(8,128)(2,1)}), bf16[64,32,128]{2,1,0:T(8,128)(2,1)S(1)}, u32[]{:S(2)}, u32[]{:S(2)}) async-start(bf16[64,32,128]{2,1,0:T(8,128)(2,1)} %get-tuple-element.20), calls=%async_computation | async-start | bytes 1048576 | tf_op jit(solution)/shard_map/all_to_all | solution.py:464
  20.4 3.6 %collective-permute-start.3 = (bf16[256,1024]{1,0:T(8,128)(2,1)S(1)}, bf16[256,1024]{1,0:T(8,128)(2,1)S(1)}, u32[]{:S(2)}, u32[]{:S(2)}) collective-permute-start(bf16[256,1024]{1,0:T(8,128)(2,1)S(1)} %collective-permute-done.1.refs_2_), channel_id=1, source_target_pairs={{0,1},{1,0},{2,3},{3,2},{4,5},{5,4},{6,7},{7,6},{8,9},{9,8},{10,11... | collective-permute-start | bytes 1572872 | tf_op jit(solution)/shard_map/ppermute | solution.py:23
  20.7 3.4 %collective-permute-start.4 = (bf16[256,1024]{1,0:T(8,128)(2,1)S(1)}, bf16[256,1024]{1,0:T(8,128)(2,1)}, u32[]{:S(2)}, u32[]{:S(2)}) collective-permute-start(bf16[256,1024]{1,0:T(8,128)(2,1)S(1)} %collective-permute-done.2.refs_3_), channel_id=1, source_target_pairs={{0,1},{1,0},{2,3},{3,2},{4,5},{5,4},{6,7},{7,6},{8,9},{9,8},{10,11... | collective-permute-start | bytes 1572872 | tf_op jit(solution)/shard_map/ppermute | solution.py:23
  23.1 0.8 copy-start.3
  24.0 1.2 %copy-start.1 = (bf16[512,1024]{1,0:T(8,128)(2,1)S(1)}, bf16[512,1024]{1,0:T(8,128)(2,1)}, u32[]{:S(2)}) copy-start(bf16[512,1024]{1,0:T(8,128)(2,1)} %refs_0_.1) | copy-start | bytes 3145732
  25.3 0.7 copy-start.5
  29.8 1.9 %copy-start.2 = (bf16[4,512,1024]{2,1,0:T(8,128)(2,1)}, bf16[4,512,1024]{2,1,0:T(8,128)(2,1)S(1)}, u32[]{:S(2)}) copy-start(bf16[4,512,1024]{2,1,0:T(8,128)(2,1)S(1)} %get-tuple-element.31.far_ref) | copy-start | bytes 12582916
  31.7 32.2 %copy-start.4 = (bf16[8,256,128]{2,1,0:T(8,128)(2,1)S(1)}, bf16[8,256,128]{2,1,0:T(8,128)(2,1)}, u32[]{:S(2)}) copy-start(bf16[8,256,128]{2,1,0:T(8,128)(2,1)} %copy-done.3) | copy-start | bytes 1572868
  42.6 5.4 %collective-permute-start.5 = (bf16[48,512]{1,0:T(8,128)(2,1)S(1)}, bf16[48,512]{1,0:T(8,128)(2,1)S(1)}, u32[]{:S(2)}, u32[]{:S(2)}) collective-permute-start(bf16[48,512]{1,0:T(8,128)(2,1)S(1)} %table_piece.1.refs_0_), channel_id=1, source_target_pairs={{0,16},{16,32},{32,48},{48,64},{64,80},{80,96},{96,112},{112,0},{1... | collective-permute-start | bytes 147464 | tf_op jit(solution)/shard_map/ppermute | solution.py:23
  44.9 4.5 %collective-permute-start.9 = (bf16[48,512]{1,0:T(8,128)(2,1)S(1)}, bf16[48,512]{1,0:T(8,128)(2,1)S(1)}, u32[]{:S(2)}, u32[]{:S(2)}) collective-permute-start(bf16[48,512]{1,0:T(8,128)(2,1)S(1)} %table_piece.1.refs_0_), channel_id=1, source_target_pairs={{0,112},{16,0},{32,16},{48,32},{64,48},{80,64},{96,80},{112,96},{1... | collective-permute-start | bytes 147464 | tf_op jit(solution)/shard_map/ppermute | solution.py:23
  48.0 5.3 %collective-permute-start.6 = (bf16[48,512]{1,0:T(8,128)(2,1)S(1)}, bf16[48,512]{1,0:T(8,128)(2,1)S(1)}, u32[]{:S(2)}, u32[]{:S(2)}) collective-permute-start(bf16[48,512]{1,0:T(8,128)(2,1)S(1)} %collective-permute-done.5.refs_1_), channel_id=1, source_target_pairs={{0,16},{16,32},{32,48},{48,64},{64,80},{80,96},{96,112},{112,0},{1... | collective-permute-start | bytes 147464 | tf_op jit(solution)/shard_map/ppermute | solution.py:23
  49.3 4.2 %collective-permute-start.10 = (bf16[48,512]{1,0:T(8,128)(2,1)S(1)}, bf16[48,512]{1,0:T(8,128)(2,1)S(1)}, u32[]{:S(2)}, u32[]{:S(2)}) collective-permute-start(bf16[48,512]{1,0:T(8,128)(2,1)S(1)} %collective-permute-done.9.refs_7_), channel_id=1, source_target_pairs={{0,112},{16,0},{32,16},{48,32},{64,48},{80,64},{96,80},{112,96},{1... | collective-permute-start | bytes 147464 | tf_op jit(solution)/shard_map/ppermute | solution.py:23
  53.3 5.3 %collective-permute-start.7 = (bf16[48,512]{1,0:T(8,128)(2,1)S(1)}, bf16[48,512]{1,0:T(8,128)(2,1)S(1)}, u32[]{:S(2)}, u32[]{:S(2)}) collective-permute-start(bf16[48,512]{1,0:T(8,128)(2,1)S(1)} %collective-permute-done.6.refs_2_), channel_id=1, source_target_pairs={{0,16},{16,32},{32,48},{48,64},{64,80},{80,96},{96,112},{112,0},{1... | collective-permute-start | bytes 147464 | tf_op jit(solution)/shard_map/ppermute | solution.py:23
  53.5 6.8 %collective-permute-start.11 = (bf16[48,512]{1,0:T(8,128)(2,1)S(1)}, bf16[48,512]{1,0:T(8,128)(2,1)S(1)}, u32[]{:S(2)}, u32[]{:S(2)}) collective-permute-start(bf16[48,512]{1,0:T(8,128)(2,1)S(1)} %collective-permute-done.10.refs_6_), channel_id=1, source_target_pairs={{0,112},{16,0},{32,16},{48,32},{64,48},{80,64},{96,80},{112,96},{1... | collective-permute-start | bytes 147464 | tf_op jit(solution)/shard_map/ppermute | solution.py:23
  58.6 5.3 %collective-permute-start.8 = (bf16[48,512]{1,0:T(8,128)(2,1)S(1)}, bf16[48,512]{1,0:T(8,128)(2,1)S(1)}, u32[]{:S(2)}, u32[]{:S(2)}) collective-permute-start(bf16[48,512]{1,0:T(8,128)(2,1)S(1)} %collective-permute-done.7.refs_3_), channel_id=1, source_target_pairs={{0,16},{16,32},{32,48},{48,64},{64,80},{80,96},{96,112},{112,0},{1... | collective-permute-start | bytes 147464 | tf_op jit(solution)/shard_map/ppermute | solution.py:23

commit v8 on v7

--- a/solution.py
+++ b/solution.py
@@ -24,14 +24,13 @@
 
 
 def payload_kernel(
-    far_weight_ref, far_ids_ref, table_ref, out_ref, upper_ref, lower_ref, weight_ref, ids_ref, sems
+    far_weight_ref, table_ref, out_ref, upper_ref, lower_ref, weight_ref, sems
 ):
     half = upper_ref.shape[0]
     moves = [
         (far_weight_ref.at[0], weight_ref.at[0]),
         (far_weight_ref.at[1], weight_ref.at[1]),
         (far_weight_ref.at[2], weight_ref.at[2]),
-        (far_ids_ref, ids_ref),
         (table_ref.at[pl.ds(0, half), :], upper_ref),
         (table_ref.at[pl.ds(half, half), :], lower_ref),
     ]
@@ -41,14 +40,11 @@
     ]
     for copy in copies:
         copy.start()
-    for copy in copies[:4]:
+    for copy in copies[:3]:
         copy.wait()
     streams, rows, width = weight_ref.shape
     tiles = width // LANES
     columns = out_ref.shape[0] // tiles
-    values = ids_ref[...]
-    coded = jnp.where(values < 256, values, 255 - values).astype(F32)
-    coded = jnp.concatenate([coded, jnp.zeros_like(coded)], axis=0)
     for tile in range(tiles):
         lanes = slice(tile * LANES, (tile + 1) * LANES)
         pair = jnp.concatenate([weight_ref[0, :, lanes], weight_ref[1, :, lanes]], axis=0)
@@ -60,10 +56,8 @@
             to = (tile // 4 * columns + part) * 4 + tile % 4
             at = part * GROUP
             out_ref[to, :GROUP, :] = pair[at : at + GROUP].astype(BF)
-            out_ref[to, GROUP:, :] = jnp.concatenate([third[at : at + 8], coded], axis=0).astype(
-                BF
-            )
-    for copy in copies[4:]:
+            out_ref[to, GROUP:, :] = third[at : at + 8].astype(BF)
+    for copy in copies[3:]:
         copy.wait()
 
 
@@ -75,23 +69,22 @@
     return pl.CostEstimate(flops=flops, bytes_accessed=moved, transcendentals=0)
 
 
-def payload(in_weight, ids_rows, embed_table, parts):
+def payload(in_weight, embed_table, parts):
     vocab, width = embed_table.shape
     half = jax.ShapeDtypeStruct((vocab // 2, width), BF)
     return pl.pallas_call(
         payload_kernel,
-        out_shape=(jax.ShapeDtypeStruct((parts, 2 * GROUP, LANES), BF), half, half),
-        in_specs=[pl.BlockSpec(memory_space=pl.ANY)] * 3,
+        out_shape=(jax.ShapeDtypeStruct((parts, GROUP + 8, LANES), BF), half, half),
+        in_specs=[pl.BlockSpec(memory_space=pl.ANY)] * 2,
         out_specs=tuple(in_vmem(3)),
         scratch_shapes=[
             pltpu.VMEM(in_weight.shape, BF),
-            pltpu.VMEM(ids_rows.shape, jnp.int32),
-            pltpu.SemaphoreType.DMA((6,)),
+            pltpu.SemaphoreType.DMA((5,)),
         ],
         compiler_params=pltpu.CompilerParams(vmem_limit_bytes=66800000),
         cost_estimate=cost(0, 2900000),
         name="payload",
-    )(in_weight, ids_rows, embed_table)
+    )(in_weight, embed_table)
 
 
 def norm_kernel(spot_ref, *refs):
@@ -153,8 +146,8 @@
         weight_ref[GROUP : 2 * GROUP, lanes] = jnp.where(
             low, pltpu.roll(first, 64, 1), second
         ).astype(BF)
-        first = pieces_ref[2 * m, GROUP:, :].astype(F32)[:8]
-        second = pieces_ref[2 * m + 1, GROUP:, :].astype(F32)[:8]
+        first = pieces_ref[2 * m, GROUP:, :].astype(F32)
+        second = pieces_ref[2 * m + 1, GROUP:, :].astype(F32)
         third = jnp.concatenate(
             [
                 jnp.where(low[:8], first, pltpu.roll(second, 64, 1)),
@@ -215,10 +208,11 @@
     )(taps_row)
 
 
-def column_of(coded):
-    known = jnp.where(coded < 0.0, 255.0 - coded, coded)
+def column_of(known):
     rows = known.shape[0]
-    padded = jnp.concatenate([known, jnp.zeros((8 - rows, LANES), F32)], axis=0)
+    padded = jnp.concatenate(
+        [known.astype(F32), jnp.zeros((8 - rows, LANES), F32)], axis=0
+    )
     return jnp.transpose(padded).astype(jnp.int32)
 
 
@@ -227,36 +221,37 @@
     return jnp.where(hit, 1.0, 0.0).astype(BF)
 
 
-def ids_of(pieces_ref, index):
-    return pieces_ref[index, GROUP:, :].astype(F32)[8:12]
-
-
-def hot_kernel(spot_ref, pieces_ref, out_ref, lead_ref):
-    z = spot_ref[0]
-    step = pl.program_id(0)
-    devices = pieces_ref.shape[0]
+def hot_kernel(spot_ref, mine_ref, other_ref, tail_ref, far_tail_ref, out_ref, lead_ref):
+    z, yh, x = spot_ref[0], spot_ref[1], spot_ref[2]
+    segment = pl.program_id(0) // 2
     half, tokens, vocab = out_ref.shape
     lead = lead_ref.shape[0] // 2
-
-    @pl.when(step == 0)
+    own = segment == yh
+
+    @pl.when(pl.program_id(0) % 2 == 0)
     def _():
-        for segment in range(2):
-            start = segment * (devices // 2) + z * 4
-            rows = ids_of(pieces_ref, (start + devices - 1) % devices)
-            column = column_of(rows[2:])
-            column = jnp.concatenate([column[2 * LANES - lead :, 0:1], column[:, 1:2]], axis=0)
-            lead_ref[segment * lead : (segment + 1) * lead, :] = one_hot(column, vocab)
+        near = own != (z == 0)
+        rows = jnp.where(near, tail_ref[...], far_tail_ref[...])
+        column = column_of(rows)
+        column = jnp.concatenate([column[2 * LANES - lead :, 0:1], column[:, 1:2]], axis=0)
+        at = pl.multiple_of(segment * lead, lead)
+        lead_ref[pl.ds(at, lead), :] = one_hot(column, vocab)
 
     for block in range(half):
-        index = step * half + block
-        source = index // 4 * (devices // 2) + z * 4 + index % 4
-        column = column_of(ids_of(pieces_ref, source))
+        place = (x - (pl.program_id(0) % 2 * half + block) + 4) % 4
+        rows = jnp.where(own, mine_ref[place], other_ref[place])
+        column = column_of(rows)
         for j in range(tokens // LANES):
             out_ref[block, j * LANES : (j + 1) * LANES, :] = one_hot(column[:, j : j + 1], vocab)
 
 
-def hot_rows(spot, pieces, blocks, tokens, vocab):
+def hot_rows(spot, mine, other, tail, far_tail, tokens, vocab):
     half = 2
+    blocks = 2 * mine.shape[0]
+
+    def whole(value):
+        return pl.BlockSpec(value.shape, lambda i: (0,) * value.ndim)
+
     return pl.pallas_call(
         hot_kernel,
         out_shape=(
@@ -264,10 +259,8 @@
             jax.ShapeDtypeStruct((2 * HALO, vocab), BF),
         ),
         grid=(blocks // half,),
-        in_specs=[
-            pl.BlockSpec(memory_space=pltpu.SMEM),
-            pl.BlockSpec(pieces.shape, lambda i: (0, 0, 0)),
-        ],
+        in_specs=[pl.BlockSpec(memory_space=pltpu.SMEM)]
+        + [whole(value) for value in (mine, other, tail, far_tail)],
         out_specs=(
             pl.BlockSpec((half, tokens, vocab), lambda i: (i, 0, 0)),
             pl.BlockSpec((2 * HALO, vocab), lambda i: (0, 0)),
@@ -275,7 +268,7 @@
         compiler_params=pltpu.CompilerParams(vmem_limit_bytes=GRANT),
         cost_estimate=cost(5000000, 4500000),
         name="hot_rows",
-    )(spot, pieces)
+    )(spot, mine, other, tail, far_tail)
 
 
 def mix_kernel(spot_ref, hot_ref, lead_hot_ref, *refs):
@@ -458,7 +451,7 @@
     tile = yh * x_count + x
     tiles = width_local // LANES
 
-    load, upper, lower = payload(in_weight, ids.reshape(-1, LANES), embed_table, tiles * z_count)
+    load, upper, lower = payload(in_weight, embed_table, tiles * z_count)
     got_up = shifted(upper, ("yh", "yl"), -1)
     got_down = shifted(lower, ("yh", "yl"), 1)
     pieces = lax.all_to_all(load, ctx, 0, 0, tiled=True)
@@ -474,17 +467,31 @@
     scale = lax.dynamic_slice_in_dim(in_scale, tile * LANES + z * GROUP, GROUP, 1)
     scale = scale.reshape(STREAMS * GROUP, 1)
 
-    swapped, near_filter = lax.optimization_barrier((embed_table, near_filter))
+    swapped, local, got_up = lax.optimization_barrier(
+        (embed_table, ids.reshape(-1, LANES), got_up)
+    )
     got_core = shifted(swapped, "core", 1)
     far_up = shifted(got_up, "core", 1)
     far_down = shifted(got_down, "core", 1)
+    mine_ids = jnp.stack([local] + [shifted(local, "x", step) for step in (1, 2, 3)])
+    other_ids = shifted(mine_ids, "yh", 1)
+    last = lax.dynamic_index_in_dim(mine_ids, (x + 1) % x_count, 0, keepdims=False)[2:]
+    tail = shifted(last, "z", 1)
+    pairs = [
+        (a * z_count + b, (1 - a) * z_count + (b + 1) % z_count)
+        for a in range(2)
+        for b in range(z_count)
+    ]
+    far_tail = lax.ppermute(last, ("yh", "z"), pairs)
     mine = yl * 2 + core
     order = jnp.stack([mine, mine ^ 1, mine ^ 2, mine ^ 3]).astype(jnp.int32)
     normed, token = normed_rows(
         order, [embed_table, got_core, got_up, got_down, far_up, far_down], norm_gain.reshape(1, -1)
     )
-    pieces, toep, near_filter, token = lax.optimization_barrier(
-        (pieces, toep, near_filter, token)
+    pieces, toep, near_filter, token, mine_ids, other_ids, tail, far_tail = (
+        lax.optimization_barrier(
+            (pieces, toep, near_filter, token, mine_ids, other_ids, tail, far_tail)
+        )
     )
     normed = pltpu.with_memory_space_constraint(normed, pltpu.HBM)
     piece = table_piece(normed, pieces, scale, token)
@@ -495,8 +502,8 @@
             last = shifted(last, "z", -1)
             downs.append(last)
 
-    spot = z.reshape(1).astype(jnp.int32)
-    hot, lead_hot = hot_rows(spot, pieces, tiles, tokens, vocab)
+    spot = jnp.stack([z, yh, x]).astype(jnp.int32)
+    hot, lead_hot = hot_rows(spot, mine_ids, other_ids, tail, far_tail, tokens, vocab)
     blocks = mixed_blocks(spot, hot, lead_hot, ups + downs[::-1], near_filter, toep)
     result = lax.all_to_all(blocks, ("yh", "x"), 0, 0, tiled=True)
     return placed_columns(result)

time: 92.4 us -> 99.9 us (1.081)
  starting transfers between devices: 27.4 us -> 38.6 us
  waiting for transfers between devices: 17.5 us -> 9.94 us
  blocking collectives: 17.3 us -> 19.2 us
    ppermute x12 -> x17, starting transfers between devices: 12.7 us -> 22.6 us  [shifted(): return lax.ppermute(value, axis, pairs)]
    all_to_all x1, waiting for transfers between devices: 7.78 us -> 0.01 us  [per_device(): pieces = lax.all_to_all(load, ctx, 0, 0, tiled=True)]
    all_to_all x1, blocking collectives: 17.3 us -> 19.2 us  [per_device(): result = lax.all_to_all(blocks, ('yh', 'x'), 0, 0, tiled=True)]
    ppermute x0 -> x1, starting transfers between devices: none -> 1.35 us  [per_device(): far_tail = lax.ppermute(last, ('yh', 'z'), pairs)]
    ppermute x12 -> x17, waiting for transfers between devices: 9.67 us -> 9.94 us  [shifted(): return lax.ppermute(value, axis, pairs)]
  transfers between devices with their start and end apart: 13 -> 19, of which waited for: 6 -> 7; matrix products, arithmetic and copies ran while one was open for 3% -> 3% of each run, Pallas kernels for 6% -> 7%
where the time goes in v8:
time: 99.9 us; the launch traced here: 99.4 us
  starting transfers between devices  38.6 us (39%)
  Pallas kernels  23.3 us (23%)
  blocking collectives  19.2 us (19%)
  waiting for transfers between devices  9.94 us (10%)
  local copies, waits for them, and re-layouts  7.09 us (7%)
    ppermute x17, starting transfers between devices, shifted(): return lax.ppermute(value, axis, pairs)  22.6 us
    all_to_all x1, blocking collectives, per_device(): result = lax.all_to_all(blocks, ('yh', 'x'), 0, 0, tiled=True)  19.2 us
    all_to_all x1, starting transfers between devices, per_device(): pieces = lax.all_to_all(load, ctx, 0, 0, tiled=True)  14.7 us
    ppermute x17, waiting for transfers between devices, shifted(): return lax.ppermute(value, axis, pairs)  9.94 us
    pallas_call x1, Pallas kernels, mixed_blocks(): pl.pallas_call(mix_kernel, out_shape=jax.ShapeDtypeStruct((blocks, tokens...  9.79 us
    unnamed x12, local copies, waits for them, and re-layouts  4.67 us
    pallas_call x1, Pallas kernels, normed_rows(): pl.pallas_call(norm_kernel, out_shape=(jax.ShapeDtypeStruct((4, vocab, wi...  3.78 us
    pallas_call x1, Pallas kernels, table_piece(): pl.pallas_call(table_kernel, out_shape=jax.ShapeDtypeStruct((rows, vocab)...  3.11 us
  transfers between devices with their start and end apart: 19, of which 7 were waited for; matrix products, arithmetic and copies ran while one was open for 3% of the time, Pallas kernels for 7%

profile of v8, /device:TPU:8, one launch (start us, length us, event | category | flops | bytes accessed | tf_op | source)
XLA Modules:
  0.0 99.4 jit_solution(7335429525958780340)
XLA Ops:
  0.0 0.0 copy-start
  0.0 2.6 %payload.1 = (bf16[64,24,128]{2,1,0:T(8,128)(2,1)}, bf16[256,1024]{1,0:T(8,128)(2,1)}, bf16[256,1024]{1,0:T(8,128)(2,1)}) custom-call(bf16[3,64,1024]{2,1,0:T(8,128)(2,1)} %far_weight_ref.1, bf16[512,1024]{1,0:T(8,128)(2,1)} %refs_0_.1), custom_call_target="tpu_custom_call" | custom-call | bytes 2900000 | tf_op jit(solution)/shard_map/payload/pallas_call | solution.py:75
  2.6 2.3 %collective-permute-start = (bf16[256,1024]{1,0:T(8,128)(2,1)}, bf16[256,1024]{1,0:T(8,128)(2,1)S(1)}, u32[]{:S(2)}, u32[]{:S(2)}) collective-permute-start(bf16[256,1024]{1,0:T(8,128)(2,1)} %get-tuple-element.28), channel_id=1, source_target_pairs={{0,130},{2,0},{128,2},{130,128},{1,131},{3,1},{129,3},{131,129},{4... | collective-permute-start | bytes 1572872 | tf_op jit(solution)/shard_map/ppermute | solution.py:23
  4.9 0.0 collective-permute-start.2
  4.9 14.7 %all-to-all-start = ((bf16[64,24,128]{2,1,0:T(8,128)(2,1)}), bf16[64,24,128]{2,1,0:T(8,128)(2,1)S(1)}, u32[]{:S(2)}, u32[]{:S(2)}) async-start(bf16[64,24,128]{2,1,0:T(8,128)(2,1)} %get-tuple-element.25), calls=%async_computation | async-start | bytes 786432 | tf_op jit(solution)/shard_map/all_to_all | solution.py:457
  19.6 0.0 collective-permute-done.refs_2_
  19.7 0.1 collective-permute-start.1
  19.8 0.7 constant_dynamic-slice_fusion.3
  20.5 0.7 dynamic_slice.17
  21.2 0.1 fusion
  21.3 0.0 copy-done
  21.3 1.6 %collective-permute-start.5 = (s32[4,128]{1,0:T(4,128)}, s32[4,128]{1,0:T(4,128)S(1)}, u32[]{:S(2)}, u32[]{:S(2)}) collective-permute-start(s32[4,128]{1,0:T(4,128)} %bitcast.18), channel_id=1, source_target_pairs={{0,4},{4,8},{8,12},{12,0},{1,5},{5,9},{9,13},{13,1},{2,6},{6,10},{... | collective-permute-start | bytes 6152 | tf_op jit(solution)/shard_map/ppermute | solution.py:23
  22.9 0.8 constant_dynamic-slice_fusion
  23.7 2.7 %collective-permute-start.6 = (s32[4,128]{1,0:T(4,128)}, s32[4,128]{1,0:T(4,128)S(1)}, u32[]{:S(2)}, u32[]{:S(2)}) collective-permute-start(s32[4,128]{1,0:T(4,128)} %bitcast.19), channel_id=1, source_target_pairs={{0,8},{4,12},{8,0},{12,4},{1,9},{5,13},{9,1},{13,5},{2,10},{6,14},... | collective-permute-start | bytes 6152 | tf_op jit(solution)/shard_map/ppermute | solution.py:23
  26.3 1.5 %collective-permute-start.7 = (s32[4,128]{1,0:T(4,128)}, s32[4,128]{1,0:T(4,128)S(1)}, u32[]{:S(2)}, u32[]{:S(2)}) collective-permute-start(s32[4,128]{1,0:T(4,128)} %bitcast.20), channel_id=1, source_target_pairs={{0,12},{4,0},{8,4},{12,8},{1,13},{5,1},{9,5},{13,9},{2,14},{6,2},{... | collective-permute-start | bytes 6152 | tf_op jit(solution)/shard_map/ppermute | solution.py:23
  27.8 0.0 collective-permute-done.2.refs_3_
  27.8 0.0 collective-permute-start.3
  27.8 0.0 collective-permute-done.5
  27.8 0.5 collective-permute-start.4
  28.3 0.1 pad_add_fusion.2.spot_ref
  28.4 0.1 rev.3
  28.5 0.1 reshape.15.scale_ref
  28.6 0.1 pad.4.taps_ref
  28.6 0.4 toeplitz.1.refs_9_
  29.0 0.0 copy-start.3
  29.0 0.8 copy-done.3
  29.8 0.0 collective-permute-done.6
  29.8 0.3 collective-permute-done.7
  30.1 0.7 pad_add_fusion.mine_ref
  30.8 3.1 %collective-permute-start.8 = (s32[4,4,128]{2,1,0:T(4,128)S(1)}, s32[4,4,128]{2,1,0:T(4,128)S(1)}, u32[]{:S(2)}, u32[]{:S(2)}) collective-permute-start(s32[4,4,128]{2,1,0:T(4,128)S(1)} %pad_add_fusion.mine_ref), channel_id=1, source_target_pairs={{0,128},{128,0},{1,129},{129,1},{2,130},{130,2},{3,131},{131,3},{4... | collective-permute-start | bytes 24584 | tf_op jit(solution)/shard_map/ppermute | solution.py:23
  33.9 1.3 %collective-permute-start.10 = (s32[2,128]{1,0:T(2,128)S(1)}, s32[2,128]{1,0:T(2,128)S(1)}, u32[]{:S(2)}, u32[]{:S(2)}) collective-permute-start(s32[2,128]{1,0:T(2,128)S(1)} %slice_bitcast_fusion), channel_id=1, source_target_pairs={{0,144},{16,160},{32,176},{48,192},{64,208},{80,224},{96,240},{112... | collective-permute-start | bytes 3080 | tf_op jit(solution)/shard_map/ppermute | solution.py:485
  35.3 0.0 collective-permute-done.3.refs_4_
  35.3 1.5 %collective-permute-start.9 = (s32[2,128]{1,0:T(2,128)S(1)}, s32[2,128]{1,0:T(2,128)S(1)}, u32[]{:S(2)}, u32[]{:S(2)}) collective-permute-start(s32[2,128]{1,0:T(2,128)S(1)} %slice_bitcast_fusion), channel_id=1, source_target_pairs={{0,16},{16,32},{32,48},{48,64},{64,80},{80,96},{96,112},{112,0},{1... | collective-permute-start | bytes 3080 | tf_op jit(solution)/shard_map/ppermute | solution.py:23
  36.8 0.0 collective-permute-done.4.refs_5_
  36.8 0.0 collective-permute-done.1.refs_1_
  36.8 1.2 %copy-done.1 = bf16[512,1024]{1,0:T(8,128)(2,1)S(1)} copy-done((bf16[512,1024]{1,0:T(8,128)(2,1)S(1)}, bf16[512,1024]{1,0:T(8,128)(2,1)}, u32[]{:S(2)}) %copy-start.1) | copy-done | bytes 1048600
  38.0 0.7 copy-done.5
  38.7 3.8 %normed_rows.1 = (bf16[4,512,1024]{2,1,0:T(8,128)(2,1)S(1)}, f32[8,128]{1,0:T(8,128)S(1)}) custom-call(s32[4]{0:T(128)S(1)} %pad_add_fusion.2.spot_ref, bf16[512,1024]{1,0:T(8,128)(2,1)S(1)} %copy-done.1, bf16[512,1024]{1,0:T(8,128)(2,1)S(1)} %collective-permute-done.1.refs_1_, bf16[256,1024]{1,0:T(8,128)(2,1)S(1)} %collective-permute-done.refs_2_, ...), custom_call_target="tpu_custom_call" | custom-call | flops 10485760 | bytes 8388608 | tf_op jit(solution)/shard_map/normed_rows/pallas_call | solution.py:119
  42.5 0.0 copy-start.2
  42.5 1.9 %copy-done.2 = bf16[4,512,1024]{2,1,0:T(8,128)(2,1)} copy-done((bf16[4,512,1024]{2,1,0:T(8,128)(2,1)}, bf16[4,512,1024]{2,1,0:T(8,128)(2,1)S(1)}, u32[]{:S(2)}) %copy-start.2) | copy-done | bytes 4194328
  44.4 0.0 collective-permute-done.10.far_tail_ref
  44.4 0.0 collective-permute-done.9.tail_ref
  44.4 0.0 collective-permute-done.8.other_ref
  44.5 0.0 all-to-all-done.pieces_ref
  44.5 3.1 %table_piece.1.refs_0_ = bf16[48,512]{1,0:T(8,128)(2,1)S(1)} custom-call(bf16[4,512,1024]{2,1,0:T(8,128)(2,1)} %copy-done.2, bf16[64,24,128]{2,1,0:T(8,128)(2,1)S(1)} %all-to-all-done.pieces_ref, f32[48,1]{1,0:T(8,128)S(1)} %reshape.15.scale_ref, f32[8,128]{1,0:T(8,128)S(1)} %get-tuple-element.42._), custom_call_target="tpu_custom_call" | custom-call | flops 201326592 | bytes 5000000 | tf_op jit(solution)/shard_map/table_piece/pallas_call | solution.py:175
  47.6 1.5 %collective-permute-start.11 = (bf16[48,512]{1,0:T(8,128)(2,1)S(1)}, bf16[48,512]{1,0:T(8,128)(2,1)S(1)}, u32[]{:S(2)}, u32[]{:S(2)}) collective-permute-start(bf16[48,512]{1,0:T(8,128)(2,1)S(1)} %table_piece.1.refs_0_), channel_id=1, source_target_pairs={{0,16},{16,32},{32,48},{48,64},{64,80},{80,96},{96,112},{112,0},{1... | collective-permute-start | bytes 147464 | tf_op jit(solution)/shard_map/ppermute | solution.py:23
  49.1 1.8 %collective-permute-start.15 = (bf16[48,512]{1,0:T(8,128)(2,1)S(1)}, bf16[48,512]{1,0:T(8,128)(2,1)S(1)}, u32[]{:S(2)}, u32[]{:S(2)}) collective-permute-start(bf16[48,512]{1,0:T(8,128)(2,1)S(1)} %table_piece.1.refs_0_), channel_id=1, source_target_pairs={{0,112},{16,0},{32,16},{48,32},{64,48},{80,64},{96,80},{112,96},{1... | collective-permute-start | bytes 147464 | tf_op jit(solution)/shard_map/ppermute | solution.py:23
  50.9 2.1 %collective-permute-done.11.refs_1_ = bf16[48,512]{1,0:T(8,128)(2,1)S(1)} collective-permute-done((bf16[48,512]{1,0:T(8,128)(2,1)S(1)}, bf16[48,512]{1,0:T(8,128)(2,1)S(1)}, u32[]{:S(2)}, u32[]{:S(2)}) %collective-permute-start.11) | collective-permute-done | bytes 49184 | tf_op jit(solution)/shard_map/ppermute | solution.py:23
  53.0 0.6 collective-permute-start.12
  53.5 0.3 collective-permute-done.15.refs_7_
  53.9 2.3 %collective-permute-start.16 = (bf16[48,512]{1,0:T(8,128)(2,1)S(1)}, bf16[48,512]{1,0:T(8,128)(2,1)S(1)}, u32[]{:S(2)}, u32[]{:S(2)}) collective-permute-start(bf16[48,512]{1,0:T(8,128)(2,1)S(1)} %collective-permute-done.15.refs_7_), channel_id=1, source_target_pairs={{0,112},{16,0},{32,16},{48,32},{64,48},{80,64},{96,80},{112,96},{1... | collective-permute-start | bytes 147464 | tf_op jit(solution)/shard_map/ppermute | solution.py:23
  56.2 2.1 %collective-permute-done.12.refs_2_ = bf16[48,512]{1,0:T(8,128)(2,1)S(1)} collective-permute-done((bf16[48,512]{1,0:T(8,128)(2,1)S(1)}, bf16[48,512]{1,0:T(8,128)(2,1)S(1)}, u32[]{:S(2)}, u32[]{:S(2)}) %collective-permute-start.12) | collective-permute-done | bytes 49184 | tf_op jit(solution)/shard_map/ppermute | solution.py:23
  58.3 0.0 collective-permute-start.13
  58.3 0.1 collective-permute-done.16.refs_6_
  58.4 3.1 %collective-permute-start.17 = (bf16[48,512]{1,0:T(8,128)(2,1)S(1)}, bf16[48,512]{1,0:T(8,128)(2,1)S(1)}, u32[]{:S(2)}, u32[]{:S(2)}) collective-permute-start(bf16[48,512]{1,0:T(8,128)(2,1)S(1)} %collective-permute-done.16.refs_6_), channel_id=1, source_target_pairs={{0,112},{16,0},{32,16},{48,32},{64,48},{80,64},{96,80},{112,96},{1... | collective-permute-start | bytes 147464 | tf_op jit(solution)/shard_map/ppermute | solution.py:23
  61.5 2.4 %collective-permute-done.13.refs_3_ = bf16[48,512]{1,0:T(8,128)(2,1)S(1)} collective-permute-done((bf16[48,512]{1,0:T(8,128)(2,1)S(1)}, bf16[48,512]{1,0:T(8,128)(2,1)S(1)}, u32[]{:S(2)}, u32[]{:S(2)}) %collective-permute-start.13) | collective-permute-done | bytes 49184 | tf_op jit(solution)/shard_map/ppermute | solution.py:23
  63.9 0.0 collective-permute-start.14
  63.9 0.1 pad_add_fusion.1.spot_ref
  64.0 2.6 %hot_rows.1 = (bf16[8,512,512]{2,1,0:T(8,128)(2,1)S(1)}, bf16[288,512]{1,0:T(8,128)(2,1)S(1)}) custom-call(s32[3]{0:T(128)S(1)} %pad_add_fusion.1.spot_ref, s32[4,4,128]{2,1,0:T(4,128)S(1)} %pad_add_fusion.mine_ref, s32[4,4,128]{2,1,0:T(4,128)S(1)} %collective-permute-done.8.other_ref, s32[2,128]{1,0:T(2,128)S(1)} %collective-permute-done.9.tail_ref, ...), custom_call_target="tpu_custom_call" | custom-call | flops 5000000 | bytes 4500000 | tf_op jit(solution)/shard_map/hot_rows/pallas_call | solution.py:255
  66.6 0.0 collective-permute-done.17.refs_5_
  66.6 2.6 %collective-permute-done.14.refs_4_ = bf16[48,512]{1,0:T(8,128)(2,1)S(1)} collective-permute-done((bf16[48,512]{1,0:T(8,128)(2,1)S(1)}, bf16[48,512]{1,0:T(8,128)(2,1)S(1)}, u32[]{:S(2)}, u32[]{:S(2)}) %collective-permute-start.14) | collective-permute-done | bytes 49184 | tf_op jit(solution)/shard_map/ppermute | solution.py:23
  69.2 9.8 %mixed_blocks.1 = bf16[8,512,128]{2,1,0:T(8,128)(2,1)S(1)} custom-call(s32[3]{0:T(128)S(1)} %pad_add_fusion.1.spot_ref, bf16[8,512,512]{2,1,0:T(8,128)(2,1)S(1)} %get-tuple-element.38.hot_ref, bf16[288,512]{1,0:T(8,128)(2,1)S(1)} %get-tuple-element.39.lead_hot_ref, bf16[48,512]{1,0:T(8,128)(2,1)S(1)} %table_piece.1.refs_0_, ...), custom_call_target="tpu_custom_call" | custom-call | flops 5000000000 | bytes 6000000 | tf_op jit(solution)/shard_map/mixed_blocks/pallas_call | solution.py:381
  79.0 19.2 %all_to_all.10.blocks_ref = bf16[8,512,128]{2,1,0:T(8,128)(2,1)S(1)} all-to-all(bf16[8,512,128]{2,1,0:T(8,128)(2,1)S(1)} %mixed_blocks.1), channel_id=1, replica_groups=mesh['yh'=2,'z'=8,'x'=4,'yl'=2,'core'=2] {'yh','x'}, dimensions={0} | all-to-all | bytes 2097152 | tf_op jit(solution)/shard_map/all_to_all | solution.py:508
  98.2 1.0 %placed_columns.1 = bf16[512,1024]{1,0:T(8,128)(2,1)} custom-call(bf16[8,512,128]{2,1,0:T(8,128)(2,1)S(1)} %all_to_all.10.blocks_ref), custom_call_target="tpu_custom_call" | custom-call | bytes 2000000 | tf_op jit(solution)/shard_map/placed_columns/pallas_call | solution.py:428
  (8 shorter events, 0.0 us)
Async XLA Ops:
  0.0 21.3 %copy-start = (f32[3,7,1024]{2,1,0:T(8,128)S(1)}, f32[3,7,1024]{2,1,0:T(8,128)}, u32[]{:S(2)}) copy-start(f32[3,7,1024]{2,1,0:T(8,128)} %param.13) | copy-start | bytes 258052
  2.6 17.0 %collective-permute-start = (bf16[256,1024]{1,0:T(8,128)(2,1)}, bf16[256,1024]{1,0:T(8,128)(2,1)S(1)}, u32[]{:S(2)}, u32[]{:S(2)}) collective-permute-start(bf16[256,1024]{1,0:T(8,128)(2,1)} %get-tuple-element.28), channel_id=1, source_target_pairs={{0,130},{2,0},{128,2},{130,128},{1,131},{3,1},{129,3},{131,129},{4... | collective-permute-start | bytes 1572872 | tf_op jit(solution)/shard_map/ppermute | solution.py:23
  4.9 22.9 %collective-permute-start.2 = (bf16[256,1024]{1,0:T(8,128)(2,1)}, bf16[256,1024]{1,0:T(8,128)(2,1)S(1)}, u32[]{:S(2)}, u32[]{:S(2)}) collective-permute-start(bf16[256,1024]{1,0:T(8,128)(2,1)} %get-tuple-element.31), channel_id=1, source_target_pairs={{0,2},{2,128},{128,130},{130,0},{1,3},{3,129},{129,131},{131,1},{4... | collective-permute-start | bytes 1572872 | tf_op jit(solution)/shard_map/ppermute | solution.py:23
  4.9 39.5 %all-to-all-start = ((bf16[64,24,128]{2,1,0:T(8,128)(2,1)}), bf16[64,24,128]{2,1,0:T(8,128)(2,1)S(1)}, u32[]{:S(2)}, u32[]{:S(2)}) async-start(bf16[64,24,128]{2,1,0:T(8,128)(2,1)} %get-tuple-element.25), calls=%async_computation | async-start | bytes 786432 | tf_op jit(solution)/shard_map/all_to_all | solution.py:457
  19.7 17.1 %collective-permute-start.1 = (bf16[512,1024]{1,0:T(8,128)(2,1)}, bf16[512,1024]{1,0:T(8,128)(2,1)S(1)}, u32[]{:S(2)}, u32[]{:S(2)}) collective-permute-start(bf16[512,1024]{1,0:T(8,128)(2,1)} %refs_0_.1), channel_id=1, source_target_pairs={{0,1},{1,0},{2,3},{3,2},{4,5},{5,4},{6,7},{7,6},{8,9},{9,8},{10,11... | collective-permute-start | bytes 3145736 | tf_op jit(solution)/shard_map/ppermute | solution.py:23
  21.3 6.5 %collective-permute-start.5 = (s32[4,128]{1,0:T(4,128)}, s32[4,128]{1,0:T(4,128)S(1)}, u32[]{:S(2)}, u32[]{:S(2)}) collective-permute-start(s32[4,128]{1,0:T(4,128)} %bitcast.18), channel_id=1, source_target_pairs={{0,4},{4,8},{8,12},{12,0},{1,5},{5,9},{9,13},{13,1},{2,6},{6,10},{... | collective-permute-start | bytes 6152 | tf_op jit(solution)/shard_map/ppermute | solution.py:23
  23.7 6.2 %collective-permute-start.6 = (s32[4,128]{1,0:T(4,128)}, s32[4,128]{1,0:T(4,128)S(1)}, u32[]{:S(2)}, u32[]{:S(2)}) collective-permute-start(s32[4,128]{1,0:T(4,128)} %bitcast.19), channel_id=1, source_target_pairs={{0,8},{4,12},{8,0},{12,4},{1,9},{5,13},{9,1},{13,5},{2,10},{6,14},... | collective-permute-start | bytes 6152 | tf_op jit(solution)/shard_map/ppermute | solution.py:23
  26.3 3.8 %collective-permute-start.7 = (s32[4,128]{1,0:T(4,128)}, s32[4,128]{1,0:T(4,128)S(1)}, u32[]{:S(2)}, u32[]{:S(2)}) collective-permute-start(s32[4,128]{1,0:T(4,128)} %bitcast.20), channel_id=1, source_target_pairs={{0,12},{4,0},{8,4},{12,8},{1,13},{5,1},{9,5},{13,9},{2,14},{6,2},{... | collective-permute-start | bytes 6152 | tf_op jit(solution)/shard_map/ppermute | solution.py:23
  27.8 7.5 %collective-permute-start.3 = (bf16[256,1024]{1,0:T(8,128)(2,1)S(1)}, bf16[256,1024]{1,0:T(8,128)(2,1)S(1)}, u32[]{:S(2)}, u32[]{:S(2)}) collective-permute-start(bf16[256,1024]{1,0:T(8,128)(2,1)S(1)} %collective-permute-done.refs_2_), channel_id=1, source_target_pairs={{0,1},{1,0},{2,3},{3,2},{4,5},{5,4},{6,7},{7,6},{8,9},{9,8},{10,11... | collective-permute-start | bytes 1572872 | tf_op jit(solution)/shard_map/ppermute | solution.py:23
  27.8 8.9 %collective-permute-start.4 = (bf16[256,1024]{1,0:T(8,128)(2,1)S(1)}, bf16[256,1024]{1,0:T(8,128)(2,1)}, u32[]{:S(2)}, u32[]{:S(2)}) collective-permute-start(bf16[256,1024]{1,0:T(8,128)(2,1)S(1)} %collective-permute-done.2.refs_3_), channel_id=1, source_target_pairs={{0,1},{1,0},{2,3},{3,2},{4,5},{5,4},{6,7},{7,6},{8,9},{9,8},{10,11... | collective-permute-start | bytes 1572872 | tf_op jit(solution)/shard_map/ppermute | solution.py:23
  29.0 0.8 copy-start.3
  30.8 13.6 %collective-permute-start.8 = (s32[4,4,128]{2,1,0:T(4,128)S(1)}, s32[4,4,128]{2,1,0:T(4,128)S(1)}, u32[]{:S(2)}, u32[]{:S(2)}) collective-permute-start(s32[4,4,128]{2,1,0:T(4,128)S(1)} %pad_add_fusion.mine_ref), channel_id=1, source_target_pairs={{0,128},{128,0},{1,129},{129,1},{2,130},{130,2},{3,131},{131,3},{4... | collective-permute-start | bytes 24584 | tf_op jit(solution)/shard_map/ppermute | solution.py:23
  33.9 10.5 %collective-permute-start.10 = (s32[2,128]{1,0:T(2,128)S(1)}, s32[2,128]{1,0:T(2,128)S(1)}, u32[]{:S(2)}, u32[]{:S(2)}) collective-permute-start(s32[2,128]{1,0:T(2,128)S(1)} %slice_bitcast_fusion), channel_id=1, source_target_pairs={{0,144},{16,160},{32,176},{48,192},{64,208},{80,224},{96,240},{112... | collective-permute-start | bytes 3080 | tf_op jit(solution)/shard_map/ppermute | solution.py:485
  35.3 9.2 %collective-permute-start.9 = (s32[2,128]{1,0:T(2,128)S(1)}, s32[2,128]{1,0:T(2,128)S(1)}, u32[]{:S(2)}, u32[]{:S(2)}) collective-permute-start(s32[2,128]{1,0:T(2,128)S(1)} %slice_bitcast_fusion), channel_id=1, source_target_pairs={{0,16},{16,32},{32,48},{48,64},{64,80},{80,96},{96,112},{112,0},{1... | collective-permute-start | bytes 3080 | tf_op jit(solution)/shard_map/ppermute | solution.py:23
  36.8 1.2 %copy-start.1 = (bf16[512,1024]{1,0:T(8,128)(2,1)S(1)}, bf16[512,1024]{1,0:T(8,128)(2,1)}, u32[]{:S(2)}) copy-start(bf16[512,1024]{1,0:T(8,128)(2,1)} %refs_0_.1) | copy-start | bytes 3145732
  38.0 0.7 copy-start.5
  42.5 1.9 %copy-start.2 = (bf16[4,512,1024]{2,1,0:T(8,128)(2,1)}, bf16[4,512,1024]{2,1,0:T(8,128)(2,1)S(1)}, u32[]{:S(2)}) copy-start(bf16[4,512,1024]{2,1,0:T(8,128)(2,1)S(1)} %get-tuple-element.40.far_ref) | copy-start | bytes 12582916
  44.4 24.8 %copy-start.4 = (bf16[8,256,128]{2,1,0:T(8,128)(2,1)S(1)}, bf16[8,256,128]{2,1,0:T(8,128)(2,1)}, u32[]{:S(2)}) copy-start(bf16[8,256,128]{2,1,0:T(8,128)(2,1)} %copy-done.3) | copy-start | bytes 1572868
  47.6 5.4 %collective-permute-start.11 = (bf16[48,512]{1,0:T(8,128)(2,1)S(1)}, bf16[48,512]{1,0:T(8,128)(2,1)S(1)}, u32[]{:S(2)}, u32[]{:S(2)}) collective-permute-start(bf16[48,512]{1,0:T(8,128)(2,1)S(1)} %table_piece.1.refs_0_), channel_id=1, source_target_pairs={{0,16},{16,32},{32,48},{48,64},{64,80},{80,96},{96,112},{112,0},{1... | collective-permute-start | bytes 147464 | tf_op jit(solution)/shard_map/ppermute | solution.py:23
  49.1 4.7 %collective-permute-start.15 = (bf16[48,512]{1,0:T(8,128)(2,1)S(1)}, bf16[48,512]{1,0:T(8,128)(2,1)S(1)}, u32[]{:S(2)}, u32[]{:S(2)}) collective-permute-start(bf16[48,512]{1,0:T(8,128)(2,1)S(1)} %table_piece.1.refs_0_), channel_id=1, source_target_pairs={{0,112},{16,0},{32,16},{48,32},{64,48},{80,64},{96,80},{112,96},{1... | collective-permute-start | bytes 147464 | tf_op jit(solution)/shard_map/ppermute | solution.py:23
  53.0 5.3 %collective-permute-start.12 = (bf16[48,512]{1,0:T(8,128)(2,1)S(1)}, bf16[48,512]{1,0:T(8,128)(2,1)S(1)}, u32[]{:S(2)}, u32[]{:S(2)}) collective-permute-start(bf16[48,512]{1,0:T(8,128)(2,1)S(1)} %collective-permute-done.11.refs_1_), channel_id=1, source_target_pairs={{0,16},{16,32},{32,48},{48,64},{64,80},{80,96},{96,112},{112,0},{1... | collective-permute-start | bytes 147464 | tf_op jit(solution)/shard_map/ppermute | solution.py:23
  53.9 4.5 %collective-permute-start.16 = (bf16[48,512]{1,0:T(8,128)(2,1)S(1)}, bf16[48,512]{1,0:T(8,128)(2,1)S(1)}, u32[]{:S(2)}, u32[]{:S(2)}) collective-permute-start(bf16[48,512]{1,0:T(8,128)(2,1)S(1)} %collective-permute-done.15.refs_7_), channel_id=1, source_target_pairs={{0,112},{16,0},{32,16},{48,32},{64,48},{80,64},{96,80},{112,96},{1... | collective-permute-start | bytes 147464 | tf_op jit(solution)/shard_map/ppermute | solution.py:23
  58.3 5.6 %collective-permute-start.13 = (bf16[48,512]{1,0:T(8,128)(2,1)S(1)}, bf16[48,512]{1,0:T(8,128)(2,1)S(1)}, u32[]{:S(2)}, u32[]{:S(2)}) collective-permute-start(bf16[48,512]{1,0:T(8,128)(2,1)S(1)} %collective-permute-done.12.refs_2_), channel_id=1, source_target_pairs={{0,16},{16,32},{32,48},{48,64},{64,80},{80,96},{96,112},{112,0},{1... | collective-permute-start | bytes 147464 | tf_op jit(solution)/shard_map/ppermute | solution.py:23
  58.4 8.2 %collective-permute-start.17 = (bf16[48,512]{1,0:T(8,128)(2,1)S(1)}, bf16[48,512]{1,0:T(8,128)(2,1)S(1)}, u32[]{:S(2)}, u32[]{:S(2)}) collective-permute-start(bf16[48,512]{1,0:T(8,128)(2,1)S(1)} %collective-permute-done.16.refs_6_), channel_id=1, source_target_pairs={{0,112},{16,0},{32,16},{48,32},{64,48},{80,64},{96,80},{112,96},{1... | collective-permute-start | bytes 147464 | tf_op jit(solution)/shard_map/ppermute | solution.py:23
  63.9 5.3 %collective-permute-start.14 = (bf16[48,512]{1,0:T(8,128)(2,1)S(1)}, bf16[48,512]{1,0:T(8,128)(2,1)S(1)}, u32[]{:S(2)}, u32[]{:S(2)}) collective-permute-start(bf16[48,512]{1,0:T(8,128)(2,1)S(1)} %collective-permute-done.13.refs_3_), channel_id=1, source_target_pairs={{0,16},{16,32},{32,48},{48,64},{64,80},{80,96},{96,112},{112,0},{1... | collective-permute-start | bytes 147464 | tf_op jit(solution)/shard_map/ppermute | solution.py:23

commit v9 on v7

--- a/solution.py
+++ b/solution.py
@@ -347,10 +347,23 @@
         for j in range(count):
             conv_ref[j, rows, :] = full[j * GROUP : (j + 1) * GROUP]
 
-    select(0, tokens)
-    for g in range(groups):
-        convolved(g)
-        filtered(g * chunk)
+    final = pl.num_programs(0) - 1
+
+    @pl.when(step == 0)
+    def _():
+        select(0, tokens)
+
+    @pl.when((step > 0) & (step < final))
+    def _():
+        select(0, tokens)
+        for g in range(groups):
+            convolved(g)
+            filtered(g * chunk)
+
+    @pl.when(step == final)
+    def _():
+        for g in range(groups):
+            convolved(g)
 
     @pl.when(step >= 0)
     def _():

time: 92.4 us -> 91.3 us (0.988)
  Pallas kernels: 22.5 us -> 21.4 us
    pallas_call x1, Pallas kernels: 9.79 us -> 8.71 us  [mixed_blocks(): pl.pallas_call(mix_kernel, out_shape=jax.ShapeDtypeStruct((blocks, tokens...]
  transfers between devices with their start and end apart: 13 -> 13, of which waited for: 6 -> 6; matrix products, arithmetic and copies ran while one was open for 3% -> 3% of each run, Pallas kernels for 6% -> 7%
where the time goes in v9:
time: 91.3 us; the launch traced here: 90.9 us
  starting transfers between devices  27.4 us (30%)
  Pallas kernels  21.4 us (23%)
  waiting for transfers between devices  17.5 us (19%)
  blocking collectives  17.3 us (19%)
  local copies, waits for them, and re-layouts  7.09 us (8%)
    all_to_all x1, blocking collectives, per_device(): result = lax.all_to_all(blocks, ('yh', 'x'), 0, 0, tiled=True)  17.3 us
    all_to_all x1, starting transfers between devices, per_device(): pieces = lax.all_to_all(load, ctx, 0, 0, tiled=True)  14.6 us
    ppermute x12, starting transfers between devices, shifted(): return lax.ppermute(value, axis, pairs)  12.7 us
    ppermute x12, waiting for transfers between devices, shifted(): return lax.ppermute(value, axis, pairs)  9.67 us
    pallas_call x1, Pallas kernels, mixed_blocks(): pl.pallas_call(mix_kernel, out_shape=jax.ShapeDtypeStruct((blocks, tokens...  8.71 us
    all_to_all x1, waiting for transfers between devices, per_device(): pieces = lax.all_to_all(load, ctx, 0, 0, tiled=True)  7.78 us
    unnamed x12, local copies, waits for them, and re-layouts  4.68 us
    pallas_call x1, Pallas kernels, normed_rows(): pl.pallas_call(norm_kernel, out_shape=(jax.ShapeDtypeStruct((4, vocab, wi...  3.78 us
  transfers between devices with their start and end apart: 13, of which 6 were waited for; matrix products, arithmetic and copies ran while one was open for 3% of the time, Pallas kernels for 7%

profile of v9, /device:TPU:8, one launch (start us, length us, event | category | flops | bytes accessed | tf_op | source)
XLA Modules:
  0.0 90.9 jit_solution(5369711412811070893)
XLA Ops:
  0.0 0.0 copy-start
  0.0 2.7 %payload.1 = (bf16[64,32,128]{2,1,0:T(8,128)(2,1)}, bf16[256,1024]{1,0:T(8,128)(2,1)}, bf16[256,1024]{1,0:T(8,128)(2,1)}) custom-call(bf16[3,64,1024]{2,1,0:T(8,128)(2,1)} %far_weight_ref.1, s32[4,128]{1,0:T(4,128)} %bitcast.10, bf16[512,1024]{1,0:T(8,128)(2,1)} %refs_0_.1), custom_call_target="tpu_custom_call" | custom-call | bytes 2900000 | tf_op jit(solution)/shard_map/payload/pallas_call | solution.py:81
  2.7 2.3 %collective-permute-start.1 = (bf16[256,1024]{1,0:T(8,128)(2,1)}, bf16[256,1024]{1,0:T(8,128)(2,1)S(1)}, u32[]{:S(2)}, u32[]{:S(2)}) collective-permute-start(bf16[256,1024]{1,0:T(8,128)(2,1)} %get-tuple-element.25), channel_id=1, source_target_pairs={{0,130},{2,0},{128,2},{130,128},{1,131},{3,1},{129,3},{131,129},{4... | collective-permute-start | bytes 1572872 | tf_op jit(solution)/shard_map/ppermute | solution.py:23
  5.0 0.0 collective-permute-start.2
  5.0 0.0 copy-done
  5.0 0.1 collective-permute-start
  5.1 14.6 %all-to-all-start = ((bf16[64,32,128]{2,1,0:T(8,128)(2,1)}), bf16[64,32,128]{2,1,0:T(8,128)(2,1)S(1)}, u32[]{:S(2)}, u32[]{:S(2)}) async-start(bf16[64,32,128]{2,1,0:T(8,128)(2,1)} %get-tuple-element.20), calls=%async_computation | async-start | bytes 1048576 | tf_op jit(solution)/shard_map/all_to_all | solution.py:477
  19.7 0.7 dynamic_slice.13
  20.4 0.0 collective-permute-done.1.refs_2_
  20.4 0.2 collective-permute-start.3
  20.7 0.0 collective-permute-done.2.refs_3_
  20.7 0.3 collective-permute-start.4
  21.0 0.7 constant_dynamic-slice_fusion.2
  21.7 0.1 fusion
  21.7 0.1 rev.3
  21.8 0.8 constant_dynamic-slice_fusion
  22.6 0.1 reshape.18.scale_ref
  22.7 0.1 pad.4.taps_ref
  22.7 0.4 toeplitz.1.refs_9_
  23.1 0.0 copy-start.3
  23.1 0.8 copy-done.3
  23.9 0.1 pad_add_fusion.spot_ref
  24.0 0.0 collective-permute-done.refs_1_
  24.0 0.0 collective-permute-done.3.refs_4_
  24.0 0.0 collective-permute-done.4.refs_5_
  24.0 0.0 copy-start.1
  24.0 1.2 %copy-done.1 = bf16[512,1024]{1,0:T(8,128)(2,1)S(1)} copy-done((bf16[512,1024]{1,0:T(8,128)(2,1)S(1)}, bf16[512,1024]{1,0:T(8,128)(2,1)}, u32[]{:S(2)}) %copy-start.1) | copy-done | bytes 1048600
  25.3 0.0 copy-start.5
  25.3 0.7 copy-done.5
  26.0 3.8 %normed_rows.1 = (bf16[4,512,1024]{2,1,0:T(8,128)(2,1)S(1)}, f32[8,128]{1,0:T(8,128)S(1)}) custom-call(s32[4]{0:T(128)S(1)} %pad_add_fusion.spot_ref, bf16[512,1024]{1,0:T(8,128)(2,1)S(1)} %copy-done.1, bf16[512,1024]{1,0:T(8,128)(2,1)S(1)} %collective-permute-done.refs_1_, bf16[256,1024]{1,0:T(8,128)(2,1)S(1)} %collective-permute-done.1.refs_2_, ...), custom_call_target="tpu_custom_call" | custom-call | flops 10485760 | bytes 8388608 | tf_op jit(solution)/shard_map/normed_rows/pallas_call | solution.py:126
  29.8 0.0 copy-start.2
  29.8 1.9 %copy-done.2 = bf16[4,512,1024]{2,1,0:T(8,128)(2,1)} copy-done((bf16[4,512,1024]{2,1,0:T(8,128)(2,1)}, bf16[4,512,1024]{2,1,0:T(8,128)(2,1)S(1)}, u32[]{:S(2)}) %copy-start.2) | copy-done | bytes 4194328
  31.7 0.0 copy-start.4
  31.7 7.8 %all-to-all-done.pieces_ref = bf16[64,32,128]{2,1,0:T(8,128)(2,1)S(1)} async-done(((bf16[64,32,128]{2,1,0:T(8,128)(2,1)}), bf16[64,32,128]{2,1,0:T(8,128)(2,1)S(1)}, u32[]{:S(2)}, u32[]{:S(2)}) %all-to-all-start) | async-done | bytes 524320 | tf_op jit(solution)/shard_map/all_to_all | solution.py:477
  39.5 3.1 %table_piece.1.refs_0_ = bf16[48,512]{1,0:T(8,128)(2,1)S(1)} custom-call(bf16[4,512,1024]{2,1,0:T(8,128)(2,1)} %copy-done.2, bf16[64,32,128]{2,1,0:T(8,128)(2,1)S(1)} %all-to-all-done.pieces_ref, f32[48,1]{1,0:T(8,128)S(1)} %reshape.18.scale_ref, f32[8,128]{1,0:T(8,128)S(1)} %get-tuple-element.32._), custom_call_target="tpu_custom_call" | custom-call | flops 201326592 | bytes 5000000 | tf_op jit(solution)/shard_map/table_piece/pallas_call | solution.py:182
  42.6 2.3 %collective-permute-start.5 = (bf16[48,512]{1,0:T(8,128)(2,1)S(1)}, bf16[48,512]{1,0:T(8,128)(2,1)S(1)}, u32[]{:S(2)}, u32[]{:S(2)}) collective-permute-start(bf16[48,512]{1,0:T(8,128)(2,1)S(1)} %table_piece.1.refs_0_), channel_id=1, source_target_pairs={{0,16},{16,32},{32,48},{48,64},{64,80},{80,96},{96,112},{112,0},{1... | collective-permute-start | bytes 147464 | tf_op jit(solution)/shard_map/ppermute | solution.py:23
  44.9 1.0 %collective-permute-start.9 = (bf16[48,512]{1,0:T(8,128)(2,1)S(1)}, bf16[48,512]{1,0:T(8,128)(2,1)S(1)}, u32[]{:S(2)}, u32[]{:S(2)}) collective-permute-start(bf16[48,512]{1,0:T(8,128)(2,1)S(1)} %table_piece.1.refs_0_), channel_id=1, source_target_pairs={{0,112},{16,0},{32,16},{48,32},{64,48},{80,64},{96,80},{112,96},{1... | collective-permute-start | bytes 147464 | tf_op jit(solution)/shard_map/ppermute | solution.py:23
  45.9 2.1 %collective-permute-done.5.refs_1_ = bf16[48,512]{1,0:T(8,128)(2,1)S(1)} collective-permute-done((bf16[48,512]{1,0:T(8,128)(2,1)S(1)}, bf16[48,512]{1,0:T(8,128)(2,1)S(1)}, u32[]{:S(2)}, u32[]{:S(2)}) %collective-permute-start.5) | collective-permute-done | bytes 49184 | tf_op jit(solution)/shard_map/ppermute | solution.py:23
  48.0 1.2 %collective-permute-start.6 = (bf16[48,512]{1,0:T(8,128)(2,1)S(1)}, bf16[48,512]{1,0:T(8,128)(2,1)S(1)}, u32[]{:S(2)}, u32[]{:S(2)}) collective-permute-start(bf16[48,512]{1,0:T(8,128)(2,1)S(1)} %collective-permute-done.5.refs_1_), channel_id=1, source_target_pairs={{0,16},{16,32},{32,48},{48,64},{64,80},{80,96},{96,112},{112,0},{1... | collective-permute-start | bytes 147464 | tf_op jit(solution)/shard_map/ppermute | solution.py:23
  49.1 0.2 collective-permute-done.9.refs_7_
  49.3 1.9 %collective-permute-start.10 = (bf16[48,512]{1,0:T(8,128)(2,1)S(1)}, bf16[48,512]{1,0:T(8,128)(2,1)S(1)}, u32[]{:S(2)}, u32[]{:S(2)}) collective-permute-start(bf16[48,512]{1,0:T(8,128)(2,1)S(1)} %collective-permute-done.9.refs_7_), channel_id=1, source_target_pairs={{0,112},{16,0},{32,16},{48,32},{64,48},{80,64},{96,80},{112,96},{1... | collective-permute-start | bytes 147464 | tf_op jit(solution)/shard_map/ppermute | solution.py:23
  51.2 2.1 %collective-permute-done.6.refs_2_ = bf16[48,512]{1,0:T(8,128)(2,1)S(1)} collective-permute-done((bf16[48,512]{1,0:T(8,128)(2,1)S(1)}, bf16[48,512]{1,0:T(8,128)(2,1)S(1)}, u32[]{:S(2)}, u32[]{:S(2)}) %collective-permute-start.6) | collective-permute-done | bytes 49184 | tf_op jit(solution)/shard_map/ppermute | solution.py:23
  53.3 0.2 collective-permute-start.7
  53.5 0.0 collective-permute-done.10.refs_6_
  53.5 3.3 %collective-permute-start.11 = (bf16[48,512]{1,0:T(8,128)(2,1)S(1)}, bf16[48,512]{1,0:T(8,128)(2,1)S(1)}, u32[]{:S(2)}, u32[]{:S(2)}) collective-permute-start(bf16[48,512]{1,0:T(8,128)(2,1)S(1)} %collective-permute-done.10.refs_6_), channel_id=1, source_target_pairs={{0,112},{16,0},{32,16},{48,32},{64,48},{80,64},{96,80},{112,96},{1... | collective-permute-start | bytes 147464 | tf_op jit(solution)/shard_map/ppermute | solution.py:23
  56.8 1.8 %collective-permute-done.7.refs_3_ = bf16[48,512]{1,0:T(8,128)(2,1)S(1)} collective-permute-done((bf16[48,512]{1,0:T(8,128)(2,1)S(1)}, bf16[48,512]{1,0:T(8,128)(2,1)S(1)}, u32[]{:S(2)}, u32[]{:S(2)}) %collective-permute-start.7) | collective-permute-done | bytes 49184 | tf_op jit(solution)/shard_map/ppermute | solution.py:23
  58.6 0.0 collective-permute-start.8
  58.6 1.8 %hot_rows.1 = (bf16[8,512,512]{2,1,0:T(8,128)(2,1)S(1)}, bf16[288,512]{1,0:T(8,128)(2,1)S(1)}) custom-call(s32[1]{0:T(128)} %bitcast.spot_ref, bf16[64,32,128]{2,1,0:T(8,128)(2,1)S(1)} %all-to-all-done.pieces_ref), custom_call_target="tpu_custom_call" | custom-call | flops 5000000 | bytes 4500000 | tf_op jit(solution)/shard_map/hot_rows/pallas_call | solution.py:260
  60.3 0.0 collective-permute-done.11.refs_5_
  60.4 3.5 %collective-permute-done.8.refs_4_ = bf16[48,512]{1,0:T(8,128)(2,1)S(1)} collective-permute-done((bf16[48,512]{1,0:T(8,128)(2,1)S(1)}, bf16[48,512]{1,0:T(8,128)(2,1)S(1)}, u32[]{:S(2)}, u32[]{:S(2)}) %collective-permute-start.8) | collective-permute-done | bytes 49184 | tf_op jit(solution)/shard_map/ppermute | solution.py:23
  63.9 0.0 copy-done.4
  63.9 8.7 %mixed_blocks.1 = bf16[8,512,128]{2,1,0:T(8,128)(2,1)S(1)} custom-call(s32[1]{0:T(128)} %bitcast.spot_ref, bf16[8,512,512]{2,1,0:T(8,128)(2,1)S(1)} %get-tuple-element.29.hot_ref, bf16[288,512]{1,0:T(8,128)(2,1)S(1)} %get-tuple-element.30.lead_hot_ref, bf16[48,512]{1,0:T(8,128)(2,1)S(1)} %table_piece.1.refs_0_, ...), custom_call_target="tpu_custom_call" | custom-call | flops 5000000000 | bytes 6000000 | tf_op jit(solution)/shard_map/mixed_blocks/pallas_call | solution.py:401
  72.6 17.3 %all_to_all.10.blocks_ref = bf16[8,512,128]{2,1,0:T(8,128)(2,1)S(1)} all-to-all(bf16[8,512,128]{2,1,0:T(8,128)(2,1)S(1)} %mixed_blocks.1), channel_id=1, replica_groups=mesh['yh'=2,'z'=8,'x'=4,'yl'=2,'core'=2] {'yh','x'}, dimensions={0} | all-to-all | bytes 2097152 | tf_op jit(solution)/shard_map/all_to_all | solution.py:514
  89.9 1.0 %placed_columns.1 = bf16[512,1024]{1,0:T(8,128)(2,1)} custom-call(bf16[8,512,128]{2,1,0:T(8,128)(2,1)S(1)} %all_to_all.10.blocks_ref), custom_call_target="tpu_custom_call" | custom-call | bytes 2000000 | tf_op jit(solution)/shard_map/placed_columns/pallas_call | solution.py:448
  (2 shorter events, 0.0 us)
Async XLA Ops:
  0.0 5.0 %copy-start = (f32[3,7,1024]{2,1,0:T(8,128)S(1)}, f32[3,7,1024]{2,1,0:T(8,128)}, u32[]{:S(2)}) copy-start(f32[3,7,1024]{2,1,0:T(8,128)} %param.13) | copy-start | bytes 258052
  2.7 17.8 %collective-permute-start.1 = (bf16[256,1024]{1,0:T(8,128)(2,1)}, bf16[256,1024]{1,0:T(8,128)(2,1)S(1)}, u32[]{:S(2)}, u32[]{:S(2)}) collective-permute-start(bf16[256,1024]{1,0:T(8,128)(2,1)} %get-tuple-element.25), channel_id=1, source_target_pairs={{0,130},{2,0},{128,2},{130,128},{1,131},{3,1},{129,3},{131,129},{4... | collective-permute-start | bytes 1572872 | tf_op jit(solution)/shard_map/ppermute | solution.py:23
  5.0 15.7 %collective-permute-start.2 = (bf16[256,1024]{1,0:T(8,128)(2,1)}, bf16[256,1024]{1,0:T(8,128)(2,1)S(1)}, u32[]{:S(2)}, u32[]{:S(2)}) collective-permute-start(bf16[256,1024]{1,0:T(8,128)(2,1)} %get-tuple-element.26), channel_id=1, source_target_pairs={{0,2},{2,128},{128,130},{130,0},{1,3},{3,129},{129,131},{131,1},{4... | collective-permute-start | bytes 1572872 | tf_op jit(solution)/shard_map/ppermute | solution.py:23
  5.0 19.1 %collective-permute-start = (bf16[512,1024]{1,0:T(8,128)(2,1)}, bf16[512,1024]{1,0:T(8,128)(2,1)S(1)}, u32[]{:S(2)}, u32[]{:S(2)}) collective-permute-start(bf16[512,1024]{1,0:T(8,128)(2,1)} %refs_0_.1), channel_id=1, source_target_pairs={{0,1},{1,0},{2,3},{3,2},{4,5},{5,4},{6,7},{7,6},{8,9},{9,8},{10,11... | collective-permute-start | bytes 3145736 | tf_op jit(solution)/shard_map/ppermute | solution.py:23
  5.1 34.4 %all-to-all-start = ((bf16[64,32,128]{2,1,0:T(8,128)(2,1)}), bf16[64,32,128]{2,1,0:T(8,128)(2,1)S(1)}, u32[]{:S(2)}, u32[]{:S(2)}) async-start(bf16[64,32,128]{2,1,0:T(8,128)(2,1)} %get-tuple-element.20), calls=%async_computation | async-start | bytes 1048576 | tf_op jit(solution)/shard_map/all_to_all | solution.py:477
  20.4 3.6 %collective-permute-start.3 = (bf16[256,1024]{1,0:T(8,128)(2,1)S(1)}, bf16[256,1024]{1,0:T(8,128)(2,1)S(1)}, u32[]{:S(2)}, u32[]{:S(2)}) collective-permute-start(bf16[256,1024]{1,0:T(8,128)(2,1)S(1)} %collective-permute-done.1.refs_2_), channel_id=1, source_target_pairs={{0,1},{1,0},{2,3},{3,2},{4,5},{5,4},{6,7},{7,6},{8,9},{9,8},{10,11... | collective-permute-start | bytes 1572872 | tf_op jit(solution)/shard_map/ppermute | solution.py:23
  20.7 3.4 %collective-permute-start.4 = (bf16[256,1024]{1,0:T(8,128)(2,1)S(1)}, bf16[256,1024]{1,0:T(8,128)(2,1)}, u32[]{:S(2)}, u32[]{:S(2)}) collective-permute-start(bf16[256,1024]{1,0:T(8,128)(2,1)S(1)} %collective-permute-done.2.refs_3_), channel_id=1, source_target_pairs={{0,1},{1,0},{2,3},{3,2},{4,5},{5,4},{6,7},{7,6},{8,9},{9,8},{10,11... | collective-permute-start | bytes 1572872 | tf_op jit(solution)/shard_map/ppermute | solution.py:23
  23.1 0.8 copy-start.3
  24.0 1.2 %copy-start.1 = (bf16[512,1024]{1,0:T(8,128)(2,1)S(1)}, bf16[512,1024]{1,0:T(8,128)(2,1)}, u32[]{:S(2)}) copy-start(bf16[512,1024]{1,0:T(8,128)(2,1)} %refs_0_.1) | copy-start | bytes 3145732
  25.3 0.7 copy-start.5
  29.8 1.9 %copy-start.2 = (bf16[4,512,1024]{2,1,0:T(8,128)(2,1)}, bf16[4,512,1024]{2,1,0:T(8,128)(2,1)S(1)}, u32[]{:S(2)}) copy-start(bf16[4,512,1024]{2,1,0:T(8,128)(2,1)S(1)} %get-tuple-element.31.far_ref) | copy-start | bytes 12582916
  31.7 32.2 %copy-start.4 = (bf16[8,256,128]{2,1,0:T(8,128)(2,1)S(1)}, bf16[8,256,128]{2,1,0:T(8,128)(2,1)}, u32[]{:S(2)}) copy-start(bf16[8,256,128]{2,1,0:T(8,128)(2,1)} %copy-done.3) | copy-start | bytes 1572868
  42.6 5.4 %collective-permute-start.5 = (bf16[48,512]{1,0:T(8,128)(2,1)S(1)}, bf16[48,512]{1,0:T(8,128)(2,1)S(1)}, u32[]{:S(2)}, u32[]{:S(2)}) collective-permute-start(bf16[48,512]{1,0:T(8,128)(2,1)S(1)} %table_piece.1.refs_0_), channel_id=1, source_target_pairs={{0,16},{16,32},{32,48},{48,64},{64,80},{80,96},{96,112},{112,0},{1... | collective-permute-start | bytes 147464 | tf_op jit(solution)/shard_map/ppermute | solution.py:23
  44.9 4.5 %collective-permute-start.9 = (bf16[48,512]{1,0:T(8,128)(2,1)S(1)}, bf16[48,512]{1,0:T(8,128)(2,1)S(1)}, u32[]{:S(2)}, u32[]{:S(2)}) collective-permute-start(bf16[48,512]{1,0:T(8,128)(2,1)S(1)} %table_piece.1.refs_0_), channel_id=1, source_target_pairs={{0,112},{16,0},{32,16},{48,32},{64,48},{80,64},{96,80},{112,96},{1... | collective-permute-start | bytes 147464 | tf_op jit(solution)/shard_map/ppermute | solution.py:23
  48.0 5.3 %collective-permute-start.6 = (bf16[48,512]{1,0:T(8,128)(2,1)S(1)}, bf16[48,512]{1,0:T(8,128)(2,1)S(1)}, u32[]{:S(2)}, u32[]{:S(2)}) collective-permute-start(bf16[48,512]{1,0:T(8,128)(2,1)S(1)} %collective-permute-done.5.refs_1_), channel_id=1, source_target_pairs={{0,16},{16,32},{32,48},{48,64},{64,80},{80,96},{96,112},{112,0},{1... | collective-permute-start | bytes 147464 | tf_op jit(solution)/shard_map/ppermute | solution.py:23
  49.3 4.2 %collective-permute-start.10 = (bf16[48,512]{1,0:T(8,128)(2,1)S(1)}, bf16[48,512]{1,0:T(8,128)(2,1)S(1)}, u32[]{:S(2)}, u32[]{:S(2)}) collective-permute-start(bf16[48,512]{1,0:T(8,128)(2,1)S(1)} %collective-permute-done.9.refs_7_), channel_id=1, source_target_pairs={{0,112},{16,0},{32,16},{48,32},{64,48},{80,64},{96,80},{112,96},{1... | collective-permute-start | bytes 147464 | tf_op jit(solution)/shard_map/ppermute | solution.py:23
  53.3 5.3 %collective-permute-start.7 = (bf16[48,512]{1,0:T(8,128)(2,1)S(1)}, bf16[48,512]{1,0:T(8,128)(2,1)S(1)}, u32[]{:S(2)}, u32[]{:S(2)}) collective-permute-start(bf16[48,512]{1,0:T(8,128)(2,1)S(1)} %collective-permute-done.6.refs_2_), channel_id=1, source_target_pairs={{0,16},{16,32},{32,48},{48,64},{64,80},{80,96},{96,112},{112,0},{1... | collective-permute-start | bytes 147464 | tf_op jit(solution)/shard_map/ppermute | solution.py:23
  53.5 6.8 %collective-permute-start.11 = (bf16[48,512]{1,0:T(8,128)(2,1)S(1)}, bf16[48,512]{1,0:T(8,128)(2,1)S(1)}, u32[]{:S(2)}, u32[]{:S(2)}) collective-permute-start(bf16[48,512]{1,0:T(8,128)(2,1)S(1)} %collective-permute-done.10.refs_6_), channel_id=1, source_target_pairs={{0,112},{16,0},{32,16},{48,32},{64,48},{80,64},{96,80},{112,96},{1... | collective-permute-start | bytes 147464 | tf_op jit(solution)/shard_map/ppermute | solution.py:23
  58.6 5.3 %collective-permute-start.8 = (bf16[48,512]{1,0:T(8,128)(2,1)S(1)}, bf16[48,512]{1,0:T(8,128)(2,1)S(1)}, u32[]{:S(2)}, u32[]{:S(2)}) collective-permute-start(bf16[48,512]{1,0:T(8,128)(2,1)S(1)} %collective-permute-done.7.refs_3_), channel_id=1, source_target_pairs={{0,16},{16,32},{32,48},{48,64},{64,80},{80,96},{96,112},{112,0},{1... | collective-permute-start | bytes 147464 | tf_op jit(solution)/shard_map/ppermute | solution.py:23

commit v10 on v9

--- a/solution.py
+++ b/solution.py
@@ -367,11 +367,6 @@
 
     @pl.when(step >= 0)
     def _():
-        for j in range(count):
-            at = j * LONG_TAPS
-            conv = jnp.transpose(conv_ref[j])
-            out_ref[0, at : at + LONG_TAPS, :] = (gate_ref[at : at + LONG_TAPS, :] * conv).astype(BF)
-
         starts = step % 4 == 0
         segment = jnp.minimum(step // 4, 1)
         for p in range(STREAMS):
@@ -379,6 +374,10 @@
                 starts, head_ref[segment, p], proj_ref[p, tokens:, :]
             )
             proj_ref[p, margin:, :] = next_ref[p]
+        for j in range(count):
+            at = j * LONG_TAPS
+            conv = jnp.transpose(conv_ref[j])
+            out_ref[0, at : at + LONG_TAPS, :] = (gate_ref[at : at + LONG_TAPS, :] * conv).astype(BF)
         starts = (step + 3) % 4 == 0
         segment = jnp.minimum((step + 3) // 4 - 1, 1)
         segment = jnp.maximum(segment, 0)
@@ -501,15 +500,17 @@
     )
     normed = pltpu.with_memory_space_constraint(normed, pltpu.HBM)
     piece = table_piece(normed, pieces, scale, token)
+    spot = z.reshape(1).astype(jnp.int32)
+    hot, lead_hot = hot_rows(spot, pieces, tiles, tokens, vocab)
     ups, downs, last = [piece], [], piece
     for step in range(4):
+        if step == 3:
+            ups[-1], hot, lead_hot = lax.optimization_barrier((ups[-1], hot, lead_hot))
         ups.append(shifted(ups[-1], "z", 1))
         if step < 3:
             last = shifted(last, "z", -1)
             downs.append(last)
 
-    spot = z.reshape(1).astype(jnp.int32)
-    hot, lead_hot = hot_rows(spot, pieces, tiles, tokens, vocab)
     blocks = mixed_blocks(spot, hot, lead_hot, ups + downs[::-1], near_filter, toep)
     result = lax.all_to_all(blocks, ("yh", "x"), 0, 0, tiled=True)
     return placed_columns(result)

time: 91.3 us -> 91.4 us (level)
  transfers between devices with their start and end apart: 13 -> 13, of which waited for: 6 -> 7; matrix products, arithmetic and copies ran while one was open for 3% -> 3% of each run, Pallas kernels for 7% -> 7%
where the time goes in v10:
time: 91.4 us; the launch traced here: 91 us
  starting transfers between devices  27.2 us (30%)
  Pallas kernels  21.4 us (23%)
  waiting for transfers between devices  18 us (20%)
  blocking collectives  17 us (19%)
  local copies, waits for them, and re-layouts  7.09 us (8%)
    all_to_all x1, blocking collectives, per_device(): result = lax.all_to_all(blocks, ('yh', 'x'), 0, 0, tiled=True)  17 us
    all_to_all x1, starting transfers between devices, per_device(): pieces = lax.all_to_all(load, ctx, 0, 0, tiled=True)  14.6 us
    ppermute x12, starting transfers between devices, shifted(): return lax.ppermute(value, axis, pairs)  12.6 us
    ppermute x12, waiting for transfers between devices, shifted(): return lax.ppermute(value, axis, pairs)  10.2 us
    pallas_call x1, Pallas kernels, mixed_blocks(): pl.pallas_call(mix_kernel, out_shape=jax.ShapeDtypeStruct((blocks, tokens...  8.72 us
    all_to_all x1, waiting for transfers between devices, per_device(): pieces = lax.all_to_all(load, ctx, 0, 0, tiled=True)  7.78 us
    unnamed x12, local copies, waits for them, and re-layouts  4.68 us
    pallas_call x1, Pallas kernels, normed_rows(): pl.pallas_call(norm_kernel, out_shape=(jax.ShapeDtypeStruct((4, vocab, wi...  3.78 us
  transfers between devices with their start and end apart: 13, of which 7 were waited for; matrix products, arithmetic and copies ran while one was open for 3% of the time, Pallas kernels for 7%

profile of v10, /device:TPU:8, one launch (start us, length us, event | category | flops | bytes accessed | tf_op | source)
XLA Modules:
  0.0 91.0 jit_solution(6596723477129905011)
XLA Ops:
  0.0 0.0 copy-start
  0.0 2.7 %payload.1 = (bf16[64,32,128]{2,1,0:T(8,128)(2,1)}, bf16[256,1024]{1,0:T(8,128)(2,1)}, bf16[256,1024]{1,0:T(8,128)(2,1)}) custom-call(bf16[3,64,1024]{2,1,0:T(8,128)(2,1)} %far_weight_ref.1, s32[4,128]{1,0:T(4,128)} %bitcast.10, bf16[512,1024]{1,0:T(8,128)(2,1)} %refs_0_.1), custom_call_target="tpu_custom_call" | custom-call | bytes 2900000 | tf_op jit(solution)/shard_map/payload/pallas_call | solution.py:81
  2.7 2.3 %collective-permute-start.1 = (bf16[256,1024]{1,0:T(8,128)(2,1)}, bf16[256,1024]{1,0:T(8,128)(2,1)S(1)}, u32[]{:S(2)}, u32[]{:S(2)}) collective-permute-start(bf16[256,1024]{1,0:T(8,128)(2,1)} %get-tuple-element.24), channel_id=1, source_target_pairs={{0,130},{2,0},{128,2},{130,128},{1,131},{3,1},{129,3},{131,129},{4... | collective-permute-start | bytes 1572872 | tf_op jit(solution)/shard_map/ppermute | solution.py:23
  5.0 0.0 collective-permute-start.2
  5.0 0.0 copy-done
  5.0 0.1 collective-permute-start
  5.1 14.6 %all-to-all-start = ((bf16[64,32,128]{2,1,0:T(8,128)(2,1)}), bf16[64,32,128]{2,1,0:T(8,128)(2,1)S(1)}, u32[]{:S(2)}, u32[]{:S(2)}) async-start(bf16[64,32,128]{2,1,0:T(8,128)(2,1)} %get-tuple-element.27), calls=%async_computation | async-start | bytes 1048576 | tf_op jit(solution)/shard_map/all_to_all | solution.py:476
  19.7 0.7 dynamic_slice.14
  20.4 0.0 collective-permute-done.1.refs_2_
  20.5 0.2 collective-permute-start.3
  20.7 0.0 collective-permute-done.2.refs_3_
  20.7 0.3 collective-permute-start.4
  21.0 0.7 constant_dynamic-slice_fusion.1
  21.7 0.1 fusion
  21.8 0.1 rev.3
  21.8 0.8 constant_dynamic-slice_fusion
  22.6 0.1 reshape.18.scale_ref
  22.7 0.1 pad.4.taps_ref
  22.7 0.4 toeplitz.1.refs_9_
  23.1 0.0 copy-start.3
  23.1 0.8 copy-done.3
  23.9 0.1 pad_add_fusion.spot_ref
  24.0 0.0 collective-permute-done.refs_1_
  24.0 0.0 collective-permute-done.3.refs_4_
  24.0 0.0 collective-permute-done.4.refs_5_
  24.0 0.0 copy-start.1
  24.1 1.2 %copy-done.1 = bf16[512,1024]{1,0:T(8,128)(2,1)S(1)} copy-done((bf16[512,1024]{1,0:T(8,128)(2,1)S(1)}, bf16[512,1024]{1,0:T(8,128)(2,1)}, u32[]{:S(2)}) %copy-start.1) | copy-done | bytes 1048600
  25.3 0.0 copy-start.5
  25.3 0.7 copy-done.5
  26.0 3.8 %normed_rows.1 = (bf16[4,512,1024]{2,1,0:T(8,128)(2,1)S(1)}, f32[8,128]{1,0:T(8,128)S(1)}) custom-call(s32[4]{0:T(128)S(1)} %pad_add_fusion.spot_ref, bf16[512,1024]{1,0:T(8,128)(2,1)S(1)} %copy-done.1, bf16[512,1024]{1,0:T(8,128)(2,1)S(1)} %collective-permute-done.refs_1_, bf16[256,1024]{1,0:T(8,128)(2,1)S(1)} %collective-permute-done.1.refs_2_, ...), custom_call_target="tpu_custom_call" | custom-call | flops 10485760 | bytes 8388608 | tf_op jit(solution)/shard_map/normed_rows/pallas_call | solution.py:126
  29.8 0.0 copy-start.2
  29.8 1.9 %copy-done.2 = bf16[4,512,1024]{2,1,0:T(8,128)(2,1)} copy-done((bf16[4,512,1024]{2,1,0:T(8,128)(2,1)}, bf16[4,512,1024]{2,1,0:T(8,128)(2,1)S(1)}, u32[]{:S(2)}) %copy-start.2) | copy-done | bytes 4194328
  31.7 0.0 copy-start.4
  31.7 7.8 %all-to-all-done.pieces_ref = bf16[64,32,128]{2,1,0:T(8,128)(2,1)S(1)} async-done(((bf16[64,32,128]{2,1,0:T(8,128)(2,1)}), bf16[64,32,128]{2,1,0:T(8,128)(2,1)S(1)}, u32[]{:S(2)}, u32[]{:S(2)}) %all-to-all-start) | async-done | bytes 524320 | tf_op jit(solution)/shard_map/all_to_all | solution.py:476
  39.5 3.1 %table_piece.1.refs_0_ = bf16[48,512]{1,0:T(8,128)(2,1)S(1)} custom-call(bf16[4,512,1024]{2,1,0:T(8,128)(2,1)} %copy-done.2, bf16[64,32,128]{2,1,0:T(8,128)(2,1)S(1)} %all-to-all-done.pieces_ref, f32[48,1]{1,0:T(8,128)S(1)} %reshape.18.scale_ref, f32[8,128]{1,0:T(8,128)S(1)} %get-tuple-element.33._), custom_call_target="tpu_custom_call" | custom-call | flops 201326592 | bytes 5000000 | tf_op jit(solution)/shard_map/table_piece/pallas_call | solution.py:182
  42.6 2.3 %collective-permute-start.5 = (bf16[48,512]{1,0:T(8,128)(2,1)S(1)}, bf16[48,512]{1,0:T(8,128)(2,1)S(1)}, u32[]{:S(2)}, u32[]{:S(2)}) collective-permute-start(bf16[48,512]{1,0:T(8,128)(2,1)S(1)} %table_piece.1.refs_0_), channel_id=1, source_target_pairs={{0,16},{16,32},{32,48},{48,64},{64,80},{80,96},{96,112},{112,0},{1... | collective-permute-start | bytes 147464 | tf_op jit(solution)/shard_map/ppermute | solution.py:23
  44.9 1.0 %collective-permute-start.9 = (bf16[48,512]{1,0:T(8,128)(2,1)S(1)}, bf16[48,512]{1,0:T(8,128)(2,1)S(1)}, u32[]{:S(2)}, u32[]{:S(2)}) collective-permute-start(bf16[48,512]{1,0:T(8,128)(2,1)S(1)} %table_piece.1.refs_0_), channel_id=1, source_target_pairs={{0,112},{16,0},{32,16},{48,32},{64,48},{80,64},{96,80},{112,96},{1... | collective-permute-start | bytes 147464 | tf_op jit(solution)/shard_map/ppermute | solution.py:23
  45.9 2.1 %collective-permute-done.5.refs_1_ = bf16[48,512]{1,0:T(8,128)(2,1)S(1)} collective-permute-done((bf16[48,512]{1,0:T(8,128)(2,1)S(1)}, bf16[48,512]{1,0:T(8,128)(2,1)S(1)}, u32[]{:S(2)}, u32[]{:S(2)}) %collective-permute-start.5) | collective-permute-done | bytes 49184 | tf_op jit(solution)/shard_map/ppermute | solution.py:23
  48.0 1.2 %collective-permute-start.6 = (bf16[48,512]{1,0:T(8,128)(2,1)S(1)}, bf16[48,512]{1,0:T(8,128)(2,1)S(1)}, u32[]{:S(2)}, u32[]{:S(2)}) collective-permute-start(bf16[48,512]{1,0:T(8,128)(2,1)S(1)} %collective-permute-done.5.refs_1_), channel_id=1, source_target_pairs={{0,16},{16,32},{32,48},{48,64},{64,80},{80,96},{96,112},{112,0},{1... | collective-permute-start | bytes 147464 | tf_op jit(solution)/shard_map/ppermute | solution.py:23
  49.1 0.2 collective-permute-done.9.refs_7_
  49.3 1.9 %collective-permute-start.10 = (bf16[48,512]{1,0:T(8,128)(2,1)S(1)}, bf16[48,512]{1,0:T(8,128)(2,1)S(1)}, u32[]{:S(2)}, u32[]{:S(2)}) collective-permute-start(bf16[48,512]{1,0:T(8,128)(2,1)S(1)} %collective-permute-done.9.refs_7_), channel_id=1, source_target_pairs={{0,112},{16,0},{32,16},{48,32},{64,48},{80,64},{96,80},{112,96},{1... | collective-permute-start | bytes 147464 | tf_op jit(solution)/shard_map/ppermute | solution.py:23
  51.2 2.1 %collective-permute-done.6.refs_2_ = bf16[48,512]{1,0:T(8,128)(2,1)S(1)} collective-permute-done((bf16[48,512]{1,0:T(8,128)(2,1)S(1)}, bf16[48,512]{1,0:T(8,128)(2,1)S(1)}, u32[]{:S(2)}, u32[]{:S(2)}) %collective-permute-start.6) | collective-permute-done | bytes 49184 | tf_op jit(solution)/shard_map/ppermute | solution.py:23
  53.3 0.2 collective-permute-start.7
  53.5 1.8 %hot_rows.1 = (bf16[8,512,512]{2,1,0:T(8,128)(2,1)S(1)}, bf16[288,512]{1,0:T(8,128)(2,1)S(1)}) custom-call(s32[1]{0:T(128)} %bitcast.spot_ref, bf16[64,32,128]{2,1,0:T(8,128)(2,1)S(1)} %all-to-all-done.pieces_ref), custom_call_target="tpu_custom_call" | custom-call | flops 5000000 | bytes 4500000 | tf_op jit(solution)/shard_map/hot_rows/pallas_call | solution.py:260
  55.3 0.0 collective-permute-done.10.refs_6_
  55.3 3.1 %collective-permute-start.11 = (bf16[48,512]{1,0:T(8,128)(2,1)S(1)}, bf16[48,512]{1,0:T(8,128)(2,1)S(1)}, u32[]{:S(2)}, u32[]{:S(2)}) collective-permute-start(bf16[48,512]{1,0:T(8,128)(2,1)S(1)} %collective-permute-done.10.refs_6_), channel_id=1, source_target_pairs={{0,112},{16,0},{32,16},{48,32},{64,48},{80,64},{96,80},{112,96},{1... | collective-permute-start | bytes 147464 | tf_op jit(solution)/shard_map/ppermute | solution.py:23
  58.3 0.6 collective-permute-done.7.refs_3_
  59.0 0.0 collective-permute-start.8
  59.0 1.1 %collective-permute-done.11.refs_5_ = bf16[48,512]{1,0:T(8,128)(2,1)S(1)} collective-permute-done((bf16[48,512]{1,0:T(8,128)(2,1)S(1)}, bf16[48,512]{1,0:T(8,128)(2,1)S(1)}, u32[]{:S(2)}, u32[]{:S(2)}) %collective-permute-start.11) | collective-permute-done | bytes 49184 | tf_op jit(solution)/shard_map/ppermute | solution.py:23
  60.1 4.2 %collective-permute-done.8.refs_4_ = bf16[48,512]{1,0:T(8,128)(2,1)S(1)} collective-permute-done((bf16[48,512]{1,0:T(8,128)(2,1)S(1)}, bf16[48,512]{1,0:T(8,128)(2,1)S(1)}, u32[]{:S(2)}, u32[]{:S(2)}) %collective-permute-start.8) | collective-permute-done | bytes 49184 | tf_op jit(solution)/shard_map/ppermute | solution.py:23
  64.3 0.0 copy-done.4
  64.3 8.7 %mixed_blocks.1 = bf16[8,512,128]{2,1,0:T(8,128)(2,1)S(1)} custom-call(s32[1]{0:T(128)} %bitcast.spot_ref, bf16[8,512,512]{2,1,0:T(8,128)(2,1)S(1)} %get-tuple-element.36.hot_ref, bf16[288,512]{1,0:T(8,128)(2,1)S(1)} %get-tuple-element.37.lead_hot_ref, bf16[48,512]{1,0:T(8,128)(2,1)S(1)} %table_piece.1.refs_0_, ...), custom_call_target="tpu_custom_call" | custom-call | flops 5000000000 | bytes 6000000 | tf_op jit(solution)/shard_map/mixed_blocks/pallas_call | solution.py:400
  73.0 17.0 %all_to_all.10.blocks_ref = bf16[8,512,128]{2,1,0:T(8,128)(2,1)S(1)} all-to-all(bf16[8,512,128]{2,1,0:T(8,128)(2,1)S(1)} %mixed_blocks.1), channel_id=1, replica_groups=mesh['yh'=2,'z'=8,'x'=4,'yl'=2,'core'=2] {'yh','x'}, dimensions={0} | all-to-all | bytes 2097152 | tf_op jit(solution)/shard_map/all_to_all | solution.py:515
  90.0 1.0 %placed_columns.1 = bf16[512,1024]{1,0:T(8,128)(2,1)} custom-call(bf16[8,512,128]{2,1,0:T(8,128)(2,1)S(1)} %all_to_all.10.blocks_ref), custom_call_target="tpu_custom_call" | custom-call | bytes 2000000 | tf_op jit(solution)/shard_map/placed_columns/pallas_call | solution.py:447
  (2 shorter events, 0.0 us)
Async XLA Ops:
  0.0 5.0 %copy-start = (f32[3,7,1024]{2,1,0:T(8,128)S(1)}, f32[3,7,1024]{2,1,0:T(8,128)}, u32[]{:S(2)}) copy-start(f32[3,7,1024]{2,1,0:T(8,128)} %param.13) | copy-start | bytes 258052
  2.7 17.8 %collective-permute-start.1 = (bf16[256,1024]{1,0:T(8,128)(2,1)}, bf16[256,1024]{1,0:T(8,128)(2,1)S(1)}, u32[]{:S(2)}, u32[]{:S(2)}) collective-permute-start(bf16[256,1024]{1,0:T(8,128)(2,1)} %get-tuple-element.24), channel_id=1, source_target_pairs={{0,130},{2,0},{128,2},{130,128},{1,131},{3,1},{129,3},{131,129},{4... | collective-permute-start | bytes 1572872 | tf_op jit(solution)/shard_map/ppermute | solution.py:23
  5.0 15.7 %collective-permute-start.2 = (bf16[256,1024]{1,0:T(8,128)(2,1)}, bf16[256,1024]{1,0:T(8,128)(2,1)S(1)}, u32[]{:S(2)}, u32[]{:S(2)}) collective-permute-start(bf16[256,1024]{1,0:T(8,128)(2,1)} %get-tuple-element.25), channel_id=1, source_target_pairs={{0,2},{2,128},{128,130},{130,0},{1,3},{3,129},{129,131},{131,1},{4... | collective-permute-start | bytes 1572872 | tf_op jit(solution)/shard_map/ppermute | solution.py:23
  5.0 19.1 %collective-permute-start = (bf16[512,1024]{1,0:T(8,128)(2,1)}, bf16[512,1024]{1,0:T(8,128)(2,1)S(1)}, u32[]{:S(2)}, u32[]{:S(2)}) collective-permute-start(bf16[512,1024]{1,0:T(8,128)(2,1)} %refs_0_.1), channel_id=1, source_target_pairs={{0,1},{1,0},{2,3},{3,2},{4,5},{5,4},{6,7},{7,6},{8,9},{9,8},{10,11... | collective-permute-start | bytes 3145736 | tf_op jit(solution)/shard_map/ppermute | solution.py:23
  5.1 34.4 %all-to-all-start = ((bf16[64,32,128]{2,1,0:T(8,128)(2,1)}), bf16[64,32,128]{2,1,0:T(8,128)(2,1)S(1)}, u32[]{:S(2)}, u32[]{:S(2)}) async-start(bf16[64,32,128]{2,1,0:T(8,128)(2,1)} %get-tuple-element.27), calls=%async_computation | async-start | bytes 1048576 | tf_op jit(solution)/shard_map/all_to_all | solution.py:476
  20.5 3.6 %collective-permute-start.3 = (bf16[256,1024]{1,0:T(8,128)(2,1)S(1)}, bf16[256,1024]{1,0:T(8,128)(2,1)S(1)}, u32[]{:S(2)}, u32[]{:S(2)}) collective-permute-start(bf16[256,1024]{1,0:T(8,128)(2,1)S(1)} %collective-permute-done.1.refs_2_), channel_id=1, source_target_pairs={{0,1},{1,0},{2,3},{3,2},{4,5},{5,4},{6,7},{7,6},{8,9},{9,8},{10,11... | collective-permute-start | bytes 1572872 | tf_op jit(solution)/shard_map/ppermute | solution.py:23
  20.7 3.4 %collective-permute-start.4 = (bf16[256,1024]{1,0:T(8,128)(2,1)S(1)}, bf16[256,1024]{1,0:T(8,128)(2,1)}, u32[]{:S(2)}, u32[]{:S(2)}) collective-permute-start(bf16[256,1024]{1,0:T(8,128)(2,1)S(1)} %collective-permute-done.2.refs_3_), channel_id=1, source_target_pairs={{0,1},{1,0},{2,3},{3,2},{4,5},{5,4},{6,7},{7,6},{8,9},{9,8},{10,11... | collective-permute-start | bytes 1572872 | tf_op jit(solution)/shard_map/ppermute | solution.py:23
  23.1 0.8 copy-start.3
  24.0 1.2 %copy-start.1 = (bf16[512,1024]{1,0:T(8,128)(2,1)S(1)}, bf16[512,1024]{1,0:T(8,128)(2,1)}, u32[]{:S(2)}) copy-start(bf16[512,1024]{1,0:T(8,128)(2,1)} %refs_0_.1) | copy-start | bytes 3145732
  25.3 0.7 copy-start.5
  29.8 1.9 %copy-start.2 = (bf16[4,512,1024]{2,1,0:T(8,128)(2,1)}, bf16[4,512,1024]{2,1,0:T(8,128)(2,1)S(1)}, u32[]{:S(2)}) copy-start(bf16[4,512,1024]{2,1,0:T(8,128)(2,1)S(1)} %get-tuple-element.26.far_ref) | copy-start | bytes 12582916
  31.7 32.5 %copy-start.4 = (bf16[8,256,128]{2,1,0:T(8,128)(2,1)S(1)}, bf16[8,256,128]{2,1,0:T(8,128)(2,1)}, u32[]{:S(2)}) copy-start(bf16[8,256,128]{2,1,0:T(8,128)(2,1)} %copy-done.3) | copy-start | bytes 1572868
  42.6 5.4 %collective-permute-start.5 = (bf16[48,512]{1,0:T(8,128)(2,1)S(1)}, bf16[48,512]{1,0:T(8,128)(2,1)S(1)}, u32[]{:S(2)}, u32[]{:S(2)}) collective-permute-start(bf16[48,512]{1,0:T(8,128)(2,1)S(1)} %table_piece.1.refs_0_), channel_id=1, source_target_pairs={{0,16},{16,32},{32,48},{48,64},{64,80},{80,96},{96,112},{112,0},{1... | collective-permute-start | bytes 147464 | tf_op jit(solution)/shard_map/ppermute | solution.py:23
  44.9 4.5 %collective-permute-start.9 = (bf16[48,512]{1,0:T(8,128)(2,1)S(1)}, bf16[48,512]{1,0:T(8,128)(2,1)S(1)}, u32[]{:S(2)}, u32[]{:S(2)}) collective-permute-start(bf16[48,512]{1,0:T(8,128)(2,1)S(1)} %table_piece.1.refs_0_), channel_id=1, source_target_pairs={{0,112},{16,0},{32,16},{48,32},{64,48},{80,64},{96,80},{112,96},{1... | collective-permute-start | bytes 147464 | tf_op jit(solution)/shard_map/ppermute | solution.py:23
  48.0 5.3 %collective-permute-start.6 = (bf16[48,512]{1,0:T(8,128)(2,1)S(1)}, bf16[48,512]{1,0:T(8,128)(2,1)S(1)}, u32[]{:S(2)}, u32[]{:S(2)}) collective-permute-start(bf16[48,512]{1,0:T(8,128)(2,1)S(1)} %collective-permute-done.5.refs_1_), channel_id=1, source_target_pairs={{0,16},{16,32},{32,48},{48,64},{64,80},{80,96},{96,112},{112,0},{1... | collective-permute-start | bytes 147464 | tf_op jit(solution)/shard_map/ppermute | solution.py:23
  49.3 6.0 %collective-permute-start.10 = (bf16[48,512]{1,0:T(8,128)(2,1)S(1)}, bf16[48,512]{1,0:T(8,128)(2,1)S(1)}, u32[]{:S(2)}, u32[]{:S(2)}) collective-permute-start(bf16[48,512]{1,0:T(8,128)(2,1)S(1)} %collective-permute-done.9.refs_7_), channel_id=1, source_target_pairs={{0,112},{16,0},{32,16},{48,32},{64,48},{80,64},{96,80},{112,96},{1... | collective-permute-start | bytes 147464 | tf_op jit(solution)/shard_map/ppermute | solution.py:23
  53.3 5.7 %collective-permute-start.7 = (bf16[48,512]{1,0:T(8,128)(2,1)S(1)}, bf16[48,512]{1,0:T(8,128)(2,1)S(1)}, u32[]{:S(2)}, u32[]{:S(2)}) collective-permute-start(bf16[48,512]{1,0:T(8,128)(2,1)S(1)} %collective-permute-done.6.refs_2_), channel_id=1, source_target_pairs={{0,16},{16,32},{32,48},{48,64},{64,80},{80,96},{96,112},{112,0},{1... | collective-permute-start | bytes 147464 | tf_op jit(solution)/shard_map/ppermute | solution.py:23
  55.3 4.8 %collective-permute-start.11 = (bf16[48,512]{1,0:T(8,128)(2,1)S(1)}, bf16[48,512]{1,0:T(8,128)(2,1)S(1)}, u32[]{:S(2)}, u32[]{:S(2)}) collective-permute-start(bf16[48,512]{1,0:T(8,128)(2,1)S(1)} %collective-permute-done.10.refs_6_), channel_id=1, source_target_pairs={{0,112},{16,0},{32,16},{48,32},{64,48},{80,64},{96,80},{112,96},{1... | collective-permute-start | bytes 147464 | tf_op jit(solution)/shard_map/ppermute | solution.py:23
  59.0 5.3 %collective-permute-start.8 = (bf16[48,512]{1,0:T(8,128)(2,1)S(1)}, bf16[48,512]{1,0:T(8,128)(2,1)S(1)}, u32[]{:S(2)}, u32[]{:S(2)}) collective-permute-start(bf16[48,512]{1,0:T(8,128)(2,1)S(1)} %collective-permute-done.7.refs_3_), channel_id=1, source_target_pairs={{0,16},{16,32},{32,48},{48,64},{64,80},{80,96},{96,112},{112,0},{1... | collective-permute-start | bytes 147464 | tf_op jit(solution)/shard_map/ppermute | solution.py:23

commit v11 on v10

--- a/solution.py
+++ b/solution.py
@@ -21,6 +21,10 @@
     count = lax.axis_size(axis)
     pairs = [(source, (source + steps) % count) for source in range(count)]
     return lax.ppermute(value, axis, pairs)
+
+
+def peer_of(index):
+    return (index % 4 * 2 + index // 32) * 8 + index // 4 % 8
 
 
 def payload_kernel(
@@ -57,7 +61,7 @@
         pair = jnp.transpose(pair.astype(F32))
         third = jnp.transpose(third)
         for part in range(columns):
-            to = (tile // 4 * columns + part) * 4 + tile % 4
+            to = peer_of((tile // 4 * columns + part) * 4 + tile % 4)
             at = part * GROUP
             out_ref[to, :GROUP, :] = pair[at : at + GROUP].astype(BF)
             out_ref[to, GROUP:, :] = jnp.concatenate([third[at : at + 8], coded], axis=0).astype(
@@ -147,14 +151,14 @@
     low = lax.broadcasted_iota(jnp.int32, (GROUP, LANES), 1) < LANES // 2
     for m in range(pieces_ref.shape[0] // 2):
         lanes = slice(m * LANES, (m + 1) * LANES)
-        first = pieces_ref[2 * m, :GROUP, :].astype(F32)
-        second = pieces_ref[2 * m + 1, :GROUP, :].astype(F32)
+        first = pieces_ref[peer_of(2 * m), :GROUP, :].astype(F32)
+        second = pieces_ref[peer_of(2 * m + 1), :GROUP, :].astype(F32)
         weight_ref[:GROUP, lanes] = jnp.where(low, first, pltpu.roll(second, 64, 1)).astype(BF)
         weight_ref[GROUP : 2 * GROUP, lanes] = jnp.where(
             low, pltpu.roll(first, 64, 1), second
         ).astype(BF)
-        first = pieces_ref[2 * m, GROUP:, :].astype(F32)[:8]
-        second = pieces_ref[2 * m + 1, GROUP:, :].astype(F32)[:8]
+        first = pieces_ref[peer_of(2 * m), GROUP:, :].astype(F32)[:8]
+        second = pieces_ref[peer_of(2 * m + 1), GROUP:, :].astype(F32)[:8]
         third = jnp.concatenate(
             [
                 jnp.where(low[:8], first, pltpu.roll(second, 64, 1)),
@@ -228,7 +232,7 @@
 
 
 def ids_of(pieces_ref, index):
-    return pieces_ref[index, GROUP:, :].astype(F32)[8:12]
+    return pieces_ref[peer_of(index), GROUP:, :].astype(F32)[8:12]
 
 
 def hot_kernel(spot_ref, pieces_ref, out_ref, lead_ref):
@@ -466,14 +470,13 @@
     core = lax.axis_index("core")
     x_count = lax.axis_size("x")
     z_count = lax.axis_size("z")
-    ctx = ("yh", "z", "x")
     tile = yh * x_count + x
     tiles = width_local // LANES
 
     load, upper, lower = payload(in_weight, ids.reshape(-1, LANES), embed_table, tiles * z_count)
     got_up = shifted(upper, ("yh", "yl"), -1)
     got_down = shifted(lower, ("yh", "yl"), 1)
-    pieces = lax.all_to_all(load, ctx, 0, 0, tiled=True)
+    pieces = lax.all_to_all(load, ("x", "yh", "z"), 0, 0, tiled=True)
 
     groups = LANES // GROUP
     steps = jnp.arange(LONG_TAPS, dtype=F32)

time: 91.4 us -> 92.1 us (level)
  transfers between devices with their start and end apart: 13 -> 13, of which waited for: 7 -> 6; matrix products, arithmetic and copies ran while one was open for 3% -> 3% of each run, Pallas kernels for 7% -> 6%
where the time goes in v11:
time: 92.1 us; the launch traced here: 91.7 us
  starting transfers between devices  27.4 us (30%)
  Pallas kernels  21.3 us (23%)
  waiting for transfers between devices  18.1 us (20%)
  blocking collectives  17.4 us (19%)
  local copies, waits for them, and re-layouts  7.09 us (8%)
    all_to_all x1, blocking collectives, per_device(): result = lax.all_to_all(blocks, ('yh', 'x'), 0, 0, tiled=True)  17.4 us
    all_to_all x1, starting transfers between devices, per_device(): pieces = lax.all_to_all(load, ('x', 'yh', 'z'), 0, 0, tiled=True)  14.6 us
    ppermute x12, starting transfers between devices, shifted(): return lax.ppermute(value, axis, pairs)  12.8 us
    ppermute x12, waiting for transfers between devices, shifted(): return lax.ppermute(value, axis, pairs)  10.1 us
    pallas_call x1, Pallas kernels, mixed_blocks(): pl.pallas_call(mix_kernel, out_shape=jax.ShapeDtypeStruct((blocks, tokens...  8.71 us
    all_to_all x1, waiting for transfers between devices, per_device(): pieces = lax.all_to_all(load, ('x', 'yh', 'z'), 0, 0, tiled=True)  8.03 us
    unnamed x12, local copies, waits for them, and re-layouts  4.68 us
    pallas_call x1, Pallas kernels, normed_rows(): pl.pallas_call(norm_kernel, out_shape=(jax.ShapeDtypeStruct((4, vocab, wi...  3.78 us
  transfers between devices with their start and end apart: 13, of which 6 were waited for; matrix products, arithmetic and copies ran while one was open for 3% of the time, Pallas kernels for 6%

profile of v11, /device:TPU:8, one launch (start us, length us, event | category | flops | bytes accessed | tf_op | source)
XLA Modules:
  0.0 91.7 jit_solution(17397731386534872167)
XLA Ops:
  0.0 0.0 copy-start
  0.0 2.7 %payload.1 = (bf16[64,32,128]{2,1,0:T(8,128)(2,1)}, bf16[256,1024]{1,0:T(8,128)(2,1)}, bf16[256,1024]{1,0:T(8,128)(2,1)}) custom-call(bf16[3,64,1024]{2,1,0:T(8,128)(2,1)} %far_weight_ref.1, s32[4,128]{1,0:T(4,128)} %bitcast.10, bf16[512,1024]{1,0:T(8,128)(2,1)} %refs_0_.1), custom_call_target="tpu_custom_call" | custom-call | bytes 2900000 | tf_op jit(solution)/shard_map/payload/pallas_call | solution.py:85
  2.7 2.3 %collective-permute-start.1 = (bf16[256,1024]{1,0:T(8,128)(2,1)}, bf16[256,1024]{1,0:T(8,128)(2,1)S(1)}, u32[]{:S(2)}, u32[]{:S(2)}) collective-permute-start(bf16[256,1024]{1,0:T(8,128)(2,1)} %get-tuple-element.24), channel_id=1, source_target_pairs={{0,130},{2,0},{128,2},{130,128},{1,131},{3,1},{129,3},{131,129},{4... | collective-permute-start | bytes 1572872 | tf_op jit(solution)/shard_map/ppermute | solution.py:23
  5.0 0.0 collective-permute-start.2
  5.0 0.0 copy-done
  5.0 0.1 collective-permute-start
  5.1 14.6 %all-to-all-start = ((bf16[64,32,128]{2,1,0:T(8,128)(2,1)}), bf16[64,32,128]{2,1,0:T(8,128)(2,1)S(1)}, u32[]{:S(2)}, u32[]{:S(2)}) async-start(bf16[64,32,128]{2,1,0:T(8,128)(2,1)} %get-tuple-element.27), calls=%async_computation | async-start | bytes 1048576 | tf_op jit(solution)/shard_map/all_to_all | solution.py:479
  19.7 0.7 dynamic_slice.14
  20.4 0.0 collective-permute-done.1.refs_2_
  20.5 0.2 collective-permute-start.3
  20.7 0.0 collective-permute-done.2.refs_3_
  20.7 0.3 collective-permute-start.4
  21.0 0.7 constant_dynamic-slice_fusion.1
  21.7 0.1 fusion
  21.8 0.1 rev.3
  21.8 0.8 constant_dynamic-slice_fusion
  22.6 0.1 reshape.18.scale_ref
  22.7 0.1 pad.4.taps_ref
  22.7 0.4 toeplitz.1.refs_9_
  23.1 0.0 copy-start.3
  23.1 0.8 copy-done.3
  23.9 0.1 pad_add_fusion.spot_ref
  24.0 0.0 collective-permute-done.refs_1_
  24.0 0.0 collective-permute-done.3.refs_4_
  24.0 0.0 collective-permute-done.4.refs_5_
  24.0 0.0 copy-start.1
  24.1 1.2 %copy-done.1 = bf16[512,1024]{1,0:T(8,128)(2,1)S(1)} copy-done((bf16[512,1024]{1,0:T(8,128)(2,1)S(1)}, bf16[512,1024]{1,0:T(8,128)(2,1)}, u32[]{:S(2)}) %copy-start.1) | copy-done | bytes 1048600
  25.3 0.0 copy-start.5
  25.3 0.7 copy-done.5
  26.0 3.8 %normed_rows.1 = (bf16[4,512,1024]{2,1,0:T(8,128)(2,1)S(1)}, f32[8,128]{1,0:T(8,128)S(1)}) custom-call(s32[4]{0:T(128)S(1)} %pad_add_fusion.spot_ref, bf16[512,1024]{1,0:T(8,128)(2,1)S(1)} %copy-done.1, bf16[512,1024]{1,0:T(8,128)(2,1)S(1)} %collective-permute-done.refs_1_, bf16[256,1024]{1,0:T(8,128)(2,1)S(1)} %collective-permute-done.1.refs_2_, ...), custom_call_target="tpu_custom_call" | custom-call | flops 10485760 | bytes 8388608 | tf_op jit(solution)/shard_map/normed_rows/pallas_call | solution.py:130
  29.8 0.0 copy-start.2
  29.8 1.9 %copy-done.2 = bf16[4,512,1024]{2,1,0:T(8,128)(2,1)} copy-done((bf16[4,512,1024]{2,1,0:T(8,128)(2,1)}, bf16[4,512,1024]{2,1,0:T(8,128)(2,1)S(1)}, u32[]{:S(2)}) %copy-start.2) | copy-done | bytes 4194328
  31.7 0.0 copy-start.4
  31.7 8.0 %all-to-all-done.pieces_ref = bf16[64,32,128]{2,1,0:T(8,128)(2,1)S(1)} async-done(((bf16[64,32,128]{2,1,0:T(8,128)(2,1)}), bf16[64,32,128]{2,1,0:T(8,128)(2,1)S(1)}, u32[]{:S(2)}, u32[]{:S(2)}) %all-to-all-start) | async-done | bytes 524320 | tf_op jit(solution)/shard_map/all_to_all | solution.py:479
  39.7 3.1 %table_piece.1.refs_0_ = bf16[48,512]{1,0:T(8,128)(2,1)S(1)} custom-call(bf16[4,512,1024]{2,1,0:T(8,128)(2,1)} %copy-done.2, bf16[64,32,128]{2,1,0:T(8,128)(2,1)S(1)} %all-to-all-done.pieces_ref, f32[48,1]{1,0:T(8,128)S(1)} %reshape.18.scale_ref, f32[8,128]{1,0:T(8,128)S(1)} %get-tuple-element.33._), custom_call_target="tpu_custom_call" | custom-call | flops 201326592 | bytes 5000000 | tf_op jit(solution)/shard_map/table_piece/pallas_call | solution.py:186
  42.8 2.1 %collective-permute-start.5 = (bf16[48,512]{1,0:T(8,128)(2,1)S(1)}, bf16[48,512]{1,0:T(8,128)(2,1)S(1)}, u32[]{:S(2)}, u32[]{:S(2)}) collective-permute-start(bf16[48,512]{1,0:T(8,128)(2,1)S(1)} %table_piece.1.refs_0_), channel_id=1, source_target_pairs={{0,16},{16,32},{32,48},{48,64},{64,80},{80,96},{96,112},{112,0},{1... | collective-permute-start | bytes 147464 | tf_op jit(solution)/shard_map/ppermute | solution.py:23
  44.9 1.2 %collective-permute-start.9 = (bf16[48,512]{1,0:T(8,128)(2,1)S(1)}, bf16[48,512]{1,0:T(8,128)(2,1)S(1)}, u32[]{:S(2)}, u32[]{:S(2)}) collective-permute-start(bf16[48,512]{1,0:T(8,128)(2,1)S(1)} %table_piece.1.refs_0_), channel_id=1, source_target_pairs={{0,112},{16,0},{32,16},{48,32},{64,48},{80,64},{96,80},{112,96},{1... | collective-permute-start | bytes 147464 | tf_op jit(solution)/shard_map/ppermute | solution.py:23
  46.1 2.1 %collective-permute-done.5.refs_1_ = bf16[48,512]{1,0:T(8,128)(2,1)S(1)} collective-permute-done((bf16[48,512]{1,0:T(8,128)(2,1)S(1)}, bf16[48,512]{1,0:T(8,128)(2,1)S(1)}, u32[]{:S(2)}, u32[]{:S(2)}) %collective-permute-start.5) | collective-permute-done | bytes 49184 | tf_op jit(solution)/shard_map/ppermute | solution.py:23
  48.2 0.8 collective-permute-start.6
  49.0 0.0 collective-permute-done.9.refs_7_
  49.0 2.4 %collective-permute-start.10 = (bf16[48,512]{1,0:T(8,128)(2,1)S(1)}, bf16[48,512]{1,0:T(8,128)(2,1)S(1)}, u32[]{:S(2)}, u32[]{:S(2)}) collective-permute-start(bf16[48,512]{1,0:T(8,128)(2,1)S(1)} %collective-permute-done.9.refs_7_), channel_id=1, source_target_pairs={{0,112},{16,0},{32,16},{48,32},{64,48},{80,64},{96,80},{112,96},{1... | collective-permute-start | bytes 147464 | tf_op jit(solution)/shard_map/ppermute | solution.py:23
  51.4 2.1 %collective-permute-done.6.refs_2_ = bf16[48,512]{1,0:T(8,128)(2,1)S(1)} collective-permute-done((bf16[48,512]{1,0:T(8,128)(2,1)S(1)}, bf16[48,512]{1,0:T(8,128)(2,1)S(1)}, u32[]{:S(2)}, u32[]{:S(2)}) %collective-permute-start.6) | collective-permute-done | bytes 49184 | tf_op jit(solution)/shard_map/ppermute | solution.py:23
  53.5 0.0 collective-permute-start.7
  53.5 1.7 %hot_rows.1 = (bf16[8,512,512]{2,1,0:T(8,128)(2,1)S(1)}, bf16[288,512]{1,0:T(8,128)(2,1)S(1)}) custom-call(s32[1]{0:T(128)} %bitcast.spot_ref, bf16[64,32,128]{2,1,0:T(8,128)(2,1)S(1)} %all-to-all-done.pieces_ref), custom_call_target="tpu_custom_call" | custom-call | flops 5000000 | bytes 4500000 | tf_op jit(solution)/shard_map/hot_rows/pallas_call | solution.py:264
  55.2 0.0 collective-permute-done.10.refs_6_
  55.2 3.3 %collective-permute-start.11 = (bf16[48,512]{1,0:T(8,128)(2,1)S(1)}, bf16[48,512]{1,0:T(8,128)(2,1)S(1)}, u32[]{:S(2)}, u32[]{:S(2)}) collective-permute-start(bf16[48,512]{1,0:T(8,128)(2,1)S(1)} %collective-permute-done.10.refs_6_), channel_id=1, source_target_pairs={{0,112},{16,0},{32,16},{48,32},{64,48},{80,64},{96,80},{112,96},{1... | collective-permute-start | bytes 147464 | tf_op jit(solution)/shard_map/ppermute | solution.py:23
  58.5 0.6 collective-permute-done.7.refs_3_
  59.2 0.0 collective-permute-start.8
  59.2 1.1 %collective-permute-done.11.refs_5_ = bf16[48,512]{1,0:T(8,128)(2,1)S(1)} collective-permute-done((bf16[48,512]{1,0:T(8,128)(2,1)S(1)}, bf16[48,512]{1,0:T(8,128)(2,1)S(1)}, u32[]{:S(2)}, u32[]{:S(2)}) %collective-permute-start.11) | collective-permute-done | bytes 49184 | tf_op jit(solution)/shard_map/ppermute | solution.py:23
  60.3 4.2 %collective-permute-done.8.refs_4_ = bf16[48,512]{1,0:T(8,128)(2,1)S(1)} collective-permute-done((bf16[48,512]{1,0:T(8,128)(2,1)S(1)}, bf16[48,512]{1,0:T(8,128)(2,1)S(1)}, u32[]{:S(2)}, u32[]{:S(2)}) %collective-permute-start.8) | collective-permute-done | bytes 49184 | tf_op jit(solution)/shard_map/ppermute | solution.py:23
  64.5 0.0 copy-done.4
  64.5 8.7 %mixed_blocks.1 = bf16[8,512,128]{2,1,0:T(8,128)(2,1)S(1)} custom-call(s32[1]{0:T(128)} %bitcast.spot_ref, bf16[8,512,512]{2,1,0:T(8,128)(2,1)S(1)} %get-tuple-element.36.hot_ref, bf16[288,512]{1,0:T(8,128)(2,1)S(1)} %get-tuple-element.37.lead_hot_ref, bf16[48,512]{1,0:T(8,128)(2,1)S(1)} %table_piece.1.refs_0_, ...), custom_call_target="tpu_custom_call" | custom-call | flops 5000000000 | bytes 6000000 | tf_op jit(solution)/shard_map/mixed_blocks/pallas_call | solution.py:404
  73.2 17.4 %all_to_all.10.blocks_ref = bf16[8,512,128]{2,1,0:T(8,128)(2,1)S(1)} all-to-all(bf16[8,512,128]{2,1,0:T(8,128)(2,1)S(1)} %mixed_blocks.1), channel_id=1, replica_groups=mesh['yh'=2,'z'=8,'x'=4,'yl'=2,'core'=2] {'yh','x'}, dimensions={0} | all-to-all | bytes 2097152 | tf_op jit(solution)/shard_map/all_to_all | solution.py:518
  90.6 1.0 %placed_columns.1 = bf16[512,1024]{1,0:T(8,128)(2,1)} custom-call(bf16[8,512,128]{2,1,0:T(8,128)(2,1)S(1)} %all_to_all.10.blocks_ref), custom_call_target="tpu_custom_call" | custom-call | bytes 2000000 | tf_op jit(solution)/shard_map/placed_columns/pallas_call | solution.py:451
  (2 shorter events, 0.0 us)
Async XLA Ops:
  0.0 5.0 %copy-start = (f32[3,7,1024]{2,1,0:T(8,128)S(1)}, f32[3,7,1024]{2,1,0:T(8,128)}, u32[]{:S(2)}) copy-start(f32[3,7,1024]{2,1,0:T(8,128)} %param.13) | copy-start | bytes 258052
  2.7 17.8 %collective-permute-start.1 = (bf16[256,1024]{1,0:T(8,128)(2,1)}, bf16[256,1024]{1,0:T(8,128)(2,1)S(1)}, u32[]{:S(2)}, u32[]{:S(2)}) collective-permute-start(bf16[256,1024]{1,0:T(8,128)(2,1)} %get-tuple-element.24), channel_id=1, source_target_pairs={{0,130},{2,0},{128,2},{130,128},{1,131},{3,1},{129,3},{131,129},{4... | collective-permute-start | bytes 1572872 | tf_op jit(solution)/shard_map/ppermute | solution.py:23
  5.0 15.7 %collective-permute-start.2 = (bf16[256,1024]{1,0:T(8,128)(2,1)}, bf16[256,1024]{1,0:T(8,128)(2,1)S(1)}, u32[]{:S(2)}, u32[]{:S(2)}) collective-permute-start(bf16[256,1024]{1,0:T(8,128)(2,1)} %get-tuple-element.25), channel_id=1, source_target_pairs={{0,2},{2,128},{128,130},{130,0},{1,3},{3,129},{129,131},{131,1},{4... | collective-permute-start | bytes 1572872 | tf_op jit(solution)/shard_map/ppermute | solution.py:23
  5.0 19.1 %collective-permute-start = (bf16[512,1024]{1,0:T(8,128)(2,1)}, bf16[512,1024]{1,0:T(8,128)(2,1)S(1)}, u32[]{:S(2)}, u32[]{:S(2)}) collective-permute-start(bf16[512,1024]{1,0:T(8,128)(2,1)} %refs_0_.1), channel_id=1, source_target_pairs={{0,1},{1,0},{2,3},{3,2},{4,5},{5,4},{6,7},{7,6},{8,9},{9,8},{10,11... | collective-permute-start | bytes 3145736 | tf_op jit(solution)/shard_map/ppermute | solution.py:23
  5.1 34.7 %all-to-all-start = ((bf16[64,32,128]{2,1,0:T(8,128)(2,1)}), bf16[64,32,128]{2,1,0:T(8,128)(2,1)S(1)}, u32[]{:S(2)}, u32[]{:S(2)}) async-start(bf16[64,32,128]{2,1,0:T(8,128)(2,1)} %get-tuple-element.27), calls=%async_computation | async-start | bytes 1048576 | tf_op jit(solution)/shard_map/all_to_all | solution.py:479
  20.5 3.6 %collective-permute-start.3 = (bf16[256,1024]{1,0:T(8,128)(2,1)S(1)}, bf16[256,1024]{1,0:T(8,128)(2,1)S(1)}, u32[]{:S(2)}, u32[]{:S(2)}) collective-permute-start(bf16[256,1024]{1,0:T(8,128)(2,1)S(1)} %collective-permute-done.1.refs_2_), channel_id=1, source_target_pairs={{0,1},{1,0},{2,3},{3,2},{4,5},{5,4},{6,7},{7,6},{8,9},{9,8},{10,11... | collective-permute-start | bytes 1572872 | tf_op jit(solution)/shard_map/ppermute | solution.py:23
  20.7 3.4 %collective-permute-start.4 = (bf16[256,1024]{1,0:T(8,128)(2,1)S(1)}, bf16[256,1024]{1,0:T(8,128)(2,1)}, u32[]{:S(2)}, u32[]{:S(2)}) collective-permute-start(bf16[256,1024]{1,0:T(8,128)(2,1)S(1)} %collective-permute-done.2.refs_3_), channel_id=1, source_target_pairs={{0,1},{1,0},{2,3},{3,2},{4,5},{5,4},{6,7},{7,6},{8,9},{9,8},{10,11... | collective-permute-start | bytes 1572872 | tf_op jit(solution)/shard_map/ppermute | solution.py:23
  23.1 0.8 copy-start.3
  24.0 1.2 %copy-start.1 = (bf16[512,1024]{1,0:T(8,128)(2,1)S(1)}, bf16[512,1024]{1,0:T(8,128)(2,1)}, u32[]{:S(2)}) copy-start(bf16[512,1024]{1,0:T(8,128)(2,1)} %refs_0_.1) | copy-start | bytes 3145732
  25.3 0.7 copy-start.5
  29.8 1.9 %copy-start.2 = (bf16[4,512,1024]{2,1,0:T(8,128)(2,1)}, bf16[4,512,1024]{2,1,0:T(8,128)(2,1)S(1)}, u32[]{:S(2)}) copy-start(bf16[4,512,1024]{2,1,0:T(8,128)(2,1)S(1)} %get-tuple-element.26.far_ref) | copy-start | bytes 12582916
  31.7 32.8 %copy-start.4 = (bf16[8,256,128]{2,1,0:T(8,128)(2,1)S(1)}, bf16[8,256,128]{2,1,0:T(8,128)(2,1)}, u32[]{:S(2)}) copy-start(bf16[8,256,128]{2,1,0:T(8,128)(2,1)} %copy-done.3) | copy-start | bytes 1572868
  42.8 5.4 %collective-permute-start.5 = (bf16[48,512]{1,0:T(8,128)(2,1)S(1)}, bf16[48,512]{1,0:T(8,128)(2,1)S(1)}, u32[]{:S(2)}, u32[]{:S(2)}) collective-permute-start(bf16[48,512]{1,0:T(8,128)(2,1)S(1)} %table_piece.1.refs_0_), channel_id=1, source_target_pairs={{0,16},{16,32},{32,48},{48,64},{64,80},{80,96},{96,112},{112,0},{1... | collective-permute-start | bytes 147464 | tf_op jit(solution)/shard_map/ppermute | solution.py:23
  44.9 4.1 %collective-permute-start.9 = (bf16[48,512]{1,0:T(8,128)(2,1)S(1)}, bf16[48,512]{1,0:T(8,128)(2,1)S(1)}, u32[]{:S(2)}, u32[]{:S(2)}) collective-permute-start(bf16[48,512]{1,0:T(8,128)(2,1)S(1)} %table_piece.1.refs_0_), channel_id=1, source_target_pairs={{0,112},{16,0},{32,16},{48,32},{64,48},{80,64},{96,80},{112,96},{1... | collective-permute-start | bytes 147464 | tf_op jit(solution)/shard_map/ppermute | solution.py:23
  48.2 5.3 %collective-permute-start.6 = (bf16[48,512]{1,0:T(8,128)(2,1)S(1)}, bf16[48,512]{1,0:T(8,128)(2,1)S(1)}, u32[]{:S(2)}, u32[]{:S(2)}) collective-permute-start(bf16[48,512]{1,0:T(8,128)(2,1)S(1)} %collective-permute-done.5.refs_1_), channel_id=1, source_target_pairs={{0,16},{16,32},{32,48},{48,64},{64,80},{80,96},{96,112},{112,0},{1... | collective-permute-start | bytes 147464 | tf_op jit(solution)/shard_map/ppermute | solution.py:23
  49.0 6.2 %collective-permute-start.10 = (bf16[48,512]{1,0:T(8,128)(2,1)S(1)}, bf16[48,512]{1,0:T(8,128)(2,1)S(1)}, u32[]{:S(2)}, u32[]{:S(2)}) collective-permute-start(bf16[48,512]{1,0:T(8,128)(2,1)S(1)} %collective-permute-done.9.refs_7_), channel_id=1, source_target_pairs={{0,112},{16,0},{32,16},{48,32},{64,48},{80,64},{96,80},{112,96},{1... | collective-permute-start | bytes 147464 | tf_op jit(solution)/shard_map/ppermute | solution.py:23
  53.5 5.7 %collective-permute-start.7 = (bf16[48,512]{1,0:T(8,128)(2,1)S(1)}, bf16[48,512]{1,0:T(8,128)(2,1)S(1)}, u32[]{:S(2)}, u32[]{:S(2)}) collective-permute-start(bf16[48,512]{1,0:T(8,128)(2,1)S(1)} %collective-permute-done.6.refs_2_), channel_id=1, source_target_pairs={{0,16},{16,32},{32,48},{48,64},{64,80},{80,96},{96,112},{112,0},{1... | collective-permute-start | bytes 147464 | tf_op jit(solution)/shard_map/ppermute | solution.py:23
  55.2 5.1 %collective-permute-start.11 = (bf16[48,512]{1,0:T(8,128)(2,1)S(1)}, bf16[48,512]{1,0:T(8,128)(2,1)S(1)}, u32[]{:S(2)}, u32[]{:S(2)}) collective-permute-start(bf16[48,512]{1,0:T(8,128)(2,1)S(1)} %collective-permute-done.10.refs_6_), channel_id=1, source_target_pairs={{0,112},{16,0},{32,16},{48,32},{64,48},{80,64},{96,80},{112,96},{1... | collective-permute-start | bytes 147464 | tf_op jit(solution)/shard_map/ppermute | solution.py:23
  59.2 5.3 %collective-permute-start.8 = (bf16[48,512]{1,0:T(8,128)(2,1)S(1)}, bf16[48,512]{1,0:T(8,128)(2,1)S(1)}, u32[]{:S(2)}, u32[]{:S(2)}) collective-permute-start(bf16[48,512]{1,0:T(8,128)(2,1)S(1)} %collective-permute-done.7.refs_3_), channel_id=1, source_target_pairs={{0,16},{16,32},{32,48},{48,64},{64,80},{80,96},{96,112},{112,0},{1... | collective-permute-start | bytes 147464 | tf_op jit(solution)/shard_map/ppermute | solution.py:23

commit v12 on v10

--- a/solution.py
+++ b/solution.py
@@ -88,7 +88,7 @@
             pltpu.VMEM(ids_rows.shape, jnp.int32),
             pltpu.SemaphoreType.DMA((6,)),
         ],
-        compiler_params=pltpu.CompilerParams(vmem_limit_bytes=66800000),
+        compiler_params=pltpu.CompilerParams(vmem_limit_bytes=GRANT),
         cost_estimate=cost(0, 2900000),
         name="payload",
     )(in_weight, ids_rows, embed_table)
@@ -470,7 +470,12 @@
     tile = yh * x_count + x
     tiles = width_local // LANES
 
-    load, upper, lower = payload(in_weight, ids.reshape(-1, LANES), embed_table, tiles * z_count)
+    load, upper, lower = payload(
+        pltpu.with_memory_space_constraint(in_weight, pltpu.HBM),
+        pltpu.with_memory_space_constraint(ids.reshape(-1, LANES), pltpu.HBM),
+        pltpu.with_memory_space_constraint(embed_table, pltpu.HBM),
+        tiles * z_count,
+    )
     got_up = shifted(upper, ("yh", "yl"), -1)
     got_down = shifted(lower, ("yh", "yl"), 1)
     pieces = lax.all_to_all(load, ctx, 0, 0, tiled=True)

time: 91.4 us -> 91.2 us (level)
  no operation moved by 1% of the time
where the time goes in v12:
time: 91.2 us; the launch traced here: 90.8 us
  starting transfers between devices  27.2 us (30%)
  Pallas kernels  21.3 us (23%)
  waiting for transfers between devices  18 us (20%)
  blocking collectives  17 us (19%)
  local copies, waits for them, and re-layouts  7.09 us (8%)
    all_to_all x1, blocking collectives, per_device(): result = lax.all_to_all(blocks, ('yh', 'x'), 0, 0, tiled=True)  17 us
    all_to_all x1, starting transfers between devices, per_device(): pieces = lax.all_to_all(load, ctx, 0, 0, tiled=True)  14.6 us
    ppermute x12, starting transfers between devices, shifted(): return lax.ppermute(value, axis, pairs)  12.6 us
    ppermute x12, waiting for transfers between devices, shifted(): return lax.ppermute(value, axis, pairs)  10.2 us
    pallas_call x1, Pallas kernels, mixed_blocks(): pl.pallas_call(mix_kernel, out_shape=jax.ShapeDtypeStruct((blocks, tokens...  8.71 us
    all_to_all x1, waiting for transfers between devices, per_device(): pieces = lax.all_to_all(load, ctx, 0, 0, tiled=True)  7.78 us
    unnamed x12, local copies, waits for them, and re-layouts  4.68 us
    pallas_call x1, Pallas kernels, normed_rows(): pl.pallas_call(norm_kernel, out_shape=(jax.ShapeDtypeStruct((4, vocab, wi...  3.78 us
  transfers between devices with their start and end apart: 13, of which 7 were waited for; matrix products, arithmetic and copies ran while one was open for 3% of the time, Pallas kernels for 7%

profile of v12, /device:TPU:8, one launch (start us, length us, event | category | flops | bytes accessed | tf_op | source)
XLA Modules:
  0.0 90.8 jit_solution(1972298207166969500)
XLA Ops:
  0.0 0.0 copy-start
  0.0 2.5 %payload.1 = (bf16[64,32,128]{2,1,0:T(8,128)(2,1)}, bf16[256,1024]{1,0:T(8,128)(2,1)S(1)}, bf16[256,1024]{1,0:T(8,128)(2,1)}) custom-call(bf16[3,64,1024]{2,1,0:T(8,128)(2,1)} %far_weight_ref.1, s32[4,128]{1,0:T(4,128)} %bitcast.10, bf16[512,1024]{1,0:T(8,128)(2,1)} %refs_0_.1), custom_call_target="tpu_custom_call" | custom-call | bytes 2900000 | tf_op jit(solution)/shard_map/payload/pallas_call | solution.py:81
  2.5 2.3 %collective-permute-start.1 = (bf16[256,1024]{1,0:T(8,128)(2,1)S(1)}, bf16[256,1024]{1,0:T(8,128)(2,1)S(1)}, u32[]{:S(2)}, u32[]{:S(2)}) collective-permute-start(bf16[256,1024]{1,0:T(8,128)(2,1)S(1)} %get-tuple-element.24), channel_id=1, source_target_pairs={{0,130},{2,0},{128,2},{130,128},{1,131},{3,1},{129,3},{131,129},{4... | collective-permute-start | bytes 1572872 | tf_op jit(solution)/shard_map/ppermute | solution.py:23
  4.8 0.0 collective-permute-start.2
  4.8 0.0 copy-done
  4.8 0.1 collective-permute-start
  4.9 14.6 %all-to-all-start = ((bf16[64,32,128]{2,1,0:T(8,128)(2,1)}), bf16[64,32,128]{2,1,0:T(8,128)(2,1)S(1)}, u32[]{:S(2)}, u32[]{:S(2)}) async-start(bf16[64,32,128]{2,1,0:T(8,128)(2,1)} %get-tuple-element.27), calls=%async_computation | async-start | bytes 1048576 | tf_op jit(solution)/shard_map/all_to_all | solution.py:481
  19.6 0.7 dynamic_slice.14
  20.3 0.0 collective-permute-done.1.refs_2_
  20.3 0.2 collective-permute-start.3
  20.5 0.0 collective-permute-done.2.refs_3_
  20.5 0.3 collective-permute-start.4
  20.8 0.7 constant_dynamic-slice_fusion.1
  21.5 0.1 fusion
  21.6 0.1 rev.3
  21.7 0.8 constant_dynamic-slice_fusion
  22.4 0.1 reshape.18.scale_ref
  22.5 0.1 pad.4.taps_ref
  22.6 0.4 toeplitz.1.refs_9_
  23.0 0.0 copy-start.3
  23.0 0.8 copy-done.3
  23.8 0.1 pad_add_fusion.spot_ref
  23.9 0.0 collective-permute-done.refs_1_
  23.9 0.0 collective-permute-done.3.refs_4_
  23.9 0.0 collective-permute-done.4.refs_5_
  23.9 0.0 copy-start.1
  23.9 1.2 %copy-done.1 = bf16[512,1024]{1,0:T(8,128)(2,1)S(1)} copy-done((bf16[512,1024]{1,0:T(8,128)(2,1)S(1)}, bf16[512,1024]{1,0:T(8,128)(2,1)}, u32[]{:S(2)}) %copy-start.1) | copy-done | bytes 1048600
  25.1 0.0 copy-start.5
  25.1 0.7 copy-done.5
  25.8 3.8 %normed_rows.1 = (bf16[4,512,1024]{2,1,0:T(8,128)(2,1)S(1)}, f32[8,128]{1,0:T(8,128)S(1)}) custom-call(s32[4]{0:T(128)S(1)} %pad_add_fusion.spot_ref, bf16[512,1024]{1,0:T(8,128)(2,1)S(1)} %copy-done.1, bf16[512,1024]{1,0:T(8,128)(2,1)S(1)} %collective-permute-done.refs_1_, bf16[256,1024]{1,0:T(8,128)(2,1)S(1)} %collective-permute-done.1.refs_2_, ...), custom_call_target="tpu_custom_call" | custom-call | flops 10485760 | bytes 8388608 | tf_op jit(solution)/shard_map/normed_rows/pallas_call | solution.py:126
  29.6 0.0 copy-start.2
  29.6 1.9 %copy-done.2 = bf16[4,512,1024]{2,1,0:T(8,128)(2,1)} copy-done((bf16[4,512,1024]{2,1,0:T(8,128)(2,1)}, bf16[4,512,1024]{2,1,0:T(8,128)(2,1)S(1)}, u32[]{:S(2)}) %copy-start.2) | copy-done | bytes 4194328
  31.5 0.0 copy-start.4
  31.6 7.8 %all-to-all-done.pieces_ref = bf16[64,32,128]{2,1,0:T(8,128)(2,1)S(1)} async-done(((bf16[64,32,128]{2,1,0:T(8,128)(2,1)}), bf16[64,32,128]{2,1,0:T(8,128)(2,1)S(1)}, u32[]{:S(2)}, u32[]{:S(2)}) %all-to-all-start) | async-done | bytes 524320 | tf_op jit(solution)/shard_map/all_to_all | solution.py:481
  39.3 3.1 %table_piece.1.refs_0_ = bf16[48,512]{1,0:T(8,128)(2,1)S(1)} custom-call(bf16[4,512,1024]{2,1,0:T(8,128)(2,1)} %copy-done.2, bf16[64,32,128]{2,1,0:T(8,128)(2,1)S(1)} %all-to-all-done.pieces_ref, f32[48,1]{1,0:T(8,128)S(1)} %reshape.18.scale_ref, f32[8,128]{1,0:T(8,128)S(1)} %get-tuple-element.33._), custom_call_target="tpu_custom_call" | custom-call | flops 201326592 | bytes 5000000 | tf_op jit(solution)/shard_map/table_piece/pallas_call | solution.py:182
  42.4 2.3 %collective-permute-start.5 = (bf16[48,512]{1,0:T(8,128)(2,1)S(1)}, bf16[48,512]{1,0:T(8,128)(2,1)S(1)}, u32[]{:S(2)}, u32[]{:S(2)}) collective-permute-start(bf16[48,512]{1,0:T(8,128)(2,1)S(1)} %table_piece.1.refs_0_), channel_id=1, source_target_pairs={{0,16},{16,32},{32,48},{48,64},{64,80},{80,96},{96,112},{112,0},{1... | collective-permute-start | bytes 147464 | tf_op jit(solution)/shard_map/ppermute | solution.py:23
  44.7 1.0 %collective-permute-start.9 = (bf16[48,512]{1,0:T(8,128)(2,1)S(1)}, bf16[48,512]{1,0:T(8,128)(2,1)S(1)}, u32[]{:S(2)}, u32[]{:S(2)}) collective-permute-start(bf16[48,512]{1,0:T(8,128)(2,1)S(1)} %table_piece.1.refs_0_), channel_id=1, source_target_pairs={{0,112},{16,0},{32,16},{48,32},{64,48},{80,64},{96,80},{112,96},{1... | collective-permute-start | bytes 147464 | tf_op jit(solution)/shard_map/ppermute | solution.py:23
  45.7 2.1 %collective-permute-done.5.refs_1_ = bf16[48,512]{1,0:T(8,128)(2,1)S(1)} collective-permute-done((bf16[48,512]{1,0:T(8,128)(2,1)S(1)}, bf16[48,512]{1,0:T(8,128)(2,1)S(1)}, u32[]{:S(2)}, u32[]{:S(2)}) %collective-permute-start.5) | collective-permute-done | bytes 49184 | tf_op jit(solution)/shard_map/ppermute | solution.py:23
  47.8 1.2 %collective-permute-start.6 = (bf16[48,512]{1,0:T(8,128)(2,1)S(1)}, bf16[48,512]{1,0:T(8,128)(2,1)S(1)}, u32[]{:S(2)}, u32[]{:S(2)}) collective-permute-start(bf16[48,512]{1,0:T(8,128)(2,1)S(1)} %collective-permute-done.5.refs_1_), channel_id=1, source_target_pairs={{0,16},{16,32},{32,48},{48,64},{64,80},{80,96},{96,112},{112,0},{1... | collective-permute-start | bytes 147464 | tf_op jit(solution)/shard_map/ppermute | solution.py:23
  49.0 0.2 collective-permute-done.9.refs_7_
  49.1 1.9 %collective-permute-start.10 = (bf16[48,512]{1,0:T(8,128)(2,1)S(1)}, bf16[48,512]{1,0:T(8,128)(2,1)S(1)}, u32[]{:S(2)}, u32[]{:S(2)}) collective-permute-start(bf16[48,512]{1,0:T(8,128)(2,1)S(1)} %collective-permute-done.9.refs_7_), channel_id=1, source_target_pairs={{0,112},{16,0},{32,16},{48,32},{64,48},{80,64},{96,80},{112,96},{1... | collective-permute-start | bytes 147464 | tf_op jit(solution)/shard_map/ppermute | solution.py:23
  51.0 2.1 %collective-permute-done.6.refs_2_ = bf16[48,512]{1,0:T(8,128)(2,1)S(1)} collective-permute-done((bf16[48,512]{1,0:T(8,128)(2,1)S(1)}, bf16[48,512]{1,0:T(8,128)(2,1)S(1)}, u32[]{:S(2)}, u32[]{:S(2)}) %collective-permute-start.6) | collective-permute-done | bytes 49184 | tf_op jit(solution)/shard_map/ppermute | solution.py:23
  53.1 0.2 collective-permute-start.7
  53.3 1.8 %hot_rows.1 = (bf16[8,512,512]{2,1,0:T(8,128)(2,1)S(1)}, bf16[288,512]{1,0:T(8,128)(2,1)S(1)}) custom-call(s32[1]{0:T(128)} %bitcast.spot_ref, bf16[64,32,128]{2,1,0:T(8,128)(2,1)S(1)} %all-to-all-done.pieces_ref), custom_call_target="tpu_custom_call" | custom-call | flops 5000000 | bytes 4500000 | tf_op jit(solution)/shard_map/hot_rows/pallas_call | solution.py:260
  55.1 0.0 collective-permute-done.10.refs_6_
  55.1 3.1 %collective-permute-start.11 = (bf16[48,512]{1,0:T(8,128)(2,1)S(1)}, bf16[48,512]{1,0:T(8,128)(2,1)S(1)}, u32[]{:S(2)}, u32[]{:S(2)}) collective-permute-start(bf16[48,512]{1,0:T(8,128)(2,1)S(1)} %collective-permute-done.10.refs_6_), channel_id=1, source_target_pairs={{0,112},{16,0},{32,16},{48,32},{64,48},{80,64},{96,80},{112,96},{1... | collective-permute-start | bytes 147464 | tf_op jit(solution)/shard_map/ppermute | solution.py:23
  58.2 0.6 collective-permute-done.7.refs_3_
  58.8 0.0 collective-permute-start.8
  58.8 1.1 %collective-permute-done.11.refs_5_ = bf16[48,512]{1,0:T(8,128)(2,1)S(1)} collective-permute-done((bf16[48,512]{1,0:T(8,128)(2,1)S(1)}, bf16[48,512]{1,0:T(8,128)(2,1)S(1)}, u32[]{:S(2)}, u32[]{:S(2)}) %collective-permute-start.11) | collective-permute-done | bytes 49184 | tf_op jit(solution)/shard_map/ppermute | solution.py:23
  59.9 4.2 %collective-permute-done.8.refs_4_ = bf16[48,512]{1,0:T(8,128)(2,1)S(1)} collective-permute-done((bf16[48,512]{1,0:T(8,128)(2,1)S(1)}, bf16[48,512]{1,0:T(8,128)(2,1)S(1)}, u32[]{:S(2)}, u32[]{:S(2)}) %collective-permute-start.8) | collective-permute-done | bytes 49184 | tf_op jit(solution)/shard_map/ppermute | solution.py:23
  64.1 0.0 copy-done.4
  64.1 8.7 %mixed_blocks.1 = bf16[8,512,128]{2,1,0:T(8,128)(2,1)S(1)} custom-call(s32[1]{0:T(128)} %bitcast.spot_ref, bf16[8,512,512]{2,1,0:T(8,128)(2,1)S(1)} %get-tuple-element.36.hot_ref, bf16[288,512]{1,0:T(8,128)(2,1)S(1)} %get-tuple-element.37.lead_hot_ref, bf16[48,512]{1,0:T(8,128)(2,1)S(1)} %table_piece.1.refs_0_, ...), custom_call_target="tpu_custom_call" | custom-call | flops 5000000000 | bytes 6000000 | tf_op jit(solution)/shard_map/mixed_blocks/pallas_call | solution.py:400
  72.8 17.0 %all_to_all.10.blocks_ref = bf16[8,512,128]{2,1,0:T(8,128)(2,1)S(1)} all-to-all(bf16[8,512,128]{2,1,0:T(8,128)(2,1)S(1)} %mixed_blocks.1), channel_id=1, replica_groups=mesh['yh'=2,'z'=8,'x'=4,'yl'=2,'core'=2] {'yh','x'}, dimensions={0} | all-to-all | bytes 2097152 | tf_op jit(solution)/shard_map/all_to_all | solution.py:520
  89.8 1.0 %placed_columns.1 = bf16[512,1024]{1,0:T(8,128)(2,1)} custom-call(bf16[8,512,128]{2,1,0:T(8,128)(2,1)S(1)} %all_to_all.10.blocks_ref), custom_call_target="tpu_custom_call" | custom-call | bytes 2000000 | tf_op jit(solution)/shard_map/placed_columns/pallas_call | solution.py:447
  (2 shorter events, 0.0 us)
Async XLA Ops:
  0.0 4.8 %copy-start = (f32[3,7,1024]{2,1,0:T(8,128)S(1)}, f32[3,7,1024]{2,1,0:T(8,128)}, u32[]{:S(2)}) copy-start(f32[3,7,1024]{2,1,0:T(8,128)} %param.13) | copy-start | bytes 258052
  2.5 17.8 %collective-permute-start.1 = (bf16[256,1024]{1,0:T(8,128)(2,1)S(1)}, bf16[256,1024]{1,0:T(8,128)(2,1)S(1)}, u32[]{:S(2)}, u32[]{:S(2)}) collective-permute-start(bf16[256,1024]{1,0:T(8,128)(2,1)S(1)} %get-tuple-element.24), channel_id=1, source_target_pairs={{0,130},{2,0},{128,2},{130,128},{1,131},{3,1},{129,3},{131,129},{4... | collective-permute-start | bytes 1572872 | tf_op jit(solution)/shard_map/ppermute | solution.py:23
  4.8 15.7 %collective-permute-start.2 = (bf16[256,1024]{1,0:T(8,128)(2,1)}, bf16[256,1024]{1,0:T(8,128)(2,1)S(1)}, u32[]{:S(2)}, u32[]{:S(2)}) collective-permute-start(bf16[256,1024]{1,0:T(8,128)(2,1)} %get-tuple-element.25), channel_id=1, source_target_pairs={{0,2},{2,128},{128,130},{130,0},{1,3},{3,129},{129,131},{131,1},{4... | collective-permute-start | bytes 1572872 | tf_op jit(solution)/shard_map/ppermute | solution.py:23
  4.8 19.1 %collective-permute-start = (bf16[512,1024]{1,0:T(8,128)(2,1)}, bf16[512,1024]{1,0:T(8,128)(2,1)S(1)}, u32[]{:S(2)}, u32[]{:S(2)}) collective-permute-start(bf16[512,1024]{1,0:T(8,128)(2,1)} %refs_0_.1), channel_id=1, source_target_pairs={{0,1},{1,0},{2,3},{3,2},{4,5},{5,4},{6,7},{7,6},{8,9},{9,8},{10,11... | collective-permute-start | bytes 3145736 | tf_op jit(solution)/shard_map/ppermute | solution.py:23
  4.9 34.4 %all-to-all-start = ((bf16[64,32,128]{2,1,0:T(8,128)(2,1)}), bf16[64,32,128]{2,1,0:T(8,128)(2,1)S(1)}, u32[]{:S(2)}, u32[]{:S(2)}) async-start(bf16[64,32,128]{2,1,0:T(8,128)(2,1)} %get-tuple-element.27), calls=%async_computation | async-start | bytes 1048576 | tf_op jit(solution)/shard_map/all_to_all | solution.py:481
  20.3 3.6 %collective-permute-start.3 = (bf16[256,1024]{1,0:T(8,128)(2,1)S(1)}, bf16[256,1024]{1,0:T(8,128)(2,1)S(1)}, u32[]{:S(2)}, u32[]{:S(2)}) collective-permute-start(bf16[256,1024]{1,0:T(8,128)(2,1)S(1)} %collective-permute-done.1.refs_2_), channel_id=1, source_target_pairs={{0,1},{1,0},{2,3},{3,2},{4,5},{5,4},{6,7},{7,6},{8,9},{9,8},{10,11... | collective-permute-start | bytes 1572872 | tf_op jit(solution)/shard_map/ppermute | solution.py:23
  20.5 3.4 %collective-permute-start.4 = (bf16[256,1024]{1,0:T(8,128)(2,1)S(1)}, bf16[256,1024]{1,0:T(8,128)(2,1)}, u32[]{:S(2)}, u32[]{:S(2)}) collective-permute-start(bf16[256,1024]{1,0:T(8,128)(2,1)S(1)} %collective-permute-done.2.refs_3_), channel_id=1, source_target_pairs={{0,1},{1,0},{2,3},{3,2},{4,5},{5,4},{6,7},{7,6},{8,9},{9,8},{10,11... | collective-permute-start | bytes 1572872 | tf_op jit(solution)/shard_map/ppermute | solution.py:23
  23.0 0.8 copy-start.3
  23.9 1.2 %copy-start.1 = (bf16[512,1024]{1,0:T(8,128)(2,1)S(1)}, bf16[512,1024]{1,0:T(8,128)(2,1)}, u32[]{:S(2)}) copy-start(bf16[512,1024]{1,0:T(8,128)(2,1)} %refs_0_.1) | copy-start | bytes 3145732
  25.1 0.7 copy-start.5
  29.6 1.9 %copy-start.2 = (bf16[4,512,1024]{2,1,0:T(8,128)(2,1)}, bf16[4,512,1024]{2,1,0:T(8,128)(2,1)S(1)}, u32[]{:S(2)}) copy-start(bf16[4,512,1024]{2,1,0:T(8,128)(2,1)S(1)} %get-tuple-element.26.far_ref) | copy-start | bytes 12582916
  31.5 32.5 %copy-start.4 = (bf16[8,256,128]{2,1,0:T(8,128)(2,1)S(1)}, bf16[8,256,128]{2,1,0:T(8,128)(2,1)}, u32[]{:S(2)}) copy-start(bf16[8,256,128]{2,1,0:T(8,128)(2,1)} %copy-done.3) | copy-start | bytes 1572868
  42.4 5.4 %collective-permute-start.5 = (bf16[48,512]{1,0:T(8,128)(2,1)S(1)}, bf16[48,512]{1,0:T(8,128)(2,1)S(1)}, u32[]{:S(2)}, u32[]{:S(2)}) collective-permute-start(bf16[48,512]{1,0:T(8,128)(2,1)S(1)} %table_piece.1.refs_0_), channel_id=1, source_target_pairs={{0,16},{16,32},{32,48},{48,64},{64,80},{80,96},{96,112},{112,0},{1... | collective-permute-start | bytes 147464 | tf_op jit(solution)/shard_map/ppermute | solution.py:23
  44.7 4.5 %collective-permute-start.9 = (bf16[48,512]{1,0:T(8,128)(2,1)S(1)}, bf16[48,512]{1,0:T(8,128)(2,1)S(1)}, u32[]{:S(2)}, u32[]{:S(2)}) collective-permute-start(bf16[48,512]{1,0:T(8,128)(2,1)S(1)} %table_piece.1.refs_0_), channel_id=1, source_target_pairs={{0,112},{16,0},{32,16},{48,32},{64,48},{80,64},{96,80},{112,96},{1... | collective-permute-start | bytes 147464 | tf_op jit(solution)/shard_map/ppermute | solution.py:23
  47.8 5.3 %collective-permute-start.6 = (bf16[48,512]{1,0:T(8,128)(2,1)S(1)}, bf16[48,512]{1,0:T(8,128)(2,1)S(1)}, u32[]{:S(2)}, u32[]{:S(2)}) collective-permute-start(bf16[48,512]{1,0:T(8,128)(2,1)S(1)} %collective-permute-done.5.refs_1_), channel_id=1, source_target_pairs={{0,16},{16,32},{32,48},{48,64},{64,80},{80,96},{96,112},{112,0},{1... | collective-permute-start | bytes 147464 | tf_op jit(solution)/shard_map/ppermute | solution.py:23
  49.1 6.0 %collective-permute-start.10 = (bf16[48,512]{1,0:T(8,128)(2,1)S(1)}, bf16[48,512]{1,0:T(8,128)(2,1)S(1)}, u32[]{:S(2)}, u32[]{:S(2)}) collective-permute-start(bf16[48,512]{1,0:T(8,128)(2,1)S(1)} %collective-permute-done.9.refs_7_), channel_id=1, source_target_pairs={{0,112},{16,0},{32,16},{48,32},{64,48},{80,64},{96,80},{112,96},{1... | collective-permute-start | bytes 147464 | tf_op jit(solution)/shard_map/ppermute | solution.py:23
  53.1 5.7 %collective-permute-start.7 = (bf16[48,512]{1,0:T(8,128)(2,1)S(1)}, bf16[48,512]{1,0:T(8,128)(2,1)S(1)}, u32[]{:S(2)}, u32[]{:S(2)}) collective-permute-start(bf16[48,512]{1,0:T(8,128)(2,1)S(1)} %collective-permute-done.6.refs_2_), channel_id=1, source_target_pairs={{0,16},{16,32},{32,48},{48,64},{64,80},{80,96},{96,112},{112,0},{1... | collective-permute-start | bytes 147464 | tf_op jit(solution)/shard_map/ppermute | solution.py:23
  55.1 4.8 %collective-permute-start.11 = (bf16[48,512]{1,0:T(8,128)(2,1)S(1)}, bf16[48,512]{1,0:T(8,128)(2,1)S(1)}, u32[]{:S(2)}, u32[]{:S(2)}) collective-permute-start(bf16[48,512]{1,0:T(8,128)(2,1)S(1)} %collective-permute-done.10.refs_6_), channel_id=1, source_target_pairs={{0,112},{16,0},{32,16},{48,32},{64,48},{80,64},{96,80},{112,96},{1... | collective-permute-start | bytes 147464 | tf_op jit(solution)/shard_map/ppermute | solution.py:23
  58.8 5.3 %collective-permute-start.8 = (bf16[48,512]{1,0:T(8,128)(2,1)S(1)}, bf16[48,512]{1,0:T(8,128)(2,1)S(1)}, u32[]{:S(2)}, u32[]{:S(2)}) collective-permute-start(bf16[48,512]{1,0:T(8,128)(2,1)S(1)} %collective-permute-done.7.refs_3_), channel_id=1, source_target_pairs={{0,16},{16,32},{32,48},{48,64},{64,80},{80,96},{96,112},{112,0},{1... | collective-permute-start | bytes 147464 | tf_op jit(solution)/shard_map/ppermute | solution.py:23
